TPU v7x, 32 devices: a whole 2x2x4 slice. The times are simulated.
32 devices in a mesh: dp: 8 (over y, x, core), mp: 4 (over z).
Axes of the slice: x: 2, y: 2, z: 4, core: 2. Of those that a mesh axis runs over, the one named last changes fastest.
Arguments:
- tokens: bfloat16 [8192, 1024], P('dp'), may hold values from -30 to 30
- query_key_value_weight: bfloat16 [1024, 3072], P(None, 'mp'), may hold values from -0.1875 to 0.1875
- adapter_down_weight: bfloat16 [1024, 512], P(None, 'mp'), may hold values from -0.1875 to 0.1875
- adapter_up_weight: bfloat16 [512, 3072], P('mp'), may hold values from -0.75 to 0.75
- attention_out_weight: bfloat16 [1024, 1024], P('mp'), may hold values from -0.1875 to 0.1875
- first_norm_gain: float32 [1024], replicated, may hold values from 0.5 to 1.5
- first_norm_bias: float32 [1024], replicated, may hold values from -3 to 3
- first_feed_weight: bfloat16 [1024, 4096], P(None, 'mp'), may hold values from -0.1875 to 0.1875
- first_feed_bias: float32 [4096], P('mp'), may hold values from -3 to 3
- second_feed_weight: bfloat16 [4096, 1024], P('mp'), may hold values from -0.09375 to 0.09375
- second_feed_bias: float32 [1024], replicated, may hold values from -3 to 3
- second_norm_gain: float32 [1024], replicated, may hold values from 0.5 to 1.5
- second_norm_bias: float32 [1024], replicated, may hold values from -3 to 3
- following_qkv_weight: bfloat16 [1024, 3072], P(None, 'mp'), may hold values from -0.1875 to 0.1875
- following_bias: float32 [3072], P('mp'), may hold values from -3 to 3
- request_page_count: int32 [4], replicated, may hold values from 1 to 32, 64 in all
- page_slot_table: int32 [64], replicated, may hold values from 0 to 63, each once
- request_adapter: int32 [4], replicated, may hold values from 0 to 31, as said below
Outputs:
- layer_out: bfloat16 [8192, 1024], P(('dp', 'mp'))
- next_qkv: bfloat16 [8192, 3072], P('dp', 'mp')
Inputs may be any that keep to these rules, and one draw needn't show every extreme that they name: `request_page_count`: the counts sum to 64; the longest request has exactly 32 pages. `page_slot_table`: names every page slot once. `request_adapter`: exactly min(16, 4) distinct adapters are named, adapters 0 and 31 among them; of the 8 adapters held by one index of mp at most 1 are named, and some index holds exactly 1 named ones.
All inputs are finite; a program needn't handle non-finite values.
Results may differ from a plain program's by a relative error of at most 0.015.
Values may be sent and summed in bfloat16 or wider, within the bound.
No kernel may reach another device: no remote copies, remote signals or barrier semaphores. Data moves between devices by JAX's collectives and lax.ppermute only.
A program may use at most 64 MiB of HBM per device.

v0:
```python
import math

import jax
import jax.numpy as jnp
from jax import lax
from jax.sharding import PartitionSpec as P

HEAD_DIM = 64
ADAPTER_RANK = 16
PAGE = 128


def request_slots(request_page_count, page_slot_table):
    slot_total = page_slot_table.shape[0]
    page_ends = jnp.cumsum(request_page_count)
    logical = jnp.arange(slot_total, dtype=jnp.int32)
    request_of = jnp.sum((logical[:, None] >= page_ends[None, :]).astype(jnp.int32), axis=1)
    matched = (page_slot_table[:, None] == logical[None, :]).astype(jnp.int32)
    return jnp.sum(matched * request_of[:, None], axis=0)


def layer_norm(values, gain_row, bias_row):
    average = jnp.mean(values, axis=-1, keepdims=True)
    centered = values - average
    variance = jnp.mean(centered * centered, axis=-1, keepdims=True)
    return centered * lax.rsqrt(variance + 1e-05) * gain_row + bias_row


def local(
    tokens,
    query_key_value_weight,
    adapter_down_weight,
    adapter_up_weight,
    attention_out_weight,
    first_norm_gain,
    first_norm_bias,
    first_feed_weight,
    first_feed_bias,
    second_feed_weight,
    second_feed_bias,
    second_norm_gain,
    second_norm_bias,
    following_qkv_weight,
    following_bias,
    request_page_count,
    page_slot_table,
    request_adapter,
):
    tok_rows = tokens.shape[0]
    mp_count = lax.axis_size("mp")
    dp_index = lax.axis_index("dp")
    mp_index = lax.axis_index("mp")
    kept_values = adapter_down_weight.shape[1] // ADAPTER_RANK
    adapter_count = kept_values * mp_count
    request_count = request_page_count.shape[0]
    slot_req = request_slots(request_page_count, page_slot_table)
    all_req = jnp.repeat(slot_req, PAGE, total_repeat_length=slot_req.shape[0] * PAGE)
    own_req = lax.dynamic_slice_in_dim(all_req, dp_index * tok_rows, tok_rows, 0)
    req_match = (own_req[:, None] == jnp.arange(request_count, dtype=jnp.int32)[None, :]).astype(
        jnp.int32
    )
    tok_adapter = jnp.sum(req_match * request_adapter[None, :], axis=1)
    grid_positions = jnp.dot(
        tokens,
        lax.all_gather(adapter_down_weight, "mp", axis=1, tiled=True),
        preferred_element_type=jnp.float32,
    )
    chosen = (tok_adapter[:, None] == jnp.arange(adapter_count, dtype=jnp.int32)[None, :]).astype(
        jnp.float32
    )
    low_rank = jnp.sum(
        grid_positions.reshape(tok_rows, adapter_count, ADAPTER_RANK) * chosen[:, :, None], axis=1
    )
    low_rank = low_rank.astype(jnp.bfloat16)
    upward_columns = lax.all_to_all(
        adapter_up_weight, "mp", split_axis=1, concat_axis=0, tiled=True
    )
    one_hot = tok_adapter[:, None] == jnp.arange(adapter_count, dtype=jnp.int32)[None, :]
    widened_rows = jnp.where(
        one_hot[:, :, None], low_rank[:, None, :], jnp.zeros((), jnp.bfloat16)
    ).reshape(tok_rows, adapter_count * ADAPTER_RANK)
    projected_rows = (
        jnp.dot(tokens, query_key_value_weight, preferred_element_type=jnp.float32)
        + jnp.dot(widened_rows, upward_columns, preferred_element_type=jnp.float32)
    ).astype(jnp.bfloat16)
    heads_dev = projected_rows.shape[1] // (3 * HEAD_DIM)
    per_head = projected_rows.reshape(tok_rows, heads_dev, 3, HEAD_DIM)
    queries = per_head[:, :, 0]
    key_value = per_head[:, :, 1:].reshape(tok_rows, heads_dev * 2 * HEAD_DIM)
    score_scale = HEAD_DIM ** (-0.5)

    def absorb_block(carry, portion, offset):
        running_max, denominator, numerator = carry
        length = portion.shape[0]
        split_rows = portion.reshape(length, heads_dev, 2, HEAD_DIM)
        key_block = split_rows[:, :, 0]
        value_block = split_rows[:, :, 1]
        key_req = lax.dynamic_slice_in_dim(all_req, offset, length, 0)
        allowed = (own_req[:, None] == key_req[None, :])[None]
        scores = (
            jnp.einsum("qhe,khe->hqk", queries, key_block, preferred_element_type=jnp.float32)
            * score_scale
        )
        block_max = jnp.max(jnp.where(allowed, scores, jnp.float32(-1e30)), axis=2)
        fresh_max = jnp.maximum(running_max, block_max)
        weights = jnp.where(allowed, jnp.exp(scores - fresh_max[:, :, None]), jnp.float32(0.0))
        shrink = jnp.exp(running_max - fresh_max)
        denominator = denominator * shrink + jnp.sum(weights, axis=2)
        numerator = numerator * shrink[:, :, None] + jnp.einsum(
            "hqk,khe->hqe",
            weights.astype(jnp.bfloat16),
            value_block,
            preferred_element_type=jnp.float32,
        )
        return (fresh_max, denominator, numerator)

    start_carry = (
        jnp.full((heads_dev, tok_rows), -1e30, jnp.float32),
        jnp.zeros((heads_dev, tok_rows), jnp.float32),
        jnp.zeros((heads_dev, tok_rows, HEAD_DIM), jnp.float32),
    )
    portion = lax.all_gather(key_value, "dp", axis=0, tiled=True)
    length = portion.shape[0]
    block_rows = math.gcd(length, 1024)

    def visit(block_index, inner):
        sub_rows = lax.dynamic_slice_in_dim(portion, block_index * block_rows, block_rows, 0)
        return absorb_block(inner, sub_rows, block_index * block_rows)

    final_max, denominator, numerator = lax.fori_loop(0, length // block_rows, visit, start_carry)
    context = (
        jnp.transpose(numerator / denominator[:, :, None], (1, 0, 2))
        .reshape(tok_rows, heads_dev * HEAD_DIM)
        .astype(jnp.bfloat16)
    )
    share_rows = tok_rows // mp_count
    row_base = mp_index * share_rows
    mixed = lax.psum(
        jnp.dot(context, attention_out_weight, preferred_element_type=jnp.float32).astype(
            jnp.bfloat16
        ),
        "mp",
    ).astype(jnp.float32)
    normed = layer_norm(
        tokens.astype(jnp.float32) + mixed, first_norm_gain, first_norm_bias
    ).astype(jnp.bfloat16)
    hidden = jax.nn.gelu(
        jnp.dot(normed, first_feed_weight, preferred_element_type=jnp.float32) + first_feed_bias,
        approximate=False,
    ).astype(jnp.bfloat16)
    feed = lax.psum(
        jnp.dot(hidden, second_feed_weight, preferred_element_type=jnp.float32).astype(
            jnp.bfloat16
        ),
        "mp",
    ).astype(jnp.float32)
    layer_full = layer_norm(
        normed.astype(jnp.float32) + feed + second_feed_bias, second_norm_gain, second_norm_bias
    ).astype(jnp.bfloat16)
    next_proj = (
        jnp.dot(layer_full, following_qkv_weight, preferred_element_type=jnp.float32)
        + following_bias
    ).astype(jnp.bfloat16)
    layer_rows = lax.dynamic_slice_in_dim(layer_full, row_base, share_rows, 0)
    return (layer_rows, next_proj)


def solution(mesh):
    placed = (
        P("dp", None),
        P(None, "mp"),
        P(None, "mp"),
        P("mp", None),
        P("mp", None),
        P(),
        P(),
        P(None, "mp"),
        P("mp"),
        P("mp", None),
        P(),
        P(),
        P(),
        P(None, "mp"),
        P("mp"),
        P(),
        P(),
        P(),
    )
    return jax.shard_map(
        local,
        mesh=mesh,
        in_specs=placed,
        out_specs=(P(("dp", "mp"), None), P("dp", "mp")),
        check_vma=False,
    )
```

profile of v0, /device:TPU:0, one launch (start us, length us, event | category | flops | bytes accessed | tf_op | source)
XLA Modules:
  0.0 462.3 jit_solution(4038813248734956425)
XLA Ops:
  10.2 6.3 %all-to-all-start = ((bf16[128,4,768]{0,2,1:T(8,128)(2,1)}), bf16[128,4,768]{0,2,1:T(8,128)(2,1)S(1)}, u32[]{:S(2)}, u32[]{:S(2)}) async-start(bf16[128,4,768]{0,2,1:T(8,128)(2,1)} %bitcast.154), calls=%async_computation | async-start | bytes 1572864 | tf_op jit(solution)/shard_map/all_to_all | solution.py:75
  19.6 4.5 compare_select_fusion.1
  24.1 5.8 %compare_reduce_fusion.56 = (pred[8192]{0:T(1024)(128)(4,1)S(1)}, pred[8192]{0:T(1024)(128)(4,1)S(1)}, pred[8192]{0:T(1024)(128)(4,1)S(1)}, pred[8192]{0:T(1024)...) fusion(s32[8192,1]{0,1:T(1,128)S(1)} %get-tuple-element.259), kind=kLoop, calls=%fused_computation.118 | loop fusion | flops 466944 | bytes 499712 | tf_op jit(solution)/shard_map/jit(_take)/gather | solution.py:57
  31.4 36.0 %select_select_fusion = s32[8192]{0:T(1024)S(1)} fusion(pred[8192]{0:T(1024)(128)(4,1)S(1)} %get-tuple-element.239, pred[8192]{0:T(1024)(128)(4,1)S(1)} %get-tuple-element.238, pred[8192]{0:T(1024)(128)(4,1)S(1)} %get-tuple-element.237, pred[8192]{0:T(1024)(128)(4,1)S(1)} %get-tuple-element.236, pred[8192]{0:T(1024)(128)(4,1)S(1)} %get-tuple-element.235, ...), kind=kLoop, calls=%fused_computation.126 | loop fusion | flops 540672 | bytes 532708 | tf_op jit(solution)/shard_map/jit(_take)/select_n | solution.py:57
  67.5 5.6 %fusion.72 = f32[1024,768]{0,1:T(8,128)} fusion(bf16[1024,1024]{1,0:T(8,128)(2,1)} %param.22, bf16[1024,768]{1,0:T(8,128)(2,1)} %param.23), kind=kOutput, calls=%fused_computation.176 | convolution fusion | flops 1610612736 | bytes 6815744 | tf_op jit(solution)/shard_map/dot_general | solution.py:83
  84.7 54.1 %all-gather.5.cloned.1.call-done = bf16[8192,512]{0,1:T(8,128)(2,1)} async-done(((bf16[1024,512]{0,1:T(8,128)(2,1)}), bf16[8192,512]{0,1:T(8,128)(2,1)}) %all-gather.5.cloned.1.call-update) | async-done | bytes 8388624 | tf_op jit(solution)/shard_map/all_gather | solution.py:122
  138.8 109.0 %while.19 = (s32[]{:T(128)}, f32[4,1024]{1,0:T(4,128)S(1)}, f32[4,1024]{1,0:T(4,128)S(1)}, f32[4,1024,64]{1,2,0:T(8,128)S(1)}, s32[1024]{0:T(1024)S(1)}, /*index...) while((s32[]{:T(128)}, f32[4,1024]{1,0:T(4,128)S(1)}, ...), condition=%wide.region_8.9_spmd.clone, body=%wide.region_5.8_spmd.clone.sunk | while | flops 1121734656 | bytes 60571836 | solution.py:130
  140.8 4.1 fusion.96
  144.8 3.7 fusion.97
  148.5 3.8 fusion.99
  154.4 4.1 fusion.96
  158.5 3.7 fusion.97
  162.2 3.8 fusion.99
  168.0 4.1 fusion.96
  172.1 3.7 fusion.97
  175.8 3.8 fusion.99
  181.6 4.1 fusion.96
  185.7 3.7 fusion.97
  189.4 3.8 fusion.99
  195.3 4.1 fusion.96
  199.3 3.7 fusion.97
  203.0 3.8 fusion.99
  208.9 4.1 fusion.96
  213.0 3.7 fusion.97
  216.7 3.8 fusion.99
  222.5 4.1 fusion.96
  230.3 3.8 fusion.99
  236.1 4.1 fusion.96
  243.9 3.8 fusion.99
  251.1 86.6 %all-reduce.3.cloned.1.call-done = bf16[1024,1024]{1,0:T(8,128)(2,1)} async-done(((bf16[1024,1024]{1,0:T(8,128)(2,1)}), bf16[1024,1024]{1,0:T(8,128)(2,1)}) %all-reduce.3.cloned.1.call-update) | async-done | bytes 2097168 | tf_op jit(solution)/shard_map/psum | solution.py:138
  344.5 15.8 %fusion.32 = bf16[1024,1024]{1,0:T(8,128)(2,1)} fusion(bf16[1024,1024]{1,0:T(8,128)(2,1)S(1)} %copy-done, f32[1024]{0:T(1024)S(1)} %copy-done.15, bf16[1024,1024]{1,0:T(8,128)(2,1)} %add_convert_fusion.1, bf16[1024,1024]{1,0:T(8,128)(2,1)} %param.29), kind=kOutput, calls=%fused_computation.56 | convolution fusion | flops 4365221888 | bytes 8392704 | tf_op jit(solution)/shard_map/dot_general | solution.py:152
  360.3 85.6 %all-reduce.5.cloned.1.call-done = bf16[1024,1024]{1,0:T(8,128)(2,1)} async-done(((bf16[1024,1024]{1,0:T(8,128)(2,1)}), bf16[1024,1024]{1,0:T(8,128)(2,1)}) %all-reduce.5.cloned.1.call-update) | async-done | bytes 2097168 | tf_op jit(solution)/shard_map/psum | solution.py:151
  (131 shorter events, 62.4 us)
Async XLA Ops:
  7.2 337.3 %copy-start = (bf16[1024,1024]{1,0:T(8,128)(2,1)S(1)}, bf16[1024,1024]{1,0:T(8,128)(2,1)}, u32[]{:S(2)}) copy-start(bf16[1024,1024]{1,0:T(8,128)(2,1)} %param.31) | copy-start | bytes 6291460
  7.2 60.2 %copy-start.13 = (s32[4]{0:T(128)S(1)}, s32[4]{0:T(128)}, u32[]{:S(2)}) copy-start(s32[4]{0:T(128)} %param.39) | copy-start | bytes 52
  7.2 68.2 %all-gather.3.cloned.1.call-start = ((), (), s32[]{:S(2)}) async-start(), calls=%async_computation.1 | async-start | bytes 1310720 | tf_op jit(solution)/shard_map/all_gather | solution.py:65
  10.2 62.9 %all-to-all-start = ((bf16[128,4,768]{0,2,1:T(8,128)(2,1)}), bf16[128,4,768]{0,2,1:T(8,128)(2,1)S(1)}, u32[]{:S(2)}, u32[]{:S(2)}) async-start(bf16[128,4,768]{0,2,1:T(8,128)(2,1)} %bitcast.154), calls=%async_computation | async-start | bytes 1572864 | tf_op jit(solution)/shard_map/all_to_all | solution.py:75
  16.5 122.3 %all-gather.5.cloned.1.call-start = ((), (), s32[]{:S(2)}) async-start(), calls=%async_computation.2 | async-start | bytes 9437184 | tf_op jit(solution)/shard_map/all_gather | solution.py:122
  73.1 0.9 copy-start.7
  75.4 3.8 copy-start.6
  80.3 1.1 copy-start.5
  82.8 254.9 %all-reduce.3.cloned.1.call-start = ((), (), s32[]{:S(2)}) async-start(), calls=%async_computation.3 | async-start | bytes 4194304 | tf_op jit(solution)/shard_map/psum | solution.py:138
  251.0 91.1 %copy-start.9 = (f32[1024]{0:T(1024)S(1)}, f32[1024]{0:T(1024)}, u32[]{:S(2)}) copy-start(f32[1024]{0:T(1024)} %param.28) | copy-start | bytes 12292
  251.0 91.1 %copy-start.10 = (f32[1024]{0:T(1024)S(1)}, f32[1024]{0:T(1024)}, u32[]{:S(2)}) copy-start(f32[1024]{0:T(1024)} %param.27) | copy-start | bytes 12292
  251.0 194.9 %all-reduce.5.cloned.1.call-start = ((), (), s32[]{:S(2)}) async-start(), calls=%async_computation.4 | async-start | bytes 4194304 | tf_op jit(solution)/shard_map/psum | solution.py:151
  337.6 3.0 copy-start.2
  337.6 3.5 copy-start.3
  342.0 2.4 copy-start.15
  344.5 101.4 %copy-start.8 = (f32[1024]{0:T(1024)S(1)}, f32[1024]{0:T(1024)}, u32[]{:S(2)}) copy-start(f32[1024]{0:T(1024)} %param.32) | copy-start | bytes 12292
  360.3 90.2 %copy-start.11 = (f32[1024]{0:T(1024)S(1)}, f32[1024]{0:T(1024)}, u32[]{:S(2)}) copy-start(f32[1024]{0:T(1024)} %param.34) | copy-start | bytes 12292
  360.3 90.2 %copy-start.12 = (f32[1024]{0:T(1024)S(1)}, f32[1024]{0:T(1024)}, u32[]{:S(2)}) copy-start(f32[1024]{0:T(1024)} %param.33) | copy-start | bytes 12292
  445.9 3.1 copy-start.1
  445.9 3.5 copy-start.4
  450.4 2.4 copy-start.14
  450.4 2.4 copy-start.16
Sparse Core Ops, SparseCore 0:
  9.6 44.6 all-gather.2
  82.9 55.8 all-gather.4
  251.1 86.4 all-reduce.2
  360.4 85.4 all-reduce.4
where the time goes:
time: 464 us; the launch traced here: 462 us
  waiting for transfers between devices  227 us (49%)
  other arithmetic  95.4 us (21%)
  matrix products  94.8 us (20%)
  local copies, waits for them, and re-layouts  24 us (5%)
  between operations  14.1 us (3%)
  starting transfers between devices  6.44 us (1%)
    psum x1, waiting for transfers between devices, local(): lax.psum(jnp.dot(context, attention_out_weight, preferred_element_type=jn...  86.6 us
    psum x1, waiting for transfers between devices, local(): lax.psum(jnp.dot(hidden, second_feed_weight, preferred_element_type=jnp.f...  85.6 us
    all_gather x1, waiting for transfers between devices, local(): portion = lax.all_gather(key_value, 'dp', axis=0, tiled=True)  54.1 us
    select_n x1, other arithmetic, local(): jnp.repeat(slot_req, PAGE, total_repeat_length=slot_req.shape[0] * PAGE)  36 us
    dot_general x8, matrix products, absorb_block(): jnp.einsum('qhe,khe->hqk', queries, key_block, preferred_element_type=jnp...  32.6 us
    dot_general x8, matrix products, absorb_block(): jnp.einsum('hqk,khe->hqe', weights.astype(jnp.bfloat16), value_block, pre...  30.5 us
    reduce_sum x8, other arithmetic, absorb_block(): denominator = denominator * shrink + jnp.sum(weights, axis=2)  29.3 us
    dot_general x1, matrix products, local(): jnp.dot(hidden, second_feed_weight, preferred_element_type=jnp.float32)  15.8 us
  transfers between devices with their start and end apart: 5, of which 3 were waited for; matrix products, arithmetic and copies ran while one was open for 13% of the time, Pallas kernels for 0%

commit v1 on v0

v1 whole, which is shorter than its diff:
```python
import functools
import math

import jax
import jax.numpy as jnp
from jax import lax
from jax.experimental import pallas as pl
from jax.experimental.pallas import tpu as pltpu
from jax.sharding import PartitionSpec as P

HEAD_DIM = 64
ADAPTER_RANK = 16
PAGE = 128
PAIR = 2 * HEAD_DIM
NEG = -1e30
EXP_SCALE = math.log2(math.e) * HEAD_DIM**-0.5
MIB = 1 << 20


def params(vmem=48):
    return pltpu.CompilerParams(
        dimension_semantics=("arbitrary",), vmem_limit_bytes=vmem * MIB
    )


def request_of(k, counts, requests):
    end = counts[0]
    request = (k >= end).astype(jnp.int32)
    for r in range(1, requests - 1):
        end = end + counts[r]
        request = request + (k >= end).astype(jnp.int32)
    return request


def normalize(values, gain_row, bias_row):
    average = jnp.mean(values, axis=-1, keepdims=True)
    centered = values - average
    variance = jnp.mean(centered * centered, axis=-1, keepdims=True)
    return centered * lax.rsqrt(variance + 1e-05) * gain_row + bias_row


def project_kernel(
    counts, table, owners, bases, x_ref, w_ref, down_ref, up_ref, q_ref, kv_ref, page_owner,
    *, requests, slots, pages, per_piece,
):
    step = pl.program_id(0)

    @pl.when(step == 0)
    def _():
        def fill(k, carry):
            page_owner[table[k]] = owners[request_of(k, counts, requests)]
            return carry

        lax.fori_loop(0, slots, fill, 0)

    x = x_ref[...]
    low = jnp.dot(x, down_ref[...], preferred_element_type=jnp.float32)
    lane_owner = lax.broadcasted_iota(jnp.int32, (PAGE, low.shape[1]), 1) // ADAPTER_RANK
    kept = []
    for p in range(pages):
        page = step * pages + p
        slot = bases[page // per_piece] + page % per_piece
        kept.append(
            jnp.where(lane_owner == page_owner[slot], low[p * PAGE : (p + 1) * PAGE], 0.0)
        )
    low_rank = jnp.concatenate(kept, axis=0).astype(jnp.bfloat16)
    rows = jnp.dot(x, w_ref[...], preferred_element_type=jnp.float32) + jnp.dot(
        low_rank, up_ref[...], preferred_element_type=jnp.float32
    )
    rows = rows.astype(jnp.bfloat16)
    q_cols = q_ref.shape[1]
    q_ref[...] = rows[:, :q_cols]
    kv_ref[...] = rows[:, q_cols:]


def project(counts, table, owners, bases, x, weight, down, up, per_piece):
    tok, width = x.shape
    cols = weight.shape[1]
    pages = 2
    block = pages * PAGE
    slots = table.shape[0]
    whole = lambda i, *_: (0, 0)
    rows = lambda i, *_: (i, 0)
    return pl.pallas_call(
        functools.partial(
            project_kernel,
            requests=counts.shape[0], slots=slots, pages=pages, per_piece=per_piece,
        ),
        grid_spec=pltpu.PrefetchScalarGridSpec(
            num_scalar_prefetch=4,
            grid=(tok // block,),
            in_specs=[
                pl.BlockSpec((block, width), rows),
                pl.BlockSpec(weight.shape, whole),
                pl.BlockSpec(down.shape, whole),
                pl.BlockSpec(up.shape, whole),
            ],
            out_specs=[
                pl.BlockSpec((block, cols // 3), rows),
                pl.BlockSpec((block, 2 * cols // 3), rows),
            ],
            scratch_shapes=[pltpu.SMEM((slots,), jnp.int32)],
        ),
        out_shape=[
            jax.ShapeDtypeStruct((tok, cols // 3), jnp.bfloat16),
            jax.ShapeDtypeStruct((tok, 2 * cols // 3), jnp.bfloat16),
        ],
        compiler_params=params(),
        cost_estimate=pl.CostEstimate(
            flops=2 * tok * width * cols, bytes_accessed=2 * tok * (width + cols), transcendentals=0
        ),
        name="project",
    )(counts, table, owners, bases, x, weight, down, up)


def attend_kernel(
    counts, table, q_bases, kv_bases, q_ref, *refs,
    requests, slots, q_per_piece, sizes, first, last, group,
):
    refs = list(refs)
    kv_hbm = [refs.pop(0) for _ in sizes]
    if not first:
        acc_in, stat_in = refs.pop(0), refs.pop(0)
    if last:
        out_ref = refs.pop(0)
    else:
        acc_out, stat_out = refs.pop(0), refs.pop(0)
    kv, scores, listed, amount, page_req, sems = refs
    step = pl.program_id(0)

    @pl.when(step == 0)
    def _():
        copies = []
        offset = 0
        for i, size in enumerate(sizes):
            copy = pltpu.make_async_copy(
                kv_hbm[i], kv.at[pl.ds(offset * PAGE, size * PAGE)], sems.at[i]
            )
            copy.start()
            copies.append(copy)
            offset += size
        for r in range(requests):
            amount[r] = 0

        def clear(k, carry):
            for r in range(requests):
                listed[r, k] = 0
            return carry

        lax.fori_loop(0, sum(sizes) + group, clear, 0)

        def fill(k, carry):
            r = request_of(k, counts, requests)
            slot = table[k]
            page_req[slot] = r
            place = jnp.int32(-1)
            offset = 0
            for i, size in enumerate(sizes):
                local = slot - kv_bases[i]
                place = jnp.where((local >= 0) & (local < size), local + offset, place)
                offset += size
            n = amount[r]

            @pl.when(place >= 0)
            def _():
                listed[r, n] = place
                amount[r] = n + 1

            return carry

        lax.fori_loop(0, slots, fill, 0)
        for copy in copies:
            copy.wait()

    slot = q_bases[step // q_per_piece] + step % q_per_piece
    r = page_req[slot]
    n = amount[r]
    blocks = (n + group - 1) // group
    q = q_ref[...]
    lane = lax.broadcasted_iota(jnp.int32, (PAGE, PAIR), 1)
    zero = jnp.zeros_like(q)
    both = jnp.concatenate(
        [jnp.where(lane < HEAD_DIM, q, zero), jnp.where(lane < HEAD_DIM, zero, q)], axis=0
    )
    rows = 2 * PAGE

    def pages_of(j, low):
        parts = []
        for i in range(group):
            at = pl.multiple_of(listed[r, j * group + i] * PAGE, PAGE)
            parts.append(kv[pl.ds(at, PAGE), low : low + PAIR])
        return jnp.concatenate(parts, axis=0)

    def score(j, top):
        s = lax.dot_general(
            both, pages_of(j, 0), (((1,), (1,)), ((), ())), preferred_element_type=jnp.float32
        )
        for i in range(group):
            piece = s[:, i * PAGE : (i + 1) * PAGE]
            piece = jnp.where(j * group + i < n, piece, NEG)
            scores[j, :, i * PAGE : (i + 1) * PAGE] = piece
            top = jnp.maximum(top, piece)
        return top

    top = lax.fori_loop(0, blocks, score, jnp.full((rows, PAGE), NEG, jnp.float32))
    peak = jnp.max(top, axis=1, keepdims=True)
    if not first:
        old_peak = stat_in[:, 0:1]
        peak = jnp.maximum(peak, old_peak)
    shift = peak * EXP_SCALE

    def weigh(j, carry):
        total, acc = carry
        w = jnp.exp2(scores[j] * EXP_SCALE - shift)
        for i in range(group):
            total = total + w[:, i * PAGE : (i + 1) * PAGE]
        acc = acc + jnp.dot(
            w.astype(jnp.bfloat16), pages_of(j, PAIR), preferred_element_type=jnp.float32
        )
        return total, acc

    total, acc = lax.fori_loop(
        0, blocks, weigh,
        (jnp.zeros((rows, PAGE), jnp.float32), jnp.zeros((rows, PAIR), jnp.float32)),
    )
    total = jnp.sum(total, axis=1, keepdims=True)
    if not first:
        shrink = jnp.exp2((old_peak - peak) * EXP_SCALE)
        total = total + stat_in[:, 1:2] * shrink
        acc = acc + acc_in[...] * shrink
    if last:
        acc = acc / total
        out_ref[...] = jnp.where(lane < HEAD_DIM, acc[:PAGE], acc[PAGE:]).astype(jnp.bfloat16)
    else:
        acc_out[...] = acc
        wide = lax.broadcasted_iota(jnp.int32, (rows, PAGE), 1)
        stat_out[...] = jnp.where(wide == 0, peak, total)


def attend(counts, table, q_bases, kv_bases, q, pieces, state, last, q_per_piece):
    tok = q.shape[0]
    sizes = tuple(p.shape[0] // PAGE for p in pieces)
    first = state is None
    group = 4
    slots = table.shape[0]
    requests = counts.shape[0]
    rows = lambda i, *_: (i, 0)
    most = min(sum(sizes), slots)
    state_specs = [pl.BlockSpec((2 * PAGE, PAIR), rows), pl.BlockSpec((2 * PAGE, PAGE), rows)]
    state_shape = [
        jax.ShapeDtypeStruct((2 * tok, PAIR), jnp.float32),
        jax.ShapeDtypeStruct((2 * tok, PAGE), jnp.float32),
    ]
    flops = 2 * tok * sum(sizes) * PAGE * PAIR
    out = pl.pallas_call(
        functools.partial(
            attend_kernel,
            requests=requests, slots=slots, q_per_piece=q_per_piece, sizes=sizes,
            first=first, last=last, group=group,
        ),
        grid_spec=pltpu.PrefetchScalarGridSpec(
            num_scalar_prefetch=4,
            grid=(tok // PAGE,),
            in_specs=[pl.BlockSpec((PAGE, PAIR), rows)]
            + [pl.BlockSpec(memory_space=pl.ANY)] * len(pieces)
            + ([] if first else state_specs),
            out_specs=[pl.BlockSpec((PAGE, PAIR), rows)] if last else state_specs,
            scratch_shapes=[
                pltpu.VMEM((sum(sizes) * PAGE, 2 * PAIR), jnp.bfloat16),
                pltpu.VMEM(((most + group - 1) // group, 2 * PAGE, group * PAGE), jnp.float32),
                pltpu.SMEM((requests, sum(sizes) + group), jnp.int32),
                pltpu.SMEM((requests,), jnp.int32),
                pltpu.SMEM((slots,), jnp.int32),
                pltpu.SemaphoreType.DMA((len(pieces),)),
            ],
        ),
        out_shape=[jax.ShapeDtypeStruct((tok, PAIR), jnp.bfloat16)] if last else state_shape,
        compiler_params=params(),
        cost_estimate=pl.CostEstimate(
            flops=flops, bytes_accessed=4 * tok * PAIR + 4 * PAGE * PAIR * sum(sizes),
            transcendentals=tok * sum(sizes) * PAGE,
        ),
        name="attend",
    )(counts, table, q_bases, kv_bases, q, *pieces, *([] if first else state))
    return out[0] if last else out


def mix_kernel(x_ref, ctx_ref, wo_ref, gain_ref, bias_ref, out_ref):
    mixed = x_ref[...].astype(jnp.float32)
    for j in range(ctx_ref.shape[0]):
        mixed = mixed + jnp.dot(ctx_ref[j], wo_ref[j], preferred_element_type=jnp.float32)
    out_ref[...] = normalize(mixed, gain_ref[...], bias_ref[...]).astype(jnp.bfloat16)


def mix(x, ctx, wo, gain, bias):
    tok, width = x.shape
    groups, _, cols = ctx.shape
    block = 256
    rows = lambda i: (i, 0)
    return pl.pallas_call(
        mix_kernel,
        grid=(tok // block,),
        in_specs=[
            pl.BlockSpec((block, width), rows),
            pl.BlockSpec((groups, block, cols), lambda i: (0, i, 0)),
            pl.BlockSpec(wo.shape, lambda i: (0, 0, 0)),
            pl.BlockSpec((1, width), lambda i: (0, 0)),
            pl.BlockSpec((1, width), lambda i: (0, 0)),
        ],
        out_specs=pl.BlockSpec((block, width), rows),
        out_shape=jax.ShapeDtypeStruct((tok, width), jnp.bfloat16),
        compiler_params=params(),
        cost_estimate=pl.CostEstimate(
            flops=2 * tok * width * groups * cols, bytes_accessed=8 * tok * width, transcendentals=0
        ),
        name="mix",
    )(x, ctx, wo, gain[None], bias[None])


def layer_norm(values, gain_row, bias_row):
    return normalize(values, gain_row, bias_row)


def local(
    tokens,
    query_key_value_weight,
    adapter_down_weight,
    adapter_up_weight,
    attention_out_weight,
    first_norm_gain,
    first_norm_bias,
    first_feed_weight,
    first_feed_bias,
    second_feed_weight,
    second_feed_bias,
    second_norm_gain,
    second_norm_bias,
    following_qkv_weight,
    following_bias,
    request_page_count,
    page_slot_table,
    request_adapter,
):
    tok_rows, width = tokens.shape
    dp_count = lax.axis_size("dp")
    mp_count = lax.axis_size("mp")
    dp_index = lax.axis_index("dp")
    mp_index = lax.axis_index("mp")
    kept_values = adapter_down_weight.shape[1] // ADAPTER_RANK
    heads_dev = query_key_value_weight.shape[1] // (3 * HEAD_DIM)
    pages = tok_rows // PAGE
    shared = dp_count == 8 and heads_dev == 4

    owners = request_adapter // kept_values
    level = jnp.sum(jnp.where(owners == mp_index, request_adapter % kept_values, 0))
    down = lax.dynamic_slice_in_dim(
        adapter_down_weight, level * ADAPTER_RANK, ADAPTER_RANK, 1
    )
    up = lax.dynamic_slice_in_dim(adapter_up_weight, level * ADAPTER_RANK, ADAPTER_RANK, 0)
    up_cols = up.shape[1] // mp_count
    sent = jnp.concatenate(
        [
            jnp.broadcast_to(down.T[:, None, :], (ADAPTER_RANK, mp_count, width)),
            up.reshape(ADAPTER_RANK, mp_count, up_cols),
        ],
        axis=2,
    ).reshape(ADAPTER_RANK, mp_count * (width + up_cols))
    got = lax.all_to_all(sent, "mp", split_axis=1, concat_axis=0, tiled=True)
    downs = got[:, :width].T
    ups = got[:, width:]

    def by_kind(matrix):
        split = matrix.reshape(matrix.shape[0], heads_dev, 3, HEAD_DIM)
        if shared:
            split = lax.dynamic_slice_in_dim(split, (dp_index % 2) * 2, 2, 1)
        return jnp.swapaxes(split, 1, 2).reshape(matrix.shape[0], -1)

    weight = by_kind(query_key_value_weight)
    ups = by_kind(ups)
    if shared:
        swap = [(i, i ^ 1) for i in range(8)]
        across = [(i, i ^ 2) for i in range(8)]
        along = [(i, i ^ 4) for i in range(8)]
        move = lambda value, pairs: lax.ppermute(value, "dp", pairs)
        x = jnp.concatenate([tokens, move(tokens, swap)], axis=0)
        at = lambda flip: (dp_index ^ flip) * pages
        bases = jnp.stack([at(0), at(1)])
    else:
        x = tokens
        bases = jnp.stack([dp_index * pages])
    args = (request_page_count, page_slot_table)
    q, kv = project(*args, owners, bases, x, weight, downs, ups, pages)
    if shared:
        kv_x = move(kv, across)
        kv_y = move(kv, along)
        kv_d0 = move(kv_y[:tok_rows], across)
        kv_d1 = move(kv_x[tok_rows:], along)
        step = functools.partial(attend, *args, bases)
        state = step(
            bases, q, [kv[:tok_rows], kv[tok_rows:]], None, False, pages
        )
        near = jnp.stack([at(2), at(3), at(4), at(5)])
        state = step(
            near, q, [kv_x[:tok_rows], kv_x[tok_rows:], kv_y[:tok_rows], kv_y[tok_rows:]],
            state, False, pages,
        )
        far = jnp.stack([at(6), at(7)])
        context = step(far, q, [kv_d0, kv_d1], state, True, pages)
        mine, theirs = context[:tok_rows], move(context[tok_rows:], swap)
        even = dp_index % 2 == 0
        context = jnp.concatenate(
            [jnp.where(even, mine, theirs), jnp.where(even, theirs, mine)], axis=1
        )
    else:
        everything = lax.all_gather(kv, "dp", axis=0, tiled=True)
        context = attend(
            *args, bases, jnp.zeros((1,), jnp.int32), q, [everything], None, True, pages
        )
    out_weight = lax.all_gather(attention_out_weight, "mp", axis=0)
    contexts = lax.all_gather(context, "mp", axis=0)
    normed = mix(tokens, contexts, out_weight, first_norm_gain, first_norm_bias)
    share_rows = tok_rows // mp_count
    row_base = mp_index * share_rows
    hidden = jax.nn.gelu(
        jnp.dot(normed, first_feed_weight, preferred_element_type=jnp.float32) + first_feed_bias,
        approximate=False,
    ).astype(jnp.bfloat16)
    feed = lax.psum(
        jnp.dot(hidden, second_feed_weight, preferred_element_type=jnp.float32).astype(
            jnp.bfloat16
        ),
        "mp",
    ).astype(jnp.float32)
    layer_full = layer_norm(
        normed.astype(jnp.float32) + feed + second_feed_bias, second_norm_gain, second_norm_bias
    ).astype(jnp.bfloat16)
    next_proj = (
        jnp.dot(layer_full, following_qkv_weight, preferred_element_type=jnp.float32)
        + following_bias
    ).astype(jnp.bfloat16)
    layer_rows = lax.dynamic_slice_in_dim(layer_full, row_base, share_rows, 0)
    return (layer_rows, next_proj)


def solution(mesh):
    placed = (
        P("dp", None),
        P(None, "mp"),
        P(None, "mp"),
        P("mp", None),
        P("mp", None),
        P(),
        P(),
        P(None, "mp"),
        P("mp"),
        P("mp", None),
        P(),
        P(),
        P(),
        P(None, "mp"),
        P("mp"),
        P(),
        P(),
        P(),
    )
    return jax.shard_map(
        local,
        mesh=mesh,
        in_specs=placed,
        out_specs=(P(("dp", "mp"), None), P("dp", "mp")),
        check_vma=False,
    )
```

time: 464 us -> 336 us (0.72)
  Pallas kernels: 0 us -> 103 us
  other arithmetic: 95.4 us -> 13.8 us
  matrix products: 94.8 us -> 18.5 us
  waiting for transfers between devices: 227 us -> 155 us
  starting transfers between devices: 6.44 us -> 12.9 us
  local copies, waits for them, and re-layouts: 24 us -> 18 us
    pallas_call x0 -> x5, Pallas kernels: none -> 103 us  [the longest x3 88.6 us: attend(): pl.pallas_call(functools.partial(attend_kernel, requests=requests, slots=...]
    psum x1 -> x0, waiting for transfers between devices: 86.6 us -> none  [local(): lax.psum(jnp.dot(context, attention_out_weight, preferred_element_type=jn...]
    dot_general x20 -> x0, matrix products: 76.1 us -> none  [the longest x8 32.6 us: absorb_block(): jnp.einsum('qhe,khe->hqk', queries, key_block, preferred_element_type=jnp...]
    select_n x2 -> x1, other arithmetic: 36.1 us -> 0.04 us  [local(): jnp.where(even, mine, theirs)]
    reduce_sum x16 -> x3, other arithmetic: 38.5 us -> 5.57 us  [the longest x1 3.12 us: normalize(): average = jnp.mean(values, axis=-1, keepdims=True)]
    ppermute x0 -> x6, waiting for transfers between devices: none -> 21.5 us  [local(): move = lambda value, pairs: lax.ppermute(value, 'dp', pairs)]
    gather x2 -> x0, other arithmetic: 10.3 us -> none  [local(): jnp.repeat(slot_req, PAGE, total_repeat_length=slot_req.shape[0] * PAGE)]
    dynamic_slice x17 -> x1, local copies, waits for them, and re-layouts: 10.5 us -> 0.91 us  [local(): lax.dynamic_slice_in_dim(adapter_up_weight, level * ADAPTER_RANK, ADAPTER...]
  transfers between devices with their start and end apart: 5 -> 10, of which waited for: 3 -> 5; matrix products, arithmetic and copies ran while one was open for 13% -> 6% of each run, Pallas kernels for 0% -> 29%
where the time goes in v1:
time: 336 us
  waiting for transfers between devices  155 us (46%)
  Pallas kernels  103 us (31%)
  matrix products  18.5 us (6%)
  local copies, waits for them, and re-layouts  18 us (5%)
  between operations  14.8 us (4%)
  other arithmetic  13.8 us (4%)
  starting transfers between devices  12.9 us (4%)
    pallas_call x3, Pallas kernels, attend(): pl.pallas_call(functools.partial(attend_kernel, requests=requests, slots=...  88.6 us
    psum x1, waiting for transfers between devices, local(): lax.psum(jnp.dot(hidden, second_feed_weight, preferred_element_type=jnp.f...  85.3 us
    all_gather x1, waiting for transfers between devices, local(): contexts = lax.all_gather(context, 'mp', axis=0)  44.9 us
    ppermute x6, waiting for transfers between devices, local(): move = lambda value, pairs: lax.ppermute(value, 'dp', pairs)  21.5 us
    dot_general x1, matrix products, local(): jnp.dot(hidden, second_feed_weight, preferred_element_type=jnp.float32)  15.6 us
    unnamed x42, local copies, waits for them, and re-layouts  9.56 us
    pallas_call x1, Pallas kernels, project(): pl.pallas_call(functools.partial(project_kernel, requests=counts.shape[0]...  8.5 us
    ppermute x6, starting transfers between devices, local(): move = lambda value, pairs: lax.ppermute(value, 'dp', pairs)  6.73 us
  transfers between devices with their start and end apart: 10, of which 5 were waited for; matrix products, arithmetic and copies ran while one was open for 6% of the time, Pallas kernels for 29%

profile of v1, /device:TPU:0, one launch (start us, length us, event | category | flops | bytes accessed | tf_op | source)
XLA Modules:
  0.0 336.3 jit_solution(9013653869749131420)
XLA Ops:
  7.7 1.4 fusion.18
  9.8 1.1 dynamic-slice_bitcast_fusion.1
  12.6 5.9 %all-to-all-start = ((bf16[16,4,1792]{2,0,1:T(8,128)(2,1)}), bf16[16,4,1792]{2,0,1:T(8,128)(2,1)S(1)}, u32[]{:S(2)}, u32[]{:S(2)}) async-start(bf16[16,4,1792]{2,0,1:T(8,128)(2,1)} %pad_maximum_fusion.2), calls=%async_computation | async-start | bytes 458752 | tf_op jit(solution)/shard_map/all_to_all | solution.py:368
  19.3 2.6 copy.29
  21.9 1.2 dynamic-slice_bitcast_fusion
  23.2 1.2 copy.35.w_ref
  24.4 2.8 all-to-all-done
  27.9 5.0 %pad_maximum_fusion.x_ref = bf16[2048,1024]{1,0:T(8,128)(2,1)} fusion(bf16[1024,1024]{1,0:T(8,128)(2,1)} %collective-permute-done, bf16[1024,1024]{1,0:T(8,128)(2,1)} %x_ref.1), kind=kLoop, calls=%fused_computation.4 | loop fusion | flops 8388608 | bytes 8388608 | tf_op jit(solution)/shard_map/concatenate | solution.py:385
  32.9 8.5 %project.1 = (bf16[2048,128]{1,0:T(8,128)(2,1)S(1)}, bf16[2048,256]{1,0:T(8,128)(2,1)S(1)}) custom-call(s32[4]{0:T(128)S(1)} %copy-done.7, s32[64]{0:T(128)S(1)} %copy-done.8, s32[4]{0:T(128)S(1)} %get-tuple-element.15.owners, s32[2]{0:T(128)S(1)} %pad_add_fusion.bases.q_bases.kv_bases, bf16[2048,1024]{1,0:T(8,128)(2,1)} %pad_maximum_fusion.x_ref, ...), custom_call_target="tpu_custom_call" | custom-call | flops 1610612736 | bytes 5767168 | tf_op jit(solution)/shard_map/project/pallas_call | solution.py:84
  42.2 1.5 collective-permute-start.1
  43.7 1.5 collective-permute-start.3
  45.3 20.0 %collective-permute-done.1 = bf16[2048,256]{1,0:T(8,128)(2,1)} collective-permute-done((bf16[2048,256]{1,0:T(8,128)(2,1)S(1)}, bf16[2048,256]{1,0:T(8,128)(2,1)}, u32[]{:S(2)}, u32[]{:S(2)}) %collective-permute-start.1) | collective-permute-done | bytes 1048608 | tf_op jit(solution)/shard_map/ppermute | solution.py:384
  65.3 1.3 fusion.50
  66.6 1.6 collective-permute-start.2
  68.2 1.3 fusion.51
  69.5 1.6 collective-permute-start.4
  71.1 23.0 %attend.3 = (f32[4096,128]{1,0:T(8,128)S(1)}, f32[4096,128]{1,0:T(8,128)S(1)}) custom-call(s32[4]{0:T(128)S(1)} %copy-done.7, s32[64]{0:T(128)S(1)} %copy-done.8, s32[2]{0:T(128)S(1)} %pad_add_fusion.bases.q_bases.kv_bases, s32[2]{0:T(128)S(1)} %pad_add_fusion.bases.q_bases.kv_bases, bf16[2048,128]{1,0:T(8,128)(2,1)S(1)} %copy-done.10, ...), custom_call_target="tpu_custom_call" | custom-call | flops 1073741824 | bytes 2097152 | tf_op jit(solution)/shard_map/attend/pallas_call | solution.py:255
  94.2 1.3 copy-done.11
  95.5 1.3 copy-done.12
  96.8 41.3 %attend.4 = (f32[4096,128]{1,0:T(8,128)S(1)}, f32[4096,128]{1,0:T(8,128)}) custom-call(s32[4]{0:T(128)S(1)} %copy-done.7, s32[64]{0:T(128)S(1)} %copy-done.8, s32[2]{0:T(128)S(1)} %pad_add_fusion.bases.q_bases.kv_bases, s32[4]{0:T(128)S(1)} %pad_add_fusion.2.kv_bases, bf16[2048,128]{1,0:T(8,128)(2,1)S(1)} %copy-done.10, ...), custom_call_target="tpu_custom_call" | custom-call | flops 2147483648 | bytes 3145728 | tf_op jit(solution)/shard_map/attend/pallas_call | solution.py:255
  138.2 24.2 %attend.5 = bf16[2048,128]{1,0:T(8,128)(2,1)S(1)} custom-call(s32[4]{0:T(128)S(1)} %copy-done.7, s32[64]{0:T(128)S(1)} %copy-done.8, s32[2]{0:T(128)S(1)} %pad_add_fusion.bases.q_bases.kv_bases, s32[2]{0:T(128)S(1)} %pad_add_fusion.1.kv_bases, bf16[2048,128]{1,0:T(8,128)(2,1)S(1)} %copy-done.10, bf16[1024,256]{1,0:T(8,128)(2,1)S(1)} %collective-permute-done.2.refs_0_, ...), custom_call_target="tpu_custom_call" | custom-call | flops 1073741824 | bytes 2097152 | tf_op jit(solution)/shard_map/attend/pallas_call | solution.py:255
  162.5 1.5 collective-permute-done.5
  165.2 44.9 %all-gather.5.cloned.1.call-done = bf16[4096,256]{1,0:T(8,128)(2,1)} async-done(((bf16[1024,256]{1,0:T(8,128)(2,1)}), bf16[4096,256]{1,0:T(8,128)(2,1)}) %all-gather.5.cloned.1.call-update) | async-done | bytes 2097168 | tf_op jit(solution)/shard_map/all_gather | solution.py:420
  210.1 1.6 copy-done.3
  211.7 5.9 %mix.1 = bf16[1024,1024]{1,0:T(8,128)(2,1)S(1)} custom-call(bf16[1024,1024]{1,0:T(8,128)(2,1)S(1)} %copy-done.3, bf16[4,1024,256]{2,1,0:T(8,128)(2,1)} %bitcast.39, bf16[4,256,1024]{2,1,0:T(8,128)(2,1)} %bitcast.38, f32[1,1024]{1,0:T(1,128)S(1)} %bitcast.34, f32[1,1024]{1,0:T(1,128)S(1)} %bitcast.35), custom_call_target="tpu_custom_call" | custom-call | flops 2147483648 | bytes 8388608 | tf_op jit(solution)/shard_map/mix/pallas_call | solution.py:300
  217.6 1.3 copy-done.1
  219.0 15.6 %fusion.15 = bf16[1024,1024]{1,0:T(8,128)(2,1)} fusion(bf16[1024,1024]{1,0:T(8,128)(2,1)S(1)} %copy-done, f32[1024]{0:T(1024)S(1)} %copy-done.18, bf16[1024,1024]{1,0:T(8,128)(2,1)} %copy-done.1, bf16[1024,1024]{1,0:T(8,128)(2,1)} %param.25), kind=kOutput, calls=%fused_computation.27 | convolution fusion | flops 4365221888 | bytes 8392704 | tf_op jit(solution)/shard_map/dot_general | solution.py:429
  234.6 85.3 %all-reduce.2.cloned.1.call-done = bf16[1024,1024]{1,0:T(8,128)(2,1)} async-done(((bf16[1024,1024]{1,0:T(8,128)(2,1)}), bf16[1024,1024]{1,0:T(8,128)(2,1)}) %all-reduce.2.cloned.1.call-update) | async-done | bytes 2097168 | tf_op jit(solution)/shard_map/psum | solution.py:428
  319.9 3.1 fusion.10
  323.4 1.0 multiply_reduce_fusion
  324.5 1.5 add_convert_fusion
  326.9 2.9 add_convert_fusion.1
  (72 shorter events, 7.3 us)
Async XLA Ops:
  7.2 211.8 %copy-start = (bf16[1024,1024]{1,0:T(8,128)(2,1)S(1)}, bf16[1024,1024]{1,0:T(8,128)(2,1)}, u32[]{:S(2)}) copy-start(bf16[1024,1024]{1,0:T(8,128)(2,1)} %param.27) | copy-start | bytes 6291460
  7.2 20.7 %collective-permute-start = (bf16[1024,1024]{1,0:T(8,128)(2,1)}, bf16[1024,1024]{1,0:T(8,128)(2,1)}, u32[]{:S(2)}, u32[]{:S(2)}) collective-permute-start(bf16[1024,1024]{1,0:T(8,128)(2,1)} %x_ref.1), channel_id=1, source_target_pairs={{0,4},{4,0},{8,12},{12,8},{16,20},{20,16},{24,28},{28,24},{1,5},{5... | collective-permute-start | bytes 6291464 | tf_op jit(solution)/shard_map/ppermute | solution.py:384
  12.6 14.6 %all-to-all-start = ((bf16[16,4,1792]{2,0,1:T(8,128)(2,1)}), bf16[16,4,1792]{2,0,1:T(8,128)(2,1)S(1)}, u32[]{:S(2)}, u32[]{:S(2)}) async-start(bf16[16,4,1792]{2,0,1:T(8,128)(2,1)} %pad_maximum_fusion.2), calls=%async_computation | async-start | bytes 458752 | tf_op jit(solution)/shard_map/all_to_all | solution.py:368
  18.5 146.7 %all-gather.7.cloned.1.call-start = ((), (), s32[]{:S(2)}) async-start(), calls=%async_computation.3 | async-start | bytes 2621440 | tf_op jit(solution)/shard_map/all_gather | solution.py:419
  19.3 190.9 %all-gather.5.cloned.1.call-start = ((), (), s32[]{:S(2)}) async-start(), calls=%async_computation.2 | async-start | bytes 2621440 | tf_op jit(solution)/shard_map/all_gather | solution.py:420
  27.9 5.0 %copy-start.4 = (bf16[1024,384]{1,0:T(8,128)(2,1)S(1)}, bf16[1024,384]{1,0:T(8,128)(2,1)}, u32[]{:S(2)}) copy-start(bf16[1024,384]{1,0:T(8,128)(2,1)} %copy.35.w_ref) | copy-start | bytes 2359300
  27.9 5.0 %copy-start.7 = (s32[4]{0:T(128)S(1)}, s32[4]{0:T(128)}, u32[]{:S(2)}) copy-start(s32[4]{0:T(128)} %counts.7) | copy-start | bytes 52
  27.9 5.0 %copy-start.8 = (s32[64]{0:T(128)S(1)}, s32[64]{0:T(128)}, u32[]{:S(2)}) copy-start(s32[64]{0:T(128)} %table.7) | copy-start | bytes 772
  41.4 0.8 copy-start.9
  42.2 23.1 %collective-permute-start.1 = (bf16[2048,256]{1,0:T(8,128)(2,1)S(1)}, bf16[2048,256]{1,0:T(8,128)(2,1)}, u32[]{:S(2)}, u32[]{:S(2)}) collective-permute-start(bf16[2048,256]{1,0:T(8,128)(2,1)S(1)} %get-tuple-element.9), channel_id=1, source_target_pairs={{0,16},{4,20},{8,24},{12,28},{16,0},{20,4},{24,8},{28,12},{1,17},{... | collective-permute-start | bytes 3145736 | tf_op jit(solution)/shard_map/ppermute | solution.py:384
  43.7 24.5 %collective-permute-start.3 = (bf16[2048,256]{1,0:T(8,128)(2,1)S(1)}, bf16[2048,256]{1,0:T(8,128)(2,1)}, u32[]{:S(2)}, u32[]{:S(2)}) collective-permute-start(bf16[2048,256]{1,0:T(8,128)(2,1)S(1)} %get-tuple-element.9), channel_id=1, source_target_pairs={{0,8},{4,12},{8,0},{12,4},{16,24},{20,28},{24,16},{28,20},{1,9},{5... | collective-permute-start | bytes 3145736 | tf_op jit(solution)/shard_map/ppermute | solution.py:384
  45.2 25.9 %copy-start.10 = (bf16[2048,128]{1,0:T(8,128)(2,1)S(1)}, bf16[2048,128]{1,0:T(8,128)(2,1)}, u32[]{:S(2)}) copy-start(bf16[2048,128]{1,0:T(8,128)(2,1)} %copy-done.9) | copy-start | bytes 1572868
  66.6 71.6 %collective-permute-start.2 = (bf16[1024,256]{1,0:T(8,128)(2,1)S(1)}, bf16[1024,256]{1,0:T(8,128)(2,1)S(1)}, u32[]{:S(2)}, u32[]{:S(2)}) collective-permute-start(bf16[1024,256]{1,0:T(8,128)(2,1)S(1)} %get-tuple-element.19.refs_2_), channel_id=1, source_target_pairs={{0,8},{4,12},{8,0},{12,4},{16,24},{20,28},{24,16},{28,20},{1,9},{5... | collective-permute-start | bytes 1572872 | tf_op jit(solution)/shard_map/ppermute | solution.py:384
  69.5 68.7 %collective-permute-start.4 = (bf16[1024,256]{1,0:T(8,128)(2,1)S(1)}, bf16[1024,256]{1,0:T(8,128)(2,1)S(1)}, u32[]{:S(2)}, u32[]{:S(2)}) collective-permute-start(bf16[1024,256]{1,0:T(8,128)(2,1)S(1)} %get-tuple-element.21.refs_1_), channel_id=1, source_target_pairs={{0,16},{4,20},{8,24},{12,28},{16,0},{20,4},{24,8},{28,12},{1,17},{... | collective-permute-start | bytes 1572872 | tf_op jit(solution)/shard_map/ppermute | solution.py:384
  94.1 1.4 copy-start.11
  95.5 1.3 copy-start.12
  138.2 71.9 %copy-start.5 = (f32[1024]{0:T(1024)S(1)}, f32[1024]{0:T(1024)}, u32[]{:S(2)}) copy-start(f32[1024]{0:T(1024)} %param.23) | copy-start | bytes 12292
  138.2 71.9 %copy-start.6 = (f32[1024]{0:T(1024)S(1)}, f32[1024]{0:T(1024)}, u32[]{:S(2)}) copy-start(f32[1024]{0:T(1024)} %param.24) | copy-start | bytes 12292
  162.5 1.6 collective-permute-start.5
  165.0 155.0 %all-reduce.2.cloned.1.call-start = ((), (), s32[]{:S(2)}) async-start(), calls=%async_computation.1 | async-start | bytes 4194304 | tf_op jit(solution)/shard_map/psum | solution.py:428
  210.1 1.6 copy-start.3
  211.7 7.3 %copy-start.18 = (f32[1024]{0:T(1024)S(1)}, f32[1024]{0:T(1024)}, u32[]{:S(2)}) copy-start(f32[1024]{0:T(1024)} %param.26) | copy-start | bytes 12292
  217.6 1.4 copy-start.1
  219.0 101.0 %copy-start.14 = (f32[1024]{0:T(1024)S(1)}, f32[1024]{0:T(1024)}, u32[]{:S(2)}) copy-start(f32[1024]{0:T(1024)} %param.28) | copy-start | bytes 12292
  234.6 89.9 %copy-start.15 = (f32[1024]{0:T(1024)S(1)}, f32[1024]{0:T(1024)}, u32[]{:S(2)}) copy-start(f32[1024]{0:T(1024)} %param.30) | copy-start | bytes 12292
  234.6 89.9 %copy-start.16 = (f32[1024]{0:T(1024)S(1)}, f32[1024]{0:T(1024)}, u32[]{:S(2)}) copy-start(f32[1024]{0:T(1024)} %param.29) | copy-start | bytes 12292
  319.9 3.1 copy-start.2
  319.9 3.5 %copy-start.13 = (bf16[1024,1024]{1,0:T(8,128)(2,1)S(1)}, bf16[1024,1024]{1,0:T(8,128)(2,1)}, u32[]{:S(2)}) copy-start(bf16[1024,1024]{1,0:T(8,128)(2,1)} %all-reduce.2.cloned.1.call-done) | copy-start | bytes 6291460
  324.5 2.4 copy-start.17
  324.5 2.4 copy-start.19
Sparse Core Ops, SparseCore 0:
  20.9 47.4 all-gather.6
  165.1 44.9 all-gather.4
  234.7 85.2 all-reduce.1

commit v2 on v1

v2 whole, which is shorter than its diff:
```python
import functools
import math

import jax
import jax.numpy as jnp
from jax import lax
from jax.experimental import pallas as pl
from jax.experimental.pallas import tpu as pltpu
from jax.sharding import PartitionSpec as P

HEAD_DIM = 64
ADAPTER_RANK = 16
PAGE = 128
PAIR = 2 * HEAD_DIM
NEG = -1e30
EXP_SCALE = math.log2(math.e) * HEAD_DIM**-0.5
MIB = 1 << 20


def params(vmem=48):
    return pltpu.CompilerParams(
        dimension_semantics=("arbitrary",), vmem_limit_bytes=vmem * MIB
    )


def request_of(k, counts, requests):
    end = counts[0]
    request = (k >= end).astype(jnp.int32)
    for r in range(1, requests - 1):
        end = end + counts[r]
        request = request + (k >= end).astype(jnp.int32)
    return request


def normalize(values, gain_row, bias_row):
    average = jnp.mean(values, axis=-1, keepdims=True)
    centered = values - average
    variance = jnp.mean(centered * centered, axis=-1, keepdims=True)
    return centered * lax.rsqrt(variance + 1e-05) * gain_row + bias_row


def project_kernel(
    counts, table, owners, bases, *refs, requests, slots, pages, per_piece, parts,
):
    x_refs = refs[:parts]
    w_ref, down_ref, up_ref, q_ref, kv_ref, joined, page_owner = refs[parts:]
    step = pl.program_id(0)
    cols = w_ref.shape[1]

    @pl.when(step == 0)
    def _():
        joined[:, :cols] = w_ref[...]
        joined[:, cols:] = down_ref[...]

        def fill(k, carry):
            page_owner[table[k]] = owners[request_of(k, counts, requests)]
            return carry

        lax.fori_loop(0, slots, fill, 0)

    piece = step * pages // per_piece

    def block(x_ref):
        both = jnp.dot(x_ref[...], joined[...], preferred_element_type=jnp.float32)
        low = both[:, cols:]
        lane_owner = lax.broadcasted_iota(jnp.int32, (PAGE, low.shape[1]), 1) // ADAPTER_RANK
        kept = []
        for p in range(pages):
            page = step * pages + p
            slot = bases[page // per_piece] + page % per_piece
            kept.append(
                jnp.where(lane_owner == page_owner[slot], low[p * PAGE : (p + 1) * PAGE], 0.0)
            )
        low_rank = jnp.concatenate(kept, axis=0).astype(jnp.bfloat16)
        rows = both[:, :cols] + jnp.dot(
            low_rank, up_ref[...], preferred_element_type=jnp.float32
        )
        rows = rows.astype(jnp.bfloat16)
        q_cols = q_ref.shape[1]
        q_ref[...] = rows[:, :q_cols]
        kv_ref[...] = rows[:, q_cols:]

    for i in range(parts):
        pl.when(piece == i)(functools.partial(block, x_refs[i]))


def project(counts, table, owners, bases, xs, weight, down, up, per_piece):
    tok, width = xs[0].shape
    cols = weight.shape[1]
    pages = 2
    rows_step = pages * PAGE
    slots = table.shape[0]
    parts = len(xs)
    each = tok // rows_step
    total = tok * parts
    whole = lambda i, *_: (0, 0)
    rows = lambda i, *_: (i, 0)

    def own(part):
        return lambda i, *_: (jnp.clip(i - part * each, 0, each - 1), 0)

    return pl.pallas_call(
        functools.partial(
            project_kernel,
            requests=counts.shape[0], slots=slots, pages=pages, per_piece=per_piece, parts=parts,
        ),
        grid_spec=pltpu.PrefetchScalarGridSpec(
            num_scalar_prefetch=4,
            grid=(total // rows_step,),
            in_specs=[pl.BlockSpec((rows_step, width), own(i)) for i in range(parts)]
            + [
                pl.BlockSpec(weight.shape, whole),
                pl.BlockSpec(down.shape, whole),
                pl.BlockSpec(up.shape, whole),
            ],
            out_specs=[
                pl.BlockSpec((rows_step, cols // 3), rows),
                pl.BlockSpec((rows_step, 2 * cols // 3), rows),
            ],
            scratch_shapes=[
                pltpu.VMEM((width, cols + down.shape[1]), jnp.bfloat16),
                pltpu.SMEM((slots,), jnp.int32),
            ],
        ),
        out_shape=[
            jax.ShapeDtypeStruct((total, cols // 3), jnp.bfloat16),
            jax.ShapeDtypeStruct((total, 2 * cols // 3), jnp.bfloat16),
        ],
        compiler_params=params(),
        cost_estimate=pl.CostEstimate(
            flops=2 * total * width * cols, bytes_accessed=2 * total * (width + cols),
            transcendentals=0,
        ),
        name="project",
    )(counts, table, owners, bases, *xs, weight, down, up)


def attend_kernel(
    counts, table, q_bases, kv_bases, q_ref, *refs,
    requests, slots, q_size, sizes, first, last, group,
):
    refs = list(refs)
    kv_hbm = [refs.pop(0) for _ in sizes]
    if not first:
        acc_in, stat_in = refs.pop(0), refs.pop(0)
    if last:
        out_ref = refs.pop(0)
    else:
        acc_out, stat_out = refs.pop(0), refs.pop(0)
    kv, scores, listed, amount, asked, q_amount, sems = refs
    copies = []
    offset = 0
    for i, size in enumerate(sizes):
        copy = pltpu.make_async_copy(
            kv_hbm[i], kv.at[pl.ds(offset * PAGE, size * PAGE)], sems.at[i]
        )
        copy.start()
        copies.append(copy)
        offset += size
    for r in range(requests):
        amount[r] = 0
        q_amount[r] = 0

    def place_of(slot, bases, extents):
        place = jnp.int32(-1)
        offset = 0
        for i, size in enumerate(extents):
            near = slot - bases[i]
            place = jnp.where((near >= 0) & (near < size), near + offset, place)
            offset += size
        return place

    q_sizes = (q_size,) * (q_ref.shape[0] // (q_size * PAGE))

    def fill(k, carry):
        r = request_of(k, counts, requests)
        slot = table[k]
        place = place_of(slot, kv_bases, sizes)
        q_place = place_of(slot, q_bases, q_sizes)

        @pl.when(place >= 0)
        def _():
            n = amount[r]
            listed[r, n] = place
            amount[r] = n + 1

        @pl.when(q_place >= 0)
        def _():
            n = q_amount[r]
            asked[r, n] = q_place
            q_amount[r] = n + 1

        return carry

    lax.fori_loop(0, slots, fill, 0)
    for copy in copies:
        copy.wait()
    lane = lax.broadcasted_iota(jnp.int32, (PAGE, PAIR), 1)
    low_lane = lane < HEAD_DIM
    rows = 4 * PAGE

    def one_pair(r, p):
        n = amount[r]
        full = n // group
        blocks = (n + group - 1) // group
        count = q_amount[r]
        a = asked[r, 2 * p]
        b = asked[r, jnp.minimum(2 * p + 1, count - 1)]
        spots = [pl.ds(pl.multiple_of(t * PAGE, PAGE), PAGE) for t in (a, b)]
        parts = []
        for spot in spots:
            q = q_ref[spot, :]
            zero = jnp.zeros_like(q)
            parts += [jnp.where(low_lane, q, zero), jnp.where(low_lane, zero, q)]
        stacked = jnp.concatenate(parts, axis=0)

        def pages_of(j, low):
            found = []
            for i in range(group):
                index = jnp.minimum(j * group + i, n - 1)
                at = pl.multiple_of(listed[r, index] * PAGE, PAGE)
                found.append(kv[pl.ds(at, PAGE), low : low + PAIR])
            return jnp.concatenate(found, axis=0)

        def score(masked, j, top):
            s = lax.dot_general(
                stacked, pages_of(j, 0), (((1,), (1,)), ((), ())),
                preferred_element_type=jnp.float32,
            )
            for i in range(group):
                piece = s[:, i * PAGE : (i + 1) * PAGE]
                if masked and i:
                    piece = jnp.where(j * group + i < n, piece, NEG)
                scores[j, :, i * PAGE : (i + 1) * PAGE] = piece
                top = jnp.maximum(top, piece)
            return top

        top = jnp.full((rows, PAGE), NEG, jnp.float32)
        top = lax.fori_loop(0, full, functools.partial(score, False), top)
        top = lax.fori_loop(full, blocks, functools.partial(score, True), top)
        peak = jnp.max(top, axis=1, keepdims=True)
        if not first:
            old = jnp.concatenate(
                [stat_in[spot, h : h + 1] for spot in spots for h in (0, 1)], axis=0
            )
            peak = jnp.maximum(peak, old)
        shift = peak * EXP_SCALE

        def weigh(j, carry):
            total, acc = carry
            w = jnp.exp2(scores[j] * EXP_SCALE - shift)
            for i in range(group):
                total = total + w[:, i * PAGE : (i + 1) * PAGE]
            acc = acc + jnp.dot(
                w.astype(jnp.bfloat16), pages_of(j, PAIR), preferred_element_type=jnp.float32
            )
            return total, acc

        total, acc = lax.fori_loop(
            0, blocks, weigh,
            (jnp.zeros((rows, PAGE), jnp.float32), jnp.zeros((rows, PAIR), jnp.float32)),
        )
        total = jnp.sum(total, axis=1, keepdims=True)
        if not first:
            shrink = jnp.exp2((old - peak) * EXP_SCALE)
            total = total + shrink * jnp.concatenate(
                [stat_in[spot, h : h + 1] for spot in spots for h in (2, 3)], axis=0
            )
        for t, spot in enumerate(spots):
            h0 = slice(2 * t * PAGE, (2 * t + 1) * PAGE)
            h1 = slice((2 * t + 1) * PAGE, (2 * t + 2) * PAGE)
            value = jnp.where(low_lane, acc[h0], acc[h1])
            if not first:
                value = value + acc_in[spot, :] * jnp.where(low_lane, shrink[h0], shrink[h1])
            if last:
                value = value / jnp.where(low_lane, total[h0], total[h1])
                out_ref[spot, :] = value.astype(jnp.bfloat16)
            else:
                acc_out[spot, :] = value
                stat = jnp.where(lane == 0, peak[h0], peak[h1])
                stat = jnp.where(lane == 2, total[h0], stat)
                stat_out[spot, :] = jnp.where(lane == 3, total[h1], stat)

    def visit_request(r, carry):
        def visit(p, inner):
            one_pair(r, p)
            return inner

        return lax.fori_loop(0, (q_amount[r] + 1) // 2, visit, carry)

    lax.fori_loop(0, requests, visit_request, 0)


def attend(counts, table, q_bases, kv_bases, q, pieces, state, last, q_size):
    tok = q.shape[0]
    sizes = tuple(p.shape[0] // PAGE for p in pieces)
    first = state is None
    group = 4
    slots = table.shape[0]
    requests = counts.shape[0]
    most = min(sum(sizes), slots)
    vmem = pl.BlockSpec(memory_space=pltpu.VMEM)
    state_shape = [jax.ShapeDtypeStruct((tok, PAIR), jnp.float32)] * 2
    out = pl.pallas_call(
        functools.partial(
            attend_kernel,
            requests=requests, slots=slots, q_size=q_size, sizes=sizes,
            first=first, last=last, group=group,
        ),
        grid_spec=pltpu.PrefetchScalarGridSpec(
            num_scalar_prefetch=4,
            grid=(1,),
            in_specs=[pl.BlockSpec((tok, PAIR), lambda i, *_: (0, 0))]
            + [pl.BlockSpec(memory_space=pl.ANY)] * len(pieces)
            + ([] if first else [pl.BlockSpec((tok, PAIR), lambda i, *_: (0, 0))] * 2),
            out_specs=[pl.BlockSpec((tok, PAIR), lambda i, *_: (0, 0))] * (1 if last else 2),
            scratch_shapes=[
                pltpu.VMEM((sum(sizes) * PAGE, 2 * PAIR), jnp.bfloat16),
                pltpu.VMEM(((most + group - 1) // group, 4 * PAGE, group * PAGE), jnp.float32),
                pltpu.SMEM((requests, sum(sizes)), jnp.int32),
                pltpu.SMEM((requests,), jnp.int32),
                pltpu.SMEM((requests, tok // PAGE), jnp.int32),
                pltpu.SMEM((requests,), jnp.int32),
                pltpu.SemaphoreType.DMA((len(pieces),)),
            ],
        ),
        out_shape=[jax.ShapeDtypeStruct((tok, PAIR), jnp.bfloat16)] if last else state_shape,
        compiler_params=params(),
        cost_estimate=pl.CostEstimate(
            flops=2 * tok * sum(sizes) * PAGE * PAIR,
            bytes_accessed=4 * tok * PAIR + 4 * PAGE * PAIR * sum(sizes),
            transcendentals=tok * sum(sizes) * PAGE,
        ),
        name="attend",
    )(counts, table, q_bases, kv_bases, q, *pieces, *([] if first else state))
    return out[0] if last else out


def mix_kernel(x_ref, ctx_ref, wo_ref, gain_ref, bias_ref, out_ref):
    mixed = x_ref[...].astype(jnp.float32)
    for j in range(ctx_ref.shape[0]):
        mixed = mixed + jnp.dot(ctx_ref[j], wo_ref[j], preferred_element_type=jnp.float32)
    out_ref[...] = normalize(mixed, gain_ref[...], bias_ref[...]).astype(jnp.bfloat16)


def mix(x, ctx, wo, gain, bias):
    tok, width = x.shape
    groups, _, cols = ctx.shape
    block = 256
    rows = lambda i: (i, 0)
    return pl.pallas_call(
        mix_kernel,
        grid=(tok // block,),
        in_specs=[
            pl.BlockSpec((block, width), rows),
            pl.BlockSpec((groups, block, cols), lambda i: (0, i, 0)),
            pl.BlockSpec(wo.shape, lambda i: (0, 0, 0)),
            pl.BlockSpec((1, width), lambda i: (0, 0)),
            pl.BlockSpec((1, width), lambda i: (0, 0)),
        ],
        out_specs=pl.BlockSpec((block, width), rows),
        out_shape=jax.ShapeDtypeStruct((tok, width), jnp.bfloat16),
        compiler_params=params(),
        cost_estimate=pl.CostEstimate(
            flops=2 * tok * width * groups * cols, bytes_accessed=8 * tok * width, transcendentals=0
        ),
        name="mix",
    )(x, ctx, wo, gain[None], bias[None])


def layer_norm(values, gain_row, bias_row):
    return normalize(values, gain_row, bias_row)


def local(
    tokens,
    query_key_value_weight,
    adapter_down_weight,
    adapter_up_weight,
    attention_out_weight,
    first_norm_gain,
    first_norm_bias,
    first_feed_weight,
    first_feed_bias,
    second_feed_weight,
    second_feed_bias,
    second_norm_gain,
    second_norm_bias,
    following_qkv_weight,
    following_bias,
    request_page_count,
    page_slot_table,
    request_adapter,
):
    tok_rows, width = tokens.shape
    dp_count = lax.axis_size("dp")
    mp_count = lax.axis_size("mp")
    dp_index = lax.axis_index("dp")
    mp_index = lax.axis_index("mp")
    kept_values = adapter_down_weight.shape[1] // ADAPTER_RANK
    heads_dev = query_key_value_weight.shape[1] // (3 * HEAD_DIM)
    pages = tok_rows // PAGE
    shared = dp_count == 8 and heads_dev == 4

    owners = request_adapter // kept_values
    level = jnp.sum(jnp.where(owners == mp_index, request_adapter % kept_values, 0))
    down = lax.dynamic_slice_in_dim(
        adapter_down_weight, level * ADAPTER_RANK, ADAPTER_RANK, 1
    )
    up = lax.dynamic_slice_in_dim(adapter_up_weight, level * ADAPTER_RANK, ADAPTER_RANK, 0)
    up_cols = up.shape[1] // mp_count
    sent = jnp.concatenate(
        [
            jnp.broadcast_to(down.T[:, None, :], (ADAPTER_RANK, mp_count, width)),
            up.reshape(ADAPTER_RANK, mp_count, up_cols),
        ],
        axis=2,
    ).reshape(ADAPTER_RANK, mp_count * (width + up_cols))
    got = lax.all_to_all(sent, "mp", split_axis=1, concat_axis=0, tiled=True)
    downs = got[:, :width].T
    ups = got[:, width:]

    def by_kind(matrix):
        split = matrix.reshape(matrix.shape[0], heads_dev, 3, HEAD_DIM)
        if shared:
            split = lax.dynamic_slice_in_dim(split, (dp_index % 2) * 2, 2, 1)
        return jnp.swapaxes(split, 1, 2).reshape(matrix.shape[0], -1)

    weight = by_kind(query_key_value_weight)
    ups = by_kind(ups)
    if shared:
        swap = [(i, i ^ 1) for i in range(8)]
        across = [(i, i ^ 2) for i in range(8)]
        along = [(i, i ^ 4) for i in range(8)]
        move = lambda value, pairs: lax.ppermute(value, "dp", pairs)
        xs = [tokens, move(tokens, swap)]
        at = lambda flip: (dp_index ^ flip) * pages
        bases = jnp.stack([at(0), at(1)])
    else:
        xs = [tokens]
        bases = jnp.stack([dp_index * pages])
    args = (request_page_count, page_slot_table)
    q, kv = project(*args, owners, bases, xs, weight, downs, ups, pages)
    if shared:
        kv_x = move(kv, across)
        kv_y = move(kv, along)
        step = functools.partial(attend, *args, bases)
        state = step(bases, q, [kv[:tok_rows], kv[tok_rows:]], None, False, pages)
        kv_x, kv_y, state = lax.optimization_barrier((kv_x, kv_y, state))
        kv_d0 = move(kv_y[:tok_rows], across)
        kv_d1 = move(kv_x[tok_rows:], along)
        near = jnp.stack([at(2), at(3), at(4), at(5)])
        state = step(
            near, q, [kv_x[:tok_rows], kv_x[tok_rows:], kv_y[:tok_rows], kv_y[tok_rows:]],
            state, False, pages,
        )
        far = jnp.stack([at(6), at(7)])
        context = step(far, q, [kv_d0, kv_d1], state, True, pages)
        mine, theirs = context[:tok_rows], move(context[tok_rows:], swap)
        even = dp_index % 2 == 0
        context = jnp.concatenate(
            [jnp.where(even, mine, theirs), jnp.where(even, theirs, mine)], axis=1
        )
    else:
        everything = lax.all_gather(kv, "dp", axis=0, tiled=True)
        context = attend(
            *args, bases, jnp.zeros((1,), jnp.int32), q, [everything], None, True, pages
        )
    out_weight = lax.all_gather(attention_out_weight, "mp", axis=0)
    contexts = lax.all_gather(context, "mp", axis=0)
    normed = mix(tokens, contexts, out_weight, first_norm_gain, first_norm_bias)
    share_rows = tok_rows // mp_count
    row_base = mp_index * share_rows
    hidden = jax.nn.gelu(
        jnp.dot(normed, first_feed_weight, preferred_element_type=jnp.float32) + first_feed_bias,
        approximate=False,
    ).astype(jnp.bfloat16)
    feed = lax.psum(
        jnp.dot(hidden, second_feed_weight, preferred_element_type=jnp.float32).astype(
            jnp.bfloat16
        ),
        "mp",
    ).astype(jnp.float32)
    layer_full = layer_norm(
        normed.astype(jnp.float32) + feed + second_feed_bias, second_norm_gain, second_norm_bias
    ).astype(jnp.bfloat16)
    next_proj = (
        jnp.dot(layer_full, following_qkv_weight, preferred_element_type=jnp.float32)
        + following_bias
    ).astype(jnp.bfloat16)
    layer_rows = lax.dynamic_slice_in_dim(layer_full, row_base, share_rows, 0)
    return (layer_rows, next_proj)


def solution(mesh):
    placed = (
        P("dp", None),
        P(None, "mp"),
        P(None, "mp"),
        P("mp", None),
        P("mp", None),
        P(),
        P(),
        P(None, "mp"),
        P("mp"),
        P("mp", None),
        P(),
        P(),
        P(),
        P(None, "mp"),
        P("mp"),
        P(),
        P(),
        P(),
    )
    return jax.shard_map(
        local,
        mesh=mesh,
        in_specs=placed,
        out_specs=(P(("dp", "mp"), None), P("dp", "mp")),
        check_vma=False,
    )
```

time: 336 us -> 301 us (0.90)
  waiting for transfers between devices: 155 us -> 139 us
  Pallas kernels: 103 us -> 87.5 us
  other arithmetic: 13.8 us -> 8.87 us
    ppermute x6, waiting for transfers between devices: 21.5 us -> 2.64 us  [local(): move = lambda value, pairs: lax.ppermute(value, 'dp', pairs)]
    pallas_call x3, Pallas kernels: 88.6 us -> 73.3 us  [attend(): pl.pallas_call(functools.partial(attend_kernel, requests=requests, slots=...]
    concatenate x1 -> x0, other arithmetic: 4.96 us -> none  [local(): x = jnp.concatenate([tokens, move(tokens, swap)], axis=0)]
    all_gather x1, waiting for transfers between devices: 44.9 us -> 48.8 us  [local(): contexts = lax.all_gather(context, 'mp', axis=0)]
    unnamed x42 -> x48, local copies, waits for them, and re-layouts: 9.56 us -> 11.1 us
  transfers between devices with their start and end apart: 10 -> 10, of which waited for: 5 -> 5; matrix products, arithmetic and copies ran while one was open for 6% -> 4% of each run, Pallas kernels for 29% -> 27%
where the time goes in v2:
time: 301 us; the launch traced here: 300 us
  waiting for transfers between devices  139 us (46%)
  Pallas kernels  87.5 us (29%)
  local copies, waits for them, and re-layouts  19.5 us (6%)
  matrix products  18.5 us (6%)
  between operations  14.7 us (5%)
  starting transfers between devices  11.9 us (4%)
  other arithmetic  8.87 us (3%)
    psum x1, waiting for transfers between devices, local(): lax.psum(jnp.dot(hidden, second_feed_weight, preferred_element_type=jnp.f...  85.4 us
    pallas_call x3, Pallas kernels, attend(): pl.pallas_call(functools.partial(attend_kernel, requests=requests, slots=...  73.3 us
    all_gather x1, waiting for transfers between devices, local(): contexts = lax.all_gather(context, 'mp', axis=0)  48.8 us
    dot_general x1, matrix products, local(): jnp.dot(hidden, second_feed_weight, preferred_element_type=jnp.float32)  15.6 us
    unnamed x48, local copies, waits for them, and re-layouts  11.1 us
    pallas_call x1, Pallas kernels, project(): pl.pallas_call(functools.partial(project_kernel, requests=counts.shape[0]...  8.3 us
  transfers between devices with their start and end apart: 10, of which 5 were waited for; matrix products, arithmetic and copies ran while one was open for 4% of the time, Pallas kernels for 27%

profile of v2, /device:TPU:0, one launch (start us, length us, event | category | flops | bytes accessed | tf_op | source)
XLA Modules:
  0.0 300.0 jit_solution(3576761235542228169)
XLA Ops:
  7.7 1.5 fusion.18
  9.7 1.1 dynamic-slice_bitcast_fusion.1
  12.6 5.9 %all-to-all-start = ((bf16[16,4,1792]{2,0,1:T(8,128)(2,1)}), bf16[16,4,1792]{2,0,1:T(8,128)(2,1)S(1)}, u32[]{:S(2)}, u32[]{:S(2)}) async-start(bf16[16,4,1792]{2,0,1:T(8,128)(2,1)} %pad_maximum_fusion.1), calls=%async_computation | async-start | bytes 458752 | tf_op jit(solution)/shard_map/all_to_all | solution.py:419
  19.3 2.6 copy.29
  21.9 1.2 dynamic-slice_bitcast_fusion
  23.2 1.0 copy.30
  24.1 1.5 copy.35.refs_2_
  25.6 1.5 all-to-all-done
  27.9 1.7 copy-done.3
  29.6 8.3 %project.1 = (bf16[2048,128]{1,0:T(8,128)(2,1)S(1)}, bf16[2048,256]{1,0:T(8,128)(2,1)S(1)}) custom-call(s32[4]{0:T(128)S(1)} %copy-done.8, s32[64]{0:T(128)S(1)} %copy-done.9, s32[4]{0:T(128)S(1)} %get-tuple-element.23.owners, s32[2]{0:T(128)S(1)} %pad_add_fusion.bases.q_bases.kv_bases, bf16[1024,1024]{1,0:T(8,128)(2,1)S(1)} %copy-done.3, ...), custom_call_target="tpu_custom_call" | custom-call | flops 1610612736 | bytes 5767168 | tf_op jit(solution)/shard_map/project/pallas_call | solution.py:102
  37.9 1.5 collective-permute-start.1
  39.4 1.5 collective-permute-start.2
  41.0 20.5 %attend.3 = (f32[2048,128]{1,0:T(8,128)S(1)}, f32[2048,128]{1,0:T(8,128)S(1)}) custom-call(s32[4]{0:T(128)S(1)} %copy-done.8, s32[64]{0:T(128)S(1)} %copy-done.9, s32[2]{0:T(128)S(1)} %pad_add_fusion.bases.q_bases.kv_bases, s32[2]{0:T(128)S(1)} %pad_add_fusion.bases.q_bases.kv_bases, bf16[2048,128]{1,0:T(8,128)(2,1)S(1)} %get-tuple-element.12.q_ref, ...), custom_call_target="tpu_custom_call" | custom-call | flops 1073741824 | bytes 2097152 | tf_op jit(solution)/shard_map/attend/pallas_call | solution.py:304
  61.6 1.1 collective-permute-done.2
  63.4 1.1 fusion.50
  64.5 1.5 collective-permute-start.4
  66.1 1.0 copy-done.5
  67.1 1.0 copy-done.11
  68.2 1.2 copy-done.14
  69.4 32.5 %attend.4 = (f32[2048,128]{1,0:T(8,128)S(1)}, f32[2048,128]{1,0:T(8,128)S(1)}) custom-call(s32[4]{0:T(128)S(1)} %copy-done.8, s32[64]{0:T(128)S(1)} %copy-done.9, s32[2]{0:T(128)S(1)} %pad_add_fusion.bases.q_bases.kv_bases, s32[4]{0:T(128)S(1)} %get-tuple-element.32.kv_bases, bf16[2048,128]{1,0:T(8,128)(2,1)S(1)} %copy-done.11, ...), custom_call_target="tpu_custom_call" | custom-call | flops 2147483648 | bytes 3145728 | tf_op jit(solution)/shard_map/attend/pallas_call | solution.py:304
  101.9 20.3 %attend.5 = bf16[2048,128]{1,0:T(8,128)(2,1)S(1)} custom-call(s32[4]{0:T(128)S(1)} %copy-done.8, s32[64]{0:T(128)S(1)} %copy-done.9, s32[2]{0:T(128)S(1)} %pad_add_fusion.bases.q_bases.kv_bases, s32[2]{0:T(128)S(1)} %pad_add_fusion.1.kv_bases, bf16[2048,128]{1,0:T(8,128)(2,1)S(1)} %copy-done.12, bf16[1024,256]{1,0:T(8,128)(2,1)} %collective-permute-done.3.refs_0_, ...), custom_call_target="tpu_custom_call" | custom-call | flops 1073741824 | bytes 2097152 | tf_op jit(solution)/shard_map/attend/pallas_call | solution.py:304
  122.3 1.5 collective-permute-done.5
  125.0 48.8 %all-gather.5.cloned.1.call-done = bf16[4096,256]{1,0:T(8,128)(2,1)} async-done(((bf16[1024,256]{1,0:T(8,128)(2,1)}), bf16[4096,256]{1,0:T(8,128)(2,1)}) %all-gather.5.cloned.1.call-update) | async-done | bytes 2097168 | tf_op jit(solution)/shard_map/all_gather | solution.py:470
  173.8 1.6 copy-done.4
  175.4 5.9 %mix.1 = bf16[1024,1024]{1,0:T(8,128)(2,1)S(1)} custom-call(bf16[1024,1024]{1,0:T(8,128)(2,1)S(1)} %copy-done.4, bf16[4,1024,256]{2,1,0:T(8,128)(2,1)} %bitcast.39, bf16[4,256,1024]{2,1,0:T(8,128)(2,1)} %bitcast.38, f32[1,1024]{1,0:T(1,128)S(1)} %bitcast.34, f32[1,1024]{1,0:T(1,128)S(1)} %bitcast.35), custom_call_target="tpu_custom_call" | custom-call | flops 2147483648 | bytes 8388608 | tf_op jit(solution)/shard_map/mix/pallas_call | solution.py:351
  181.3 1.3 copy-done.1
  182.7 15.6 %fusion.15 = bf16[1024,1024]{1,0:T(8,128)(2,1)} fusion(bf16[1024,1024]{1,0:T(8,128)(2,1)S(1)} %copy-done, f32[1024]{0:T(1024)S(1)} %copy-done.21, bf16[1024,1024]{1,0:T(8,128)(2,1)} %copy-done.1, bf16[1024,1024]{1,0:T(8,128)(2,1)} %param.25), kind=kOutput, calls=%fused_computation.26 | convolution fusion | flops 4365221888 | bytes 8392704 | tf_op jit(solution)/shard_map/dot_general | solution.py:479
  198.3 85.4 %all-reduce.2.cloned.1.call-done = bf16[1024,1024]{1,0:T(8,128)(2,1)} async-done(((bf16[1024,1024]{1,0:T(8,128)(2,1)}), bf16[1024,1024]{1,0:T(8,128)(2,1)}) %all-reduce.2.cloned.1.call-update) | async-done | bytes 2097168 | tf_op jit(solution)/shard_map/psum | solution.py:478
  283.7 3.1 %fusion.10 = f32[1024]{0:T(1024)S(1)} fusion(bf16[1024,1024]{1,0:T(8,128)(2,1)} %all-reduce.2.cloned.1.call-done, bf16[1024,1024]{1,0:T(8,128)(2,1)} %copy-done.1, f32[1024]{0:T(1024)S(1)} %copy-done.17), kind=kLoop, calls=%fused_computation.22 | loop fusion | flops 5241856 | bytes 4202496 | tf_op jit(solution)/shard_map/reduce_sum | solution.py:36
  287.1 1.0 multiply_reduce_fusion
  288.2 1.5 add_convert_fusion
  290.6 2.9 add_convert_fusion.1
  (76 shorter events, 7.1 us)
Async XLA Ops:
  7.2 175.5 %copy-start = (bf16[1024,1024]{1,0:T(8,128)(2,1)S(1)}, bf16[1024,1024]{1,0:T(8,128)(2,1)}, u32[]{:S(2)}) copy-start(bf16[1024,1024]{1,0:T(8,128)(2,1)} %param.27) | copy-start | bytes 6291460
  7.2 20.7 %collective-permute-start = (bf16[1024,1024]{1,0:T(8,128)(2,1)}, bf16[1024,1024]{1,0:T(8,128)(2,1)}, u32[]{:S(2)}, u32[]{:S(2)}) collective-permute-start(bf16[1024,1024]{1,0:T(8,128)(2,1)} %x_ref.1), channel_id=1, source_target_pairs={{0,4},{4,0},{8,12},{12,8},{16,20},{20,16},{24,28},{28,24},{1,5},{5... | collective-permute-start | bytes 6291464 | tf_op jit(solution)/shard_map/ppermute | solution.py:435
  12.6 14.6 %all-to-all-start = ((bf16[16,4,1792]{2,0,1:T(8,128)(2,1)}), bf16[16,4,1792]{2,0,1:T(8,128)(2,1)S(1)}, u32[]{:S(2)}, u32[]{:S(2)}) async-start(bf16[16,4,1792]{2,0,1:T(8,128)(2,1)} %pad_maximum_fusion.1), calls=%async_computation | async-start | bytes 458752 | tf_op jit(solution)/shard_map/all_to_all | solution.py:419
  18.5 106.5 %all-gather.7.cloned.1.call-start = ((), (), s32[]{:S(2)}) async-start(), calls=%async_computation.3 | async-start | bytes 2621440 | tf_op jit(solution)/shard_map/all_gather | solution.py:469
  19.2 154.6 %all-gather.5.cloned.1.call-start = ((), (), s32[]{:S(2)}) async-start(), calls=%async_computation.2 | async-start | bytes 2621440 | tf_op jit(solution)/shard_map/all_gather | solution.py:470
  24.1 3.8 %copy-start.8 = (s32[4]{0:T(128)S(1)}, s32[4]{0:T(128)}, u32[]{:S(2)}) copy-start(s32[4]{0:T(128)} %counts.7) | copy-start | bytes 52
  24.1 3.8 %copy-start.9 = (s32[64]{0:T(128)S(1)}, s32[64]{0:T(128)}, u32[]{:S(2)}) copy-start(s32[64]{0:T(128)} %table.7) | copy-start | bytes 772
  27.9 1.7 copy-start.3
  37.9 23.6 %copy-start.10 = (bf16[2048,128]{1,0:T(8,128)(2,1)}, bf16[2048,128]{1,0:T(8,128)(2,1)S(1)}, u32[]{:S(2)}) copy-start(bf16[2048,128]{1,0:T(8,128)(2,1)S(1)} %get-tuple-element.12.q_ref) | copy-start | bytes 1572868
  37.9 23.6 %collective-permute-start.1 = (bf16[2048,256]{1,0:T(8,128)(2,1)S(1)}, bf16[2048,256]{1,0:T(8,128)(2,1)S(1)}, u32[]{:S(2)}, u32[]{:S(2)}) collective-permute-start(bf16[2048,256]{1,0:T(8,128)(2,1)S(1)} %get-tuple-element.13), channel_id=1, source_target_pairs={{0,8},{4,12},{8,0},{12,4},{16,24},{20,28},{24,16},{28,20},{1,9},{5... | collective-permute-start | bytes 3145736 | tf_op jit(solution)/shard_map/ppermute | solution.py:435
  39.4 23.3 %collective-permute-start.2 = (bf16[2048,256]{1,0:T(8,128)(2,1)S(1)}, bf16[2048,256]{1,0:T(8,128)(2,1)S(1)}, u32[]{:S(2)}, u32[]{:S(2)}) collective-permute-start(bf16[2048,256]{1,0:T(8,128)(2,1)S(1)} %get-tuple-element.13), channel_id=1, source_target_pairs={{0,16},{4,20},{8,24},{12,28},{16,0},{20,4},{24,8},{28,12},{1,17},{... | collective-permute-start | bytes 3145736 | tf_op jit(solution)/shard_map/ppermute | solution.py:435
  61.6 2.9 copy-start.13
  61.6 2.9 copy-start.15
  62.8 39.1 %collective-permute-start.3 = (bf16[1024,256]{1,0:T(8,128)(2,1)S(1)}, bf16[1024,256]{1,0:T(8,128)(2,1)}, u32[]{:S(2)}, u32[]{:S(2)}) collective-permute-start(bf16[1024,256]{1,0:T(8,128)(2,1)S(1)} %get-tuple-element.25.refs_2_), channel_id=1, source_target_pairs={{0,8},{4,12},{8,0},{12,4},{16,24},{20,28},{24,16},{28,20},{1,9},{5... | collective-permute-start | bytes 1572872 | tf_op jit(solution)/shard_map/ppermute | solution.py:435
  64.5 37.4 %collective-permute-start.4 = (bf16[1024,256]{1,0:T(8,128)(2,1)}, bf16[1024,256]{1,0:T(8,128)(2,1)}, u32[]{:S(2)}, u32[]{:S(2)}) collective-permute-start(bf16[1024,256]{1,0:T(8,128)(2,1)} %get-tuple-element.27.refs_1_), channel_id=1, source_target_pairs={{0,16},{4,20},{8,24},{12,28},{16,0},{20,4},{24,8},{28,12},{1,17},{... | collective-permute-start | bytes 1572872 | tf_op jit(solution)/shard_map/ppermute | solution.py:435
  67.1 1.0 copy-start.11
  68.2 1.2 copy-start.14
  69.4 32.5 %copy-start.12 = (bf16[2048,128]{1,0:T(8,128)(2,1)S(1)}, bf16[2048,128]{1,0:T(8,128)(2,1)}, u32[]{:S(2)}) copy-start(bf16[2048,128]{1,0:T(8,128)(2,1)} %copy-done.10) | copy-start | bytes 1572868
  122.2 51.6 %copy-start.6 = (f32[1024]{0:T(1024)S(1)}, f32[1024]{0:T(1024)}, u32[]{:S(2)}) copy-start(f32[1024]{0:T(1024)} %param.23) | copy-start | bytes 12292
  122.2 51.6 %copy-start.7 = (f32[1024]{0:T(1024)S(1)}, f32[1024]{0:T(1024)}, u32[]{:S(2)}) copy-start(f32[1024]{0:T(1024)} %param.24) | copy-start | bytes 12292
  122.3 1.6 collective-permute-start.5
  124.8 158.9 %all-reduce.2.cloned.1.call-start = ((), (), s32[]{:S(2)}) async-start(), calls=%async_computation.1 | async-start | bytes 4194304 | tf_op jit(solution)/shard_map/psum | solution.py:478
  173.8 1.6 copy-start.4
  175.4 7.2 %copy-start.21 = (f32[1024]{0:T(1024)S(1)}, f32[1024]{0:T(1024)}, u32[]{:S(2)}) copy-start(f32[1024]{0:T(1024)} %param.26) | copy-start | bytes 12292
  181.3 1.3 copy-start.1
  198.2 85.4 %copy-start.17 = (f32[1024]{0:T(1024)S(1)}, f32[1024]{0:T(1024)}, u32[]{:S(2)}) copy-start(f32[1024]{0:T(1024)} %param.28) | copy-start | bytes 12292
  283.6 3.1 %copy-start.2 = (bf16[1024,1024]{1,0:T(8,128)(2,1)S(1)}, bf16[1024,1024]{1,0:T(8,128)(2,1)}, u32[]{:S(2)}) copy-start(bf16[1024,1024]{1,0:T(8,128)(2,1)} %copy-done.1) | copy-start | bytes 6291460
  283.7 3.5 %copy-start.16 = (bf16[1024,1024]{1,0:T(8,128)(2,1)S(1)}, bf16[1024,1024]{1,0:T(8,128)(2,1)}, u32[]{:S(2)}) copy-start(bf16[1024,1024]{1,0:T(8,128)(2,1)} %all-reduce.2.cloned.1.call-done) | copy-start | bytes 6291460
  287.1 1.1 copy-start.18
  287.1 1.1 copy-start.19
  288.2 2.4 copy-start.20
  288.2 2.4 copy-start.22
  (1 other events, 1.0 us)
Sparse Core Ops, SparseCore 0:
  20.9 47.3 all-gather.6
  124.9 48.8 all-gather.4
  198.4 85.2 all-reduce.1

commit v3 on v2

--- a/solution.py
+++ b/solution.py
@@ -336,40 +336,178 @@
     return out[0] if last else out
 
 
-def mix_kernel(x_ref, ctx_ref, wo_ref, gain_ref, bias_ref, out_ref):
+def mix_kernel(bases, x_ref, ctx_ref, *refs, plan):
+    count = len({index for index, *_ in plan})
+    wo_refs = refs[:count]
+    gain_ref, bias_ref, out_ref, wo, sems = refs[count:]
+
+    @pl.when(pl.program_id(0) == 0)
+    def _():
+        copies = []
+        for n, (index, row, rows, half, flip, extra) in enumerate(plan):
+            near = wo.shape[1] // 2
+            at = half * near + (bases[0] ^ flip) * (near // bases_of(plan)) + extra
+            copy = pltpu.make_async_copy(
+                wo_refs[index].at[:, pl.ds(row, rows), :],
+                wo.at[:, pl.ds(pl.multiple_of(at, 16), rows), :],
+                sems.at[n],
+            )
+            copy.start()
+            copies.append(copy)
+        for copy in copies:
+            copy.wait()
+
     mixed = x_ref[...].astype(jnp.float32)
     for j in range(ctx_ref.shape[0]):
-        mixed = mixed + jnp.dot(ctx_ref[j], wo_ref[j], preferred_element_type=jnp.float32)
+        mixed = mixed + jnp.dot(ctx_ref[j], wo[j], preferred_element_type=jnp.float32)
     out_ref[...] = normalize(mixed, gain_ref[...], bias_ref[...]).astype(jnp.bfloat16)
 
 
-def mix(x, ctx, wo, gain, bias):
+def bases_of(plan):
+    return max(flip for *_, flip, _ in plan) + 1
+
+
+def mix(place, x, ctx, wo_arrays, plan, gain, bias):
     tok, width = x.shape
     groups, _, cols = ctx.shape
     block = 256
-    rows = lambda i: (i, 0)
+    rows = lambda i, *_: (i, 0)
+    fixed = lambda i, *_: (0, 0)
     return pl.pallas_call(
-        mix_kernel,
-        grid=(tok // block,),
-        in_specs=[
-            pl.BlockSpec((block, width), rows),
-            pl.BlockSpec((groups, block, cols), lambda i: (0, i, 0)),
-            pl.BlockSpec(wo.shape, lambda i: (0, 0, 0)),
-            pl.BlockSpec((1, width), lambda i: (0, 0)),
-            pl.BlockSpec((1, width), lambda i: (0, 0)),
-        ],
-        out_specs=pl.BlockSpec((block, width), rows),
+        functools.partial(mix_kernel, plan=plan),
+        grid_spec=pltpu.PrefetchScalarGridSpec(
+            num_scalar_prefetch=1,
+            grid=(tok // block,),
+            in_specs=[
+                pl.BlockSpec((block, width), rows),
+                pl.BlockSpec((groups, block, cols), lambda i, *_: (0, i, 0)),
+            ]
+            + [pl.BlockSpec(memory_space=pl.ANY)] * len(wo_arrays)
+            + [pl.BlockSpec((1, width), fixed)] * 2,
+            out_specs=pl.BlockSpec((block, width), rows),
+            scratch_shapes=[
+                pltpu.VMEM((groups, cols, width), jnp.bfloat16),
+                pltpu.SemaphoreType.DMA((len(plan),)),
+            ],
+        ),
         out_shape=jax.ShapeDtypeStruct((tok, width), jnp.bfloat16),
         compiler_params=params(),
         cost_estimate=pl.CostEstimate(
             flops=2 * tok * width * groups * cols, bytes_accessed=8 * tok * width, transcendentals=0
         ),
         name="mix",
-    )(x, ctx, wo, gain[None], bias[None])
-
-
-def layer_norm(values, gain_row, bias_row):
-    return normalize(values, gain_row, bias_row)
+    )(place, x, ctx, *wo_arrays, gain[None], bias[None])
+
+
+def feed_kernel(place, normed_ref, bias_ref, *refs, halves, shape, last_step):
+    refs = list(refs)
+    sets = []
+    for _ in range(halves):
+        w1 = refs.pop(0)
+        sets.append((w1, [refs.pop(0) for _ in shape]))
+    b2_ref, gain_ref, bias2_ref, next_w_ref, next_b_ref = refs[:5]
+    layer_ref, next_ref, acc, done = refs[5:]
+    step = pl.program_id(0)
+    tok = normed_ref.shape[0]
+    block = min(256, tok)
+    groups = (last_step + 1) // halves
+
+    @pl.when(step == 0)
+    def _():
+        acc[...] = jnp.zeros_like(acc)
+
+    def absorb(w1_ref, w2_refs):
+        w1 = w1_ref[0]
+        w2 = jnp.concatenate(
+            [ref[0][:rows] for ref, rows in zip(w2_refs, shape)], axis=0
+        )
+        for t in range(tok // block):
+            rows = slice(t * block, (t + 1) * block)
+            pre = jnp.dot(normed_ref[rows, :], w1, preferred_element_type=jnp.float32)
+            pre = pre + bias_ref[0]
+            hidden = 0.5 * pre * (1.0 + lax.erf(pre * math.sqrt(0.5)))
+            acc[rows, :] += jnp.dot(
+                hidden.astype(jnp.bfloat16), w2, preferred_element_type=jnp.float32
+            )
+
+    for h in range(halves):
+        pl.when(step // groups == h)(functools.partial(absorb, *sets[h]))
+
+    @pl.when(step == last_step)
+    def _():
+        for t in range(tok // block):
+            rows = slice(t * block, (t + 1) * block)
+            total = normed_ref[rows, :].astype(jnp.float32) + acc[rows, :] + b2_ref[...]
+            layer = normalize(total, gain_ref[...], bias2_ref[...]).astype(jnp.bfloat16)
+            done[rows, :] = layer
+            next_ref[rows, :] = (
+                jnp.dot(layer, next_w_ref[...], preferred_element_type=jnp.float32)
+                + next_b_ref[...]
+            ).astype(jnp.bfloat16)
+        share = layer_ref.shape[0]
+        layer_ref[...] = done[pl.ds(pl.multiple_of(place[0] * share, share), share), :]
+
+
+def feed(place, normed, bias, sets, shape, b2, gain, bias2, next_w, next_b, share):
+    tok, width = normed.shape
+    halves = len(sets)
+    groups, _, cols = sets[0][0].shape
+    steps = halves * groups
+    fixed = lambda i, *_: (0, 0)
+    specs, arrays = [], []
+    for h, (w1, w2s) in enumerate(sets):
+        at = lambda i, *_, h=h: (jnp.clip(i - h * groups, 0, groups - 1), 0, 0)
+        for array in (w1, *w2s):
+            specs.append(pl.BlockSpec((1,) + array.shape[1:], at))
+            arrays.append(array)
+    next_cols = next_w.shape[1]
+    return pl.pallas_call(
+        functools.partial(feed_kernel, halves=halves, shape=shape, last_step=steps - 1),
+        grid_spec=pltpu.PrefetchScalarGridSpec(
+            num_scalar_prefetch=1,
+            grid=(steps,),
+            in_specs=[
+                pl.BlockSpec((tok, width), fixed),
+                pl.BlockSpec((1, 1, cols), lambda i, *_: (i, 0, 0)),
+            ]
+            + specs
+            + [
+                pl.BlockSpec((1, width), fixed),
+                pl.BlockSpec((1, width), fixed),
+                pl.BlockSpec((1, width), fixed),
+                pl.BlockSpec((width, next_cols), fixed),
+                pl.BlockSpec((1, next_cols), fixed),
+            ],
+            out_specs=[
+                pl.BlockSpec((share, width), fixed),
+                pl.BlockSpec((tok, next_cols), fixed),
+            ],
+            scratch_shapes=[
+                pltpu.VMEM((tok, width), jnp.float32),
+                pltpu.VMEM((tok, width), jnp.bfloat16),
+            ],
+        ),
+        out_shape=[
+            jax.ShapeDtypeStruct((share, width), jnp.bfloat16),
+            jax.ShapeDtypeStruct((tok, next_cols), jnp.bfloat16),
+        ],
+        compiler_params=params(),
+        cost_estimate=pl.CostEstimate(
+            flops=4 * tok * width * cols * steps, bytes_accessed=4 * width * cols * steps,
+            transcendentals=tok * cols * steps,
+        ),
+        name="feed",
+    )(
+        place, normed, bias, *arrays,
+        b2[None], gain[None], bias2[None], next_w, next_b[None],
+    )
+
+
+def three_parts(values):
+    high = lax.reduce_precision(values, 8, 7)
+    middle = lax.reduce_precision(values - high, 8, 7)
+    rest = values - high - middle
+    return [part.astype(jnp.bfloat16) for part in (high, middle, rest)]
 
 
 def local(
@@ -426,6 +564,50 @@
             split = lax.dynamic_slice_in_dim(split, (dp_index % 2) * 2, 2, 1)
         return jnp.swapaxes(split, 1, 2).reshape(matrix.shape[0], -1)
 
+    place = jnp.stack([dp_index // 2 if shared else 0, mp_index]).astype(jnp.int32)
+    hidden_dev = first_feed_weight.shape[1]
+    if shared:
+        core, chip = dp_index % 2, dp_index // 2
+        unit = hidden_dev // 8
+        out_unit = attention_out_weight.shape[0] // 8
+
+        def half_columns(values, half):
+            axis = values.ndim - 1
+            return jnp.concatenate(
+                [
+                    lax.dynamic_slice_in_dim(values, (half * 4 + (chip ^ r)) * unit, unit, axis)
+                    for r in range(4)
+                ],
+                axis=axis,
+            )
+
+        bias_parts = jnp.stack(
+            three_parts(
+                jnp.concatenate(
+                    [half_columns(first_feed_bias, core), half_columns(first_feed_bias, 1 - core)]
+                )
+            )
+        )
+        spread = jnp.concatenate(
+            [
+                lax.dynamic_slice_in_dim(second_feed_weight, (core * 4 + chip) * unit, unit, 0),
+                lax.dynamic_slice_in_dim(
+                    attention_out_weight, (core * 4 + chip) * out_unit, out_unit, 0
+                ),
+                jnp.pad(bias_parts, ((0, 13), (0, 0))),
+            ],
+            axis=0,
+        )
+        spread = lax.all_gather(spread, "mp", axis=0)
+        first_half = half_columns(first_feed_weight, core)
+        first_half, spread = lax.optimization_barrier((first_half, spread))
+        first_mine = lax.all_gather(first_half, "mp", axis=0)
+        body = unit + out_unit
+        bias_rows = jnp.sum(spread[:, body : body + 3].astype(jnp.float32), axis=1)
+        feed_bias = jnp.swapaxes(bias_rows.reshape(mp_count, 2, 4 * unit), 0, 1)
+        feed_bias = feed_bias.reshape(2 * mp_count, 1, 4 * unit)
+        spread = spread[:, :body]
+
     weight = by_kind(query_key_value_weight)
     ups = by_kind(ups)
     if shared:
@@ -455,40 +637,48 @@
             state, False, pages,
         )
         far = jnp.stack([at(6), at(7)])
+        spread, kv_d0, kv_d1 = lax.optimization_barrier((spread, kv_d0, kv_d1))
+        spread_x = move(spread, across)
+        spread_y = move(spread, along)
+        cut = body // 2
+        spread_d0 = move(spread_y[:, :cut], across)
+        spread_d1 = move(spread_x[:, cut:], along)
+        mine = [spread, spread_x, spread_y, spread_d0, spread_d1]
+        other = [move(piece, swap) for piece in mine]
+        first_other = move(first_mine, swap)
         context = step(far, q, [kv_d0, kv_d1], state, True, pages)
-        mine, theirs = context[:tok_rows], move(context[tok_rows:], swap)
-        even = dp_index % 2 == 0
         context = jnp.concatenate(
-            [jnp.where(even, mine, theirs), jnp.where(even, theirs, mine)], axis=1
-        )
+            [context[:tok_rows], move(context[tok_rows:], swap)], axis=1
+        )
+        shape = (unit, unit, unit, cut, unit - cut)
+        sets = [(first_mine, mine), (first_other, other)]
+        wo_arrays = mine + other
+        plan = []
+        for half in range(2):
+            for n, flip in enumerate((0, 1, 2)):
+                plan.append((5 * half + n, unit, out_unit, half, flip, 0))
+            plan.append((5 * half + 4, unit - cut, out_unit, half, 3, 0))
+        wo_used = sorted({index for index, *_ in plan})
+        plan = tuple((wo_used.index(index), *rest) for index, *rest in plan)
+        wo_arrays = [wo_arrays[index] for index in wo_used]
     else:
         everything = lax.all_gather(kv, "dp", axis=0, tiled=True)
         context = attend(
             *args, bases, jnp.zeros((1,), jnp.int32), q, [everything], None, True, pages
         )
-    out_weight = lax.all_gather(attention_out_weight, "mp", axis=0)
+        first_all = lax.all_gather(first_feed_weight, "mp", axis=0)
+        second_all = lax.all_gather(second_feed_weight, "mp", axis=0)
+        feed_bias = lax.all_gather(first_feed_bias, "mp", axis=0)[:, None]
+        sets = [(first_all, [second_all])]
+        shape = (hidden_dev,)
+        wo_arrays = [lax.all_gather(attention_out_weight, "mp", axis=0)]
+        plan = ((0, 0, attention_out_weight.shape[0], 0, 0, 0),)
     contexts = lax.all_gather(context, "mp", axis=0)
-    normed = mix(tokens, contexts, out_weight, first_norm_gain, first_norm_bias)
-    share_rows = tok_rows // mp_count
-    row_base = mp_index * share_rows
-    hidden = jax.nn.gelu(
-        jnp.dot(normed, first_feed_weight, preferred_element_type=jnp.float32) + first_feed_bias,
-        approximate=False,
-    ).astype(jnp.bfloat16)
-    feed = lax.psum(
-        jnp.dot(hidden, second_feed_weight, preferred_element_type=jnp.float32).astype(
-            jnp.bfloat16
-        ),
-        "mp",
-    ).astype(jnp.float32)
-    layer_full = layer_norm(
-        normed.astype(jnp.float32) + feed + second_feed_bias, second_norm_gain, second_norm_bias
-    ).astype(jnp.bfloat16)
-    next_proj = (
-        jnp.dot(layer_full, following_qkv_weight, preferred_element_type=jnp.float32)
-        + following_bias
-    ).astype(jnp.bfloat16)
-    layer_rows = lax.dynamic_slice_in_dim(layer_full, row_base, share_rows, 0)
+    normed = mix(place, tokens, contexts, wo_arrays, plan, first_norm_gain, first_norm_bias)
+    layer_rows, next_proj = feed(
+        place[1:], normed, feed_bias, sets, shape, second_feed_bias, second_norm_gain,
+        second_norm_bias, following_qkv_weight, following_bias, tok_rows // mp_count,
+    )
     return (layer_rows, next_proj)
 
 

time: 301 us -> 303 us (level); the launches traced: 300 us -> 298 us
  Pallas kernels: 87.5 us -> 114 us
  waiting for transfers between devices: 139 us -> 118 us
  matrix products: 18.5 us -> 0 us
  local copies, waits for them, and re-layouts: 19.5 us -> 28.9 us
  starting transfers between devices: 11.9 us -> 17.6 us
  other arithmetic: 8.87 us -> 5.2 us
    psum x1 -> x0, waiting for transfers between devices: 85.4 us -> none  [local(): lax.psum(jnp.dot(hidden, second_feed_weight, preferred_element_type=jnp.f...]
    all_gather x1 -> x2, waiting for transfers between devices: 0.02 us -> 57.3 us  [the longest x1 35.3 us: local(): spread = lax.all_gather(spread, 'mp', axis=0)]
    ppermute x6 -> x16, waiting for transfers between devices: 2.64 us -> 53.2 us  [local(): move = lambda value, pairs: lax.ppermute(value, 'dp', pairs)]
    all_gather x1, waiting for transfers between devices: 48.8 us -> 0.02 us  [local(): contexts = lax.all_gather(context, 'mp', axis=0)]
    pallas_call x1 -> x2, Pallas kernels: 5.89 us -> 40.7 us  [the longest x1 32 us: feed(): pl.pallas_call(functools.partial(feed_kernel, halves=halves, shape=shape,...]
    dot_general x2 -> x0, matrix products: 18.5 us -> none  [the longest x1 15.6 us: local(): jnp.dot(hidden, second_feed_weight, preferred_element_type=jnp.float32)]
    ppermute x6 -> x16, starting transfers between devices: 5.72 us -> 14.1 us  [local(): move = lambda value, pairs: lax.ppermute(value, 'dp', pairs)]
    pallas_call x3, Pallas kernels: 73.3 us -> 65.1 us  [attend(): pl.pallas_call(functools.partial(attend_kernel, requests=requests, slots=...]
  transfers between devices with their start and end apart: 10 -> 20, of which waited for: 5 -> 10; matrix products, arithmetic and copies ran while one was open for 4% -> 7% of each run, Pallas kernels for 27% -> 27%
where the time goes in v3:
time: 303 us; the launch traced here: 298 us
  waiting for transfers between devices  118 us (39%)
  Pallas kernels  114 us (38%)
  local copies, waits for them, and re-layouts  28.9 us (10%)
  starting transfers between devices  17.6 us (6%)
  between operations  15 us (5%)
  other arithmetic  5.2 us (2%)
    pallas_call x3, Pallas kernels, attend(): pl.pallas_call(functools.partial(attend_kernel, requests=requests, slots=...  65.1 us
    ppermute x16, waiting for transfers between devices, local(): move = lambda value, pairs: lax.ppermute(value, 'dp', pairs)  53.2 us
    all_gather x1, waiting for transfers between devices, local(): spread = lax.all_gather(spread, 'mp', axis=0)  35.3 us
    pallas_call x1, Pallas kernels, feed(): pl.pallas_call(functools.partial(feed_kernel, halves=halves, shape=shape,...  32 us
    all_gather x1, waiting for transfers between devices, local(): first_mine = lax.all_gather(first_half, 'mp', axis=0)  22 us
    unnamed x53, local copies, waits for them, and re-layouts  14.3 us
    ppermute x16, starting transfers between devices, local(): move = lambda value, pairs: lax.ppermute(value, 'dp', pairs)  14.1 us
    pallas_call x1, Pallas kernels, mix(): pl.pallas_call(functools.partial(mix_kernel, plan=plan), grid_spec=pltpu....  8.69 us
  transfers between devices with their start and end apart: 20, of which 10 were waited for; matrix products, arithmetic and copies ran while one was open for 7% of the time, Pallas kernels for 27%

profile of v3, /device:TPU:0, one launch (start us, length us, event | category | flops | bytes accessed | tf_op | source)
XLA Modules:
  0.0 298.5 jit_solution(18335523505850234236)
XLA Ops:
  15.3 1.3 constant_dynamic-slice_fusion.5
  16.7 1.1 pad_maximum_fusion
  17.7 35.3 %all-gather.7.cloned.1.call-done = bf16[704,1024]{1,0:T(8,128)(2,1)} async-done(((bf16[176,1024]{1,0:T(8,128)(2,1)}), bf16[704,1024]{1,0:T(8,128)(2,1)}) %all-gather.7.cloned.1.call-update) | async-done | bytes 1441808 | tf_op jit(solution)/shard_map/all_gather | solution.py:601
  56.5 3.4 %all-to-all-start = ((bf16[16,4,1792]{2,0,1:T(8,128)(2,1)}), bf16[16,4,1792]{2,0,1:T(8,128)(2,1)S(1)}, u32[]{:S(2)}, u32[]{:S(2)}) async-start(bf16[16,4,1792]{2,0,1:T(8,128)(2,1)} %pad_maximum_fusion.3), calls=%async_computation | async-start | bytes 458752 | tf_op jit(solution)/shard_map/all_to_all | solution.py:557
  60.0 2.7 copy.29
  62.7 1.3 dynamic-slice_bitcast_fusion
  64.9 1.5 copy.35.refs_2_
  66.5 7.1 %all-to-all-done = bf16[16,4,1792]{2,0,1:T(8,128)(2,1)S(1)} async-done(((bf16[16,4,1792]{2,0,1:T(8,128)(2,1)}), bf16[16,4,1792]{2,0,1:T(8,128)(2,1)S(1)}, u32[]{:S(2)}, u32[]{:S(2)}) %all-to-all-start) | async-done | bytes 229408 | tf_op jit(solution)/shard_map/all_to_all | solution.py:557
  76.0 1.6 copy-done.1
  77.6 8.3 %project.1 = (bf16[2048,128]{1,0:T(8,128)(2,1)S(1)}, bf16[2048,256]{1,0:T(8,128)(2,1)S(1)}) custom-call(s32[4]{0:T(128)S(1)} %copy-done.9, s32[64]{0:T(128)S(1)} %copy-done.10, s32[4]{0:T(128)S(1)} %get-tuple-element.33.owners, s32[2]{0:T(128)S(1)} %get-tuple-element.49.bases.q_bases.kv_bases, bf16[1024,1024]{1,0:T(8,128)(2,1)S(1)} %copy-done.1, ...), custom_call_target="tpu_custom_call" | custom-call | flops 1610612736 | bytes 5767168 | tf_op jit(solution)/shard_map/project/pallas_call | solution.py:102
  85.9 1.5 collective-permute-start.2
  87.4 1.5 collective-permute-start.1
  89.0 14.9 %attend.3 = (f32[2048,128]{1,0:T(8,128)S(1)}, f32[2048,128]{1,0:T(8,128)S(1)}) custom-call(s32[4]{0:T(128)S(1)} %copy-done.9, s32[64]{0:T(128)S(1)} %copy-done.10, s32[2]{0:T(128)S(1)} %get-tuple-element.49.bases.q_bases.kv_bases, s32[2]{0:T(128)S(1)} %get-tuple-element.49.bases.q_bases.kv_bases, bf16[2048,128]{1,0:T(8,128)(2,1)S(1)} %get-tuple-element.17.q_ref, ...), custom_call_target="tpu_custom_call" | custom-call | flops 1073741824 | bytes 2097152 | tf_op jit(solution)/shard_map/attend/pallas_call | solution.py:304
  103.9 6.0 %collective-permute-done.2 = bf16[2048,256]{1,0:T(8,128)(2,1)S(1)} collective-permute-done((bf16[2048,256]{1,0:T(8,128)(2,1)S(1)}, bf16[2048,256]{1,0:T(8,128)(2,1)S(1)}, u32[]{:S(2)}, u32[]{:S(2)}) %collective-permute-start.2) | collective-permute-done | bytes 1048608 | tf_op jit(solution)/shard_map/ppermute | solution.py:617
  109.8 1.2 collective-permute-done.1
  112.1 1.5 collective-permute-start.3
  115.3 22.0 %all-gather.11.cloned.1.call-done = bf16[4096,512]{1,0:T(8,128)(2,1)} async-done(((bf16[1024,512]{1,0:T(8,128)(2,1)}), bf16[4096,512]{1,0:T(8,128)(2,1)}) %all-gather.11.cloned.1.call-update) | async-done | bytes 4194320 | tf_op jit(solution)/shard_map/all_gather | solution.py:604
  140.4 1.2 copy-done.15
  141.6 29.3 %attend.4 = (f32[2048,128]{1,0:T(8,128)S(1)}, f32[2048,128]{1,0:T(8,128)S(1)}) custom-call(s32[4]{0:T(128)S(1)} %copy-done.9, s32[64]{0:T(128)S(1)} %copy-done.10, s32[2]{0:T(128)S(1)} %get-tuple-element.49.bases.q_bases.kv_bases, s32[4]{0:T(128)S(1)} %get-tuple-element.51.kv_bases, bf16[2048,128]{1,0:T(8,128)(2,1)S(1)} %copy-done.12, ...), custom_call_target="tpu_custom_call" | custom-call | flops 2147483648 | bytes 3145728 | tf_op jit(solution)/shard_map/attend/pallas_call | solution.py:304
  171.0 20.8 %attend.5 = bf16[2048,128]{1,0:T(8,128)(2,1)S(1)} custom-call(s32[4]{0:T(128)S(1)} %copy-done.9, s32[64]{0:T(128)S(1)} %copy-done.10, s32[2]{0:T(128)S(1)} %get-tuple-element.49.bases.q_bases.kv_bases, s32[2]{0:T(128)S(1)} %get-tuple-element.50.kv_bases, bf16[2048,128]{1,0:T(8,128)(2,1)S(1)} %copy-done.13, bf16[1024,256]{1,0:T(8,128)(2,1)} %collective-permute-done.3.refs_0_, ...), custom_call_target="tpu_custom_call" | custom-call | flops 1073741824 | bytes 2097152 | tf_op jit(solution)/shard_map/attend/pallas_call | solution.py:304
  192.4 1.2 collective-permute-done.5
  194.5 4.8 %collective-permute-start.6 = (bf16[4,160,1024]{2,1,0:T(8,128)(2,1)S(1)}, bf16[4,160,1024]{2,1,0:T(8,128)(2,1)}, u32[]{:S(2)}, u32[]{:S(2)}) collective-permute-start(bf16[4,160,1024]{2,1,0:T(8,128)(2,1)S(1)} %slice.46.refs_0_.refs_1_), channel_id=1, source_target_pairs={{0,8},{4,12},{8,0},{12,4},{16,24},{20,28},{24,16},{28,20},{1,9},{5... | collective-permute-start | bytes 3932168 | tf_op jit(solution)/shard_map/ppermute | solution.py:617
  199.4 26.3 %collective-permute-done.7.refs_2_.refs_3_ = bf16[4,160,1024]{2,1,0:T(8,128)(2,1)} collective-permute-done((bf16[4,160,1024]{2,1,0:T(8,128)(2,1)S(1)}, bf16[4,160,1024]{2,1,0:T(8,128)(2,1)}, u32[]{:S(2)}, u32[]{:S(2)}) %collective-permute-start.7) | collective-permute-done | bytes 1310752 | tf_op jit(solution)/shard_map/ppermute | solution.py:617
  225.7 3.0 %collective-permute-done.6.refs_1_.refs_2_ = bf16[4,160,1024]{2,1,0:T(8,128)(2,1)} collective-permute-done((bf16[4,160,1024]{2,1,0:T(8,128)(2,1)S(1)}, bf16[4,160,1024]{2,1,0:T(8,128)(2,1)}, u32[]{:S(2)}, u32[]{:S(2)}) %collective-permute-start.6) | collective-permute-done | bytes 1310752 | tf_op jit(solution)/shard_map/ppermute | solution.py:617
  228.7 1.1 slice.62
  229.8 1.7 collective-permute-start.8
  231.6 1.1 slice.63
  232.7 1.8 collective-permute-start.13
  234.5 11.9 %collective-permute-done.8.refs_3_.refs_5_ = bf16[4,80,1024]{2,1,0:T(8,128)(2,1)} collective-permute-done((bf16[4,80,1024]{2,1,0:T(8,128)(2,1)S(1)}, bf16[4,80,1024]{2,1,0:T(8,128)(2,1)}, u32[]{:S(2)}, u32[]{:S(2)}) %collective-permute-start.8) | collective-permute-done | bytes 655392 | tf_op jit(solution)/shard_map/ppermute | solution.py:617
  246.4 3.6 %collective-permute-done.13.refs_4_ = bf16[4,80,1024]{2,1,0:T(8,128)(2,1)} collective-permute-done((bf16[4,80,1024]{2,1,0:T(8,128)(2,1)S(1)}, bf16[4,80,1024]{2,1,0:T(8,128)(2,1)}, u32[]{:S(2)}, u32[]{:S(2)}) %collective-permute-start.13) | collective-permute-done | bytes 655392 | tf_op jit(solution)/shard_map/ppermute | solution.py:617
  251.2 8.7 %mix.1.normed_ref = bf16[1024,1024]{1,0:T(8,128)(2,1)} custom-call(s32[2]{0:T(128)S(1)} %pad_add_fusion.bases, bf16[1024,1024]{1,0:T(8,128)(2,1)} %x_ref.1, bf16[4,1024,256]{2,1,0:T(8,128)(2,1)} %bitcast.61, bf16[4,160,1024]{2,1,0:T(8,128)(2,1)S(1)} %slice.46.refs_0_.refs_1_, bf16[4,160,1024]{2,1,0:T(8,128)(2,1)} %collective-permute-done.6.refs_1_.refs_2_, ...), custom_call_target="tpu_custom_call" | custom-call | flops 2147483648 | bytes 8388608 | tf_op jit(solution)/shard_map/mix/pallas_call | solution.py:376
  259.9 32.0 %feed.1 = (bf16[256,1024]{1,0:T(8,128)(2,1)}, bf16[1024,768]{1,0:T(8,128)(2,1)}) custom-call(s32[1]{0:T(128)} %bitcast.place, bf16[1024,1024]{1,0:T(8,128)(2,1)} %mix.1.normed_ref, f32[8,1,512]{2,1,0:T(1,128)S(1)} %reshape.346.bias_ref, bf16[4,1024,512]{2,1,0:T(8,128)(2,1)} %bitcast.70, bf16[4,160,1024]{2,1,0:T(8,128)(2,1)S(1)} %slice.46.refs_0_.refs_1_, ...), custom_call_target="tpu_custom_call" | custom-call | flops 17179869184 | bytes 16777216 | tf_op jit(solution)/shard_map/feed/pallas_call | solution.py:464
  (107 shorter events, 22.7 us)
Async XLA Ops:
  7.2 45.9 %all-gather.7.cloned.1.call-start = ((), (), s32[]{:S(2)}) async-start(), calls=%async_computation.1 | async-start | bytes 1802240 | tf_op jit(solution)/shard_map/all_gather | solution.py:601
  15.3 122.0 %all-gather.11.cloned.1.call-start = ((), (), s32[]{:S(2)}) async-start(), calls=%async_computation.3 | async-start | bytes 5242880 | tf_op jit(solution)/shard_map/all_gather | solution.py:604
  16.6 36.6 %copy-start.21 = (s32[4]{0:T(128)S(1)}, s32[4]{0:T(128)}, u32[]{:S(2)}) copy-start(s32[4]{0:T(128)} %param.35) | copy-start | bytes 52
  16.6 38.9 %copy-start.19 = (bf16[1024,128]{1,0:T(8,128)(2,1)S(1)}, bf16[1024,128]{1,0:T(8,128)(2,1)}, u32[]{:S(2)}) copy-start(bf16[1024,128]{1,0:T(8,128)(2,1)} %param.20) | copy-start | bytes 786436
  53.1 22.8 %collective-permute-start = (bf16[1024,1024]{1,0:T(8,128)(2,1)}, bf16[1024,1024]{1,0:T(8,128)(2,1)}, u32[]{:S(2)}, u32[]{:S(2)}) collective-permute-start(bf16[1024,1024]{1,0:T(8,128)(2,1)} %x_ref.1), channel_id=1, source_target_pairs={{0,4},{4,0},{8,12},{12,8},{16,20},{20,16},{24,28},{28,24},{1,5},{5... | collective-permute-start | bytes 6291464 | tf_op jit(solution)/shard_map/ppermute | solution.py:617
  56.5 17.1 %all-to-all-start = ((bf16[16,4,1792]{2,0,1:T(8,128)(2,1)}), bf16[16,4,1792]{2,0,1:T(8,128)(2,1)S(1)}, u32[]{:S(2)}, u32[]{:S(2)}) async-start(bf16[16,4,1792]{2,0,1:T(8,128)(2,1)} %pad_maximum_fusion.3), calls=%async_computation | async-start | bytes 458752 | tf_op jit(solution)/shard_map/all_to_all | solution.py:557
  59.9 191.2 %all-gather.9.cloned.1.call-start = ((), (), s32[]{:S(2)}) async-start(), calls=%async_computation.2 | async-start | bytes 2621440 | tf_op jit(solution)/shard_map/all_gather | solution.py:676
  64.9 11.0 %copy-start.9 = (s32[4]{0:T(128)S(1)}, s32[4]{0:T(128)}, u32[]{:S(2)}) copy-start(s32[4]{0:T(128)} %counts.7) | copy-start | bytes 52
  64.9 11.0 %copy-start.10 = (s32[64]{0:T(128)S(1)}, s32[64]{0:T(128)}, u32[]{:S(2)}) copy-start(s32[64]{0:T(128)} %table.7) | copy-start | bytes 772
  85.9 18.0 %copy-start.11 = (bf16[2048,128]{1,0:T(8,128)(2,1)}, bf16[2048,128]{1,0:T(8,128)(2,1)S(1)}, u32[]{:S(2)}) copy-start(bf16[2048,128]{1,0:T(8,128)(2,1)S(1)} %get-tuple-element.17.q_ref) | copy-start | bytes 1572868
  85.9 24.0 %collective-permute-start.2 = (bf16[2048,256]{1,0:T(8,128)(2,1)S(1)}, bf16[2048,256]{1,0:T(8,128)(2,1)S(1)}, u32[]{:S(2)}, u32[]{:S(2)}) collective-permute-start(bf16[2048,256]{1,0:T(8,128)(2,1)S(1)} %get-tuple-element.19), channel_id=1, source_target_pairs={{0,16},{4,20},{8,24},{12,28},{16,0},{20,4},{24,8},{28,12},{1,17},{... | collective-permute-start | bytes 3145736 | tf_op jit(solution)/shard_map/ppermute | solution.py:617
  87.4 23.6 %collective-permute-start.1 = (bf16[2048,256]{1,0:T(8,128)(2,1)S(1)}, bf16[2048,256]{1,0:T(8,128)(2,1)S(1)}, u32[]{:S(2)}, u32[]{:S(2)}) collective-permute-start(bf16[2048,256]{1,0:T(8,128)(2,1)S(1)} %get-tuple-element.19), channel_id=1, source_target_pairs={{0,8},{4,12},{8,0},{12,4},{16,24},{20,28},{24,16},{28,20},{1,9},{5... | collective-permute-start | bytes 3145736 | tf_op jit(solution)/shard_map/ppermute | solution.py:617
  103.9 10.8 %copy-start.14 = (f32[2048,128]{1,0:T(8,128)}, f32[2048,128]{1,0:T(8,128)S(1)}, u32[]{:S(2)}) copy-start(f32[2048,128]{1,0:T(8,128)S(1)} %get-tuple-element.26.refs_4_) | copy-start | bytes 3145732
  103.9 10.8 %copy-start.16 = (f32[2048,128]{1,0:T(8,128)}, f32[2048,128]{1,0:T(8,128)S(1)}, u32[]{:S(2)}) copy-start(f32[2048,128]{1,0:T(8,128)S(1)} %get-tuple-element.27.refs_5_) | copy-start | bytes 3145732
  112.1 58.8 %collective-permute-start.3 = (bf16[1024,256]{1,0:T(8,128)(2,1)}, bf16[1024,256]{1,0:T(8,128)(2,1)}, u32[]{:S(2)}, u32[]{:S(2)}) collective-permute-start(bf16[1024,256]{1,0:T(8,128)(2,1)} %get-tuple-element.39.refs_2_), channel_id=1, source_target_pairs={{0,8},{4,12},{8,0},{12,4},{16,24},{20,28},{24,16},{28,20},{1,9},{5... | collective-permute-start | bytes 1572872 | tf_op jit(solution)/shard_map/ppermute | solution.py:617
  114.6 56.3 %collective-permute-start.4 = (bf16[1024,256]{1,0:T(8,128)(2,1)}, bf16[1024,256]{1,0:T(8,128)(2,1)}, u32[]{:S(2)}, u32[]{:S(2)}) collective-permute-start(bf16[1024,256]{1,0:T(8,128)(2,1)} %get-tuple-element.41.refs_1_), channel_id=1, source_target_pairs={{0,16},{4,20},{8,24},{12,28},{16,0},{20,4},{24,8},{28,12},{1,17},{... | collective-permute-start | bytes 1572872 | tf_op jit(solution)/shard_map/ppermute | solution.py:617
  137.2 122.7 %collective-permute-start.14 = (bf16[4,1024,512]{2,1,0:T(8,128)(2,1)}, bf16[4,1024,512]{2,1,0:T(8,128)(2,1)}, u32[]{:S(2)}, u32[]{:S(2)}) collective-permute-start(bf16[4,1024,512]{2,1,0:T(8,128)(2,1)} %bitcast.69), channel_id=1, source_target_pairs={{0,4},{4,0},{8,12},{12,8},{16,20},{20,16},{24,28},{28,24},{1,5},{5... | collective-permute-start | bytes 12582920 | tf_op jit(solution)/shard_map/ppermute | solution.py:617
  141.6 29.4 %copy-start.13 = (bf16[2048,128]{1,0:T(8,128)(2,1)S(1)}, bf16[2048,128]{1,0:T(8,128)(2,1)}, u32[]{:S(2)}) copy-start(bf16[2048,128]{1,0:T(8,128)(2,1)} %copy-done.11) | copy-start | bytes 1572868
  191.8 1.7 collective-permute-start.5
  193.6 56.5 %copy-start.20 = (f32[768]{0:T(1024)S(1)}, f32[768]{0:T(1024)}, u32[]{:S(2)}) copy-start(f32[768]{0:T(1024)} %param.32) | copy-start | bytes 9220
  193.6 57.6 %copy-start.4 = (f32[1024]{0:T(1024)S(1)}, f32[1024]{0:T(1024)}, u32[]{:S(2)}) copy-start(f32[1024]{0:T(1024)} %param.23) | copy-start | bytes 12292
  193.6 57.6 %copy-start.5 = (f32[1024]{0:T(1024)S(1)}, f32[1024]{0:T(1024)}, u32[]{:S(2)}) copy-start(f32[1024]{0:T(1024)} %param.24) | copy-start | bytes 12292
  194.5 31.2 %collective-permute-start.7 = (bf16[4,160,1024]{2,1,0:T(8,128)(2,1)S(1)}, bf16[4,160,1024]{2,1,0:T(8,128)(2,1)}, u32[]{:S(2)}, u32[]{:S(2)}) collective-permute-start(bf16[4,160,1024]{2,1,0:T(8,128)(2,1)S(1)} %slice.46.refs_0_.refs_1_), channel_id=1, source_target_pairs={{0,16},{4,20},{8,24},{12,28},{16,0},{20,4},{24,8},{28,12},{1,17},{... | collective-permute-start | bytes 3932168 | tf_op jit(solution)/shard_map/ppermute | solution.py:617
  194.5 34.2 %collective-permute-start.6 = (bf16[4,160,1024]{2,1,0:T(8,128)(2,1)S(1)}, bf16[4,160,1024]{2,1,0:T(8,128)(2,1)}, u32[]{:S(2)}, u32[]{:S(2)}) collective-permute-start(bf16[4,160,1024]{2,1,0:T(8,128)(2,1)S(1)} %slice.46.refs_0_.refs_1_), channel_id=1, source_target_pairs={{0,8},{4,12},{8,0},{12,4},{16,24},{20,28},{24,16},{28,20},{1,9},{5... | collective-permute-start | bytes 3932168 | tf_op jit(solution)/shard_map/ppermute | solution.py:617
  199.3 33.4 %collective-permute-start.9 = (bf16[4,160,1024]{2,1,0:T(8,128)(2,1)S(1)}, bf16[4,160,1024]{2,1,0:T(8,128)(2,1)S(1)}, u32[]{:S(2)}, u32[]{:S(2)}) collective-permute-start(bf16[4,160,1024]{2,1,0:T(8,128)(2,1)S(1)} %slice.46.refs_0_.refs_1_), channel_id=1, source_target_pairs={{0,4},{4,0},{8,12},{12,8},{16,20},{20,16},{24,28},{28,24},{1,5},{5... | collective-permute-start | bytes 3932168 | tf_op jit(solution)/shard_map/ppermute | solution.py:617
  225.7 25.4 %collective-permute-start.11 = (bf16[4,160,1024]{2,1,0:T(8,128)(2,1)}, bf16[4,160,1024]{2,1,0:T(8,128)(2,1)}, u32[]{:S(2)}, u32[]{:S(2)}) collective-permute-start(bf16[4,160,1024]{2,1,0:T(8,128)(2,1)} %collective-permute-done.7.refs_2_.refs_3_), channel_id=1, source_target_pairs={{0,4},{4,0},{8,12},{12,8},{16,20},{20,16},{24,28},{28,24},{1,5},{5... | collective-permute-start | bytes 3932168 | tf_op jit(solution)/shard_map/ppermute | solution.py:617
  229.8 16.6 %collective-permute-start.8 = (bf16[4,80,1024]{2,1,0:T(8,128)(2,1)S(1)}, bf16[4,80,1024]{2,1,0:T(8,128)(2,1)}, u32[]{:S(2)}, u32[]{:S(2)}) collective-permute-start(bf16[4,80,1024]{2,1,0:T(8,128)(2,1)S(1)} %slice.62), channel_id=1, source_target_pairs={{0,16},{4,20},{8,24},{12,28},{16,0},{20,4},{24,8},{28,12},{1,17},{... | collective-permute-start | bytes 1966088 | tf_op jit(solution)/shard_map/ppermute | solution.py:617
  231.6 19.5 %collective-permute-start.10 = (bf16[4,160,1024]{2,1,0:T(8,128)(2,1)}, bf16[4,160,1024]{2,1,0:T(8,128)(2,1)}, u32[]{:S(2)}, u32[]{:S(2)}) collective-permute-start(bf16[4,160,1024]{2,1,0:T(8,128)(2,1)} %collective-permute-done.6.refs_1_.refs_2_), channel_id=1, source_target_pairs={{0,4},{4,0},{8,12},{12,8},{16,20},{20,16},{24,28},{28,24},{1,5},{5... | collective-permute-start | bytes 3932168 | tf_op jit(solution)/shard_map/ppermute | solution.py:617
  232.7 18.3 %copy-start.17 = (bf16[4,160,1024]{2,1,0:T(8,128)(2,1)}, bf16[4,160,1024]{2,1,0:T(8,128)(2,1)S(1)}, u32[]{:S(2)}) copy-start(bf16[4,160,1024]{2,1,0:T(8,128)(2,1)S(1)} %collective-permute-done.9.refs_4_.refs_7_) | copy-start | bytes 3932164
  232.7 17.3 %collective-permute-start.13 = (bf16[4,80,1024]{2,1,0:T(8,128)(2,1)S(1)}, bf16[4,80,1024]{2,1,0:T(8,128)(2,1)}, u32[]{:S(2)}, u32[]{:S(2)}) collective-permute-start(bf16[4,80,1024]{2,1,0:T(8,128)(2,1)S(1)} %slice.63), channel_id=1, source_target_pairs={{0,8},{4,12},{8,0},{12,4},{16,24},{20,28},{24,16},{28,20},{1,9},{5... | collective-permute-start | bytes 1966088 | tf_op jit(solution)/shard_map/ppermute | solution.py:617
  246.4 4.6 %collective-permute-start.12 = (bf16[4,80,1024]{2,1,0:T(8,128)(2,1)}, bf16[4,80,1024]{2,1,0:T(8,128)(2,1)}, u32[]{:S(2)}, u32[]{:S(2)}) collective-permute-start(bf16[4,80,1024]{2,1,0:T(8,128)(2,1)} %collective-permute-done.8.refs_3_.refs_5_), channel_id=1, source_target_pairs={{0,4},{4,0},{8,12},{12,8},{16,20},{20,16},{24,28},{28,24},{1,5},{5... | collective-permute-start | bytes 1966088 | tf_op jit(solution)/shard_map/ppermute | solution.py:617
  250.0 9.8 %collective-permute-start.15 = (bf16[4,80,1024]{2,1,0:T(8,128)(2,1)}, bf16[4,80,1024]{2,1,0:T(8,128)(2,1)}, u32[]{:S(2)}, u32[]{:S(2)}) collective-permute-start(bf16[4,80,1024]{2,1,0:T(8,128)(2,1)} %collective-permute-done.13.refs_4_), channel_id=1, source_target_pairs={{0,4},{4,0},{8,12},{12,8},{16,20},{20,16},{24,28},{28,24},{1,5},{5... | collective-permute-start | bytes 1966088 | tf_op jit(solution)/shard_map/ppermute | solution.py:617
  (10 other events, 42.7 us)
Sparse Core Ops, SparseCore 0:
  15.4 37.6 all-gather.6
  54.6 82.5 all-gather.10
  194.6 47.2 all-gather.8

commit v4 on v2

--- a/solution.py
+++ b/solution.py
@@ -336,40 +336,180 @@
     return out[0] if last else out
 
 
-def mix_kernel(x_ref, ctx_ref, wo_ref, gain_ref, bias_ref, out_ref):
+def mix_kernel(x_ref, ctx_ref, *refs, parts):
+    out_w_refs = refs[:parts]
+    gain_ref, bias_ref, out_ref, joined = refs[parts:]
+
+    @pl.when(pl.program_id(0) == 0)
+    def _():
+        near = out_w_refs[0].shape[1]
+        for i in range(parts):
+            joined[:, i * near : (i + 1) * near] = out_w_refs[i][...]
+
     mixed = x_ref[...].astype(jnp.float32)
     for j in range(ctx_ref.shape[0]):
-        mixed = mixed + jnp.dot(ctx_ref[j], wo_ref[j], preferred_element_type=jnp.float32)
+        mixed = mixed + jnp.dot(ctx_ref[j], joined[j], preferred_element_type=jnp.float32)
     out_ref[...] = normalize(mixed, gain_ref[...], bias_ref[...]).astype(jnp.bfloat16)
 
 
-def mix(x, ctx, wo, gain, bias):
+def mix(x, ctx, outs, gain, bias):
     tok, width = x.shape
     groups, _, cols = ctx.shape
     block = 256
     rows = lambda i: (i, 0)
+    fixed = lambda i: (0, 0)
     return pl.pallas_call(
-        mix_kernel,
+        functools.partial(mix_kernel, parts=len(outs)),
         grid=(tok // block,),
         in_specs=[
             pl.BlockSpec((block, width), rows),
             pl.BlockSpec((groups, block, cols), lambda i: (0, i, 0)),
-            pl.BlockSpec(wo.shape, lambda i: (0, 0, 0)),
-            pl.BlockSpec((1, width), lambda i: (0, 0)),
-            pl.BlockSpec((1, width), lambda i: (0, 0)),
-        ],
+        ]
+        + [pl.BlockSpec(w.shape, lambda i: (0, 0, 0)) for w in outs]
+        + [pl.BlockSpec((1, width), fixed)] * 2,
         out_specs=pl.BlockSpec((block, width), rows),
+        scratch_shapes=[pltpu.VMEM((groups, cols, width), jnp.bfloat16)],
         out_shape=jax.ShapeDtypeStruct((tok, width), jnp.bfloat16),
         compiler_params=params(),
         cost_estimate=pl.CostEstimate(
             flops=2 * tok * width * groups * cols, bytes_accessed=8 * tok * width, transcendentals=0
         ),
         name="mix",
-    )(x, ctx, wo, gain[None], bias[None])
-
-
-def layer_norm(values, gain_row, bias_row):
-    return normalize(values, gain_row, bias_row)
+    )(x, ctx, *outs, gain[None], bias[None])
+
+
+def feed_kernel(place, normed_ref, bias_ref, *refs, counts, last_step):
+    refs = list(refs)
+    sets = []
+    for n1, n2 in counts:
+        w1s, refs = refs[:n1], refs[n1:]
+        w2s, refs = refs[:n2], refs[n2:]
+        sets.append((w1s, w2s))
+    b2_ref, gain_ref, bias2_ref, next_w_ref, next_b_ref = refs[:5]
+    layer_ref, next_ref, acc, done = refs[5:]
+    step = pl.program_id(0)
+    tok = normed_ref.shape[0]
+    block = min(256, tok)
+    halves = len(sets)
+    groups = (last_step + 1) // halves
+
+    @pl.when(step == 0)
+    def _():
+        acc[...] = jnp.zeros_like(acc)
+
+    def absorb(h, w1_refs, w2_refs):
+        if len(w1_refs) == 1:
+            w1 = w1_refs[0][0]
+            starts, cols = [0], w1.shape[1]
+        else:
+            diagonal = jnp.concatenate([w1_refs[3][0], w1_refs[4][0]], axis=0)
+            w1 = jnp.concatenate([ref[0] for ref in w1_refs[:3]] + [diagonal], axis=1)
+            cols = diagonal.shape[1]
+            core = place[2] if h == 0 else 1 - place[2]
+            starts = [
+                pl.multiple_of((core * 4 + (place[1] ^ r)) * cols, cols) for r in range(4)
+            ]
+        w2 = jnp.concatenate([ref[0] for ref in w2_refs], axis=0)
+        bias = jnp.concatenate(
+            [
+                jnp.sum(
+                    bias_ref[0, :, pl.ds(start, cols)].astype(jnp.float32), axis=0, keepdims=True
+                )
+                for start in starts
+            ],
+            axis=1,
+        )
+        for t in range(tok // block):
+            rows = slice(t * block, (t + 1) * block)
+            pre = jnp.dot(normed_ref[rows, :], w1, preferred_element_type=jnp.float32) + bias
+            hidden = 0.5 * pre * (1.0 + lax.erf(pre * math.sqrt(0.5)))
+            acc[rows, :] += jnp.dot(
+                hidden.astype(jnp.bfloat16), w2, preferred_element_type=jnp.float32
+            )
+
+    for h in range(halves):
+        pl.when(step // groups == h)(functools.partial(absorb, h, *sets[h]))
+
+    @pl.when(step == last_step)
+    def _():
+        for t in range(tok // block):
+            rows = slice(t * block, (t + 1) * block)
+            total = normed_ref[rows, :].astype(jnp.float32) + acc[rows, :] + b2_ref[...]
+            layer = normalize(total, gain_ref[...], bias2_ref[...]).astype(jnp.bfloat16)
+            done[rows, :] = layer
+            next_ref[rows, :] = (
+                jnp.dot(layer, next_w_ref[...], preferred_element_type=jnp.float32)
+                + next_b_ref[...]
+            ).astype(jnp.bfloat16)
+        share = layer_ref.shape[0]
+        layer_ref[...] = done[pl.ds(pl.multiple_of(place[0] * share, share), share), :]
+
+
+def feed(place, normed, bias, sets, b2, gain, bias2, next_w, next_b, share):
+    tok, width = normed.shape
+    halves = len(sets)
+    groups = bias.shape[0]
+    cols = bias.shape[2] // halves
+    steps = halves * groups
+    fixed = lambda i, *_: (0, 0)
+    specs, arrays = [], []
+    for h, (w1s, w2s) in enumerate(sets):
+        at = lambda i, *_, h=h: (jnp.clip(i - h * groups, 0, groups - 1), 0, 0)
+        for array in (*w1s, *w2s):
+            specs.append(pl.BlockSpec((1,) + array.shape[1:], at))
+            arrays.append(array)
+    next_cols = next_w.shape[1]
+    return pl.pallas_call(
+        functools.partial(
+            feed_kernel,
+            counts=tuple((len(w1s), len(w2s)) for w1s, w2s in sets),
+            last_step=steps - 1,
+        ),
+        grid_spec=pltpu.PrefetchScalarGridSpec(
+            num_scalar_prefetch=1,
+            grid=(steps,),
+            in_specs=[
+                pl.BlockSpec((tok, width), fixed),
+                pl.BlockSpec((1,) + bias.shape[1:], lambda i, *_: (i % groups, 0, 0)),
+            ]
+            + specs
+            + [
+                pl.BlockSpec((1, width), fixed),
+                pl.BlockSpec((1, width), fixed),
+                pl.BlockSpec((1, width), fixed),
+                pl.BlockSpec((width, next_cols), fixed),
+                pl.BlockSpec((1, next_cols), fixed),
+            ],
+            out_specs=[
+                pl.BlockSpec((share, width), fixed),
+                pl.BlockSpec((tok, next_cols), fixed),
+            ],
+            scratch_shapes=[
+                pltpu.VMEM((tok, width), jnp.float32),
+                pltpu.VMEM((tok, width), jnp.bfloat16),
+            ],
+        ),
+        out_shape=[
+            jax.ShapeDtypeStruct((share, width), jnp.bfloat16),
+            jax.ShapeDtypeStruct((tok, next_cols), jnp.bfloat16),
+        ],
+        compiler_params=params(),
+        cost_estimate=pl.CostEstimate(
+            flops=4 * tok * width * cols * steps, bytes_accessed=4 * width * cols * steps,
+            transcendentals=tok * cols * steps,
+        ),
+        name="feed",
+    )(
+        place, normed, bias, *arrays,
+        b2[None], gain[None], bias2[None], next_w, next_b[None],
+    )
+
+
+def three_parts(values):
+    high = lax.reduce_precision(values, 8, 7)
+    middle = lax.reduce_precision(values - high, 8, 7)
+    rest = values - high - middle
+    return [part.astype(jnp.bfloat16) for part in (high, middle, rest)]
 
 
 def local(
@@ -426,6 +566,16 @@
             split = lax.dynamic_slice_in_dim(split, (dp_index % 2) * 2, 2, 1)
         return jnp.swapaxes(split, 1, 2).reshape(matrix.shape[0], -1)
 
+    place = jnp.stack(
+        [mp_index] + ([dp_index // 2, dp_index % 2] if shared else [0, 0])
+    ).astype(jnp.int32)
+    hidden_dev = first_feed_weight.shape[1]
+    if shared:
+        unit = hidden_dev // 8
+        turn = (dp_index % 2) * 4 + dp_index // 2
+        first = lax.dynamic_slice_in_dim(first_feed_weight, turn * unit, unit, 1)
+        first = lax.all_gather(first, "mp", axis=0)
+
     weight = by_kind(query_key_value_weight)
     ups = by_kind(ups)
     if shared:
@@ -444,51 +594,77 @@
     if shared:
         kv_x = move(kv, across)
         kv_y = move(kv, along)
+        second = jnp.concatenate(
+            [lax.dynamic_slice_in_dim(second_feed_weight, turn * unit, unit, 0)]
+            + [jnp.pad(jnp.stack(three_parts(first_feed_bias)), ((0, 13), (0, 0)))],
+            axis=0,
+        )
+        second, _ = lax.optimization_barrier((second, kv))
+        second = lax.all_gather(second, "mp", axis=0)
         step = functools.partial(attend, *args, bases)
         state = step(bases, q, [kv[:tok_rows], kv[tok_rows:]], None, False, pages)
-        kv_x, kv_y, state = lax.optimization_barrier((kv_x, kv_y, state))
+        kv_x, kv_y, state, first = lax.optimization_barrier((kv_x, kv_y, state, first))
         kv_d0 = move(kv_y[:tok_rows], across)
         kv_d1 = move(kv_x[tok_rows:], along)
+        first_x = move(first, across)
+        first_y = move(first, along)
+        out_rows = attention_out_weight.shape[0] // 2
+        out_half = lax.dynamic_slice_in_dim(
+            attention_out_weight, (dp_index % 2) * out_rows, out_rows, 0
+        )
+        out_half, kv_x = lax.optimization_barrier((out_half, kv_x))
+        out_mine = lax.all_gather(out_half, "mp", axis=0)
         near = jnp.stack([at(2), at(3), at(4), at(5)])
         state = step(
             near, q, [kv_x[:tok_rows], kv_x[tok_rows:], kv_y[:tok_rows], kv_y[tok_rows:]],
             state, False, pages,
         )
+        kv_d0, kv_d1, first_x, first_y, state = lax.optimization_barrier(
+            (kv_d0, kv_d1, first_x, first_y, state)
+        )
+        cut = width // 2
+        first_d0 = move(first_y[:, :cut], across)
+        first_d1 = move(first_x[:, cut:], along)
+        first_near = [move(piece, swap) for piece in (first, first_x, first_y)]
         far = jnp.stack([at(6), at(7)])
         context = step(far, q, [kv_d0, kv_d1], state, True, pages)
-        mine, theirs = context[:tok_rows], move(context[tok_rows:], swap)
-        even = dp_index % 2 == 0
+        context, first_d0, first_d1, second, out_mine = lax.optimization_barrier(
+            (context, first_d0, first_d1, second, out_mine)
+        )
+        bias_rows = second[:, unit:]
+        second = second[:, :unit]
+        second_x = move(second, across)
+        second_y = move(second, along)
         context = jnp.concatenate(
-            [jnp.where(even, mine, theirs), jnp.where(even, theirs, mine)], axis=1
-        )
+            [context[:tok_rows], move(context[tok_rows:], swap)], axis=1
+        )
+        contexts = lax.all_gather(context, "mp", axis=0)
+        out_other = move(out_mine, swap)
+        firsts = [first, first_x, first_y, first_d0, first_d1]
+        first_others = first_near + [move(first_d0, swap), move(first_d1, swap)]
+        half = unit // 2
+        second_d0 = move(second_y[:, :half], across)
+        second_d1 = move(second_x[:, half:], along)
+        seconds = [second, second_x, second_y, second_d0, second_d1]
+        second_others = [move(piece, swap) for piece in seconds]
+        sets = [(firsts, seconds), (first_others, second_others)]
+        outs = [out_mine, out_other]
     else:
         everything = lax.all_gather(kv, "dp", axis=0, tiled=True)
         context = attend(
             *args, bases, jnp.zeros((1,), jnp.int32), q, [everything], None, True, pages
         )
-    out_weight = lax.all_gather(attention_out_weight, "mp", axis=0)
-    contexts = lax.all_gather(context, "mp", axis=0)
-    normed = mix(tokens, contexts, out_weight, first_norm_gain, first_norm_bias)
-    share_rows = tok_rows // mp_count
-    row_base = mp_index * share_rows
-    hidden = jax.nn.gelu(
-        jnp.dot(normed, first_feed_weight, preferred_element_type=jnp.float32) + first_feed_bias,
-        approximate=False,
-    ).astype(jnp.bfloat16)
-    feed = lax.psum(
-        jnp.dot(hidden, second_feed_weight, preferred_element_type=jnp.float32).astype(
-            jnp.bfloat16
-        ),
-        "mp",
-    ).astype(jnp.float32)
-    layer_full = layer_norm(
-        normed.astype(jnp.float32) + feed + second_feed_bias, second_norm_gain, second_norm_bias
-    ).astype(jnp.bfloat16)
-    next_proj = (
-        jnp.dot(layer_full, following_qkv_weight, preferred_element_type=jnp.float32)
-        + following_bias
-    ).astype(jnp.bfloat16)
-    layer_rows = lax.dynamic_slice_in_dim(layer_full, row_base, share_rows, 0)
+        bias_rows = jnp.pad(jnp.stack(three_parts(first_feed_bias)), ((0, 13), (0, 0)))
+        second = lax.all_gather(second_feed_weight, "mp", axis=0)
+        bias_rows = lax.all_gather(bias_rows, "mp", axis=0)
+        sets = [([lax.all_gather(first_feed_weight, "mp", axis=0)], [second])]
+        outs = [lax.all_gather(attention_out_weight, "mp", axis=0)]
+        contexts = lax.all_gather(context, "mp", axis=0)
+    normed = mix(tokens, contexts, outs, first_norm_gain, first_norm_bias)
+    layer_rows, next_proj = feed(
+        place, normed, bias_rows, sets, second_feed_bias, second_norm_gain,
+        second_norm_bias, following_qkv_weight, following_bias, tok_rows // mp_count,
+    )
     return (layer_rows, next_proj)
 
 

time: 301 us -> 253 us (0.84)
  waiting for transfers between devices: 139 us -> 45.8 us
  Pallas kernels: 87.5 us -> 118 us
  local copies, waits for them, and re-layouts: 19.5 us -> 44.5 us
  matrix products: 18.5 us -> 0 us
  starting transfers between devices: 11.9 us -> 22.3 us
  other arithmetic: 8.87 us -> 3.95 us
    psum x1 -> x0, waiting for transfers between devices: 85.4 us -> none  [local(): lax.psum(jnp.dot(hidden, second_feed_weight, preferred_element_type=jnp.f...]
    all_gather x1, waiting for transfers between devices: 48.8 us -> 0.02 us  [local(): contexts = lax.all_gather(context, 'mp', axis=0)]
    ppermute x6 -> x25, waiting for transfers between devices: 2.64 us -> 38.2 us  [local(): move = lambda value, pairs: lax.ppermute(value, 'dp', pairs)]
    pallas_call x1 -> x2, Pallas kernels: 5.89 us -> 38.2 us  [the longest x1 32.4 us: feed(): pl.pallas_call(functools.partial(feed_kernel, counts=tuple(((len(w1s), le...]
    dot_general x2 -> x0, matrix products: 18.5 us -> none  [the longest x1 15.6 us: local(): jnp.dot(hidden, second_feed_weight, preferred_element_type=jnp.float32)]
    unnamed x48 -> x90, local copies, waits for them, and re-layouts: 11.1 us -> 24 us
    ppermute x6 -> x25, starting transfers between devices: 5.72 us -> 15.9 us  [local(): move = lambda value, pairs: lax.ppermute(value, 'dp', pairs)]
    slice x2 -> x9, local copies, waits for them, and re-layouts: 1.12 us -> 10.7 us  [the longest x1 2.45 us: local(): second = second[:, :unit]]
  transfers between devices with their start and end apart: 10 -> 30, of which waited for: 5 -> 7; matrix products, arithmetic and copies ran while one was open for 4% -> 11% of each run, Pallas kernels for 27% -> 34%
where the time goes in v4:
time: 253 us; the launch traced here: 250 us
  Pallas kernels  118 us (47%)
  waiting for transfers between devices  45.8 us (18%)
  local copies, waits for them, and re-layouts  44.5 us (18%)
  starting transfers between devices  22.3 us (9%)
  between operations  15.1 us (6%)
  other arithmetic  3.95 us (2%)
    pallas_call x3, Pallas kernels, attend(): pl.pallas_call(functools.partial(attend_kernel, requests=requests, slots=...  71.9 us
    ppermute x25, waiting for transfers between devices, local(): move = lambda value, pairs: lax.ppermute(value, 'dp', pairs)  38.2 us
    pallas_call x1, Pallas kernels, feed(): pl.pallas_call(functools.partial(feed_kernel, counts=tuple(((len(w1s), le...  32.4 us
    unnamed x90, local copies, waits for them, and re-layouts  24 us
    ppermute x25, starting transfers between devices, local(): move = lambda value, pairs: lax.ppermute(value, 'dp', pairs)  15.9 us
    pallas_call x1, Pallas kernels, project(): pl.pallas_call(functools.partial(project_kernel, requests=counts.shape[0]...  8.27 us
    all_to_all x1, waiting for transfers between devices, local(): got = lax.all_to_all(sent, 'mp', split_axis=1, concat_axis=0, tiled=True)  7.53 us
    all_to_all x1, starting transfers between devices, local(): got = lax.all_to_all(sent, 'mp', split_axis=1, concat_axis=0, tiled=True)  6.32 us
  transfers between devices with their start and end apart: 30, of which 7 were waited for; matrix products, arithmetic and copies ran while one was open for 11% of the time, Pallas kernels for 34%

profile of v4, /device:TPU:0, one launch (start us, length us, event | category | flops | bytes accessed | tf_op | source)
XLA Modules:
  0.0 250.0 jit_solution(4259806102348542046)
XLA Ops:
  9.6 1.4 fusion.6
  14.4 6.3 %all-to-all-start = ((bf16[16,4,1792]{2,0,1:T(8,128)(2,1)}), bf16[16,4,1792]{2,0,1:T(8,128)(2,1)S(1)}, u32[]{:S(2)}, u32[]{:S(2)}) async-start(bf16[16,4,1792]{2,0,1:T(8,128)(2,1)} %pad_maximum_fusion.2), calls=%async_computation | async-start | bytes 458752 | tf_op jit(solution)/shard_map/all_to_all | solution.py:559
  20.8 2.6 %copy.29 = bf16[1024,768]{0,1:T(8,128)(2,1)} copy(bf16[1024,768]{1,0:T(8,128)(2,1)} %param.19) | data formatting | bytes 3145728 | tf_op args[1]
  23.4 1.2 dynamic-slice_bitcast_fusion
  24.7 1.2 copy.35.refs_2_
  27.7 7.5 %all-to-all-done = bf16[16,4,1792]{2,0,1:T(8,128)(2,1)S(1)} async-done(((bf16[16,4,1792]{2,0,1:T(8,128)(2,1)}), bf16[16,4,1792]{2,0,1:T(8,128)(2,1)S(1)}, u32[]{:S(2)}, u32[]{:S(2)}) %all-to-all-start) | async-done | bytes 229408 | tf_op jit(solution)/shard_map/all_to_all | solution.py:559
  36.0 1.6 copy-done.1
  37.6 1.1 copy-done.6
  38.7 8.3 %project.1 = (bf16[2048,128]{1,0:T(8,128)(2,1)S(1)}, bf16[2048,256]{1,0:T(8,128)(2,1)S(1)}) custom-call(s32[4]{0:T(128)S(1)} %copy-done.24, s32[64]{0:T(128)S(1)} %copy-done.25, s32[4]{0:T(128)S(1)} %get-tuple-element.53.owners, s32[2]{0:T(128)S(1)} %pad_add_fusion.1.bases.q_bases.kv_bases, bf16[1024,1024]{1,0:T(8,128)(2,1)S(1)} %copy-done.1, ...), custom_call_target="tpu_custom_call" | custom-call | flops 1610612736 | bytes 5767168 | tf_op jit(solution)/shard_map/project/pallas_call | solution.py:102
  47.8 1.6 collective-permute-start.2
  49.5 1.5 collective-permute-start.1
  52.0 19.1 %attend.3 = (f32[2048,128]{1,0:T(8,128)S(1)}, f32[2048,128]{1,0:T(8,128)S(1)}) custom-call(s32[4]{0:T(128)S(1)} %copy-done.24, s32[64]{0:T(128)S(1)} %copy-done.25, s32[2]{0:T(128)S(1)} %pad_add_fusion.1.bases.q_bases.kv_bases, s32[2]{0:T(128)S(1)} %pad_add_fusion.1.bases.q_bases.kv_bases, bf16[2048,128]{1,0:T(8,128)(2,1)S(1)} %copy-done.27, ...), custom_call_target="tpu_custom_call" | custom-call | flops 1073741824 | bytes 2097152 | tf_op jit(solution)/shard_map/attend/pallas_call | solution.py:304
  74.1 1.5 collective-permute-start.5
  75.6 1.7 constant_dynamic-slice_fusion.1
  78.5 1.7 collective-permute-start.4
  80.1 1.3 fusion.7
  82.0 1.3 fusion.8
  83.3 33.3 %attend.4 = (f32[2048,128]{1,0:T(8,128)S(1)}, f32[2048,128]{1,0:T(8,128)S(1)}) custom-call(s32[4]{0:T(128)S(1)} %copy-done.24, s32[64]{0:T(128)S(1)} %copy-done.25, s32[2]{0:T(128)S(1)} %pad_add_fusion.1.bases.q_bases.kv_bases, s32[4]{0:T(128)S(1)} %get-tuple-element.65.kv_bases, bf16[2048,128]{1,0:T(8,128)(2,1)S(1)} %copy-done.28, ...), custom_call_target="tpu_custom_call" | custom-call | flops 2147483648 | bytes 3145728 | tf_op jit(solution)/shard_map/attend/pallas_call | solution.py:304
  119.8 1.9 slice.62
  126.4 1.2 copy-done.31
  127.7 1.2 copy-done.33
  128.9 19.5 %attend.5 = bf16[2048,128]{1,0:T(8,128)(2,1)S(1)} custom-call(s32[4]{0:T(128)S(1)} %copy-done.24, s32[64]{0:T(128)S(1)} %copy-done.25, s32[2]{0:T(128)S(1)} %pad_add_fusion.1.bases.q_bases.kv_bases, s32[2]{0:T(128)S(1)} %pad_add_fusion.2.kv_bases, bf16[2048,128]{1,0:T(8,128)(2,1)S(1)} %copy-done.29, bf16[1024,256]{1,0:T(8,128)(2,1)S(1)} %copy-done.20, ...), custom_call_target="tpu_custom_call" | custom-call | flops 1073741824 | bytes 2097152 | tf_op jit(solution)/shard_map/attend/pallas_call | solution.py:304
  149.4 1.5 collective-permute-done.9
  152.0 2.5 slice.66.refs_5_
  154.5 2.9 %collective-permute-start.12 = (bf16[4,128,1024]{2,1,0:T(8,128)(2,1)}, bf16[4,128,1024]{2,1,0:T(8,128)(2,1)}, u32[]{:S(2)}, u32[]{:S(2)}) collective-permute-start(bf16[4,128,1024]{2,1,0:T(8,128)(2,1)} %slice.66.refs_5_), channel_id=1, source_target_pairs={{0,16},{4,20},{8,24},{12,28},{16,0},{20,4},{24,8},{28,12},{1,17},{... | collective-permute-start | bytes 3145736 | tf_op jit(solution)/shard_map/ppermute | solution.py:585
  158.6 22.7 %collective-permute-done.12.refs_7_ = bf16[4,128,1024]{2,1,0:T(8,128)(2,1)} collective-permute-done((bf16[4,128,1024]{2,1,0:T(8,128)(2,1)}, bf16[4,128,1024]{2,1,0:T(8,128)(2,1)}, u32[]{:S(2)}, u32[]{:S(2)}) %collective-permute-start.12) | collective-permute-done | bytes 1048608 | tf_op jit(solution)/shard_map/ppermute | solution.py:585
  181.3 1.5 collective-permute-done.11.refs_6_
  189.6 11.4 %collective-permute-done.13.refs_8_ = bf16[4,64,1024]{2,1,0:T(8,128)(2,1)} collective-permute-done((bf16[4,64,1024]{2,1,0:T(8,128)(2,1)S(1)}, bf16[4,64,1024]{2,1,0:T(8,128)(2,1)}, u32[]{:S(2)}, u32[]{:S(2)}) %collective-permute-start.13) | collective-permute-done | bytes 524320 | tf_op jit(solution)/shard_map/ppermute | solution.py:585
  202.6 1.2 copy-done.5
  203.9 5.8 %mix.1.normed_ref = bf16[1024,1024]{1,0:T(8,128)(2,1)S(1)} custom-call(bf16[1024,1024]{1,0:T(8,128)(2,1)} %x_ref.1, bf16[4,1024,256]{2,1,0:T(8,128)(2,1)} %bitcast.50, bf16[4,128,1024]{2,1,0:T(8,128)(2,1)S(1)} %bitcast.37, bf16[4,128,1024]{2,1,0:T(8,128)(2,1)S(1)} %copy-done.5, f32[1,1024]{1,0:T(1,128)S(1)} %bitcast.39, f32[1,1024]{1,0:T(1,128)S(1)} %bitcast.40), custom_call_target="tpu_custom_call" | custom-call | flops 2147483648 | bytes 8388608 | tf_op jit(solution)/shard_map/mix/pallas_call | solution.py:361
  209.7 1.3 copy-done.2
  211.1 32.4 %feed.1 = (bf16[256,1024]{1,0:T(8,128)(2,1)}, bf16[1024,768]{1,0:T(8,128)(2,1)}) custom-call(s32[3]{0:T(128)S(1)} %pad_add_fusion.place, bf16[1024,1024]{1,0:T(8,128)(2,1)} %copy-done.2, bf16[4,16,1024]{2,1,0:T(8,128)(2,1)S(1)} %slice.65.bias_ref, bf16[4,1024,128]{2,1,0:T(8,128)(2,1)S(1)} %bitcast.44, bf16[4,1024,128]{2,1,0:T(8,128)(2,1)} %collective-permute-done.5.refs_1_, ...), custom_call_target="tpu_custom_call" | custom-call | flops 17179869184 | bytes 16777216 | tf_op jit(solution)/shard_map/feed/pallas_call | solution.py:462
  (169 shorter events, 33.9 us)
Async XLA Ops:
  7.2 65.9 %all-gather.9.cloned.1.call-start = ((), (), s32[]{:S(2)}) async-start(), calls=%async_computation.1 | async-start | bytes 1310720 | tf_op jit(solution)/shard_map/all_gather | solution.py:577
  7.2 28.7 %collective-permute-start = (bf16[1024,1024]{1,0:T(8,128)(2,1)}, bf16[1024,1024]{1,0:T(8,128)(2,1)}, u32[]{:S(2)}, u32[]{:S(2)}) collective-permute-start(bf16[1024,1024]{1,0:T(8,128)(2,1)} %x_ref.1), channel_id=1, source_target_pairs={{0,4},{4,0},{8,12},{12,8},{16,20},{20,16},{24,28},{28,24},{1,5},{5... | collective-permute-start | bytes 6291464 | tf_op jit(solution)/shard_map/ppermute | solution.py:585
  14.4 20.8 %all-to-all-start = ((bf16[16,4,1792]{2,0,1:T(8,128)(2,1)}), bf16[16,4,1792]{2,0,1:T(8,128)(2,1)S(1)}, u32[]{:S(2)}, u32[]{:S(2)}) async-start(bf16[16,4,1792]{2,0,1:T(8,128)(2,1)} %pad_maximum_fusion.2), calls=%async_computation | async-start | bytes 458752 | tf_op jit(solution)/shard_map/all_to_all | solution.py:559
  20.8 127.6 %all-gather.11.cloned.1.call-start = ((), (), s32[]{:S(2)}) async-start(), calls=%async_computation.2 | async-start | bytes 1474560 | tf_op jit(solution)/shard_map/all_gather | solution.py:603
  47.8 100.6 %all-gather.13.cloned.1.call-start = ((), (), s32[]{:S(2)}) async-start(), calls=%async_computation.3 | async-start | bytes 1310720 | tf_op jit(solution)/shard_map/all_gather | solution.py:616
  47.8 25.2 %collective-permute-start.2 = (bf16[2048,256]{1,0:T(8,128)(2,1)S(1)}, bf16[2048,256]{1,0:T(8,128)(2,1)}, u32[]{:S(2)}, u32[]{:S(2)}) collective-permute-start(bf16[2048,256]{1,0:T(8,128)(2,1)S(1)} %get-tuple-element.28), channel_id=1, source_target_pairs={{0,16},{4,20},{8,24},{12,28},{16,0},{20,4},{24,8},{28,12},{1,17},{... | collective-permute-start | bytes 3145736 | tf_op jit(solution)/shard_map/ppermute | solution.py:585
  49.5 24.2 %collective-permute-start.1 = (bf16[2048,256]{1,0:T(8,128)(2,1)S(1)}, bf16[2048,256]{1,0:T(8,128)(2,1)}, u32[]{:S(2)}, u32[]{:S(2)}) collective-permute-start(bf16[2048,256]{1,0:T(8,128)(2,1)S(1)} %get-tuple-element.28), channel_id=1, source_target_pairs={{0,8},{4,12},{8,0},{12,4},{16,24},{20,28},{24,16},{28,20},{1,9},{5... | collective-permute-start | bytes 3145736 | tf_op jit(solution)/shard_map/ppermute | solution.py:585
  73.7 44.9 %collective-permute-start.6 = (bf16[4,1024,128]{2,1,0:T(8,128)(2,1)}, bf16[4,1024,128]{2,1,0:T(8,128)(2,1)S(1)}, u32[]{:S(2)}, u32[]{:S(2)}) collective-permute-start(bf16[4,1024,128]{2,1,0:T(8,128)(2,1)} %bitcast.41), channel_id=1, source_target_pairs={{0,16},{4,20},{8,24},{12,28},{16,0},{20,4},{24,8},{28,12},{1,17},{... | collective-permute-start | bytes 3145736 | tf_op jit(solution)/shard_map/ppermute | solution.py:585
  74.1 44.5 %collective-permute-start.5 = (bf16[4,1024,128]{2,1,0:T(8,128)(2,1)}, bf16[4,1024,128]{2,1,0:T(8,128)(2,1)}, u32[]{:S(2)}, u32[]{:S(2)}) collective-permute-start(bf16[4,1024,128]{2,1,0:T(8,128)(2,1)} %bitcast.42), channel_id=1, source_target_pairs={{0,8},{4,12},{8,0},{12,4},{16,24},{20,28},{24,16},{28,20},{1,9},{5... | collective-permute-start | bytes 3145736 | tf_op jit(solution)/shard_map/ppermute | solution.py:585
  77.3 125.3 %all-gather.15.cloned.1.call-start = ((), (), s32[]{:S(2)}) async-start(), calls=%async_computation.4 | async-start | bytes 2621440 | tf_op jit(solution)/shard_map/all_gather | solution.py:641
  78.5 40.1 %collective-permute-start.4 = (bf16[1024,256]{1,0:T(8,128)(2,1)S(1)}, bf16[1024,256]{1,0:T(8,128)(2,1)S(1)}, u32[]{:S(2)}, u32[]{:S(2)}) collective-permute-start(bf16[1024,256]{1,0:T(8,128)(2,1)S(1)} %slice.57), channel_id=1, source_target_pairs={{0,16},{4,20},{8,24},{12,28},{16,0},{20,4},{24,8},{28,12},{1,17},{... | collective-permute-start | bytes 1572872 | tf_op jit(solution)/shard_map/ppermute | solution.py:585
  81.4 37.1 %collective-permute-start.3 = (bf16[1024,256]{1,0:T(8,128)(2,1)S(1)}, bf16[1024,256]{1,0:T(8,128)(2,1)S(1)}, u32[]{:S(2)}, u32[]{:S(2)}) collective-permute-start(bf16[1024,256]{1,0:T(8,128)(2,1)S(1)} %get-tuple-element.55.refs_2_), channel_id=1, source_target_pairs={{0,8},{4,12},{8,0},{12,4},{16,24},{20,28},{24,16},{28,20},{1,9},{5... | collective-permute-start | bytes 1572872 | tf_op jit(solution)/shard_map/ppermute | solution.py:585
  121.7 26.7 %collective-permute-start.8 = (bf16[4,512,128]{2,1,0:T(8,128)(2,1)}, bf16[4,512,128]{2,1,0:T(8,128)(2,1)S(1)}, u32[]{:S(2)}, u32[]{:S(2)}) collective-permute-start(bf16[4,512,128]{2,1,0:T(8,128)(2,1)} %slice.62), channel_id=1, source_target_pairs={{0,16},{4,20},{8,24},{12,28},{16,0},{20,4},{24,8},{28,12},{1,17},{... | collective-permute-start | bytes 1572872 | tf_op jit(solution)/shard_map/ppermute | solution.py:585
  122.1 26.3 %collective-permute-start.7 = (bf16[4,512,128]{2,1,0:T(8,128)(2,1)}, bf16[4,512,128]{2,1,0:T(8,128)(2,1)}, u32[]{:S(2)}, u32[]{:S(2)}) collective-permute-start(bf16[4,512,128]{2,1,0:T(8,128)(2,1)} %slice.61), channel_id=1, source_target_pairs={{0,8},{4,12},{8,0},{12,4},{16,24},{20,28},{24,16},{28,20},{1,9},{5... | collective-permute-start | bytes 1572872 | tf_op jit(solution)/shard_map/ppermute | solution.py:585
  149.3 1.6 collective-permute-start.9
  151.8 50.8 %copy-start.7 = (f32[1024]{0:T(1024)S(1)}, f32[1024]{0:T(1024)}, u32[]{:S(2)}) copy-start(f32[1024]{0:T(1024)} %param.23) | copy-start | bytes 12292
  151.8 50.8 %copy-start.8 = (f32[1024]{0:T(1024)S(1)}, f32[1024]{0:T(1024)}, u32[]{:S(2)}) copy-start(f32[1024]{0:T(1024)} %param.24) | copy-start | bytes 12292
  151.8 6.7 %collective-permute-start.15 = (bf16[4,1024,128]{2,1,0:T(8,128)(2,1)}, bf16[4,1024,128]{2,1,0:T(8,128)(2,1)S(1)}, u32[]{:S(2)}, u32[]{:S(2)}) collective-permute-start(bf16[4,1024,128]{2,1,0:T(8,128)(2,1)} %bitcast.43), channel_id=1, source_target_pairs={{0,4},{4,0},{8,12},{12,8},{16,20},{20,16},{24,28},{28,24},{1,5},{5... | collective-permute-start | bytes 3145736 | tf_op jit(solution)/shard_map/ppermute | solution.py:585
  154.5 26.9 %collective-permute-start.12 = (bf16[4,128,1024]{2,1,0:T(8,128)(2,1)}, bf16[4,128,1024]{2,1,0:T(8,128)(2,1)}, u32[]{:S(2)}, u32[]{:S(2)}) collective-permute-start(bf16[4,128,1024]{2,1,0:T(8,128)(2,1)} %slice.66.refs_5_), channel_id=1, source_target_pairs={{0,16},{4,20},{8,24},{12,28},{16,0},{20,4},{24,8},{28,12},{1,17},{... | collective-permute-start | bytes 3145736 | tf_op jit(solution)/shard_map/ppermute | solution.py:585
  157.3 25.5 %collective-permute-start.11 = (bf16[4,128,1024]{2,1,0:T(8,128)(2,1)}, bf16[4,128,1024]{2,1,0:T(8,128)(2,1)}, u32[]{:S(2)}, u32[]{:S(2)}) collective-permute-start(bf16[4,128,1024]{2,1,0:T(8,128)(2,1)} %slice.66.refs_5_), channel_id=1, source_target_pairs={{0,8},{4,12},{8,0},{12,4},{16,24},{20,28},{24,16},{28,20},{1,9},{5... | collective-permute-start | bytes 3145736 | tf_op jit(solution)/shard_map/ppermute | solution.py:585
  158.0 29.7 %collective-permute-start.17 = (bf16[4,1024,128]{2,1,0:T(8,128)(2,1)S(1)}, bf16[4,1024,128]{2,1,0:T(8,128)(2,1)S(1)}, u32[]{:S(2)}, u32[]{:S(2)}) collective-permute-start(bf16[4,1024,128]{2,1,0:T(8,128)(2,1)S(1)} %copy-done.38), channel_id=1, source_target_pairs={{0,4},{4,0},{8,12},{12,8},{16,20},{20,16},{24,28},{28,24},{1,5},{5... | collective-permute-start | bytes 3145736 | tf_op jit(solution)/shard_map/ppermute | solution.py:585
  158.0 30.1 %collective-permute-start.16 = (bf16[4,1024,128]{2,1,0:T(8,128)(2,1)}, bf16[4,1024,128]{2,1,0:T(8,128)(2,1)S(1)}, u32[]{:S(2)}, u32[]{:S(2)}) collective-permute-start(bf16[4,1024,128]{2,1,0:T(8,128)(2,1)} %collective-permute-done.5.refs_1_), channel_id=1, source_target_pairs={{0,4},{4,0},{8,12},{12,8},{16,20},{20,16},{24,28},{28,24},{1,5},{5... | collective-permute-start | bytes 3145736 | tf_op jit(solution)/shard_map/ppermute | solution.py:585
  158.5 29.6 %collective-permute-start.10 = (bf16[4,128,1024]{2,1,0:T(8,128)(2,1)S(1)}, bf16[4,128,1024]{2,1,0:T(8,128)(2,1)S(1)}, u32[]{:S(2)}, u32[]{:S(2)}) collective-permute-start(bf16[4,128,1024]{2,1,0:T(8,128)(2,1)S(1)} %bitcast.36), channel_id=1, source_target_pairs={{0,4},{4,0},{8,12},{12,8},{16,20},{20,16},{24,28},{28,24},{1,5},{5... | collective-permute-start | bytes 3145736 | tf_op jit(solution)/shard_map/ppermute | solution.py:585
  181.3 3.6 %collective-permute-start.18 = (bf16[4,512,128]{2,1,0:T(8,128)(2,1)}, bf16[4,512,128]{2,1,0:T(8,128)(2,1)S(1)}, u32[]{:S(2)}, u32[]{:S(2)}) collective-permute-start(bf16[4,512,128]{2,1,0:T(8,128)(2,1)} %collective-permute-done.7.refs_3_), channel_id=1, source_target_pairs={{0,4},{4,0},{8,12},{12,8},{16,20},{20,16},{24,28},{28,24},{1,5},{5... | collective-permute-start | bytes 1572872 | tf_op jit(solution)/shard_map/ppermute | solution.py:585
  182.8 3.5 %collective-permute-start.19 = (bf16[4,512,128]{2,1,0:T(8,128)(2,1)S(1)}, bf16[4,512,128]{2,1,0:T(8,128)(2,1)S(1)}, u32[]{:S(2)}, u32[]{:S(2)}) collective-permute-start(bf16[4,512,128]{2,1,0:T(8,128)(2,1)S(1)} %copy-done.11), channel_id=1, source_target_pairs={{0,4},{4,0},{8,12},{12,8},{16,20},{20,16},{24,28},{28,24},{1,5},{5... | collective-permute-start | bytes 1572872 | tf_op jit(solution)/shard_map/ppermute | solution.py:585
  185.8 25.2 %collective-permute-start.20 = (bf16[4,128,1024]{2,1,0:T(8,128)(2,1)}, bf16[4,128,1024]{2,1,0:T(8,128)(2,1)}, u32[]{:S(2)}, u32[]{:S(2)}) collective-permute-start(bf16[4,128,1024]{2,1,0:T(8,128)(2,1)} %slice.66.refs_5_), channel_id=1, source_target_pairs={{0,4},{4,0},{8,12},{12,8},{16,20},{20,16},{24,28},{28,24},{1,5},{5... | collective-permute-start | bytes 3145736 | tf_op jit(solution)/shard_map/ppermute | solution.py:585
  187.1 13.9 %collective-permute-start.13 = (bf16[4,64,1024]{2,1,0:T(8,128)(2,1)S(1)}, bf16[4,64,1024]{2,1,0:T(8,128)(2,1)}, u32[]{:S(2)}, u32[]{:S(2)}) collective-permute-start(bf16[4,64,1024]{2,1,0:T(8,128)(2,1)S(1)} %slice.71), channel_id=1, source_target_pairs={{0,8},{4,12},{8,0},{12,4},{16,24},{20,28},{24,16},{28,20},{1,9},{5... | collective-permute-start | bytes 1572872 | tf_op jit(solution)/shard_map/ppermute | solution.py:585
  187.7 13.7 %collective-permute-start.14 = (bf16[4,64,1024]{2,1,0:T(8,128)(2,1)S(1)}, bf16[4,64,1024]{2,1,0:T(8,128)(2,1)}, u32[]{:S(2)}, u32[]{:S(2)}) collective-permute-start(bf16[4,64,1024]{2,1,0:T(8,128)(2,1)S(1)} %slice.72), channel_id=1, source_target_pairs={{0,16},{4,20},{8,24},{12,28},{16,0},{20,4},{24,8},{28,12},{1,17},{... | collective-permute-start | bytes 1572872 | tf_op jit(solution)/shard_map/ppermute | solution.py:585
  188.1 22.9 %collective-permute-start.22 = (bf16[4,128,1024]{2,1,0:T(8,128)(2,1)}, bf16[4,128,1024]{2,1,0:T(8,128)(2,1)}, u32[]{:S(2)}, u32[]{:S(2)}) collective-permute-start(bf16[4,128,1024]{2,1,0:T(8,128)(2,1)} %collective-permute-done.12.refs_7_), channel_id=1, source_target_pairs={{0,4},{4,0},{8,12},{12,8},{16,20},{20,16},{24,28},{28,24},{1,5},{5... | collective-permute-start | bytes 3145736 | tf_op jit(solution)/shard_map/ppermute | solution.py:585
  189.1 21.9 %collective-permute-start.21 = (bf16[4,128,1024]{2,1,0:T(8,128)(2,1)}, bf16[4,128,1024]{2,1,0:T(8,128)(2,1)}, u32[]{:S(2)}, u32[]{:S(2)}) collective-permute-start(bf16[4,128,1024]{2,1,0:T(8,128)(2,1)} %collective-permute-done.11.refs_6_), channel_id=1, source_target_pairs={{0,4},{4,0},{8,12},{12,8},{16,20},{20,16},{24,28},{28,24},{1,5},{5... | collective-permute-start | bytes 3145736 | tf_op jit(solution)/shard_map/ppermute | solution.py:585
  201.0 10.0 %collective-permute-start.23 = (bf16[4,64,1024]{2,1,0:T(8,128)(2,1)}, bf16[4,64,1024]{2,1,0:T(8,128)(2,1)}, u32[]{:S(2)}, u32[]{:S(2)}) collective-permute-start(bf16[4,64,1024]{2,1,0:T(8,128)(2,1)} %collective-permute-done.13.refs_8_), channel_id=1, source_target_pairs={{0,4},{4,0},{8,12},{12,8},{16,20},{20,16},{24,28},{28,24},{1,5},{5... | collective-permute-start | bytes 1572872 | tf_op jit(solution)/shard_map/ppermute | solution.py:585
  201.4 9.6 %collective-permute-start.24 = (bf16[4,64,1024]{2,1,0:T(8,128)(2,1)}, bf16[4,64,1024]{2,1,0:T(8,128)(2,1)}, u32[]{:S(2)}, u32[]{:S(2)}) collective-permute-start(bf16[4,64,1024]{2,1,0:T(8,128)(2,1)} %collective-permute-done.14.refs_9_), channel_id=1, source_target_pairs={{0,4},{4,0},{8,12},{12,8},{16,20},{20,16},{24,28},{28,24},{1,5},{5... | collective-permute-start | bytes 1572872 | tf_op jit(solution)/shard_map/ppermute | solution.py:585
  (42 other events, 290.2 us)
Sparse Core Ops, SparseCore 0:
  9.7 36.0 all-gather.8
  47.9 30.8 all-gather.10
  80.4 27.0 all-gather.12
  151.9 46.2 all-gather.14

commit v5 on v4

--- a/solution.py
+++ b/solution.py
@@ -78,7 +78,12 @@
         rows = rows.astype(jnp.bfloat16)
         q_cols = q_ref.shape[1]
         q_ref[...] = rows[:, :q_cols]
-        kv_ref[...] = rows[:, q_cols:]
+        keys = rows[:, q_cols : 2 * q_cols]
+        values = rows[:, 2 * q_cols :]
+        for p in range(pages):
+            here = slice(p * PAGE, (p + 1) * PAGE)
+            kv_ref[p, :PAIR, :] = keys[here].T
+            kv_ref[p, PAIR:, :] = values[here]
 
     for i in range(parts):
         pl.when(piece == i)(functools.partial(block, x_refs[i]))
@@ -115,7 +120,7 @@
             ],
             out_specs=[
                 pl.BlockSpec((rows_step, cols // 3), rows),
-                pl.BlockSpec((rows_step, 2 * cols // 3), rows),
+                pl.BlockSpec((pages, PAIR + PAGE, PAIR), lambda i, *_: (i, 0, 0)),
             ],
             scratch_shapes=[
                 pltpu.VMEM((width, cols + down.shape[1]), jnp.bfloat16),
@@ -124,7 +129,7 @@
         ),
         out_shape=[
             jax.ShapeDtypeStruct((total, cols // 3), jnp.bfloat16),
-            jax.ShapeDtypeStruct((total, 2 * cols // 3), jnp.bfloat16),
+            jax.ShapeDtypeStruct((total // PAGE, PAIR + PAGE, PAIR), jnp.bfloat16),
         ],
         compiler_params=params(),
         cost_estimate=pl.CostEstimate(
@@ -137,10 +142,10 @@
 
 def attend_kernel(
     counts, table, q_bases, kv_bases, q_ref, *refs,
-    requests, slots, q_size, sizes, first, last, group,
+    requests, slots, q_size, arrays, sizes, first, last, group,
 ):
     refs = list(refs)
-    kv_hbm = [refs.pop(0) for _ in sizes]
+    kv_hbm = [refs.pop(0) for _ in arrays]
     if not first:
         acc_in, stat_in = refs.pop(0), refs.pop(0)
     if last:
@@ -150,10 +155,8 @@
     kv, scores, listed, amount, asked, q_amount, sems = refs
     copies = []
     offset = 0
-    for i, size in enumerate(sizes):
-        copy = pltpu.make_async_copy(
-            kv_hbm[i], kv.at[pl.ds(offset * PAGE, size * PAGE)], sems.at[i]
-        )
+    for i, size in enumerate(arrays):
+        copy = pltpu.make_async_copy(kv_hbm[i], kv.at[pl.ds(offset, size)], sems.at[i])
         copy.start()
         copies.append(copy)
         offset += size
@@ -214,19 +217,14 @@
             parts += [jnp.where(low_lane, q, zero), jnp.where(low_lane, zero, q)]
         stacked = jnp.concatenate(parts, axis=0)
 
-        def pages_of(j, low):
-            found = []
-            for i in range(group):
-                index = jnp.minimum(j * group + i, n - 1)
-                at = pl.multiple_of(listed[r, index] * PAGE, PAGE)
-                found.append(kv[pl.ds(at, PAGE), low : low + PAIR])
-            return jnp.concatenate(found, axis=0)
+        def page_of(j, i):
+            return listed[r, jnp.minimum(j * group + i, n - 1)]
 
         def score(masked, j, top):
-            s = lax.dot_general(
-                stacked, pages_of(j, 0), (((1,), (1,)), ((), ())),
-                preferred_element_type=jnp.float32,
+            keys = jnp.concatenate(
+                [kv[page_of(j, i), :PAIR, :] for i in range(group)], axis=1
             )
+            s = jnp.dot(stacked, keys, preferred_element_type=jnp.float32)
             for i in range(group):
                 piece = s[:, i * PAGE : (i + 1) * PAGE]
                 if masked and i:
@@ -251,8 +249,11 @@
             w = jnp.exp2(scores[j] * EXP_SCALE - shift)
             for i in range(group):
                 total = total + w[:, i * PAGE : (i + 1) * PAGE]
+            values = jnp.concatenate(
+                [kv[page_of(j, i), PAIR:, :] for i in range(group)], axis=0
+            )
             acc = acc + jnp.dot(
-                w.astype(jnp.bfloat16), pages_of(j, PAIR), preferred_element_type=jnp.float32
+                w.astype(jnp.bfloat16), values, preferred_element_type=jnp.float32
             )
             return total, acc
 
@@ -293,7 +294,8 @@
 
 def attend(counts, table, q_bases, kv_bases, q, pieces, state, last, q_size):
     tok = q.shape[0]
-    sizes = tuple(p.shape[0] // PAGE for p in pieces)
+    arrays = tuple(p.shape[0] for p in pieces)
+    sizes = (sum(arrays) // kv_bases.shape[0],) * kv_bases.shape[0]
     first = state is None
     group = 4
     slots = table.shape[0]
@@ -304,7 +306,7 @@
     out = pl.pallas_call(
         functools.partial(
             attend_kernel,
-            requests=requests, slots=slots, q_size=q_size, sizes=sizes,
+            requests=requests, slots=slots, q_size=q_size, arrays=arrays, sizes=sizes,
             first=first, last=last, group=group,
         ),
         grid_spec=pltpu.PrefetchScalarGridSpec(
@@ -315,7 +317,7 @@
             + ([] if first else [pl.BlockSpec((tok, PAIR), lambda i, *_: (0, 0))] * 2),
             out_specs=[pl.BlockSpec((tok, PAIR), lambda i, *_: (0, 0))] * (1 if last else 2),
             scratch_shapes=[
-                pltpu.VMEM((sum(sizes) * PAGE, 2 * PAIR), jnp.bfloat16),
+                pltpu.VMEM((sum(sizes), PAIR + PAGE, PAIR), jnp.bfloat16),
                 pltpu.VMEM(((most + group - 1) // group, 4 * PAGE, group * PAGE), jnp.float32),
                 pltpu.SMEM((requests, sum(sizes)), jnp.int32),
                 pltpu.SMEM((requests,), jnp.int32),
@@ -327,9 +329,7 @@
         out_shape=[jax.ShapeDtypeStruct((tok, PAIR), jnp.bfloat16)] if last else state_shape,
         compiler_params=params(),
         cost_estimate=pl.CostEstimate(
-            flops=2 * tok * sum(sizes) * PAGE * PAIR,
-            bytes_accessed=4 * tok * PAIR + 4 * PAGE * PAIR * sum(sizes),
-            transcendentals=tok * sum(sizes) * PAGE,
+            flops=tok * PAIR, bytes_accessed=4 * tok * PAIR, transcendentals=0,
         ),
         name="attend",
     )(counts, table, q_bases, kv_bases, q, *pieces, *([] if first else state))
@@ -557,8 +557,6 @@
         axis=2,
     ).reshape(ADAPTER_RANK, mp_count * (width + up_cols))
     got = lax.all_to_all(sent, "mp", split_axis=1, concat_axis=0, tiled=True)
-    downs = got[:, :width].T
-    ups = got[:, width:]
 
     def by_kind(matrix):
         split = matrix.reshape(matrix.shape[0], heads_dev, 3, HEAD_DIM)
@@ -574,8 +572,11 @@
         unit = hidden_dev // 8
         turn = (dp_index % 2) * 4 + dp_index // 2
         first = lax.dynamic_slice_in_dim(first_feed_weight, turn * unit, unit, 1)
+        first, got = lax.optimization_barrier((first, got))
         first = lax.all_gather(first, "mp", axis=0)
 
+    downs = got[:, :width].T
+    ups = got[:, width:]
     weight = by_kind(query_key_value_weight)
     ups = by_kind(ups)
     if shared:
@@ -602,10 +603,10 @@
         second, _ = lax.optimization_barrier((second, kv))
         second = lax.all_gather(second, "mp", axis=0)
         step = functools.partial(attend, *args, bases)
-        state = step(bases, q, [kv[:tok_rows], kv[tok_rows:]], None, False, pages)
+        state = step(bases, q, [kv], None, False, pages)
         kv_x, kv_y, state, first = lax.optimization_barrier((kv_x, kv_y, state, first))
-        kv_d0 = move(kv_y[:tok_rows], across)
-        kv_d1 = move(kv_x[tok_rows:], along)
+        kv_d0 = move(kv_y[:pages], across)
+        kv_d1 = move(kv_x[pages:], along)
         first_x = move(first, across)
         first_y = move(first, along)
         out_rows = attention_out_weight.shape[0] // 2
@@ -615,22 +616,17 @@
         out_half, kv_x = lax.optimization_barrier((out_half, kv_x))
         out_mine = lax.all_gather(out_half, "mp", axis=0)
         near = jnp.stack([at(2), at(3), at(4), at(5)])
-        state = step(
-            near, q, [kv_x[:tok_rows], kv_x[tok_rows:], kv_y[:tok_rows], kv_y[tok_rows:]],
-            state, False, pages,
-        )
-        kv_d0, kv_d1, first_x, first_y, state = lax.optimization_barrier(
-            (kv_d0, kv_d1, first_x, first_y, state)
+        state = step(near, q, [kv_x, kv_y], state, False, pages)
+        kv_d0, kv_d1, state = lax.optimization_barrier((kv_d0, kv_d1, state))
+        far = jnp.stack([at(6), at(7)])
+        context = step(far, q, [kv_d0, kv_d1], state, True, pages)
+        context, first_x, first_y, second, out_mine = lax.optimization_barrier(
+            (context, first_x, first_y, second, out_mine)
         )
         cut = width // 2
         first_d0 = move(first_y[:, :cut], across)
         first_d1 = move(first_x[:, cut:], along)
         first_near = [move(piece, swap) for piece in (first, first_x, first_y)]
-        far = jnp.stack([at(6), at(7)])
-        context = step(far, q, [kv_d0, kv_d1], state, True, pages)
-        context, first_d0, first_d1, second, out_mine = lax.optimization_barrier(
-            (context, first_d0, first_d1, second, out_mine)
-        )
         bias_rows = second[:, unit:]
         second = second[:, :unit]
         second_x = move(second, across)

time: 253 us -> 254 us (level)
  waiting for transfers between devices: 45.8 us -> 52.4 us
  local copies, waits for them, and re-layouts: 44.5 us -> 39 us
    unnamed x90 -> x71, local copies, waits for them, and re-layouts: 24 us -> 16.7 us
    ppermute x25, waiting for transfers between devices: 38.2 us -> 44.3 us  [local(): move = lambda value, pairs: lax.ppermute(value, 'dp', pairs)]
  transfers between devices with their start and end apart: 30 -> 30, of which waited for: 7 -> 6; matrix products, arithmetic and copies ran while one was open for 11% -> 11% of each run, Pallas kernels for 34% -> 34%
where the time goes in v5:
time: 254 us; the launch traced here: 252 us
  Pallas kernels  120 us (47%)
  waiting for transfers between devices  52.4 us (21%)
  local copies, waits for them, and re-layouts  39 us (15%)
  starting transfers between devices  22.1 us (9%)
  between operations  15 us (6%)
  other arithmetic  4.01 us (2%)
    pallas_call x3, Pallas kernels, attend(): pl.pallas_call(functools.partial(attend_kernel, requests=requests, slots=...  72.6 us
    ppermute x25, waiting for transfers between devices, local(): move = lambda value, pairs: lax.ppermute(value, 'dp', pairs)  44.3 us
    pallas_call x1, Pallas kernels, feed(): pl.pallas_call(functools.partial(feed_kernel, counts=tuple(((len(w1s), le...  33 us
    unnamed x71, local copies, waits for them, and re-layouts  16.7 us
    ppermute x25, starting transfers between devices, local(): move = lambda value, pairs: lax.ppermute(value, 'dp', pairs)  16 us
    pallas_call x1, Pallas kernels, project(): pl.pallas_call(functools.partial(project_kernel, requests=counts.shape[0]...  8.41 us
    all_to_all x1, waiting for transfers between devices, local(): got = lax.all_to_all(sent, 'mp', split_axis=1, concat_axis=0, tiled=True)  7.92 us
    all_to_all x1, starting transfers between devices, local(): got = lax.all_to_all(sent, 'mp', split_axis=1, concat_axis=0, tiled=True)  5.91 us
  transfers between devices with their start and end apart: 30, of which 6 were waited for; matrix products, arithmetic and copies ran while one was open for 11% of the time, Pallas kernels for 34%

profile of v5, /device:TPU:0, one launch (start us, length us, event | category | flops | bytes accessed | tf_op | source)
XLA Modules:
  0.0 252.2 jit_solution(15182494753869420477)
XLA Ops:
  7.7 1.5 fusion.6
  12.6 5.9 %all-to-all-start = ((bf16[16,4,1792]{2,0,1:T(8,128)(2,1)}), bf16[16,4,1792]{2,0,1:T(8,128)(2,1)S(1)}, u32[]{:S(2)}, u32[]{:S(2)}) async-start(bf16[16,4,1792]{2,0,1:T(8,128)(2,1)} %pad_maximum_fusion.2), calls=%async_computation | async-start | bytes 458752 | tf_op jit(solution)/shard_map/all_to_all | solution.py:559
  19.3 7.9 %all-to-all-done = bf16[16,4,1792]{2,0,1:T(8,128)(2,1)S(1)} async-done(((bf16[16,4,1792]{2,0,1:T(8,128)(2,1)}), bf16[16,4,1792]{2,0,1:T(8,128)(2,1)S(1)}, u32[]{:S(2)}, u32[]{:S(2)}) %all-to-all-start) | async-done | bytes 229408 | tf_op jit(solution)/shard_map/all_to_all | solution.py:559
  27.4 2.6 %copy.29 = bf16[1024,768]{0,1:T(8,128)(2,1)} copy(bf16[1024,768]{1,0:T(8,128)(2,1)} %param.19) | data formatting | bytes 3145728 | tf_op args[1]
  32.1 1.5 copy.35.refs_2_
  37.9 1.6 copy-done.1
  39.5 8.4 %project.1 = (bf16[2048,128]{1,0:T(8,128)(2,1)S(1)}, bf16[16,256,128]{2,1,0:T(8,128)(2,1)S(1)}) custom-call(s32[4]{0:T(128)S(1)} %copy-done.13, s32[64]{0:T(128)S(1)} %copy-done.14, s32[4]{0:T(128)S(1)} %get-tuple-element.53.owners, s32[2]{0:T(128)S(1)} %pad_add_fusion.1.bases.q_bases.kv_bases, bf16[1024,1024]{1,0:T(8,128)(2,1)S(1)} %copy-done.1, ...), custom_call_target="tpu_custom_call" | custom-call | flops 1610612736 | bytes 5767168 | tf_op jit(solution)/shard_map/project/pallas_call | solution.py:107
  49.0 1.6 collective-permute-start.2
  50.6 1.5 collective-permute-start.1
  52.1 1.7 constant_dynamic-slice_fusion.1
  53.8 1.2 copy-done.7
  55.0 18.0 %attend.3 = (f32[2048,128]{1,0:T(8,128)S(1)}, f32[2048,128]{1,0:T(8,128)S(1)}) custom-call(s32[4]{0:T(128)S(1)} %copy-done.13, s32[64]{0:T(128)S(1)} %copy-done.14, s32[2]{0:T(128)S(1)} %pad_add_fusion.1.bases.q_bases.kv_bases, s32[2]{0:T(128)S(1)} %pad_add_fusion.1.bases.q_bases.kv_bases, bf16[2048,128]{1,0:T(8,128)(2,1)S(1)} %get-tuple-element.28.q_ref, ...), custom_call_target="tpu_custom_call" | custom-call | flops 262144 | bytes 1048576 | tf_op jit(solution)/shard_map/attend/pallas_call | solution.py:306
  75.3 1.5 collective-permute-start.5
  76.7 1.9 slice.39
  78.6 1.9 slice.38
  80.5 1.9 collective-permute-start.4
  83.1 1.2 copy-done.9
  84.3 34.5 %attend.4 = (f32[2048,128]{1,0:T(8,128)S(1)}, f32[2048,128]{1,0:T(8,128)S(1)}) custom-call(s32[4]{0:T(128)S(1)} %copy-done.13, s32[64]{0:T(128)S(1)} %copy-done.14, s32[2]{0:T(128)S(1)} %pad_add_fusion.1.bases.q_bases.kv_bases, s32[4]{0:T(128)S(1)} %get-tuple-element.59.kv_bases, bf16[2048,128]{1,0:T(8,128)(2,1)S(1)} %get-tuple-element.28.q_ref, ...), custom_call_target="tpu_custom_call" | custom-call | flops 262144 | bytes 1048576 | tf_op jit(solution)/shard_map/attend/pallas_call | solution.py:306
  120.8 20.1 %attend.5 = bf16[2048,128]{1,0:T(8,128)(2,1)S(1)} custom-call(s32[4]{0:T(128)S(1)} %copy-done.13, s32[64]{0:T(128)S(1)} %copy-done.14, s32[2]{0:T(128)S(1)} %pad_add_fusion.1.bases.q_bases.kv_bases, s32[2]{0:T(128)S(1)} %pad_add_fusion.2.kv_bases, bf16[2048,128]{1,0:T(8,128)(2,1)S(1)} %get-tuple-element.28.q_ref, ...), custom_call_target="tpu_custom_call" | custom-call | flops 262144 | bytes 1048576 | tf_op jit(solution)/shard_map/attend/pallas_call | solution.py:306
  141.0 1.5 collective-permute-done.7
  143.7 1.4 slice.45.refs_5_
  145.3 1.3 slice.43
  146.6 1.8 collective-permute-start.9
  149.5 2.0 collective-permute-start.10
  151.5 30.3 %collective-permute-done.9.refs_3_ = bf16[4,512,128]{2,1,0:T(8,128)(2,1)S(1)} collective-permute-done((bf16[4,512,128]{2,1,0:T(8,128)(2,1)S(1)}, bf16[4,512,128]{2,1,0:T(8,128)(2,1)S(1)}, u32[]{:S(2)}, u32[]{:S(2)}) %collective-permute-start.9) | collective-permute-done | bytes 524320 | tf_op jit(solution)/shard_map/ppermute | solution.py:586
  185.0 1.5 collective-permute-done.18.refs_13_
  188.6 1.7 collective-permute-start.14
  191.7 10.8 %collective-permute-done.13.refs_8_ = bf16[4,64,1024]{2,1,0:T(8,128)(2,1)} collective-permute-done((bf16[4,64,1024]{2,1,0:T(8,128)(2,1)S(1)}, bf16[4,64,1024]{2,1,0:T(8,128)(2,1)}, u32[]{:S(2)}, u32[]{:S(2)}) %collective-permute-start.13) | collective-permute-done | bytes 524320 | tf_op jit(solution)/shard_map/ppermute | solution.py:586
  204.2 1.2 copy-done.5
  205.5 5.8 %mix.1.normed_ref = bf16[1024,1024]{1,0:T(8,128)(2,1)S(1)} custom-call(bf16[1024,1024]{1,0:T(8,128)(2,1)} %x_ref.1, bf16[4,1024,256]{2,1,0:T(8,128)(2,1)} %bitcast.50, bf16[4,128,1024]{2,1,0:T(8,128)(2,1)S(1)} %bitcast.38, bf16[4,128,1024]{2,1,0:T(8,128)(2,1)S(1)} %copy-done.5, f32[1,1024]{1,0:T(1,128)S(1)} %bitcast.39, f32[1,1024]{1,0:T(1,128)S(1)} %bitcast.40), custom_call_target="tpu_custom_call" | custom-call | flops 2147483648 | bytes 8388608 | tf_op jit(solution)/shard_map/mix/pallas_call | solution.py:361
  211.3 1.3 copy-done.2
  212.7 33.0 %feed.1 = (bf16[256,1024]{1,0:T(8,128)(2,1)}, bf16[1024,768]{1,0:T(8,128)(2,1)}) custom-call(s32[3]{0:T(128)S(1)} %pad_add_fusion.place, bf16[1024,1024]{1,0:T(8,128)(2,1)} %copy-done.2, bf16[4,16,1024]{2,1,0:T(8,128)(2,1)S(1)} %slice.42.bias_ref, bf16[4,1024,128]{2,1,0:T(8,128)(2,1)S(1)} %bitcast.44, bf16[4,1024,128]{2,1,0:T(8,128)(2,1)} %collective-permute-done.5.refs_1_, ...), custom_call_target="tpu_custom_call" | custom-call | flops 17179869184 | bytes 16777216 | tf_op jit(solution)/shard_map/feed/pallas_call | solution.py:462
  (149 shorter events, 27.1 us)
Async XLA Ops:
  7.2 30.7 %collective-permute-start = (bf16[1024,1024]{1,0:T(8,128)(2,1)}, bf16[1024,1024]{1,0:T(8,128)(2,1)}, u32[]{:S(2)}, u32[]{:S(2)}) collective-permute-start(bf16[1024,1024]{1,0:T(8,128)(2,1)} %x_ref.1), channel_id=1, source_target_pairs={{0,4},{4,0},{8,12},{12,8},{16,20},{20,16},{24,28},{28,24},{1,5},{5... | collective-permute-start | bytes 6291464 | tf_op jit(solution)/shard_map/ppermute | solution.py:586
  12.6 14.6 %all-to-all-start = ((bf16[16,4,1792]{2,0,1:T(8,128)(2,1)}), bf16[16,4,1792]{2,0,1:T(8,128)(2,1)S(1)}, u32[]{:S(2)}, u32[]{:S(2)}) async-start(bf16[16,4,1792]{2,0,1:T(8,128)(2,1)} %pad_maximum_fusion.2), calls=%async_computation | async-start | bytes 458752 | tf_op jit(solution)/shard_map/all_to_all | solution.py:559
  18.5 56.6 %all-gather.9.cloned.1.call-start = ((), (), s32[]{:S(2)}) async-start(), calls=%async_computation.1 | async-start | bytes 1310720 | tf_op jit(solution)/shard_map/all_gather | solution.py:576
  27.2 113.6 %all-gather.11.cloned.1.call-start = ((), (), s32[]{:S(2)}) async-start(), calls=%async_computation.2 | async-start | bytes 1474560 | tf_op jit(solution)/shard_map/all_gather | solution.py:604
  48.9 92.0 %all-gather.13.cloned.1.call-start = ((), (), s32[]{:S(2)}) async-start(), calls=%async_computation.3 | async-start | bytes 1310720 | tf_op jit(solution)/shard_map/all_gather | solution.py:617
  49.0 26.1 %collective-permute-start.2 = (bf16[16,256,128]{2,1,0:T(8,128)(2,1)}, bf16[16,256,128]{2,1,0:T(8,128)(2,1)}, u32[]{:S(2)}, u32[]{:S(2)}) collective-permute-start(bf16[16,256,128]{2,1,0:T(8,128)(2,1)} %copy-done.6), channel_id=1, source_target_pairs={{0,16},{4,20},{8,24},{12,28},{16,0},{20,4},{24,8},{28,12},{1,17},{... | collective-permute-start | bytes 3145736 | tf_op jit(solution)/shard_map/ppermute | solution.py:586
  50.6 24.5 %collective-permute-start.1 = (bf16[16,256,128]{2,1,0:T(8,128)(2,1)}, bf16[16,256,128]{2,1,0:T(8,128)(2,1)}, u32[]{:S(2)}, u32[]{:S(2)}) collective-permute-start(bf16[16,256,128]{2,1,0:T(8,128)(2,1)} %copy-done.6), channel_id=1, source_target_pairs={{0,8},{4,12},{8,0},{12,4},{16,24},{20,28},{24,16},{28,20},{1,9},{5... | collective-permute-start | bytes 3145736 | tf_op jit(solution)/shard_map/ppermute | solution.py:586
  75.1 129.0 %all-gather.15.cloned.1.call-start = ((), (), s32[]{:S(2)}) async-start(), calls=%async_computation.4 | async-start | bytes 2621440 | tf_op jit(solution)/shard_map/all_gather | solution.py:637
  75.2 65.7 %collective-permute-start.6 = (bf16[4,1024,128]{2,1,0:T(8,128)(2,1)}, bf16[4,1024,128]{2,1,0:T(8,128)(2,1)}, u32[]{:S(2)}, u32[]{:S(2)}) collective-permute-start(bf16[4,1024,128]{2,1,0:T(8,128)(2,1)} %bitcast.41), channel_id=1, source_target_pairs={{0,16},{4,20},{8,24},{12,28},{16,0},{20,4},{24,8},{28,12},{1,17},{... | collective-permute-start | bytes 3145736 | tf_op jit(solution)/shard_map/ppermute | solution.py:586
  75.3 65.6 %collective-permute-start.5 = (bf16[4,1024,128]{2,1,0:T(8,128)(2,1)}, bf16[4,1024,128]{2,1,0:T(8,128)(2,1)}, u32[]{:S(2)}, u32[]{:S(2)}) collective-permute-start(bf16[4,1024,128]{2,1,0:T(8,128)(2,1)} %bitcast.42), channel_id=1, source_target_pairs={{0,8},{4,12},{8,0},{12,4},{16,24},{20,28},{24,16},{28,20},{1,9},{5... | collective-permute-start | bytes 3145736 | tf_op jit(solution)/shard_map/ppermute | solution.py:586
  80.5 38.4 %collective-permute-start.4 = (bf16[8,256,128]{2,1,0:T(8,128)(2,1)}, bf16[8,256,128]{2,1,0:T(8,128)(2,1)S(1)}, u32[]{:S(2)}, u32[]{:S(2)}) collective-permute-start(bf16[8,256,128]{2,1,0:T(8,128)(2,1)} %slice.39), channel_id=1, source_target_pairs={{0,16},{4,20},{8,24},{12,28},{16,0},{20,4},{24,8},{28,12},{1,17},{... | collective-permute-start | bytes 1572872 | tf_op jit(solution)/shard_map/ppermute | solution.py:586
  82.4 37.3 %collective-permute-start.3 = (bf16[8,256,128]{2,1,0:T(8,128)(2,1)}, bf16[8,256,128]{2,1,0:T(8,128)(2,1)}, u32[]{:S(2)}, u32[]{:S(2)}) collective-permute-start(bf16[8,256,128]{2,1,0:T(8,128)(2,1)} %slice.38), channel_id=1, source_target_pairs={{0,8},{4,12},{8,0},{12,4},{16,24},{20,28},{24,16},{28,20},{1,9},{5... | collective-permute-start | bytes 1572872 | tf_op jit(solution)/shard_map/ppermute | solution.py:586
  141.0 1.6 collective-permute-start.7
  143.4 8.1 %collective-permute-start.15 = (bf16[4,1024,128]{2,1,0:T(8,128)(2,1)}, bf16[4,1024,128]{2,1,0:T(8,128)(2,1)S(1)}, u32[]{:S(2)}, u32[]{:S(2)}) collective-permute-start(bf16[4,1024,128]{2,1,0:T(8,128)(2,1)} %bitcast.43), channel_id=1, source_target_pairs={{0,4},{4,0},{8,12},{12,8},{16,20},{20,16},{24,28},{28,24},{1,5},{5... | collective-permute-start | bytes 3145736 | tf_op jit(solution)/shard_map/ppermute | solution.py:586
  145.1 59.1 %copy-start.15 = (f32[1024]{0:T(1024)S(1)}, f32[1024]{0:T(1024)}, u32[]{:S(2)}) copy-start(f32[1024]{0:T(1024)} %param.23) | copy-start | bytes 12292
  145.1 59.1 %copy-start.16 = (f32[1024]{0:T(1024)S(1)}, f32[1024]{0:T(1024)}, u32[]{:S(2)}) copy-start(f32[1024]{0:T(1024)} %param.24) | copy-start | bytes 12292
  145.1 37.2 %collective-permute-start.12 = (bf16[4,128,1024]{2,1,0:T(8,128)(2,1)S(1)}, bf16[4,128,1024]{2,1,0:T(8,128)(2,1)}, u32[]{:S(2)}, u32[]{:S(2)}) collective-permute-start(bf16[4,128,1024]{2,1,0:T(8,128)(2,1)S(1)} %slice.45.refs_5_), channel_id=1, source_target_pairs={{0,16},{4,20},{8,24},{12,28},{16,0},{20,4},{24,8},{28,12},{1,17},{... | collective-permute-start | bytes 3145736 | tf_op jit(solution)/shard_map/ppermute | solution.py:586
  145.2 37.2 %collective-permute-start.11 = (bf16[4,128,1024]{2,1,0:T(8,128)(2,1)S(1)}, bf16[4,128,1024]{2,1,0:T(8,128)(2,1)}, u32[]{:S(2)}, u32[]{:S(2)}) collective-permute-start(bf16[4,128,1024]{2,1,0:T(8,128)(2,1)S(1)} %slice.45.refs_5_), channel_id=1, source_target_pairs={{0,8},{4,12},{8,0},{12,4},{16,24},{20,28},{24,16},{28,20},{1,9},{5... | collective-permute-start | bytes 3145736 | tf_op jit(solution)/shard_map/ppermute | solution.py:586
  146.6 35.2 %collective-permute-start.9 = (bf16[4,512,128]{2,1,0:T(8,128)(2,1)S(1)}, bf16[4,512,128]{2,1,0:T(8,128)(2,1)S(1)}, u32[]{:S(2)}, u32[]{:S(2)}) collective-permute-start(bf16[4,512,128]{2,1,0:T(8,128)(2,1)S(1)} %slice.43), channel_id=1, source_target_pairs={{0,8},{4,12},{8,0},{12,4},{16,24},{20,28},{24,16},{28,20},{1,9},{5... | collective-permute-start | bytes 1572872 | tf_op jit(solution)/shard_map/ppermute | solution.py:586
  149.5 32.3 %collective-permute-start.10 = (bf16[4,512,128]{2,1,0:T(8,128)(2,1)S(1)}, bf16[4,512,128]{2,1,0:T(8,128)(2,1)S(1)}, u32[]{:S(2)}, u32[]{:S(2)}) collective-permute-start(bf16[4,512,128]{2,1,0:T(8,128)(2,1)S(1)} %slice.44), channel_id=1, source_target_pairs={{0,16},{4,20},{8,24},{12,28},{16,0},{20,4},{24,8},{28,12},{1,17},{... | collective-permute-start | bytes 1572872 | tf_op jit(solution)/shard_map/ppermute | solution.py:586
  151.5 37.1 %collective-permute-start.20 = (bf16[4,128,1024]{2,1,0:T(8,128)(2,1)S(1)}, bf16[4,128,1024]{2,1,0:T(8,128)(2,1)S(1)}, u32[]{:S(2)}, u32[]{:S(2)}) collective-permute-start(bf16[4,128,1024]{2,1,0:T(8,128)(2,1)S(1)} %slice.45.refs_5_), channel_id=1, source_target_pairs={{0,4},{4,0},{8,12},{12,8},{16,20},{20,16},{24,28},{28,24},{1,5},{5... | collective-permute-start | bytes 3145736 | tf_op jit(solution)/shard_map/ppermute | solution.py:586
  181.8 8.4 %collective-permute-start.8 = (bf16[4,128,1024]{2,1,0:T(8,128)(2,1)S(1)}, bf16[4,128,1024]{2,1,0:T(8,128)(2,1)S(1)}, u32[]{:S(2)}, u32[]{:S(2)}) collective-permute-start(bf16[4,128,1024]{2,1,0:T(8,128)(2,1)S(1)} %bitcast.37), channel_id=1, source_target_pairs={{0,4},{4,0},{8,12},{12,8},{16,20},{20,16},{24,28},{28,24},{1,5},{5... | collective-permute-start | bytes 3145736 | tf_op jit(solution)/shard_map/ppermute | solution.py:586
  181.8 9.4 %collective-permute-start.16 = (bf16[4,1024,128]{2,1,0:T(8,128)(2,1)}, bf16[4,1024,128]{2,1,0:T(8,128)(2,1)S(1)}, u32[]{:S(2)}, u32[]{:S(2)}) collective-permute-start(bf16[4,1024,128]{2,1,0:T(8,128)(2,1)} %collective-permute-done.5.refs_1_), channel_id=1, source_target_pairs={{0,4},{4,0},{8,12},{12,8},{16,20},{20,16},{24,28},{28,24},{1,5},{5... | collective-permute-start | bytes 3145736 | tf_op jit(solution)/shard_map/ppermute | solution.py:586
  182.3 4.2 %collective-permute-start.18 = (bf16[4,512,128]{2,1,0:T(8,128)(2,1)S(1)}, bf16[4,512,128]{2,1,0:T(8,128)(2,1)S(1)}, u32[]{:S(2)}, u32[]{:S(2)}) collective-permute-start(bf16[4,512,128]{2,1,0:T(8,128)(2,1)S(1)} %collective-permute-done.9.refs_3_), channel_id=1, source_target_pairs={{0,4},{4,0},{8,12},{12,8},{16,20},{20,16},{24,28},{28,24},{1,5},{5... | collective-permute-start | bytes 1572872 | tf_op jit(solution)/shard_map/ppermute | solution.py:586
  182.4 5.1 %collective-permute-start.19 = (bf16[4,512,128]{2,1,0:T(8,128)(2,1)S(1)}, bf16[4,512,128]{2,1,0:T(8,128)(2,1)S(1)}, u32[]{:S(2)}, u32[]{:S(2)}) collective-permute-start(bf16[4,512,128]{2,1,0:T(8,128)(2,1)S(1)} %collective-permute-done.10.refs_4_), channel_id=1, source_target_pairs={{0,4},{4,0},{8,12},{12,8},{16,20},{20,16},{24,28},{28,24},{1,5},{5... | collective-permute-start | bytes 1572872 | tf_op jit(solution)/shard_map/ppermute | solution.py:586
  187.3 25.2 %collective-permute-start.17 = (bf16[4,1024,128]{2,1,0:T(8,128)(2,1)}, bf16[4,1024,128]{2,1,0:T(8,128)(2,1)}, u32[]{:S(2)}, u32[]{:S(2)}) collective-permute-start(bf16[4,1024,128]{2,1,0:T(8,128)(2,1)} %collective-permute-done.6.refs_2_), channel_id=1, source_target_pairs={{0,4},{4,0},{8,12},{12,8},{16,20},{20,16},{24,28},{28,24},{1,5},{5... | collective-permute-start | bytes 3145736 | tf_op jit(solution)/shard_map/ppermute | solution.py:586
  188.3 14.3 %collective-permute-start.13 = (bf16[4,64,1024]{2,1,0:T(8,128)(2,1)S(1)}, bf16[4,64,1024]{2,1,0:T(8,128)(2,1)}, u32[]{:S(2)}, u32[]{:S(2)}) collective-permute-start(bf16[4,64,1024]{2,1,0:T(8,128)(2,1)S(1)} %slice.49), channel_id=1, source_target_pairs={{0,8},{4,12},{8,0},{12,4},{16,24},{20,28},{24,16},{28,20},{1,9},{5... | collective-permute-start | bytes 1572872 | tf_op jit(solution)/shard_map/ppermute | solution.py:586
  188.6 14.1 %collective-permute-start.14 = (bf16[4,64,1024]{2,1,0:T(8,128)(2,1)S(1)}, bf16[4,64,1024]{2,1,0:T(8,128)(2,1)}, u32[]{:S(2)}, u32[]{:S(2)}) collective-permute-start(bf16[4,64,1024]{2,1,0:T(8,128)(2,1)S(1)} %slice.50), channel_id=1, source_target_pairs={{0,16},{4,20},{8,24},{12,28},{16,0},{20,4},{24,8},{28,12},{1,17},{... | collective-permute-start | bytes 1572872 | tf_op jit(solution)/shard_map/ppermute | solution.py:586
  191.2 21.4 %collective-permute-start.22 = (bf16[4,128,1024]{2,1,0:T(8,128)(2,1)}, bf16[4,128,1024]{2,1,0:T(8,128)(2,1)}, u32[]{:S(2)}, u32[]{:S(2)}) collective-permute-start(bf16[4,128,1024]{2,1,0:T(8,128)(2,1)} %collective-permute-done.12.refs_7_), channel_id=1, source_target_pairs={{0,4},{4,0},{8,12},{12,8},{16,20},{20,16},{24,28},{28,24},{1,5},{5... | collective-permute-start | bytes 3145736 | tf_op jit(solution)/shard_map/ppermute | solution.py:586
  191.2 21.4 %collective-permute-start.21 = (bf16[4,128,1024]{2,1,0:T(8,128)(2,1)}, bf16[4,128,1024]{2,1,0:T(8,128)(2,1)}, u32[]{:S(2)}, u32[]{:S(2)}) collective-permute-start(bf16[4,128,1024]{2,1,0:T(8,128)(2,1)} %collective-permute-done.11.refs_6_), channel_id=1, source_target_pairs={{0,4},{4,0},{8,12},{12,8},{16,20},{20,16},{24,28},{28,24},{1,5},{5... | collective-permute-start | bytes 3145736 | tf_op jit(solution)/shard_map/ppermute | solution.py:586
  202.6 10.0 %collective-permute-start.23 = (bf16[4,64,1024]{2,1,0:T(8,128)(2,1)}, bf16[4,64,1024]{2,1,0:T(8,128)(2,1)}, u32[]{:S(2)}, u32[]{:S(2)}) collective-permute-start(bf16[4,64,1024]{2,1,0:T(8,128)(2,1)} %collective-permute-done.13.refs_8_), channel_id=1, source_target_pairs={{0,4},{4,0},{8,12},{12,8},{16,20},{20,16},{24,28},{28,24},{1,5},{5... | collective-permute-start | bytes 1572872 | tf_op jit(solution)/shard_map/ppermute | solution.py:586
  202.7 9.9 %collective-permute-start.24 = (bf16[4,64,1024]{2,1,0:T(8,128)(2,1)}, bf16[4,64,1024]{2,1,0:T(8,128)(2,1)}, u32[]{:S(2)}, u32[]{:S(2)}) collective-permute-start(bf16[4,64,1024]{2,1,0:T(8,128)(2,1)} %collective-permute-done.14.refs_9_), channel_id=1, source_target_pairs={{0,4},{4,0},{8,12},{12,8},{16,20},{20,16},{24,28},{28,24},{1,5},{5... | collective-permute-start | bytes 1572872 | tf_op jit(solution)/shard_map/ppermute | solution.py:586
  (33 other events, 348.5 us)
Sparse Core Ops, SparseCore 0:
  27.3 27.0 all-gather.8
  56.0 29.9 all-gather.10
  87.5 27.0 all-gather.12
  143.6 43.1 all-gather.14

commit v6 on v5

--- a/solution.py
+++ b/solution.py
@@ -43,7 +43,9 @@
     counts, table, owners, bases, *refs, requests, slots, pages, per_piece, parts,
 ):
     x_refs = refs[:parts]
-    w_ref, down_ref, up_ref, q_ref, kv_ref, joined, page_owner = refs[parts:]
+    w_ref, down_ref, up_ref, q_ref = refs[parts : parts + 4]
+    kv_refs = refs[parts + 4 : 2 * parts + 4]
+    joined, page_owner = refs[2 * parts + 4 :]
     step = pl.program_id(0)
     cols = w_ref.shape[1]
 
@@ -60,7 +62,7 @@
 
     piece = step * pages // per_piece
 
-    def block(x_ref):
+    def block(x_ref, kv_ref):
         both = jnp.dot(x_ref[...], joined[...], preferred_element_type=jnp.float32)
         low = both[:, cols:]
         lane_owner = lax.broadcasted_iota(jnp.int32, (PAGE, low.shape[1]), 1) // ADAPTER_RANK
@@ -86,7 +88,7 @@
             kv_ref[p, PAIR:, :] = values[here]
 
     for i in range(parts):
-        pl.when(piece == i)(functools.partial(block, x_refs[i]))
+        pl.when(piece == i)(functools.partial(block, x_refs[i], kv_refs[i]))
 
 
 def project(counts, table, owners, bases, xs, weight, down, up, per_piece):
@@ -101,8 +103,8 @@
     whole = lambda i, *_: (0, 0)
     rows = lambda i, *_: (i, 0)
 
-    def own(part):
-        return lambda i, *_: (jnp.clip(i - part * each, 0, each - 1), 0)
+    def own(part, *zeros):
+        return lambda i, *_: (jnp.clip(i - part * each, 0, each - 1), 0, *zeros)
 
     return pl.pallas_call(
         functools.partial(
@@ -120,8 +122,8 @@
             ],
             out_specs=[
                 pl.BlockSpec((rows_step, cols // 3), rows),
-                pl.BlockSpec((pages, PAIR + PAGE, PAIR), lambda i, *_: (i, 0, 0)),
-            ],
+            ]
+            + [pl.BlockSpec((pages, PAIR + PAGE, PAIR), own(i, 0)) for i in range(parts)],
             scratch_shapes=[
                 pltpu.VMEM((width, cols + down.shape[1]), jnp.bfloat16),
                 pltpu.SMEM((slots,), jnp.int32),
@@ -129,8 +131,8 @@
         ),
         out_shape=[
             jax.ShapeDtypeStruct((total, cols // 3), jnp.bfloat16),
-            jax.ShapeDtypeStruct((total // PAGE, PAIR + PAGE, PAIR), jnp.bfloat16),
-        ],
+        ]
+        + [jax.ShapeDtypeStruct((tok // PAGE, PAIR + PAGE, PAIR), jnp.bfloat16)] * parts,
         compiler_params=params(),
         cost_estimate=pl.CostEstimate(
             flops=2 * total * width * cols, bytes_accessed=2 * total * (width + cols),
@@ -342,9 +344,9 @@
 
     @pl.when(pl.program_id(0) == 0)
     def _():
-        near = out_w_refs[0].shape[1]
+        near = joined.shape[1] // parts
         for i in range(parts):
-            joined[:, i * near : (i + 1) * near] = out_w_refs[i][...]
+            joined[:, i * near : (i + 1) * near] = out_w_refs[i][:, :near]
 
     mixed = x_ref[...].astype(jnp.float32)
     for j in range(ctx_ref.shape[0]):
@@ -470,7 +472,10 @@
             grid=(steps,),
             in_specs=[
                 pl.BlockSpec((tok, width), fixed),
-                pl.BlockSpec((1,) + bias.shape[1:], lambda i, *_: (i % groups, 0, 0)),
+                pl.BlockSpec(
+                    (1, 16, bias.shape[2]),
+                    lambda i, *_: (i % groups, bias.shape[1] // 16 - 1, 0),
+                ),
             ]
             + specs
             + [
@@ -568,13 +573,6 @@
         [mp_index] + ([dp_index // 2, dp_index % 2] if shared else [0, 0])
     ).astype(jnp.int32)
     hidden_dev = first_feed_weight.shape[1]
-    if shared:
-        unit = hidden_dev // 8
-        turn = (dp_index % 2) * 4 + dp_index // 2
-        first = lax.dynamic_slice_in_dim(first_feed_weight, turn * unit, unit, 1)
-        first, got = lax.optimization_barrier((first, got))
-        first = lax.all_gather(first, "mp", axis=0)
-
     downs = got[:, :width].T
     ups = got[:, width:]
     weight = by_kind(query_key_value_weight)
@@ -591,66 +589,76 @@
         xs = [tokens]
         bases = jnp.stack([dp_index * pages])
     args = (request_page_count, page_slot_table)
-    q, kv = project(*args, owners, bases, xs, weight, downs, ups, pages)
+    q, *kvs = project(*args, owners, bases, xs, weight, downs, ups, pages)
+    bias_rows = jnp.pad(jnp.stack(three_parts(first_feed_bias)), ((0, 13), (0, 0)))
+    out_rows = attention_out_weight.shape[0]
     if shared:
-        kv_x = move(kv, across)
-        kv_y = move(kv, along)
-        second = jnp.concatenate(
-            [lax.dynamic_slice_in_dim(second_feed_weight, turn * unit, unit, 0)]
-            + [jnp.pad(jnp.stack(three_parts(first_feed_bias)), ((0, 13), (0, 0)))],
+        unit = hidden_dev // 8
+        turn = (dp_index % 2) * 4 + dp_index // 2
+        kv_x = [move(kv, across) for kv in kvs]
+        kv_y = [move(kv, along) for kv in kvs]
+        first = lax.dynamic_slice_in_dim(first_feed_weight, turn * unit, unit, 1)
+        first, kvs = lax.optimization_barrier((first, kvs))
+        first = lax.all_gather(first, "mp", axis=0)
+        step = functools.partial(attend, *args, bases)
+        state = step(bases, q, kvs, None, False, pages)
+        second = lax.dynamic_slice_in_dim(second_feed_weight, turn * unit, unit, 0)
+        out_half = jnp.concatenate(
+            [
+                lax.dynamic_slice_in_dim(
+                    attention_out_weight, (dp_index % 2) * (out_rows // 2), out_rows // 2, 0
+                ),
+                bias_rows,
+            ],
             axis=0,
         )
-        second, _ = lax.optimization_barrier((second, kv))
+        kv_x, kv_y, state, first, second, out_half = lax.optimization_barrier(
+            (kv_x, kv_y, state, first, second, out_half)
+        )
         second = lax.all_gather(second, "mp", axis=0)
-        step = functools.partial(attend, *args, bases)
-        state = step(bases, q, [kv], None, False, pages)
-        kv_x, kv_y, state, first = lax.optimization_barrier((kv_x, kv_y, state, first))
-        kv_d0 = move(kv_y[:pages], across)
-        kv_d1 = move(kv_x[pages:], along)
+        out_mine = lax.all_gather(out_half, "mp", axis=0)
+        kv_d0 = move(kv_y[0], across)
+        kv_d1 = move(kv_x[1], along)
         first_x = move(first, across)
         first_y = move(first, along)
-        out_rows = attention_out_weight.shape[0] // 2
-        out_half = lax.dynamic_slice_in_dim(
-            attention_out_weight, (dp_index % 2) * out_rows, out_rows, 0
-        )
-        out_half, kv_x = lax.optimization_barrier((out_half, kv_x))
-        out_mine = lax.all_gather(out_half, "mp", axis=0)
         near = jnp.stack([at(2), at(3), at(4), at(5)])
-        state = step(near, q, [kv_x, kv_y], state, False, pages)
-        kv_d0, kv_d1, state = lax.optimization_barrier((kv_d0, kv_d1, state))
-        far = jnp.stack([at(6), at(7)])
-        context = step(far, q, [kv_d0, kv_d1], state, True, pages)
-        context, first_x, first_y, second, out_mine = lax.optimization_barrier(
-            (context, first_x, first_y, second, out_mine)
+        state = step(near, q, [*kv_x, *kv_y], state, False, pages)
+        kv_d0, kv_d1, first_x, first_y, state = lax.optimization_barrier(
+            (kv_d0, kv_d1, first_x, first_y, state)
         )
         cut = width // 2
         first_d0 = move(first_y[:, :cut], across)
         first_d1 = move(first_x[:, cut:], along)
-        first_near = [move(piece, swap) for piece in (first, first_x, first_y)]
-        bias_rows = second[:, unit:]
-        second = second[:, :unit]
+        far = jnp.stack([at(6), at(7)])
+        near_others = [move(piece, swap) for piece in (first, first_x, first_y)]
+        context = step(far, q, [kv_d0, kv_d1], state, True, pages)
+        context, first_d0, first_d1, near_others, second, out_mine = lax.optimization_barrier(
+            (context, first_d0, first_d1, near_others, second, out_mine)
+        )
         second_x = move(second, across)
         second_y = move(second, along)
         context = jnp.concatenate(
             [context[:tok_rows], move(context[tok_rows:], swap)], axis=1
         )
         contexts = lax.all_gather(context, "mp", axis=0)
-        out_other = move(out_mine, swap)
+        bias_rows = out_mine
         firsts = [first, first_x, first_y, first_d0, first_d1]
-        first_others = first_near + [move(first_d0, swap), move(first_d1, swap)]
+        moved = [move(piece, swap) for piece in (first_d0, first_d1, second, out_mine)]
+        second_x, second_y, moved = lax.optimization_barrier((second_x, second_y, moved))
+        first_others = [*near_others, *moved[:2]]
+        out_other = moved[3]
         half = unit // 2
         second_d0 = move(second_y[:, :half], across)
         second_d1 = move(second_x[:, half:], along)
         seconds = [second, second_x, second_y, second_d0, second_d1]
-        second_others = [move(piece, swap) for piece in seconds]
+        second_others = [moved[2]] + [move(piece, swap) for piece in seconds[1:]]
         sets = [(firsts, seconds), (first_others, second_others)]
         outs = [out_mine, out_other]
     else:
-        everything = lax.all_gather(kv, "dp", axis=0, tiled=True)
+        everything = lax.all_gather(kvs[0], "dp", axis=0, tiled=True)
         context = attend(
             *args, bases, jnp.zeros((1,), jnp.int32), q, [everything], None, True, pages
         )
-        bias_rows = jnp.pad(jnp.stack(three_parts(first_feed_bias)), ((0, 13), (0, 0)))
         second = lax.all_gather(second_feed_weight, "mp", axis=0)
         bias_rows = lax.all_gather(bias_rows, "mp", axis=0)
         sets = [([lax.all_gather(first_feed_weight, "mp", axis=0)], [second])]

time: 254 us -> 255 us (level); the launches traced: 252 us -> 250 us
  starting transfers between devices: 22.1 us -> 33.9 us
  waiting for transfers between devices: 52.4 us -> 42 us
  Pallas kernels: 120 us -> 114 us
  local copies, waits for them, and re-layouts: 39 us -> 41.9 us
    ppermute x25 -> x27, starting transfers between devices: 16 us -> 27.8 us  [local(): move = lambda value, pairs: lax.ppermute(value, 'dp', pairs)]
    unnamed x71 -> x76, local copies, waits for them, and re-layouts: 16.7 us -> 26.2 us
    all_to_all x1, waiting for transfers between devices: 7.92 us -> 1.55 us  [local(): got = lax.all_to_all(sent, 'mp', split_axis=1, concat_axis=0, tiled=True)]
    slice x4 -> x1, local copies, waits for them, and re-layouts: 6.07 us -> 0.01 us  [local(): downs = got[:, :width].T]
    pallas_call x3, Pallas kernels: 72.6 us -> 66.8 us  [attend(): pl.pallas_call(functools.partial(attend_kernel, requests=requests, slots=...]
    ppermute x25 -> x27, waiting for transfers between devices: 44.3 us -> 38.9 us  [local(): move = lambda value, pairs: lax.ppermute(value, 'dp', pairs)]
  transfers between devices with their start and end apart: 30 -> 32, of which waited for: 6 -> 8; matrix products, arithmetic and copies ran while one was open for 11% -> 9% of each run, Pallas kernels for 34% -> 29%
where the time goes in v6:
time: 255 us; the launch traced here: 250 us
  Pallas kernels  114 us (45%)
  waiting for transfers between devices  42 us (16%)
  local copies, waits for them, and re-layouts  41.9 us (16%)
  starting transfers between devices  33.9 us (13%)
  between operations  14.8 us (6%)
  other arithmetic  4.02 us (2%)
    pallas_call x3, Pallas kernels, attend(): pl.pallas_call(functools.partial(attend_kernel, requests=requests, slots=...  66.8 us
    ppermute x27, waiting for transfers between devices, local(): move = lambda value, pairs: lax.ppermute(value, 'dp', pairs)  38.9 us
    pallas_call x1, Pallas kernels, feed(): pl.pallas_call(functools.partial(feed_kernel, counts=tuple(((len(w1s), le...  32.9 us
    ppermute x27, starting transfers between devices, local(): move = lambda value, pairs: lax.ppermute(value, 'dp', pairs)  27.8 us
    unnamed x76, local copies, waits for them, and re-layouts  26.2 us
    pallas_call x1, Pallas kernels, project(): pl.pallas_call(functools.partial(project_kernel, requests=counts.shape[0]...  8.44 us
    all_to_all x1, starting transfers between devices, local(): got = lax.all_to_all(sent, 'mp', split_axis=1, concat_axis=0, tiled=True)  5.92 us
    pallas_call x1, Pallas kernels, mix(): pl.pallas_call(functools.partial(mix_kernel, parts=len(outs)), grid=(tok...  5.8 us
  transfers between devices with their start and end apart: 32, of which 8 were waited for; matrix products, arithmetic and copies ran while one was open for 9% of the time, Pallas kernels for 29%

profile of v6, /device:TPU:0, one launch (start us, length us, event | category | flops | bytes accessed | tf_op | source)
XLA Modules:
  0.0 250.4 jit_solution(15783921078224116289)
XLA Ops:
  7.7 1.5 fusion.6
  12.6 5.9 %all-to-all-start = ((bf16[16,4,1792]{2,0,1:T(8,128)(2,1)}), bf16[16,4,1792]{2,0,1:T(8,128)(2,1)S(1)}, u32[]{:S(2)}, u32[]{:S(2)}) async-start(bf16[16,4,1792]{2,0,1:T(8,128)(2,1)} %pad_maximum_fusion.2), calls=%async_computation | async-start | bytes 458752 | tf_op jit(solution)/shard_map/all_to_all | solution.py:564
  18.5 2.6 %copy.29 = bf16[1024,768]{0,1:T(8,128)(2,1)} copy(bf16[1024,768]{1,0:T(8,128)(2,1)} %param.19) | data formatting | bytes 3145728 | tf_op args[1]
  21.1 1.2 dynamic-slice_bitcast_fusion
  23.3 1.5 copy.35.refs_2_
  25.6 1.5 all-to-all-done
  28.6 1.6 copy-done.1
  31.1 8.4 %project.1 = (bf16[2048,128]{1,0:T(8,128)(2,1)S(1)}, bf16[8,256,128]{2,1,0:T(8,128)(2,1)S(1)}, bf16[8,256,128]{2,1,0:T(8,128)(2,1)S(1)}) custom-call(s32[4]{0:T(128)S(1)} %copy-done.22, s32[64]{0:T(128)S(1)} %copy-done.23, s32[4]{0:T(128)S(1)} %get-tuple-element.81.owners, s32[2]{0:T(128)S(1)} %pad_add_fusion.1.bases.q_bases.kv_bases, ...), custom_call_target="tpu_custom_call" | custom-call | flops 1610612736 | bytes 5767168 | tf_op jit(solution)/shard_map/project/pallas_call | solution.py:109
  41.2 1.6 collective-permute-start.3
  42.8 1.5 collective-permute-start.1
  45.4 1.7 constant_dynamic-slice_fusion.1
  50.9 14.8 %attend.3 = (f32[2048,128]{1,0:T(8,128)S(1)}, f32[2048,128]{1,0:T(8,128)S(1)}) custom-call(s32[4]{0:T(128)S(1)} %copy-done.22, s32[64]{0:T(128)S(1)} %copy-done.23, s32[2]{0:T(128)S(1)} %pad_add_fusion.1.bases.q_bases.kv_bases, s32[2]{0:T(128)S(1)} %pad_add_fusion.1.bases.q_bases.kv_bases, bf16[2048,128]{1,0:T(8,128)(2,1)S(1)} %get-tuple-element.41.q_ref, ...), custom_call_target="tpu_custom_call" | custom-call | flops 262144 | bytes 1048576 | tf_op jit(solution)/shard_map/attend/pallas_call | solution.py:308
  67.8 1.4 all-gather.9.cloned.1.call-done
  69.2 6.7 %collective-permute-start.8 = (bf16[4,1024,128]{2,1,0:T(8,128)(2,1)}, bf16[4,1024,128]{2,1,0:T(8,128)(2,1)}, u32[]{:S(2)}, u32[]{:S(2)}) collective-permute-start(bf16[4,1024,128]{2,1,0:T(8,128)(2,1)} %bitcast.42), channel_id=1, source_target_pairs={{0,16},{4,20},{8,24},{12,28},{16,0},{20,4},{24,8},{28,12},{1,17},{... | collective-permute-start | bytes 3145736 | tf_op jit(solution)/shard_map/ppermute | solution.py:584
  76.0 2.1 collective-permute-start.5
  78.2 1.2 copy-done.7
  79.4 34.8 %attend.4 = (f32[2048,128]{1,0:T(8,128)S(1)}, f32[2048,128]{1,0:T(8,128)S(1)}) custom-call(s32[4]{0:T(128)S(1)} %copy-done.22, s32[64]{0:T(128)S(1)} %copy-done.23, s32[2]{0:T(128)S(1)} %pad_add_fusion.1.bases.q_bases.kv_bases, s32[4]{0:T(128)S(1)} %get-tuple-element.87.kv_bases, bf16[2048,128]{1,0:T(8,128)(2,1)S(1)} %get-tuple-element.41.q_ref, ...), custom_call_target="tpu_custom_call" | custom-call | flops 262144 | bytes 1048576 | tf_op jit(solution)/shard_map/attend/pallas_call | solution.py:308
  118.4 1.9 slice.26
  120.3 1.9 slice.27
  122.2 1.2 copy-done.10
  123.4 1.2 copy-done.12
  126.8 17.1 %attend.5 = bf16[2048,128]{1,0:T(8,128)(2,1)S(1)} custom-call(s32[4]{0:T(128)S(1)} %copy-done.22, s32[64]{0:T(128)S(1)} %copy-done.23, s32[2]{0:T(128)S(1)} %pad_add_fusion.1.bases.q_bases.kv_bases, s32[2]{0:T(128)S(1)} %pad_add_fusion.2.kv_bases, bf16[2048,128]{1,0:T(8,128)(2,1)S(1)} %get-tuple-element.41.q_ref, bf16[8,256,128]{2,1,0:T(8,128)(2,1)S(1)} %copy-done.18, ...), custom_call_target="tpu_custom_call" | custom-call | flops 262144 | bytes 1048576 | tf_op jit(solution)/shard_map/attend/pallas_call | solution.py:308
  144.6 1.2 collective-permute-done.14
  147.6 11.1 %collective-permute-start.16 = (bf16[4,128,1024]{2,1,0:T(8,128)(2,1)}, bf16[4,128,1024]{2,1,0:T(8,128)(2,1)}, u32[]{:S(2)}, u32[]{:S(2)}) collective-permute-start(bf16[4,128,1024]{2,1,0:T(8,128)(2,1)} %bitcast.57), channel_id=1, source_target_pairs={{0,16},{4,20},{8,24},{12,28},{16,0},{20,4},{24,8},{28,12},{1,17},{... | collective-permute-start | bytes 3145736 | tf_op jit(solution)/shard_map/ppermute | solution.py:584
  159.5 2.0 collective-permute-done.18.refs_14_
  162.3 20.3 %collective-permute-done.16.refs_7_ = bf16[4,128,1024]{2,1,0:T(8,128)(2,1)} collective-permute-done((bf16[4,128,1024]{2,1,0:T(8,128)(2,1)}, bf16[4,128,1024]{2,1,0:T(8,128)(2,1)}, u32[]{:S(2)}, u32[]{:S(2)}) %collective-permute-start.16) | collective-permute-done | bytes 1048608 | tf_op jit(solution)/shard_map/ppermute | solution.py:584
  182.6 1.5 collective-permute-done.15.refs_6_
  188.3 13.6 %collective-permute-done.21.refs_8_ = bf16[4,64,1024]{2,1,0:T(8,128)(2,1)} collective-permute-done((bf16[4,64,1024]{2,1,0:T(8,128)(2,1)S(1)}, bf16[4,64,1024]{2,1,0:T(8,128)(2,1)}, u32[]{:S(2)}, u32[]{:S(2)}) %collective-permute-start.21) | collective-permute-done | bytes 524320 | tf_op jit(solution)/shard_map/ppermute | solution.py:584
  202.5 1.3 copy-done.5
  203.8 5.8 %mix.1.normed_ref = bf16[1024,1024]{1,0:T(8,128)(2,1)S(1)} custom-call(bf16[1024,1024]{1,0:T(8,128)(2,1)} %x_ref.1, bf16[4,1024,256]{2,1,0:T(8,128)(2,1)} %bitcast.51, bf16[4,144,1024]{2,1,0:T(8,128)(2,1)S(1)} %bitcast.38, bf16[4,144,1024]{2,1,0:T(8,128)(2,1)S(1)} %copy-done.5, f32[1,1024]{1,0:T(1,128)S(1)} %bitcast.40, f32[1,1024]{1,0:T(1,128)S(1)} %bitcast.41), custom_call_target="tpu_custom_call" | custom-call | flops 2147483648 | bytes 8388608 | tf_op jit(solution)/shard_map/mix/pallas_call | solution.py:363
  209.6 1.3 copy-done.2
  211.0 32.9 %feed.1 = (bf16[256,1024]{1,0:T(8,128)(2,1)}, bf16[1024,768]{1,0:T(8,128)(2,1)}) custom-call(s32[3]{0:T(128)S(1)} %pad_add_fusion.place, bf16[1024,1024]{1,0:T(8,128)(2,1)} %copy-done.2, bf16[4,144,1024]{2,1,0:T(8,128)(2,1)} %bitcast.37, bf16[4,1024,128]{2,1,0:T(8,128)(2,1)S(1)} %bitcast.45, bf16[4,1024,128]{2,1,0:T(8,128)(2,1)} %collective-permute-done.7.refs_1_, ...), custom_call_target="tpu_custom_call" | custom-call | flops 17179869184 | bytes 16777216 | tf_op jit(solution)/shard_map/feed/pallas_call | solution.py:464
  (153 shorter events, 31.4 us)
Async XLA Ops:
  7.2 21.3 %collective-permute-start = (bf16[1024,1024]{1,0:T(8,128)(2,1)}, bf16[1024,1024]{1,0:T(8,128)(2,1)}, u32[]{:S(2)}, u32[]{:S(2)}) collective-permute-start(bf16[1024,1024]{1,0:T(8,128)(2,1)} %x_ref.1), channel_id=1, source_target_pairs={{0,4},{4,0},{8,12},{12,8},{16,20},{20,16},{24,28},{28,24},{1,5},{5... | collective-permute-start | bytes 6291464 | tf_op jit(solution)/shard_map/ppermute | solution.py:584
  12.6 14.6 %all-to-all-start = ((bf16[16,4,1792]{2,0,1:T(8,128)(2,1)}), bf16[16,4,1792]{2,0,1:T(8,128)(2,1)S(1)}, u32[]{:S(2)}, u32[]{:S(2)}) async-start(bf16[16,4,1792]{2,0,1:T(8,128)(2,1)} %pad_maximum_fusion.2), calls=%async_computation | async-start | bytes 458752 | tf_op jit(solution)/shard_map/all_to_all | solution.py:564
  18.5 50.7 %all-gather.9.cloned.1.call-start = ((), (), s32[]{:S(2)}) async-start(), calls=%async_computation.1 | async-start | bytes 1310720 | tf_op jit(solution)/shard_map/all_gather | solution.py:602
  41.2 102.8 %all-gather.11.cloned.1.call-start = ((), (), s32[]{:S(2)}) async-start(), calls=%async_computation.2 | async-start | bytes 1310720 | tf_op jit(solution)/shard_map/all_gather | solution.py:618
  41.2 26.5 %collective-permute-start.3 = (bf16[8,256,128]{2,1,0:T(8,128)(2,1)}, bf16[8,256,128]{2,1,0:T(8,128)(2,1)S(1)}, u32[]{:S(2)}, u32[]{:S(2)}) collective-permute-start(bf16[8,256,128]{2,1,0:T(8,128)(2,1)} %copy-done.15), channel_id=1, source_target_pairs={{0,16},{4,20},{8,24},{12,28},{16,0},{20,4},{24,8},{28,12},{1,17},{... | collective-permute-start | bytes 1572872 | tf_op jit(solution)/shard_map/ppermute | solution.py:584
  42.8 25.0 %collective-permute-start.1 = (bf16[8,256,128]{2,1,0:T(8,128)(2,1)}, bf16[8,256,128]{2,1,0:T(8,128)(2,1)}, u32[]{:S(2)}, u32[]{:S(2)}) collective-permute-start(bf16[8,256,128]{2,1,0:T(8,128)(2,1)} %copy-done.15), channel_id=1, source_target_pairs={{0,8},{4,12},{8,0},{12,4},{16,24},{20,28},{24,16},{28,20},{1,9},{5... | collective-permute-start | bytes 1572872 | tf_op jit(solution)/shard_map/ppermute | solution.py:584
  44.3 23.5 %collective-permute-start.4 = (bf16[8,256,128]{2,1,0:T(8,128)(2,1)}, bf16[8,256,128]{2,1,0:T(8,128)(2,1)}, u32[]{:S(2)}, u32[]{:S(2)}) collective-permute-start(bf16[8,256,128]{2,1,0:T(8,128)(2,1)} %copy-done.13), channel_id=1, source_target_pairs={{0,16},{4,20},{8,24},{12,28},{16,0},{20,4},{24,8},{28,12},{1,17},{... | collective-permute-start | bytes 1572872 | tf_op jit(solution)/shard_map/ppermute | solution.py:584
  44.8 23.0 %collective-permute-start.2 = (bf16[8,256,128]{2,1,0:T(8,128)(2,1)}, bf16[8,256,128]{2,1,0:T(8,128)(2,1)}, u32[]{:S(2)}, u32[]{:S(2)}) collective-permute-start(bf16[8,256,128]{2,1,0:T(8,128)(2,1)} %copy-done.13), channel_id=1, source_target_pairs={{0,8},{4,12},{8,0},{12,4},{16,24},{20,28},{24,16},{28,20},{1,9},{5... | collective-permute-start | bytes 1572872 | tf_op jit(solution)/shard_map/ppermute | solution.py:584
  69.2 74.8 %all-gather.13.cloned.1.call-start = ((), (), s32[]{:S(2)}) async-start(), calls=%async_computation.3 | async-start | bytes 1474560 | tf_op jit(solution)/shard_map/all_gather | solution.py:619
  69.2 48.6 %collective-permute-start.8 = (bf16[4,1024,128]{2,1,0:T(8,128)(2,1)}, bf16[4,1024,128]{2,1,0:T(8,128)(2,1)}, u32[]{:S(2)}, u32[]{:S(2)}) collective-permute-start(bf16[4,1024,128]{2,1,0:T(8,128)(2,1)} %bitcast.42), channel_id=1, source_target_pairs={{0,16},{4,20},{8,24},{12,28},{16,0},{20,4},{24,8},{28,12},{1,17},{... | collective-permute-start | bytes 3145736 | tf_op jit(solution)/shard_map/ppermute | solution.py:584
  75.9 41.9 %collective-permute-start.7 = (bf16[4,1024,128]{2,1,0:T(8,128)(2,1)}, bf16[4,1024,128]{2,1,0:T(8,128)(2,1)}, u32[]{:S(2)}, u32[]{:S(2)}) collective-permute-start(bf16[4,1024,128]{2,1,0:T(8,128)(2,1)} %bitcast.43), channel_id=1, source_target_pairs={{0,8},{4,12},{8,0},{12,4},{16,24},{20,28},{24,16},{28,20},{1,9},{5... | collective-permute-start | bytes 3145736 | tf_op jit(solution)/shard_map/ppermute | solution.py:584
  76.0 126.5 %all-gather.15.cloned.1.call-start = ((), (), s32[]{:S(2)}) async-start(), calls=%async_computation.4 | async-start | bytes 2621440 | tf_op jit(solution)/shard_map/all_gather | solution.py:643
  76.0 40.2 %collective-permute-start.5 = (bf16[8,256,128]{2,1,0:T(8,128)(2,1)S(1)}, bf16[8,256,128]{2,1,0:T(8,128)(2,1)S(1)}, u32[]{:S(2)}, u32[]{:S(2)}) collective-permute-start(bf16[8,256,128]{2,1,0:T(8,128)(2,1)S(1)} %collective-permute-done.3.refs_2_), channel_id=1, source_target_pairs={{0,8},{4,12},{8,0},{12,4},{16,24},{20,28},{24,16},{28,20},{1,9},{5... | collective-permute-start | bytes 1572872 | tf_op jit(solution)/shard_map/ppermute | solution.py:584
  78.1 38.9 %collective-permute-start.6 = (bf16[8,256,128]{2,1,0:T(8,128)(2,1)}, bf16[8,256,128]{2,1,0:T(8,128)(2,1)S(1)}, u32[]{:S(2)}, u32[]{:S(2)}) collective-permute-start(bf16[8,256,128]{2,1,0:T(8,128)(2,1)} %collective-permute-done.2.refs_1_), channel_id=1, source_target_pairs={{0,16},{4,20},{8,24},{12,28},{16,0},{20,4},{24,8},{28,12},{1,17},{... | collective-permute-start | bytes 1572872 | tf_op jit(solution)/shard_map/ppermute | solution.py:584
  78.2 65.7 %collective-permute-start.11 = (bf16[4,1024,128]{2,1,0:T(8,128)(2,1)}, bf16[4,1024,128]{2,1,0:T(8,128)(2,1)}, u32[]{:S(2)}, u32[]{:S(2)}) collective-permute-start(bf16[4,1024,128]{2,1,0:T(8,128)(2,1)} %bitcast.44), channel_id=1, source_target_pairs={{0,4},{4,0},{8,12},{12,8},{16,20},{20,16},{24,28},{28,24},{1,5},{5... | collective-permute-start | bytes 3145736 | tf_op jit(solution)/shard_map/ppermute | solution.py:584
  117.8 26.2 %collective-permute-start.13 = (bf16[4,1024,128]{2,1,0:T(8,128)(2,1)}, bf16[4,1024,128]{2,1,0:T(8,128)(2,1)}, u32[]{:S(2)}, u32[]{:S(2)}) collective-permute-start(bf16[4,1024,128]{2,1,0:T(8,128)(2,1)} %collective-permute-done.8.refs_2_), channel_id=1, source_target_pairs={{0,4},{4,0},{8,12},{12,8},{16,20},{20,16},{24,28},{28,24},{1,5},{5... | collective-permute-start | bytes 3145736 | tf_op jit(solution)/shard_map/ppermute | solution.py:584
  118.3 25.7 %collective-permute-start.12 = (bf16[4,1024,128]{2,1,0:T(8,128)(2,1)}, bf16[4,1024,128]{2,1,0:T(8,128)(2,1)}, u32[]{:S(2)}, u32[]{:S(2)}) collective-permute-start(bf16[4,1024,128]{2,1,0:T(8,128)(2,1)} %collective-permute-done.7.refs_1_), channel_id=1, source_target_pairs={{0,4},{4,0},{8,12},{12,8},{16,20},{20,16},{24,28},{28,24},{1,5},{5... | collective-permute-start | bytes 3145736 | tf_op jit(solution)/shard_map/ppermute | solution.py:584
  122.1 21.8 %collective-permute-start.10 = (bf16[4,512,128]{2,1,0:T(8,128)(2,1)}, bf16[4,512,128]{2,1,0:T(8,128)(2,1)}, u32[]{:S(2)}, u32[]{:S(2)}) collective-permute-start(bf16[4,512,128]{2,1,0:T(8,128)(2,1)} %slice.27), channel_id=1, source_target_pairs={{0,16},{4,20},{8,24},{12,28},{16,0},{20,4},{24,8},{28,12},{1,17},{... | collective-permute-start | bytes 1572872 | tf_op jit(solution)/shard_map/ppermute | solution.py:584
  122.1 21.8 %collective-permute-start.9 = (bf16[4,512,128]{2,1,0:T(8,128)(2,1)}, bf16[4,512,128]{2,1,0:T(8,128)(2,1)}, u32[]{:S(2)}, u32[]{:S(2)}) collective-permute-start(bf16[4,512,128]{2,1,0:T(8,128)(2,1)} %slice.26), channel_id=1, source_target_pairs={{0,8},{4,12},{8,0},{12,4},{16,24},{20,28},{24,16},{28,20},{1,9},{5... | collective-permute-start | bytes 1572872 | tf_op jit(solution)/shard_map/ppermute | solution.py:584
  144.1 1.7 collective-permute-start.14
  146.6 37.5 %collective-permute-start.20 = (bf16[4,144,1024]{2,1,0:T(8,128)(2,1)}, bf16[4,144,1024]{2,1,0:T(8,128)(2,1)S(1)}, u32[]{:S(2)}, u32[]{:S(2)}) collective-permute-start(bf16[4,144,1024]{2,1,0:T(8,128)(2,1)} %bitcast.36), channel_id=1, source_target_pairs={{0,4},{4,0},{8,12},{12,8},{16,20},{20,16},{24,28},{28,24},{1,5},{5... | collective-permute-start | bytes 3538952 | tf_op jit(solution)/shard_map/ppermute | solution.py:584
  147.1 11.6 %collective-permute-start.17 = (bf16[4,512,128]{2,1,0:T(8,128)(2,1)}, bf16[4,512,128]{2,1,0:T(8,128)(2,1)S(1)}, u32[]{:S(2)}, u32[]{:S(2)}) collective-permute-start(bf16[4,512,128]{2,1,0:T(8,128)(2,1)} %collective-permute-done.9.refs_3_), channel_id=1, source_target_pairs={{0,4},{4,0},{8,12},{12,8},{16,20},{20,16},{24,28},{28,24},{1,5},{5... | collective-permute-start | bytes 1572872 | tf_op jit(solution)/shard_map/ppermute | solution.py:584
  147.2 15.1 %collective-permute-start.19 = (bf16[4,128,1024]{2,1,0:T(8,128)(2,1)}, bf16[4,128,1024]{2,1,0:T(8,128)(2,1)S(1)}, u32[]{:S(2)}, u32[]{:S(2)}) collective-permute-start(bf16[4,128,1024]{2,1,0:T(8,128)(2,1)} %bitcast.56), channel_id=1, source_target_pairs={{0,4},{4,0},{8,12},{12,8},{16,20},{20,16},{24,28},{28,24},{1,5},{5... | collective-permute-start | bytes 3145736 | tf_op jit(solution)/shard_map/ppermute | solution.py:584
  147.6 35.1 %collective-permute-start.16 = (bf16[4,128,1024]{2,1,0:T(8,128)(2,1)}, bf16[4,128,1024]{2,1,0:T(8,128)(2,1)}, u32[]{:S(2)}, u32[]{:S(2)}) collective-permute-start(bf16[4,128,1024]{2,1,0:T(8,128)(2,1)} %bitcast.57), channel_id=1, source_target_pairs={{0,16},{4,20},{8,24},{12,28},{16,0},{20,4},{24,8},{28,12},{1,17},{... | collective-permute-start | bytes 3145736 | tf_op jit(solution)/shard_map/ppermute | solution.py:584
  158.6 25.5 %collective-permute-start.15 = (bf16[4,128,1024]{2,1,0:T(8,128)(2,1)}, bf16[4,128,1024]{2,1,0:T(8,128)(2,1)}, u32[]{:S(2)}, u32[]{:S(2)}) collective-permute-start(bf16[4,128,1024]{2,1,0:T(8,128)(2,1)} %bitcast.58), channel_id=1, source_target_pairs={{0,8},{4,12},{8,0},{12,4},{16,24},{20,28},{24,16},{28,20},{1,9},{5... | collective-permute-start | bytes 3145736 | tf_op jit(solution)/shard_map/ppermute | solution.py:584
  159.4 2.1 collective-permute-start.18
  186.2 24.7 %collective-permute-start.23 = (bf16[4,128,1024]{2,1,0:T(8,128)(2,1)}, bf16[4,128,1024]{2,1,0:T(8,128)(2,1)}, u32[]{:S(2)}, u32[]{:S(2)}) collective-permute-start(bf16[4,128,1024]{2,1,0:T(8,128)(2,1)} %collective-permute-done.15.refs_6_), channel_id=1, source_target_pairs={{0,4},{4,0},{8,12},{12,8},{16,20},{20,16},{24,28},{28,24},{1,5},{5... | collective-permute-start | bytes 3145736 | tf_op jit(solution)/shard_map/ppermute | solution.py:584
  187.4 14.5 %collective-permute-start.21 = (bf16[4,64,1024]{2,1,0:T(8,128)(2,1)S(1)}, bf16[4,64,1024]{2,1,0:T(8,128)(2,1)}, u32[]{:S(2)}, u32[]{:S(2)}) collective-permute-start(bf16[4,64,1024]{2,1,0:T(8,128)(2,1)S(1)} %slice.30), channel_id=1, source_target_pairs={{0,8},{4,12},{8,0},{12,4},{16,24},{20,28},{24,16},{28,20},{1,9},{5... | collective-permute-start | bytes 1572872 | tf_op jit(solution)/shard_map/ppermute | solution.py:584
  187.7 23.2 %collective-permute-start.24 = (bf16[4,128,1024]{2,1,0:T(8,128)(2,1)}, bf16[4,128,1024]{2,1,0:T(8,128)(2,1)}, u32[]{:S(2)}, u32[]{:S(2)}) collective-permute-start(bf16[4,128,1024]{2,1,0:T(8,128)(2,1)} %collective-permute-done.16.refs_7_), channel_id=1, source_target_pairs={{0,4},{4,0},{8,12},{12,8},{16,20},{20,16},{24,28},{28,24},{1,5},{5... | collective-permute-start | bytes 3145736 | tf_op jit(solution)/shard_map/ppermute | solution.py:584
  188.0 14.2 %collective-permute-start.22 = (bf16[4,64,1024]{2,1,0:T(8,128)(2,1)S(1)}, bf16[4,64,1024]{2,1,0:T(8,128)(2,1)}, u32[]{:S(2)}, u32[]{:S(2)}) collective-permute-start(bf16[4,64,1024]{2,1,0:T(8,128)(2,1)S(1)} %slice.31), channel_id=1, source_target_pairs={{0,16},{4,20},{8,24},{12,28},{16,0},{20,4},{24,8},{28,12},{1,17},{... | collective-permute-start | bytes 1572872 | tf_op jit(solution)/shard_map/ppermute | solution.py:584
  201.9 9.1 %collective-permute-start.25 = (bf16[4,64,1024]{2,1,0:T(8,128)(2,1)}, bf16[4,64,1024]{2,1,0:T(8,128)(2,1)}, u32[]{:S(2)}, u32[]{:S(2)}) collective-permute-start(bf16[4,64,1024]{2,1,0:T(8,128)(2,1)} %collective-permute-done.21.refs_8_), channel_id=1, source_target_pairs={{0,4},{4,0},{8,12},{12,8},{16,20},{20,16},{24,28},{28,24},{1,5},{5... | collective-permute-start | bytes 1572872 | tf_op jit(solution)/shard_map/ppermute | solution.py:584
  202.2 8.7 %collective-permute-start.26 = (bf16[4,64,1024]{2,1,0:T(8,128)(2,1)}, bf16[4,64,1024]{2,1,0:T(8,128)(2,1)}, u32[]{:S(2)}, u32[]{:S(2)}) collective-permute-start(bf16[4,64,1024]{2,1,0:T(8,128)(2,1)} %collective-permute-done.22.refs_9_), channel_id=1, source_target_pairs={{0,4},{4,0},{8,12},{12,8},{16,20},{20,16},{24,28},{28,24},{1,5},{5... | collective-permute-start | bytes 1572872 | tf_op jit(solution)/shard_map/ppermute | solution.py:584
  (37 other events, 363.7 us)
Sparse Core Ops, SparseCore 0:
  41.3 27.8 all-gather.8
  70.7 30.6 all-gather.10
  103.0 29.9 all-gather.12
  146.7 54.6 all-gather.14

commit v7 on v6

--- a/solution.py
+++ b/solution.py
@@ -17,7 +17,7 @@
 MIB = 1 << 20
 
 
-def params(vmem=48):
+def params(vmem):
     return pltpu.CompilerParams(
         dimension_semantics=("arbitrary",), vmem_limit_bytes=vmem * MIB
     )
@@ -133,7 +133,7 @@
             jax.ShapeDtypeStruct((total, cols // 3), jnp.bfloat16),
         ]
         + [jax.ShapeDtypeStruct((tok // PAGE, PAIR + PAGE, PAIR), jnp.bfloat16)] * parts,
-        compiler_params=params(),
+        compiler_params=params(62),
         cost_estimate=pl.CostEstimate(
             flops=2 * total * width * cols, bytes_accessed=2 * total * (width + cols),
             transcendentals=0,
@@ -143,25 +143,31 @@
 
 
 def attend_kernel(
-    counts, table, q_bases, kv_bases, q_ref, *refs,
+    counts, table, q_bases, kv_bases, q_hbm, *refs,
     requests, slots, q_size, arrays, sizes, first, last, group,
 ):
     refs = list(refs)
     kv_hbm = [refs.pop(0) for _ in arrays]
-    if not first:
-        acc_in, stat_in = refs.pop(0), refs.pop(0)
+    state_hbm = [] if first else [refs.pop(0), refs.pop(0)]
     if last:
         out_ref = refs.pop(0)
     else:
         acc_out, stat_out = refs.pop(0), refs.pop(0)
-    kv, scores, listed, amount, asked, q_amount, sems = refs
-    copies = []
+    kv, scores, listed, amount, asked, q_amount, sems, q_ref = refs[:8]
+    if not first:
+        acc_in, stat_in = refs[8:]
+    targets = [(q_hbm, q_ref)]
     offset = 0
     for i, size in enumerate(arrays):
-        copy = pltpu.make_async_copy(kv_hbm[i], kv.at[pl.ds(offset, size)], sems.at[i])
+        targets.append((kv_hbm[i], kv.at[pl.ds(offset, size)]))
+        offset += size
+    targets += list(zip(state_hbm, refs[8:]))
+    copies = [
+        pltpu.make_async_copy(source, target, sems.at[n])
+        for n, (source, target) in enumerate(targets)
+    ]
+    for copy in copies:
         copy.start()
-        copies.append(copy)
-        offset += size
     for r in range(requests):
         amount[r] = 0
         q_amount[r] = 0
@@ -303,7 +309,6 @@
     slots = table.shape[0]
     requests = counts.shape[0]
     most = min(sum(sizes), slots)
-    vmem = pl.BlockSpec(memory_space=pltpu.VMEM)
     state_shape = [jax.ShapeDtypeStruct((tok, PAIR), jnp.float32)] * 2
     out = pl.pallas_call(
         functools.partial(
@@ -314,9 +319,7 @@
         grid_spec=pltpu.PrefetchScalarGridSpec(
             num_scalar_prefetch=4,
             grid=(1,),
-            in_specs=[pl.BlockSpec((tok, PAIR), lambda i, *_: (0, 0))]
-            + [pl.BlockSpec(memory_space=pl.ANY)] * len(pieces)
-            + ([] if first else [pl.BlockSpec((tok, PAIR), lambda i, *_: (0, 0))] * 2),
+            in_specs=[pl.BlockSpec(memory_space=pl.ANY)] * (len(pieces) + (1 if first else 3)),
             out_specs=[pl.BlockSpec((tok, PAIR), lambda i, *_: (0, 0))] * (1 if last else 2),
             scratch_shapes=[
                 pltpu.VMEM((sum(sizes), PAIR + PAGE, PAIR), jnp.bfloat16),
@@ -325,11 +328,13 @@
                 pltpu.SMEM((requests,), jnp.int32),
                 pltpu.SMEM((requests, tok // PAGE), jnp.int32),
                 pltpu.SMEM((requests,), jnp.int32),
-                pltpu.SemaphoreType.DMA((len(pieces),)),
-            ],
+                pltpu.SemaphoreType.DMA((len(pieces) + 3,)),
+                pltpu.VMEM((tok, PAIR), jnp.bfloat16),
+            ]
+            + ([] if first else [pltpu.VMEM((tok, PAIR), jnp.float32)] * 2),
         ),
         out_shape=[jax.ShapeDtypeStruct((tok, PAIR), jnp.bfloat16)] if last else state_shape,
-        compiler_params=params(),
+        compiler_params=params(62),
         cost_estimate=pl.CostEstimate(
             flops=tok * PAIR, bytes_accessed=4 * tok * PAIR, transcendentals=0,
         ),
@@ -338,66 +343,39 @@
     return out[0] if last else out
 
 
-def mix_kernel(x_ref, ctx_ref, *refs, parts):
-    out_w_refs = refs[:parts]
-    gain_ref, bias_ref, out_ref, joined = refs[parts:]
-
-    @pl.when(pl.program_id(0) == 0)
-    def _():
-        near = joined.shape[1] // parts
-        for i in range(parts):
-            joined[:, i * near : (i + 1) * near] = out_w_refs[i][:, :near]
-
-    mixed = x_ref[...].astype(jnp.float32)
-    for j in range(ctx_ref.shape[0]):
-        mixed = mixed + jnp.dot(ctx_ref[j], joined[j], preferred_element_type=jnp.float32)
-    out_ref[...] = normalize(mixed, gain_ref[...], bias_ref[...]).astype(jnp.bfloat16)
-
-
-def mix(x, ctx, outs, gain, bias):
-    tok, width = x.shape
-    groups, _, cols = ctx.shape
-    block = 256
-    rows = lambda i: (i, 0)
-    fixed = lambda i: (0, 0)
-    return pl.pallas_call(
-        functools.partial(mix_kernel, parts=len(outs)),
-        grid=(tok // block,),
-        in_specs=[
-            pl.BlockSpec((block, width), rows),
-            pl.BlockSpec((groups, block, cols), lambda i: (0, i, 0)),
-        ]
-        + [pl.BlockSpec(w.shape, lambda i: (0, 0, 0)) for w in outs]
-        + [pl.BlockSpec((1, width), fixed)] * 2,
-        out_specs=pl.BlockSpec((block, width), rows),
-        scratch_shapes=[pltpu.VMEM((groups, cols, width), jnp.bfloat16)],
-        out_shape=jax.ShapeDtypeStruct((tok, width), jnp.bfloat16),
-        compiler_params=params(),
-        cost_estimate=pl.CostEstimate(
-            flops=2 * tok * width * groups * cols, bytes_accessed=8 * tok * width, transcendentals=0
-        ),
-        name="mix",
-    )(x, ctx, *outs, gain[None], bias[None])
-
-
-def feed_kernel(place, normed_ref, bias_ref, *refs, counts, last_step):
+def finish_kernel(place, x_ref, ctx_ref, *refs, parts, counts, last_step):
     refs = list(refs)
+    out_w_refs, refs = refs[:parts], refs[parts:]
+    gain1_ref, bias1_ref, bias_ref = refs[:3]
+    refs = refs[3:]
     sets = []
     for n1, n2 in counts:
         w1s, refs = refs[:n1], refs[n1:]
         w2s, refs = refs[:n2], refs[n2:]
         sets.append((w1s, w2s))
     b2_ref, gain_ref, bias2_ref, next_w_ref, next_b_ref = refs[:5]
-    layer_ref, next_ref, acc, done = refs[5:]
+    layer_ref, next_ref, joined, normed_ref, acc, done = refs[5:]
     step = pl.program_id(0)
     tok = normed_ref.shape[0]
-    block = min(256, tok)
+    block = min(512, tok)
     halves = len(sets)
     groups = (last_step + 1) // halves
 
     @pl.when(step == 0)
     def _():
-        acc[...] = jnp.zeros_like(acc)
+        near = joined.shape[1] // parts
+        for i in range(parts):
+            joined[:, i * near : (i + 1) * near] = out_w_refs[i][:, :near]
+        for t in range(tok // block):
+            rows = slice(t * block, (t + 1) * block)
+            mixed = x_ref[rows, :].astype(jnp.float32)
+            for j in range(ctx_ref.shape[0]):
+                mixed = mixed + jnp.dot(
+                    ctx_ref[j, rows, :], joined[j], preferred_element_type=jnp.float32
+                )
+            normed = normalize(mixed, gain1_ref[...], bias1_ref[...]).astype(jnp.bfloat16)
+            normed_ref[rows, :] = normed
+            acc[rows, :] = normed.astype(jnp.float32) + b2_ref[...]
 
     def absorb(h, w1_refs, w2_refs):
         if len(w1_refs) == 1:
@@ -436,8 +414,7 @@
     def _():
         for t in range(tok // block):
             rows = slice(t * block, (t + 1) * block)
-            total = normed_ref[rows, :].astype(jnp.float32) + acc[rows, :] + b2_ref[...]
-            layer = normalize(total, gain_ref[...], bias2_ref[...]).astype(jnp.bfloat16)
+            layer = normalize(acc[rows, :], gain_ref[...], bias2_ref[...]).astype(jnp.bfloat16)
             done[rows, :] = layer
             next_ref[rows, :] = (
                 jnp.dot(layer, next_w_ref[...], preferred_element_type=jnp.float32)
@@ -447,49 +424,56 @@
         layer_ref[...] = done[pl.ds(pl.multiple_of(place[0] * share, share), share), :]
 
 
-def feed(place, normed, bias, sets, b2, gain, bias2, next_w, next_b, share):
-    tok, width = normed.shape
+def finish(
+    place, x, ctx, outs, gain1, bias1, bias, sets, b2, gain, bias2, next_w, next_b, share
+):
+    tok, width = x.shape
     halves = len(sets)
-    groups = bias.shape[0]
+    groups, _, ctx_cols = ctx.shape
     cols = bias.shape[2] // halves
     steps = halves * groups
-    fixed = lambda i, *_: (0, 0)
+
+    def whole(array):
+        return pl.BlockSpec(
+            array.shape, lambda i, *_: (0,) * array.ndim, pipeline_mode=pl.Buffered(1)
+        )
+
     specs, arrays = [], []
     for h, (w1s, w2s) in enumerate(sets):
         at = lambda i, *_, h=h: (jnp.clip(i - h * groups, 0, groups - 1), 0, 0)
         for array in (*w1s, *w2s):
             specs.append(pl.BlockSpec((1,) + array.shape[1:], at))
             arrays.append(array)
+    head = [x, ctx, *outs, gain1[None], bias1[None]]
+    tail = [b2[None], gain[None], bias2[None], next_w, next_b[None]]
     next_cols = next_w.shape[1]
+    fixed = lambda i, *_: (0, 0)
     return pl.pallas_call(
         functools.partial(
-            feed_kernel,
+            finish_kernel,
+            parts=len(outs),
             counts=tuple((len(w1s), len(w2s)) for w1s, w2s in sets),
             last_step=steps - 1,
         ),
         grid_spec=pltpu.PrefetchScalarGridSpec(
             num_scalar_prefetch=1,
             grid=(steps,),
-            in_specs=[
-                pl.BlockSpec((tok, width), fixed),
+            in_specs=[whole(array) for array in head]
+            + [
                 pl.BlockSpec(
                     (1, 16, bias.shape[2]),
                     lambda i, *_: (i % groups, bias.shape[1] // 16 - 1, 0),
                 ),
             ]
             + specs
-            + [
-                pl.BlockSpec((1, width), fixed),
-                pl.BlockSpec((1, width), fixed),
-                pl.BlockSpec((1, width), fixed),
-                pl.BlockSpec((width, next_cols), fixed),
-                pl.BlockSpec((1, next_cols), fixed),
-            ],
+            + [whole(array) for array in tail],
             out_specs=[
                 pl.BlockSpec((share, width), fixed),
                 pl.BlockSpec((tok, next_cols), fixed),
             ],
             scratch_shapes=[
+                pltpu.VMEM((groups, ctx_cols, width), jnp.bfloat16),
+                pltpu.VMEM((tok, width), jnp.bfloat16),
                 pltpu.VMEM((tok, width), jnp.float32),
                 pltpu.VMEM((tok, width), jnp.bfloat16),
             ],
@@ -498,16 +482,13 @@
             jax.ShapeDtypeStruct((share, width), jnp.bfloat16),
             jax.ShapeDtypeStruct((tok, next_cols), jnp.bfloat16),
         ],
-        compiler_params=params(),
+        compiler_params=params(62),
         cost_estimate=pl.CostEstimate(
             flops=4 * tok * width * cols * steps, bytes_accessed=4 * width * cols * steps,
             transcendentals=tok * cols * steps,
         ),
-        name="feed",
-    )(
-        place, normed, bias, *arrays,
-        b2[None], gain[None], bias2[None], next_w, next_b[None],
-    )
+        name="finish",
+    )(place, *head, bias, *arrays, *tail)
 
 
 def three_parts(values):
@@ -664,10 +645,10 @@
         sets = [([lax.all_gather(first_feed_weight, "mp", axis=0)], [second])]
         outs = [lax.all_gather(attention_out_weight, "mp", axis=0)]
         contexts = lax.all_gather(context, "mp", axis=0)
-    normed = mix(tokens, contexts, outs, first_norm_gain, first_norm_bias)
-    layer_rows, next_proj = feed(
-        place, normed, bias_rows, sets, second_feed_bias, second_norm_gain,
-        second_norm_bias, following_qkv_weight, following_bias, tok_rows // mp_count,
+    layer_rows, next_proj = finish(
+        place, tokens, contexts, outs, first_norm_gain, first_norm_bias, bias_rows, sets,
+        second_feed_bias, second_norm_gain, second_norm_bias, following_qkv_weight,
+        following_bias, tok_rows // mp_count,
     )
     return (layer_rows, next_proj)
 

time: 255 us -> 232 us (0.910)
  local copies, waits for them, and re-layouts: 41.9 us -> 16.6 us
  Pallas kernels: 114 us -> 125 us
  starting transfers between devices: 33.9 us -> 24.3 us
    unnamed x76 -> x34, local copies, waits for them, and re-layouts: 26.2 us -> 4.63 us
    pallas_call x3, Pallas kernels: 66.8 us -> 79.1 us  [attend(): pl.pallas_call(functools.partial(attend_kernel, requests=requests, slots=...]
    ppermute x27, starting transfers between devices: 27.8 us -> 18.3 us  [local(): move = lambda value, pairs: lax.ppermute(value, 'dp', pairs)]
    pallas_call x2 -> x1, Pallas kernels: 38.7 us -> 35 us  [finish(): pl.pallas_call(functools.partial(finish_kernel, parts=len(outs), counts=t...]
  transfers between devices with their start and end apart: 32 -> 32, of which waited for: 8 -> 7; matrix products, arithmetic and copies ran while one was open for 9% -> 8% of each run, Pallas kernels for 29% -> 35%
where the time goes in v7:
time: 232 us; the launch traced here: 227 us
  Pallas kernels  125 us (54%)
  waiting for transfers between devices  40.9 us (18%)
  starting transfers between devices  24.3 us (10%)
  local copies, waits for them, and re-layouts  16.6 us (7%)
  between operations  14.9 us (6%)
  other arithmetic  6 us (3%)
    pallas_call x3, Pallas kernels, attend(): pl.pallas_call(functools.partial(attend_kernel, requests=requests, slots=...  79.1 us
    ppermute x27, waiting for transfers between devices, local(): move = lambda value, pairs: lax.ppermute(value, 'dp', pairs)  37.2 us
    pallas_call x1, Pallas kernels, finish(): pl.pallas_call(functools.partial(finish_kernel, parts=len(outs), counts=t...  35 us
    ppermute x27, starting transfers between devices, local(): move = lambda value, pairs: lax.ppermute(value, 'dp', pairs)  18.3 us
    pallas_call x1, Pallas kernels, project(): pl.pallas_call(functools.partial(project_kernel, requests=counts.shape[0]...  10.6 us
    all_to_all x1, starting transfers between devices, local(): got = lax.all_to_all(sent, 'mp', split_axis=1, concat_axis=0, tiled=True)  5.95 us
  transfers between devices with their start and end apart: 32, of which 7 were waited for; matrix products, arithmetic and copies ran while one was open for 8% of the time, Pallas kernels for 35%

profile of v7, /device:TPU:0, one launch (start us, length us, event | category | flops | bytes accessed | tf_op | source)
XLA Modules:
  0.0 227.2 jit_solution(3771274523750501300)
XLA Ops:
  7.7 1.9 fusion.6
  10.3 1.1 dynamic-slice_bitcast_fusion.1
  12.2 5.9 %all-to-all-start = ((bf16[16,4,1792]{2,0,1:T(8,128)(2,1)}), bf16[16,4,1792]{2,0,1:T(8,128)(2,1)S(1)}, u32[]{:S(2)}, u32[]{:S(2)}) async-start(bf16[16,4,1792]{2,0,1:T(8,128)(2,1)} %pad_maximum_fusion.2), calls=%async_computation | async-start | bytes 458752 | tf_op jit(solution)/shard_map/all_to_all | solution.py:545
  18.2 1.7 copy.29
  20.0 1.2 copy.35.refs_2_
  21.8 1.7 constant_dynamic-slice_fusion.2
  23.4 3.5 %all-to-all-done = bf16[16,4,1792]{2,0,1:T(8,128)(2,1)S(1)} async-done(((bf16[16,4,1792]{2,0,1:T(8,128)(2,1)}), bf16[16,4,1792]{2,0,1:T(8,128)(2,1)S(1)}, u32[]{:S(2)}, u32[]{:S(2)}) %all-to-all-start) | async-done | bytes 229408 | tf_op jit(solution)/shard_map/all_to_all | solution.py:545
  28.9 10.6 %project.1 = (bf16[2048,128]{1,0:T(8,128)(2,1)}, bf16[8,256,128]{2,1,0:T(8,128)(2,1)}, bf16[8,256,128]{2,1,0:T(8,128)(2,1)}) custom-call(s32[4]{0:T(128)} %counts.7, s32[64]{0:T(128)} %table.7, s32[4]{0:T(128)} %get-tuple-element.81.owners, s32[2]{0:T(128)} %pad_add_fusion.1.bases.q_bases.kv_bases, bf16[1024,1024]{1,0:T(8,128)(2,1)} %x_ref.1, ...), custom_call_target="tpu_custom_call" | custom-call | flops 1610612736 | bytes 5767168 | tf_op jit(solution)/shard_map/project/pallas_call | solution.py:109
  39.5 1.6 collective-permute-start.3
  41.1 1.5 collective-permute-start.1
  43.7 1.7 constant_dynamic-slice_fusion.1
  45.4 1.0 constant_dynamic-slice_fusion
  47.1 21.6 %attend.3 = (f32[2048,128]{1,0:T(8,128)}, f32[2048,128]{1,0:T(8,128)}) custom-call(s32[4]{0:T(128)} %counts.7, s32[64]{0:T(128)} %table.7, s32[2]{0:T(128)} %pad_add_fusion.1.bases.q_bases.kv_bases, s32[2]{0:T(128)} %pad_add_fusion.1.bases.q_bases.kv_bases, bf16[2048,128]{1,0:T(8,128)(2,1)} %get-tuple-element.41.q_hbm, ...), custom_call_target="tpu_custom_call" | custom-call | flops 262144 | bytes 1048576 | tf_op jit(solution)/shard_map/attend/pallas_call | solution.py:313
  69.8 1.3 collective-permute-start.5
  71.1 1.9 collective-permute-start.6
  73.1 36.0 %attend.4 = (f32[2048,128]{1,0:T(8,128)}, f32[2048,128]{1,0:T(8,128)}) custom-call(s32[4]{0:T(128)} %counts.7, s32[64]{0:T(128)} %table.7, s32[2]{0:T(128)} %pad_add_fusion.1.bases.q_bases.kv_bases, s32[4]{0:T(128)} %get-tuple-element.87.kv_bases, bf16[2048,128]{1,0:T(8,128)(2,1)} %get-tuple-element.41.q_hbm, bf16[8,256,128]{2,1,0:T(8,128)(2,1)} %copy-done.2, ...), custom_call_target="tpu_custom_call" | custom-call | flops 262144 | bytes 1048576 | tf_op jit(solution)/shard_map/attend/pallas_call | solution.py:313
  109.7 1.1 slice.26
  110.8 1.1 slice.27
  112.7 21.5 %attend.5 = bf16[2048,128]{1,0:T(8,128)(2,1)} custom-call(s32[4]{0:T(128)} %counts.7, s32[64]{0:T(128)} %table.7, s32[2]{0:T(128)} %pad_add_fusion.1.bases.q_bases.kv_bases, s32[2]{0:T(128)} %pad_add_fusion.2.kv_bases, bf16[2048,128]{1,0:T(8,128)(2,1)} %get-tuple-element.41.q_hbm, bf16[8,256,128]{2,1,0:T(8,128)(2,1)} %collective-permute-done.5.refs_0_, ...), custom_call_target="tpu_custom_call" | custom-call | flops 262144 | bytes 1048576 | tf_op jit(solution)/shard_map/attend/pallas_call | solution.py:313
  134.3 1.2 fusion.7
  135.9 1.2 collective-permute-done.14
  138.9 0.9 collective-permute-start.16
  139.8 2.6 %collective-permute-start.15 = (bf16[4,128,1024]{2,1,0:T(8,128)(2,1)}, bf16[4,128,1024]{2,1,0:T(8,128)(2,1)S(1)}, u32[]{:S(2)}, u32[]{:S(2)}) collective-permute-start(bf16[4,128,1024]{2,1,0:T(8,128)(2,1)} %bitcast.21.refs_10_), channel_id=1, source_target_pairs={{0,8},{4,12},{8,0},{12,4},{16,24},{20,28},{24,16},{28,20},{1,9},{5... | collective-permute-start | bytes 3145736 | tf_op jit(solution)/shard_map/ppermute | solution.py:565
  142.4 2.1 collective-permute-done.18.refs_19_
  144.5 19.8 %collective-permute-done.16.refs_12_ = bf16[4,128,1024]{2,1,0:T(8,128)(2,1)S(1)} collective-permute-done((bf16[4,128,1024]{2,1,0:T(8,128)(2,1)}, bf16[4,128,1024]{2,1,0:T(8,128)(2,1)S(1)}, u32[]{:S(2)}, u32[]{:S(2)}) %collective-permute-start.16) | collective-permute-done | bytes 1048608 | tf_op jit(solution)/shard_map/ppermute | solution.py:565
  164.4 1.7 collective-permute-done.15.refs_11_
  166.2 1.8 collective-permute-start.21
  168.2 1.7 collective-permute-start.22
  170.0 10.7 %collective-permute-done.21.refs_13_ = bf16[4,64,1024]{2,1,0:T(8,128)(2,1)S(1)} collective-permute-done((bf16[4,64,1024]{2,1,0:T(8,128)(2,1)S(1)}, bf16[4,64,1024]{2,1,0:T(8,128)(2,1)S(1)}, u32[]{:S(2)}, u32[]{:S(2)}) %collective-permute-start.21) | collective-permute-done | bytes 524320 | tf_op jit(solution)/shard_map/ppermute | solution.py:565
  180.6 1.7 collective-permute-done.22.refs_14_
  183.7 0.9 copy-done.9
  185.7 35.0 %finish.1 = (bf16[256,1024]{1,0:T(8,128)(2,1)}, bf16[1024,768]{1,0:T(8,128)(2,1)}) custom-call(s32[3]{0:T(128)} %pad_add_fusion.place, bf16[1024,1024]{1,0:T(8,128)(2,1)} %x_ref.1, bf16[4,1024,256]{2,1,0:T(8,128)(2,1)} %bitcast.43, bf16[4,144,1024]{2,1,0:T(8,128)(2,1)} %bitcast.44, bf16[4,144,1024]{2,1,0:T(8,128)(2,1)} %collective-permute-done.20.refs_1_, ...), custom_call_target="tpu_custom_call" | custom-call | flops 17179869184 | bytes 16777216 | tf_op jit(solution)/shard_map/finish/pallas_call | solution.py:451
  (110 shorter events, 13.4 us)
Async XLA Ops:
  7.2 21.7 %collective-permute-start = (bf16[1024,1024]{1,0:T(8,128)(2,1)}, bf16[1024,1024]{1,0:T(8,128)(2,1)}, u32[]{:S(2)}, u32[]{:S(2)}) collective-permute-start(bf16[1024,1024]{1,0:T(8,128)(2,1)} %x_ref.1), channel_id=1, source_target_pairs={{0,4},{4,0},{8,12},{12,8},{16,20},{20,16},{24,28},{28,24},{1,5},{5... | collective-permute-start | bytes 6291464 | tf_op jit(solution)/shard_map/ppermute | solution.py:565
  12.2 14.7 %all-to-all-start = ((bf16[16,4,1792]{2,0,1:T(8,128)(2,1)}), bf16[16,4,1792]{2,0,1:T(8,128)(2,1)S(1)}, u32[]{:S(2)}, u32[]{:S(2)}) async-start(bf16[16,4,1792]{2,0,1:T(8,128)(2,1)} %pad_maximum_fusion.2), calls=%async_computation | async-start | bytes 458752 | tf_op jit(solution)/shard_map/all_to_all | solution.py:545
  18.2 50.6 %all-gather.9.cloned.1.call-start = ((), (), s32[]{:S(2)}) async-start(), calls=%async_computation.1 | async-start | bytes 1310720 | tf_op jit(solution)/shard_map/all_gather | solution.py:583
  39.4 94.7 %all-gather.11.cloned.1.call-start = ((), (), s32[]{:S(2)}) async-start(), calls=%async_computation.2 | async-start | bytes 1310720 | tf_op jit(solution)/shard_map/all_gather | solution.py:599
  39.5 29.1 %collective-permute-start.3 = (bf16[8,256,128]{2,1,0:T(8,128)(2,1)}, bf16[8,256,128]{2,1,0:T(8,128)(2,1)S(1)}, u32[]{:S(2)}, u32[]{:S(2)}) collective-permute-start(bf16[8,256,128]{2,1,0:T(8,128)(2,1)} %get-tuple-element.44.refs_0_), channel_id=1, source_target_pairs={{0,16},{4,20},{8,24},{12,28},{16,0},{20,4},{24,8},{28,12},{1,17},{... | collective-permute-start | bytes 1572872 | tf_op jit(solution)/shard_map/ppermute | solution.py:565
  41.1 27.6 %collective-permute-start.1 = (bf16[8,256,128]{2,1,0:T(8,128)(2,1)}, bf16[8,256,128]{2,1,0:T(8,128)(2,1)S(1)}, u32[]{:S(2)}, u32[]{:S(2)}) collective-permute-start(bf16[8,256,128]{2,1,0:T(8,128)(2,1)} %get-tuple-element.44.refs_0_), channel_id=1, source_target_pairs={{0,8},{4,12},{8,0},{12,4},{16,24},{20,28},{24,16},{28,20},{1,9},{5... | collective-permute-start | bytes 1572872 | tf_op jit(solution)/shard_map/ppermute | solution.py:565
  42.6 26.1 %collective-permute-start.4 = (bf16[8,256,128]{2,1,0:T(8,128)(2,1)}, bf16[8,256,128]{2,1,0:T(8,128)(2,1)}, u32[]{:S(2)}, u32[]{:S(2)}) collective-permute-start(bf16[8,256,128]{2,1,0:T(8,128)(2,1)} %get-tuple-element.45.refs_1_), channel_id=1, source_target_pairs={{0,16},{4,20},{8,24},{12,28},{16,0},{20,4},{24,8},{28,12},{1,17},{... | collective-permute-start | bytes 1572872 | tf_op jit(solution)/shard_map/ppermute | solution.py:565
  43.1 25.6 %collective-permute-start.2 = (bf16[8,256,128]{2,1,0:T(8,128)(2,1)}, bf16[8,256,128]{2,1,0:T(8,128)(2,1)}, u32[]{:S(2)}, u32[]{:S(2)}) collective-permute-start(bf16[8,256,128]{2,1,0:T(8,128)(2,1)} %get-tuple-element.45.refs_1_), channel_id=1, source_target_pairs={{0,8},{4,12},{8,0},{12,4},{16,24},{20,28},{24,16},{28,20},{1,9},{5... | collective-permute-start | bytes 1572872 | tf_op jit(solution)/shard_map/ppermute | solution.py:565
  68.7 65.5 %all-gather.13.cloned.1.call-start = ((), (), s32[]{:S(2)}) async-start(), calls=%async_computation.3 | async-start | bytes 1474560 | tf_op jit(solution)/shard_map/all_gather | solution.py:600
  68.8 40.3 %collective-permute-start.8 = (bf16[4,1024,128]{2,1,0:T(8,128)(2,1)}, bf16[4,1024,128]{2,1,0:T(8,128)(2,1)}, u32[]{:S(2)}, u32[]{:S(2)}) collective-permute-start(bf16[4,1024,128]{2,1,0:T(8,128)(2,1)} %bitcast.47), channel_id=1, source_target_pairs={{0,16},{4,20},{8,24},{12,28},{16,0},{20,4},{24,8},{28,12},{1,17},{... | collective-permute-start | bytes 3145736 | tf_op jit(solution)/shard_map/ppermute | solution.py:565
  68.9 40.2 %collective-permute-start.7 = (bf16[4,1024,128]{2,1,0:T(8,128)(2,1)}, bf16[4,1024,128]{2,1,0:T(8,128)(2,1)}, u32[]{:S(2)}, u32[]{:S(2)}) collective-permute-start(bf16[4,1024,128]{2,1,0:T(8,128)(2,1)} %bitcast.48), channel_id=1, source_target_pairs={{0,8},{4,12},{8,0},{12,4},{16,24},{20,28},{24,16},{28,20},{1,9},{5... | collective-permute-start | bytes 3145736 | tf_op jit(solution)/shard_map/ppermute | solution.py:565
  69.8 116.0 %all-gather.15.cloned.1.call-start = ((), (), s32[]{:S(2)}) async-start(), calls=%async_computation.4 | async-start | bytes 2621440 | tf_op jit(solution)/shard_map/all_gather | solution.py:624
  69.8 39.3 %collective-permute-start.5 = (bf16[8,256,128]{2,1,0:T(8,128)(2,1)S(1)}, bf16[8,256,128]{2,1,0:T(8,128)(2,1)}, u32[]{:S(2)}, u32[]{:S(2)}) collective-permute-start(bf16[8,256,128]{2,1,0:T(8,128)(2,1)S(1)} %collective-permute-done.3.refs_2_), channel_id=1, source_target_pairs={{0,8},{4,12},{8,0},{12,4},{16,24},{20,28},{24,16},{28,20},{1,9},{5... | collective-permute-start | bytes 1572872 | tf_op jit(solution)/shard_map/ppermute | solution.py:565
  71.1 38.0 %collective-permute-start.6 = (bf16[8,256,128]{2,1,0:T(8,128)(2,1)}, bf16[8,256,128]{2,1,0:T(8,128)(2,1)}, u32[]{:S(2)}, u32[]{:S(2)}) collective-permute-start(bf16[8,256,128]{2,1,0:T(8,128)(2,1)} %collective-permute-done.2.refs_1_), channel_id=1, source_target_pairs={{0,16},{4,20},{8,24},{12,28},{16,0},{20,4},{24,8},{28,12},{1,17},{... | collective-permute-start | bytes 1572872 | tf_op jit(solution)/shard_map/ppermute | solution.py:565
  73.0 61.1 %collective-permute-start.11 = (bf16[4,1024,128]{2,1,0:T(8,128)(2,1)}, bf16[4,1024,128]{2,1,0:T(8,128)(2,1)}, u32[]{:S(2)}, u32[]{:S(2)}) collective-permute-start(bf16[4,1024,128]{2,1,0:T(8,128)(2,1)} %bitcast.49), channel_id=1, source_target_pairs={{0,4},{4,0},{8,12},{12,8},{16,20},{20,16},{24,28},{28,24},{1,5},{5... | collective-permute-start | bytes 3145736 | tf_op jit(solution)/shard_map/ppermute | solution.py:565
  109.1 25.1 %collective-permute-start.13 = (bf16[4,1024,128]{2,1,0:T(8,128)(2,1)}, bf16[4,1024,128]{2,1,0:T(8,128)(2,1)}, u32[]{:S(2)}, u32[]{:S(2)}) collective-permute-start(bf16[4,1024,128]{2,1,0:T(8,128)(2,1)} %collective-permute-done.8.refs_7_), channel_id=1, source_target_pairs={{0,4},{4,0},{8,12},{12,8},{16,20},{20,16},{24,28},{28,24},{1,5},{5... | collective-permute-start | bytes 3145736 | tf_op jit(solution)/shard_map/ppermute | solution.py:565
  109.7 24.6 %collective-permute-start.12 = (bf16[4,1024,128]{2,1,0:T(8,128)(2,1)}, bf16[4,1024,128]{2,1,0:T(8,128)(2,1)}, u32[]{:S(2)}, u32[]{:S(2)}) collective-permute-start(bf16[4,1024,128]{2,1,0:T(8,128)(2,1)} %collective-permute-done.7.refs_6_), channel_id=1, source_target_pairs={{0,4},{4,0},{8,12},{12,8},{16,20},{20,16},{24,28},{28,24},{1,5},{5... | collective-permute-start | bytes 3145736 | tf_op jit(solution)/shard_map/ppermute | solution.py:565
  111.9 22.3 %collective-permute-start.10 = (bf16[4,512,128]{2,1,0:T(8,128)(2,1)S(1)}, bf16[4,512,128]{2,1,0:T(8,128)(2,1)}, u32[]{:S(2)}, u32[]{:S(2)}) collective-permute-start(bf16[4,512,128]{2,1,0:T(8,128)(2,1)S(1)} %slice.27), channel_id=1, source_target_pairs={{0,16},{4,20},{8,24},{12,28},{16,0},{20,4},{24,8},{28,12},{1,17},{... | collective-permute-start | bytes 1572872 | tf_op jit(solution)/shard_map/ppermute | solution.py:565
  112.0 22.2 %collective-permute-start.9 = (bf16[4,512,128]{2,1,0:T(8,128)(2,1)S(1)}, bf16[4,512,128]{2,1,0:T(8,128)(2,1)}, u32[]{:S(2)}, u32[]{:S(2)}) collective-permute-start(bf16[4,512,128]{2,1,0:T(8,128)(2,1)S(1)} %slice.26), channel_id=1, source_target_pairs={{0,8},{4,12},{8,0},{12,4},{16,24},{20,28},{24,16},{28,20},{1,9},{5... | collective-permute-start | bytes 1572872 | tf_op jit(solution)/shard_map/ppermute | solution.py:565
  135.4 1.7 collective-permute-start.14
  138.0 28.1 %collective-permute-start.20 = (bf16[4,144,1024]{2,1,0:T(8,128)(2,1)S(1)}, bf16[4,144,1024]{2,1,0:T(8,128)(2,1)}, u32[]{:S(2)}, u32[]{:S(2)}) collective-permute-start(bf16[4,144,1024]{2,1,0:T(8,128)(2,1)S(1)} %bitcast.46), channel_id=1, source_target_pairs={{0,4},{4,0},{8,12},{12,8},{16,20},{20,16},{24,28},{28,24},{1,5},{5... | collective-permute-start | bytes 3538952 | tf_op jit(solution)/shard_map/ppermute | solution.py:565
  138.4 4.0 %collective-permute-start.17 = (bf16[4,512,128]{2,1,0:T(8,128)(2,1)}, bf16[4,512,128]{2,1,0:T(8,128)(2,1)S(1)}, u32[]{:S(2)}, u32[]{:S(2)}) collective-permute-start(bf16[4,512,128]{2,1,0:T(8,128)(2,1)} %collective-permute-done.9.refs_8_), channel_id=1, source_target_pairs={{0,4},{4,0},{8,12},{12,8},{16,20},{20,16},{24,28},{28,24},{1,5},{5... | collective-permute-start | bytes 1572872 | tf_op jit(solution)/shard_map/ppermute | solution.py:565
  138.6 6.0 %collective-permute-start.19 = (bf16[4,128,1024]{2,1,0:T(8,128)(2,1)}, bf16[4,128,1024]{2,1,0:T(8,128)(2,1)S(1)}, u32[]{:S(2)}, u32[]{:S(2)}) collective-permute-start(bf16[4,128,1024]{2,1,0:T(8,128)(2,1)} %bitcast.21.refs_10_), channel_id=1, source_target_pairs={{0,4},{4,0},{8,12},{12,8},{16,20},{20,16},{24,28},{28,24},{1,5},{5... | collective-permute-start | bytes 3145736 | tf_op jit(solution)/shard_map/ppermute | solution.py:565
  138.9 25.4 %collective-permute-start.16 = (bf16[4,128,1024]{2,1,0:T(8,128)(2,1)}, bf16[4,128,1024]{2,1,0:T(8,128)(2,1)S(1)}, u32[]{:S(2)}, u32[]{:S(2)}) collective-permute-start(bf16[4,128,1024]{2,1,0:T(8,128)(2,1)} %bitcast.21.refs_10_), channel_id=1, source_target_pairs={{0,16},{4,20},{8,24},{12,28},{16,0},{20,4},{24,8},{28,12},{1,17},{... | collective-permute-start | bytes 3145736 | tf_op jit(solution)/shard_map/ppermute | solution.py:565
  139.8 26.2 %collective-permute-start.15 = (bf16[4,128,1024]{2,1,0:T(8,128)(2,1)}, bf16[4,128,1024]{2,1,0:T(8,128)(2,1)S(1)}, u32[]{:S(2)}, u32[]{:S(2)}) collective-permute-start(bf16[4,128,1024]{2,1,0:T(8,128)(2,1)} %bitcast.21.refs_10_), channel_id=1, source_target_pairs={{0,8},{4,12},{8,0},{12,4},{16,24},{20,28},{24,16},{28,20},{1,9},{5... | collective-permute-start | bytes 3145736 | tf_op jit(solution)/shard_map/ppermute | solution.py:565
  142.4 2.1 collective-permute-start.18
  166.1 17.5 %collective-permute-start.23 = (bf16[4,128,1024]{2,1,0:T(8,128)(2,1)S(1)}, bf16[4,128,1024]{2,1,0:T(8,128)(2,1)S(1)}, u32[]{:S(2)}, u32[]{:S(2)}) collective-permute-start(bf16[4,128,1024]{2,1,0:T(8,128)(2,1)S(1)} %collective-permute-done.15.refs_11_), channel_id=1, source_target_pairs={{0,4},{4,0},{8,12},{12,8},{16,20},{20,16},{24,28},{28,24},{1,5},{5... | collective-permute-start | bytes 3145736 | tf_op jit(solution)/shard_map/ppermute | solution.py:565
  166.2 14.4 %collective-permute-start.21 = (bf16[4,64,1024]{2,1,0:T(8,128)(2,1)S(1)}, bf16[4,64,1024]{2,1,0:T(8,128)(2,1)S(1)}, u32[]{:S(2)}, u32[]{:S(2)}) collective-permute-start(bf16[4,64,1024]{2,1,0:T(8,128)(2,1)S(1)} %slice.30), channel_id=1, source_target_pairs={{0,8},{4,12},{8,0},{12,4},{16,24},{20,28},{24,16},{28,20},{1,9},{5... | collective-permute-start | bytes 1572872 | tf_op jit(solution)/shard_map/ppermute | solution.py:565
  168.0 15.6 %collective-permute-start.24 = (bf16[4,128,1024]{2,1,0:T(8,128)(2,1)S(1)}, bf16[4,128,1024]{2,1,0:T(8,128)(2,1)S(1)}, u32[]{:S(2)}, u32[]{:S(2)}) collective-permute-start(bf16[4,128,1024]{2,1,0:T(8,128)(2,1)S(1)} %collective-permute-done.16.refs_12_), channel_id=1, source_target_pairs={{0,4},{4,0},{8,12},{12,8},{16,20},{20,16},{24,28},{28,24},{1,5},{5... | collective-permute-start | bytes 3145736 | tf_op jit(solution)/shard_map/ppermute | solution.py:565
  168.2 14.1 %collective-permute-start.22 = (bf16[4,64,1024]{2,1,0:T(8,128)(2,1)S(1)}, bf16[4,64,1024]{2,1,0:T(8,128)(2,1)S(1)}, u32[]{:S(2)}, u32[]{:S(2)}) collective-permute-start(bf16[4,64,1024]{2,1,0:T(8,128)(2,1)S(1)} %slice.31), channel_id=1, source_target_pairs={{0,16},{4,20},{8,24},{12,28},{16,0},{20,4},{24,8},{28,12},{1,17},{... | collective-permute-start | bytes 1572872 | tf_op jit(solution)/shard_map/ppermute | solution.py:565
  180.6 3.0 %collective-permute-start.25 = (bf16[4,64,1024]{2,1,0:T(8,128)(2,1)S(1)}, bf16[4,64,1024]{2,1,0:T(8,128)(2,1)S(1)}, u32[]{:S(2)}, u32[]{:S(2)}) collective-permute-start(bf16[4,64,1024]{2,1,0:T(8,128)(2,1)S(1)} %collective-permute-done.21.refs_13_), channel_id=1, source_target_pairs={{0,4},{4,0},{8,12},{12,8},{16,20},{20,16},{24,28},{28,24},{1,5},{5... | collective-permute-start | bytes 1572872 | tf_op jit(solution)/shard_map/ppermute | solution.py:565
  182.4 3.3 %collective-permute-start.26 = (bf16[4,64,1024]{2,1,0:T(8,128)(2,1)S(1)}, bf16[4,64,1024]{2,1,0:T(8,128)(2,1)}, u32[]{:S(2)}, u32[]{:S(2)}) collective-permute-start(bf16[4,64,1024]{2,1,0:T(8,128)(2,1)S(1)} %collective-permute-done.22.refs_14_), channel_id=1, source_target_pairs={{0,4},{4,0},{8,12},{12,8},{16,20},{20,16},{24,28},{28,24},{1,5},{5... | collective-permute-start | bytes 1572872 | tf_op jit(solution)/shard_map/ppermute | solution.py:565
  (16 other events, 190.3 us)
Sparse Core Ops, SparseCore 0:
  39.6 27.0 all-gather.8
  68.9 26.7 all-gather.10
  97.2 29.9 all-gather.12
  138.1 45.8 all-gather.14

commit v8 on v7

--- a/solution.py
+++ b/solution.py
@@ -144,7 +144,7 @@
 
 def attend_kernel(
     counts, table, q_bases, kv_bases, q_hbm, *refs,
-    requests, slots, q_size, arrays, sizes, first, last, group,
+    requests, slots, q_size, q_from, state_from, arrays, sizes, first, last, group,
 ):
     refs = list(refs)
     kv_hbm = [refs.pop(0) for _ in arrays]
@@ -156,12 +156,13 @@
     kv, scores, listed, amount, asked, q_amount, sems, q_ref = refs[:8]
     if not first:
         acc_in, stat_in = refs[8:]
-    targets = [(q_hbm, q_ref)]
+    tok = q_ref.shape[0]
+    targets = [(q_hbm.at[pl.ds(q_from, tok)], q_ref)]
     offset = 0
     for i, size in enumerate(arrays):
         targets.append((kv_hbm[i], kv.at[pl.ds(offset, size)]))
         offset += size
-    targets += list(zip(state_hbm, refs[8:]))
+    targets += [(ref.at[pl.ds(state_from, tok)], own) for ref, own in zip(state_hbm, refs[8:])]
     copies = [
         pltpu.make_async_copy(source, target, sems.at[n])
         for n, (source, target) in enumerate(targets)
@@ -300,8 +301,9 @@
     lax.fori_loop(0, requests, visit_request, 0)
 
 
-def attend(counts, table, q_bases, kv_bases, q, pieces, state, last, q_size):
-    tok = q.shape[0]
+def attend(counts, table, q_bases, kv_bases, q, pieces, state, last, q_size, q_from=0):
+    tok = q_bases.shape[0] * q_size * PAGE
+    state_from = 0 if state is None or state[0].shape[0] == tok else q_from
     arrays = tuple(p.shape[0] for p in pieces)
     sizes = (sum(arrays) // kv_bases.shape[0],) * kv_bases.shape[0]
     first = state is None
@@ -313,7 +315,7 @@
     out = pl.pallas_call(
         functools.partial(
             attend_kernel,
-            requests=requests, slots=slots, q_size=q_size, arrays=arrays, sizes=sizes,
+            requests=requests, slots=slots, q_size=q_size, q_from=q_from, state_from=state_from, arrays=arrays, sizes=sizes,
             first=first, last=last, group=group,
         ),
         grid_spec=pltpu.PrefetchScalarGridSpec(
@@ -343,8 +345,9 @@
     return out[0] if last else out
 
 
-def finish_kernel(place, x_ref, ctx_ref, *refs, parts, counts, last_step):
+def finish_kernel(place, x_ref, *refs, parts, counts, last_step):
     refs = list(refs)
+    ctx_refs, refs = refs[:parts], refs[parts:]
     out_w_refs, refs = refs[:parts], refs[parts:]
     gain1_ref, bias1_ref, bias_ref = refs[:3]
     refs = refs[3:]
@@ -369,10 +372,9 @@
         for t in range(tok // block):
             rows = slice(t * block, (t + 1) * block)
             mixed = x_ref[rows, :].astype(jnp.float32)
-            for j in range(ctx_ref.shape[0]):
-                mixed = mixed + jnp.dot(
-                    ctx_ref[j, rows, :], joined[j], preferred_element_type=jnp.float32
-                )
+            for j in range(joined.shape[0]):
+                ctx = jnp.concatenate([ref[j, rows, :] for ref in ctx_refs], axis=1)
+                mixed = mixed + jnp.dot(ctx, joined[j], preferred_element_type=jnp.float32)
             normed = normalize(mixed, gain1_ref[...], bias1_ref[...]).astype(jnp.bfloat16)
             normed_ref[rows, :] = normed
             acc[rows, :] = normed.astype(jnp.float32) + b2_ref[...]
@@ -425,11 +427,12 @@
 
 
 def finish(
-    place, x, ctx, outs, gain1, bias1, bias, sets, b2, gain, bias2, next_w, next_b, share
+    place, x, contexts, outs, gain1, bias1, bias, sets, b2, gain, bias2, next_w, next_b, share
 ):
     tok, width = x.shape
     halves = len(sets)
-    groups, _, ctx_cols = ctx.shape
+    groups = bias.shape[0]
+    ctx_cols = sum(ctx.shape[2] for ctx in contexts)
     cols = bias.shape[2] // halves
     steps = halves * groups
 
@@ -444,7 +447,7 @@
         for array in (*w1s, *w2s):
             specs.append(pl.BlockSpec((1,) + array.shape[1:], at))
             arrays.append(array)
-    head = [x, ctx, *outs, gain1[None], bias1[None]]
+    head = [x, *contexts, *outs, gain1[None], bias1[None]]
     tail = [b2[None], gain[None], bias2[None], next_w, next_b[None]]
     next_cols = next_w.shape[1]
     fixed = lambda i, *_: (0, 0)
@@ -581,8 +584,8 @@
         first = lax.dynamic_slice_in_dim(first_feed_weight, turn * unit, unit, 1)
         first, kvs = lax.optimization_barrier((first, kvs))
         first = lax.all_gather(first, "mp", axis=0)
-        step = functools.partial(attend, *args, bases)
-        state = step(bases, q, kvs, None, False, pages)
+        step = functools.partial(attend, *args)
+        state = step(bases, bases, q, kvs, None, False, pages)
         second = lax.dynamic_slice_in_dim(second_feed_weight, turn * unit, unit, 0)
         out_half = jnp.concatenate(
             [
@@ -602,37 +605,47 @@
         kv_d1 = move(kv_x[1], along)
         first_x = move(first, across)
         first_y = move(first, along)
-        near = jnp.stack([at(2), at(3), at(4), at(5)])
-        state = step(near, q, [*kv_x, *kv_y], state, False, pages)
-        kv_d0, kv_d1, first_x, first_y, state = lax.optimization_barrier(
-            (kv_d0, kv_d1, first_x, first_y, state)
+        near = [at(2), at(3), at(4), at(5)]
+        far = [at(6), at(7)]
+        swapped, own = bases[1:], bases[:1]
+        late = step(
+            swapped, jnp.stack(near), q, [*kv_x, *kv_y], state, False, pages, q_from=tok_rows
+        )
+        kv_d0, kv_d1, late = lax.optimization_barrier((kv_d0, kv_d1, late))
+        theirs = step(
+            swapped, jnp.stack(far), q, [kv_d0, kv_d1], late, True, pages, q_from=tok_rows
+        )
+        theirs, first_x, first_y, second = lax.optimization_barrier(
+            (theirs, first_x, first_y, second)
         )
         cut = width // 2
         first_d0 = move(first_y[:, :cut], across)
         first_d1 = move(first_x[:, cut:], along)
-        far = jnp.stack([at(6), at(7)])
-        near_others = [move(piece, swap) for piece in (first, first_x, first_y)]
-        context = step(far, q, [kv_d0, kv_d1], state, True, pages)
-        context, first_d0, first_d1, near_others, second, out_mine = lax.optimization_barrier(
-            (context, first_d0, first_d1, near_others, second, out_mine)
-        )
         second_x = move(second, across)
         second_y = move(second, along)
-        context = jnp.concatenate(
-            [context[:tok_rows], move(context[tok_rows:], swap)], axis=1
-        )
-        contexts = lax.all_gather(context, "mp", axis=0)
+        near_others = [move(piece, swap) for piece in (first, first_x, first_y, second)]
+        theirs = lax.all_gather(move(theirs, swap), "mp", axis=0)
+        mine = step(
+            own, jnp.stack(near + far), q, [*kv_x, *kv_y, kv_d0, kv_d1], state, True, pages
+        )
+        mine, first_d0, first_d1, near_others, second_x, second_y, out_mine = (
+            lax.optimization_barrier(
+                (mine, first_d0, first_d1, near_others, second_x, second_y, out_mine)
+            )
+        )
+        contexts = [lax.all_gather(mine, "mp", axis=0), theirs]
         bias_rows = out_mine
-        firsts = [first, first_x, first_y, first_d0, first_d1]
-        moved = [move(piece, swap) for piece in (first_d0, first_d1, second, out_mine)]
-        second_x, second_y, moved = lax.optimization_barrier((second_x, second_y, moved))
-        first_others = [*near_others, *moved[:2]]
-        out_other = moved[3]
         half = unit // 2
         second_d0 = move(second_y[:, :half], across)
         second_d1 = move(second_x[:, half:], along)
+        firsts = [first, first_x, first_y, first_d0, first_d1]
+        moved = [move(piece, swap) for piece in (first_d0, first_d1, second_x, second_y, out_mine)]
+        first_others = [*near_others[:3], *moved[:2]]
+        out_other = moved[4]
         seconds = [second, second_x, second_y, second_d0, second_d1]
-        second_others = [moved[2]] + [move(piece, swap) for piece in seconds[1:]]
+        second_others = [
+            near_others[3], *moved[2:4], move(second_d0, swap), move(second_d1, swap)
+        ]
         sets = [(firsts, seconds), (first_others, second_others)]
         outs = [out_mine, out_other]
     else:
@@ -644,7 +657,7 @@
         bias_rows = lax.all_gather(bias_rows, "mp", axis=0)
         sets = [([lax.all_gather(first_feed_weight, "mp", axis=0)], [second])]
         outs = [lax.all_gather(attention_out_weight, "mp", axis=0)]
-        contexts = lax.all_gather(context, "mp", axis=0)
+        contexts = [lax.all_gather(context, "mp", axis=0)]
     layer_rows, next_proj = finish(
         place, tokens, contexts, outs, first_norm_gain, first_norm_bias, bias_rows, sets,
         second_feed_bias, second_norm_gain, second_norm_bias, following_qkv_weight,

time: 232 us -> 238 us (1.026); the launches traced: 227 us -> 237 us
  waiting for transfers between devices: 40.9 us -> 52.4 us
  Pallas kernels: 125 us -> 119 us
  starting transfers between devices: 24.3 us -> 28.3 us
    all_gather x1 -> x2, waiting for transfers between devices: 0.01 us -> 9.44 us  [the longest x1 9.44 us: local(): contexts = [lax.all_gather(mine, 'mp', axis=0), theirs]]
    pallas_call x3 -> x4, Pallas kernels: 79.1 us -> 73.6 us  [attend(): pl.pallas_call(functools.partial(attend_kernel, requests=requests, slots=...]
    ppermute x27, starting transfers between devices: 18.3 us -> 22.2 us  [local(): move = lambda value, pairs: lax.ppermute(value, 'dp', pairs)]
  transfers between devices with their start and end apart: 32 -> 33, of which waited for: 7 -> 10; matrix products, arithmetic and copies ran while one was open for 8% -> 9% of each run, Pallas kernels for 35% -> 31%
where the time goes in v8:
time: 238 us; the launch traced here: 237 us
  Pallas kernels  119 us (50%)
  waiting for transfers between devices  52.4 us (22%)
  starting transfers between devices  28.3 us (12%)
  local copies, waits for them, and re-layouts  16.9 us (7%)
  between operations  14.8 us (6%)
  other arithmetic  5.14 us (2%)
    pallas_call x4, Pallas kernels, attend(): pl.pallas_call(functools.partial(attend_kernel, requests=requests, slots=...  73.6 us
    ppermute x27, waiting for transfers between devices, local(): move = lambda value, pairs: lax.ppermute(value, 'dp', pairs)  36.7 us
    pallas_call x1, Pallas kernels, finish(): pl.pallas_call(functools.partial(finish_kernel, parts=len(outs), counts=t...  35 us
    ppermute x27, starting transfers between devices, local(): move = lambda value, pairs: lax.ppermute(value, 'dp', pairs)  22.2 us
    pallas_call x1, Pallas kernels, project(): pl.pallas_call(functools.partial(project_kernel, requests=counts.shape[0]...  10.6 us
    all_gather x1, waiting for transfers between devices, local(): contexts = [lax.all_gather(mine, 'mp', axis=0), theirs]  9.44 us
    all_to_all x1, starting transfers between devices, local(): got = lax.all_to_all(sent, 'mp', split_axis=1, concat_axis=0, tiled=True)  5.95 us
  transfers between devices with their start and end apart: 33, of which 10 were waited for; matrix products, arithmetic and copies ran while one was open for 9% of the time, Pallas kernels for 31%

profile of v8, /device:TPU:0, one launch (start us, length us, event | category | flops | bytes accessed | tf_op | source)
XLA Modules:
  0.0 236.7 jit_solution(16313263649785564686)
XLA Ops:
  7.7 1.9 fusion.6
  10.3 1.1 dynamic-slice_bitcast_fusion.1
  12.2 5.9 %all-to-all-start = ((bf16[16,4,1792]{2,0,1:T(8,128)(2,1)}), bf16[16,4,1792]{2,0,1:T(8,128)(2,1)S(1)}, u32[]{:S(2)}, u32[]{:S(2)}) async-start(bf16[16,4,1792]{2,0,1:T(8,128)(2,1)} %pad_maximum_fusion.1), calls=%async_computation | async-start | bytes 458752 | tf_op jit(solution)/shard_map/all_to_all | solution.py:548
  18.2 1.7 copy.29
  20.0 1.2 copy.35.refs_2_
  21.8 1.7 constant_dynamic-slice_fusion.2
  23.5 3.5 %all-to-all-done = bf16[16,4,1792]{2,0,1:T(8,128)(2,1)S(1)} async-done(((bf16[16,4,1792]{2,0,1:T(8,128)(2,1)}), bf16[16,4,1792]{2,0,1:T(8,128)(2,1)S(1)}, u32[]{:S(2)}, u32[]{:S(2)}) %all-to-all-start) | async-done | bytes 229408 | tf_op jit(solution)/shard_map/all_to_all | solution.py:548
  28.9 10.6 %project.1 = (bf16[2048,128]{1,0:T(8,128)(2,1)}, bf16[8,256,128]{2,1,0:T(8,128)(2,1)}, bf16[8,256,128]{2,1,0:T(8,128)(2,1)}) custom-call(s32[4]{0:T(128)} %counts.9, s32[64]{0:T(128)} %table.9, s32[4]{0:T(128)} %get-tuple-element.77.owners, s32[2]{0:T(128)} %pad_add_fusion.1.bases.q_bases.kv_bases, bf16[1024,1024]{1,0:T(8,128)(2,1)} %x_ref.1, ...), custom_call_target="tpu_custom_call" | custom-call | flops 1610612736 | bytes 5767168 | tf_op jit(solution)/shard_map/project/pallas_call | solution.py:109
  39.6 1.6 collective-permute-start.3
  41.2 1.5 collective-permute-start.1
  43.8 1.7 constant_dynamic-slice_fusion.1
  47.1 17.6 %attend.4 = (f32[2048,128]{1,0:T(8,128)}, f32[2048,128]{1,0:T(8,128)}) custom-call(s32[4]{0:T(128)} %counts.9, s32[64]{0:T(128)} %table.9, s32[2]{0:T(128)} %pad_add_fusion.1.bases.q_bases.kv_bases, s32[2]{0:T(128)} %pad_add_fusion.1.bases.q_bases.kv_bases, bf16[2048,128]{1,0:T(8,128)(2,1)} %get-tuple-element.39.q_hbm, ...), custom_call_target="tpu_custom_call" | custom-call | flops 262144 | bytes 1048576 | tf_op jit(solution)/shard_map/attend/pallas_call | solution.py:315
  64.8 1.9 all-gather.11.cloned.1.call-done
  67.5 2.3 collective-permute-start.8
  69.9 1.5 collective-permute-start.7
  72.6 17.7 %attend.5 = (f32[1024,128]{1,0:T(8,128)}, f32[1024,128]{1,0:T(8,128)}) custom-call(s32[4]{0:T(128)} %counts.9, s32[64]{0:T(128)} %table.9, s32[1]{0:T(128)} %bitcast.10.q_bases, s32[4]{0:T(128)} %get-tuple-element.81.kv_bases, bf16[2048,128]{1,0:T(8,128)(2,1)} %get-tuple-element.39.q_hbm, bf16[8,256,128]{2,1,0:T(8,128)(2,1)} %copy-done.2, ...), custom_call_target="tpu_custom_call" | custom-call | flops 131072 | bytes 524288 | tf_op jit(solution)/shard_map/attend/pallas_call | solution.py:315
  90.3 13.6 %collective-permute-done.6.refs_5_.refs_1_ = bf16[8,256,128]{2,1,0:T(8,128)(2,1)} collective-permute-done((bf16[8,256,128]{2,1,0:T(8,128)(2,1)}, bf16[8,256,128]{2,1,0:T(8,128)(2,1)}, u32[]{:S(2)}, u32[]{:S(2)}) %collective-permute-start.6) | collective-permute-done | bytes 524320 | tf_op jit(solution)/shard_map/ppermute | solution.py:568
  103.9 1.2 collective-permute-done.5.refs_4_.refs_0_
  105.1 12.0 %attend.7 = bf16[1024,128]{1,0:T(8,128)(2,1)} custom-call(s32[4]{0:T(128)} %counts.9, s32[64]{0:T(128)} %table.9, s32[1]{0:T(128)} %bitcast.10.q_bases, s32[2]{0:T(128)} %pad_add_fusion.3.kv_bases, bf16[2048,128]{1,0:T(8,128)(2,1)} %get-tuple-element.39.q_hbm, bf16[8,256,128]{2,1,0:T(8,128)(2,1)} %collective-permute-done.5.refs_4_.refs_0_, ...), custom_call_target="tpu_custom_call" | custom-call | flops 131072 | bytes 524288 | tf_op jit(solution)/shard_map/attend/pallas_call | solution.py:315
  118.0 1.1 slice.21
  120.8 3.3 %collective-permute-start.9 = (bf16[4,512,128]{2,1,0:T(8,128)(2,1)S(1)}, bf16[4,512,128]{2,1,0:T(8,128)(2,1)}, u32[]{:S(2)}, u32[]{:S(2)}) collective-permute-start(bf16[4,512,128]{2,1,0:T(8,128)(2,1)S(1)} %slice.20), channel_id=1, source_target_pairs={{0,8},{4,12},{8,0},{12,4},{16,24},{20,28},{24,16},{28,20},{1,9},{5... | collective-permute-start | bytes 1572872 | tf_op jit(solution)/shard_map/ppermute | solution.py:568
  125.5 2.0 collective-permute-start.16
  127.5 6.5 %collective-permute-done.10.refs_11_ = bf16[4,512,128]{2,1,0:T(8,128)(2,1)} collective-permute-done((bf16[4,512,128]{2,1,0:T(8,128)(2,1)S(1)}, bf16[4,512,128]{2,1,0:T(8,128)(2,1)}, u32[]{:S(2)}, u32[]{:S(2)}) %collective-permute-start.10) | collective-permute-done | bytes 524320 | tf_op jit(solution)/shard_map/ppermute | solution.py:568
  134.0 3.8 %collective-permute-start.15 = (bf16[4,128,1024]{2,1,0:T(8,128)(2,1)}, bf16[4,128,1024]{2,1,0:T(8,128)(2,1)}, u32[]{:S(2)}, u32[]{:S(2)}) collective-permute-start(bf16[4,128,1024]{2,1,0:T(8,128)(2,1)} %bitcast.52), channel_id=1, source_target_pairs={{0,8},{4,12},{8,0},{12,4},{16,24},{20,28},{24,16},{28,20},{1,9},{5... | collective-permute-start | bytes 3145736 | tf_op jit(solution)/shard_map/ppermute | solution.py:568
  138.4 26.4 %attend.6 = bf16[1024,128]{1,0:T(8,128)(2,1)} custom-call(s32[4]{0:T(128)} %counts.9, s32[64]{0:T(128)} %table.9, s32[1]{0:T(128)} %bitcast.3.q_bases, s32[6]{0:T(128)} %stack.77.kv_bases, bf16[2048,128]{1,0:T(8,128)(2,1)} %get-tuple-element.39.q_hbm, bf16[8,256,128]{2,1,0:T(8,128)(2,1)} %copy-done.2, bf16[8,256,128]{2,1,0:T(8,128)(2,1)} %collective-permute-done.2.refs_1_, ...), custom_call_target="tpu_custom_call" | custom-call | flops 131072 | bytes 524288 | tf_op jit(solution)/shard_map/attend/pallas_call | solution.py:315
  165.0 1.3 slice.23
  167.6 10.0 %collective-permute-done.19.refs_15_ = bf16[4,64,1024]{2,1,0:T(8,128)(2,1)} collective-permute-done((bf16[4,64,1024]{2,1,0:T(8,128)(2,1)S(1)}, bf16[4,64,1024]{2,1,0:T(8,128)(2,1)}, u32[]{:S(2)}, u32[]{:S(2)}) %collective-permute-start.19) | collective-permute-done | bytes 524320 | tf_op jit(solution)/shard_map/ppermute | solution.py:568
  177.6 2.6 %collective-permute-done.20.refs_16_ = bf16[4,64,1024]{2,1,0:T(8,128)(2,1)} collective-permute-done((bf16[4,64,1024]{2,1,0:T(8,128)(2,1)S(1)}, bf16[4,64,1024]{2,1,0:T(8,128)(2,1)}, u32[]{:S(2)}, u32[]{:S(2)}) %collective-permute-start.20) | collective-permute-done | bytes 524320 | tf_op jit(solution)/shard_map/ppermute | solution.py:568
  182.0 1.6 collective-permute-done.25.refs_25_
  183.6 1.1 collective-permute-done.26.refs_26_
  185.7 9.4 %all-gather.17.cloned.1.call-done = bf16[4096,128]{1,0:T(8,128)(2,1)} async-done(((bf16[1024,128]{1,0:T(8,128)(2,1)}), bf16[4096,128]{1,0:T(8,128)(2,1)}) %all-gather.17.cloned.1.call-update) | async-done | bytes 1048592 | tf_op jit(solution)/shard_map/all_gather | solution.py:636
  195.2 35.0 %finish.1 = (bf16[256,1024]{1,0:T(8,128)(2,1)}, bf16[1024,768]{1,0:T(8,128)(2,1)}) custom-call(s32[3]{0:T(128)} %pad_add_fusion.place, bf16[1024,1024]{1,0:T(8,128)(2,1)} %x_ref.1, bf16[4,1024,128]{2,1,0:T(8,128)(2,1)} %bitcast.56, bf16[4,1024,128]{2,1,0:T(8,128)(2,1)} %bitcast.55, bf16[4,144,1024]{2,1,0:T(8,128)(2,1)} %bitcast.45, ...), custom_call_target="tpu_custom_call" | custom-call | flops 17179869184 | bytes 16777216 | tf_op jit(solution)/shard_map/finish/pallas_call | solution.py:454
  (97 shorter events, 17.7 us)
Async XLA Ops:
  7.2 21.8 %collective-permute-start = (bf16[1024,1024]{1,0:T(8,128)(2,1)}, bf16[1024,1024]{1,0:T(8,128)(2,1)}, u32[]{:S(2)}, u32[]{:S(2)}) collective-permute-start(bf16[1024,1024]{1,0:T(8,128)(2,1)} %x_ref.1), channel_id=1, source_target_pairs={{0,4},{4,0},{8,12},{12,8},{16,20},{20,16},{24,28},{28,24},{1,5},{5... | collective-permute-start | bytes 6291464 | tf_op jit(solution)/shard_map/ppermute | solution.py:568
  12.2 14.7 %all-to-all-start = ((bf16[16,4,1792]{2,0,1:T(8,128)(2,1)}), bf16[16,4,1792]{2,0,1:T(8,128)(2,1)S(1)}, u32[]{:S(2)}, u32[]{:S(2)}) async-start(bf16[16,4,1792]{2,0,1:T(8,128)(2,1)} %pad_maximum_fusion.1), calls=%async_computation | async-start | bytes 458752 | tf_op jit(solution)/shard_map/all_to_all | solution.py:548
  18.2 48.5 %all-gather.11.cloned.1.call-start = ((), (), s32[]{:S(2)}) async-start(), calls=%async_computation.1 | async-start | bytes 1310720 | tf_op jit(solution)/shard_map/all_gather | solution.py:586
  39.5 77.6 %all-gather.13.cloned.1.call-start = ((), (), s32[]{:S(2)}) async-start(), calls=%async_computation.2 | async-start | bytes 1310720 | tf_op jit(solution)/shard_map/all_gather | solution.py:602
  39.6 25.1 %collective-permute-start.3 = (bf16[8,256,128]{2,1,0:T(8,128)(2,1)}, bf16[8,256,128]{2,1,0:T(8,128)(2,1)S(1)}, u32[]{:S(2)}, u32[]{:S(2)}) collective-permute-start(bf16[8,256,128]{2,1,0:T(8,128)(2,1)} %get-tuple-element.42.refs_0_), channel_id=1, source_target_pairs={{0,16},{4,20},{8,24},{12,28},{16,0},{20,4},{24,8},{28,12},{1,17},{... | collective-permute-start | bytes 1572872 | tf_op jit(solution)/shard_map/ppermute | solution.py:568
  41.2 23.6 %collective-permute-start.1 = (bf16[8,256,128]{2,1,0:T(8,128)(2,1)}, bf16[8,256,128]{2,1,0:T(8,128)(2,1)S(1)}, u32[]{:S(2)}, u32[]{:S(2)}) collective-permute-start(bf16[8,256,128]{2,1,0:T(8,128)(2,1)} %get-tuple-element.42.refs_0_), channel_id=1, source_target_pairs={{0,8},{4,12},{8,0},{12,4},{16,24},{20,28},{24,16},{28,20},{1,9},{5... | collective-permute-start | bytes 1572872 | tf_op jit(solution)/shard_map/ppermute | solution.py:568
  42.7 22.1 %collective-permute-start.4 = (bf16[8,256,128]{2,1,0:T(8,128)(2,1)}, bf16[8,256,128]{2,1,0:T(8,128)(2,1)}, u32[]{:S(2)}, u32[]{:S(2)}) collective-permute-start(bf16[8,256,128]{2,1,0:T(8,128)(2,1)} %get-tuple-element.43.refs_1_), channel_id=1, source_target_pairs={{0,16},{4,20},{8,24},{12,28},{16,0},{20,4},{24,8},{28,12},{1,17},{... | collective-permute-start | bytes 1572872 | tf_op jit(solution)/shard_map/ppermute | solution.py:568
  43.2 21.6 %collective-permute-start.2 = (bf16[8,256,128]{2,1,0:T(8,128)(2,1)}, bf16[8,256,128]{2,1,0:T(8,128)(2,1)}, u32[]{:S(2)}, u32[]{:S(2)}) collective-permute-start(bf16[8,256,128]{2,1,0:T(8,128)(2,1)} %get-tuple-element.43.refs_1_), channel_id=1, source_target_pairs={{0,8},{4,12},{8,0},{12,4},{16,24},{20,28},{24,16},{28,20},{1,9},{5... | collective-permute-start | bytes 1572872 | tf_op jit(solution)/shard_map/ppermute | solution.py:568
  66.7 98.0 %all-gather.15.cloned.1.call-start = ((), (), s32[]{:S(2)}) async-start(), calls=%async_computation.3 | async-start | bytes 1474560 | tf_op jit(solution)/shard_map/all_gather | solution.py:603
  67.5 114.5 %all-gather.19.cloned.1.call-start = ((), (), s32[]{:S(2)}) async-start(), calls=%async_computation.5 | async-start | bytes 1310720 | tf_op jit(solution)/shard_map/all_gather | solution.py:627
  67.5 49.6 %collective-permute-start.8 = (bf16[4,1024,128]{2,1,0:T(8,128)(2,1)}, bf16[4,1024,128]{2,1,0:T(8,128)(2,1)}, u32[]{:S(2)}, u32[]{:S(2)}) collective-permute-start(bf16[4,1024,128]{2,1,0:T(8,128)(2,1)} %bitcast.47), channel_id=1, source_target_pairs={{0,16},{4,20},{8,24},{12,28},{16,0},{20,4},{24,8},{28,12},{1,17},{... | collective-permute-start | bytes 3145736 | tf_op jit(solution)/shard_map/ppermute | solution.py:568
  69.9 47.2 %collective-permute-start.7 = (bf16[4,1024,128]{2,1,0:T(8,128)(2,1)}, bf16[4,1024,128]{2,1,0:T(8,128)(2,1)}, u32[]{:S(2)}, u32[]{:S(2)}) collective-permute-start(bf16[4,1024,128]{2,1,0:T(8,128)(2,1)} %bitcast.48), channel_id=1, source_target_pairs={{0,8},{4,12},{8,0},{12,4},{16,24},{20,28},{24,16},{28,20},{1,9},{5... | collective-permute-start | bytes 3145736 | tf_op jit(solution)/shard_map/ppermute | solution.py:568
  71.3 32.6 %collective-permute-start.6 = (bf16[8,256,128]{2,1,0:T(8,128)(2,1)}, bf16[8,256,128]{2,1,0:T(8,128)(2,1)}, u32[]{:S(2)}, u32[]{:S(2)}) collective-permute-start(bf16[8,256,128]{2,1,0:T(8,128)(2,1)} %collective-permute-done.2.refs_1_), channel_id=1, source_target_pairs={{0,16},{4,20},{8,24},{12,28},{16,0},{20,4},{24,8},{28,12},{1,17},{... | collective-permute-start | bytes 1572872 | tf_op jit(solution)/shard_map/ppermute | solution.py:568
  71.4 33.7 %collective-permute-start.5 = (bf16[8,256,128]{2,1,0:T(8,128)(2,1)S(1)}, bf16[8,256,128]{2,1,0:T(8,128)(2,1)}, u32[]{:S(2)}, u32[]{:S(2)}) collective-permute-start(bf16[8,256,128]{2,1,0:T(8,128)(2,1)S(1)} %collective-permute-done.3.refs_2_), channel_id=1, source_target_pairs={{0,8},{4,12},{8,0},{12,4},{16,24},{20,28},{24,16},{28,20},{1,9},{5... | collective-permute-start | bytes 1572872 | tf_op jit(solution)/shard_map/ppermute | solution.py:568
  72.0 53.5 %collective-permute-start.11 = (bf16[4,1024,128]{2,1,0:T(8,128)(2,1)}, bf16[4,1024,128]{2,1,0:T(8,128)(2,1)}, u32[]{:S(2)}, u32[]{:S(2)}) collective-permute-start(bf16[4,1024,128]{2,1,0:T(8,128)(2,1)} %bitcast.49), channel_id=1, source_target_pairs={{0,4},{4,0},{8,12},{12,8},{16,20},{20,16},{24,28},{28,24},{1,5},{5... | collective-permute-start | bytes 3145736 | tf_op jit(solution)/shard_map/ppermute | solution.py:568
  117.1 7.0 %collective-permute-start.17 = (bf16[1024,128]{1,0:T(8,128)(2,1)}, bf16[1024,128]{1,0:T(8,128)(2,1)S(1)}, u32[]{:S(2)}, u32[]{:S(2)}) collective-permute-start(bf16[1024,128]{1,0:T(8,128)(2,1)} %attend.7), channel_id=1, source_target_pairs={{0,4},{4,0},{8,12},{12,8},{16,20},{20,16},{24,28},{28,24},{1,5},{5... | collective-permute-start | bytes 786440 | tf_op jit(solution)/shard_map/ppermute | solution.py:568
  119.0 15.0 %collective-permute-start.10 = (bf16[4,512,128]{2,1,0:T(8,128)(2,1)S(1)}, bf16[4,512,128]{2,1,0:T(8,128)(2,1)}, u32[]{:S(2)}, u32[]{:S(2)}) collective-permute-start(bf16[4,512,128]{2,1,0:T(8,128)(2,1)S(1)} %slice.21), channel_id=1, source_target_pairs={{0,16},{4,20},{8,24},{12,28},{16,0},{20,4},{24,8},{28,12},{1,17},{... | collective-permute-start | bytes 1572872 | tf_op jit(solution)/shard_map/ppermute | solution.py:568
  120.8 17.0 %collective-permute-start.9 = (bf16[4,512,128]{2,1,0:T(8,128)(2,1)S(1)}, bf16[4,512,128]{2,1,0:T(8,128)(2,1)}, u32[]{:S(2)}, u32[]{:S(2)}) collective-permute-start(bf16[4,512,128]{2,1,0:T(8,128)(2,1)S(1)} %slice.20), channel_id=1, source_target_pairs={{0,8},{4,12},{8,0},{12,4},{16,24},{20,28},{24,16},{28,20},{1,9},{5... | collective-permute-start | bytes 1572872 | tf_op jit(solution)/shard_map/ppermute | solution.py:568
  124.9 70.3 %all-gather.17.cloned.1.call-start = ((), (), s32[]{:S(2)}) async-start(), calls=%async_computation.4 | async-start | bytes 1310720 | tf_op jit(solution)/shard_map/all_gather | solution.py:636
  124.9 39.9 %collective-permute-start.13 = (bf16[4,1024,128]{2,1,0:T(8,128)(2,1)}, bf16[4,1024,128]{2,1,0:T(8,128)(2,1)}, u32[]{:S(2)}, u32[]{:S(2)}) collective-permute-start(bf16[4,1024,128]{2,1,0:T(8,128)(2,1)} %collective-permute-done.8.refs_9_), channel_id=1, source_target_pairs={{0,4},{4,0},{8,12},{12,8},{16,20},{20,16},{24,28},{28,24},{1,5},{5... | collective-permute-start | bytes 3145736 | tf_op jit(solution)/shard_map/ppermute | solution.py:568
  125.2 39.6 %collective-permute-start.12 = (bf16[4,1024,128]{2,1,0:T(8,128)(2,1)}, bf16[4,1024,128]{2,1,0:T(8,128)(2,1)}, u32[]{:S(2)}, u32[]{:S(2)}) collective-permute-start(bf16[4,1024,128]{2,1,0:T(8,128)(2,1)} %collective-permute-done.7.refs_8_), channel_id=1, source_target_pairs={{0,4},{4,0},{8,12},{12,8},{16,20},{20,16},{24,28},{28,24},{1,5},{5... | collective-permute-start | bytes 3145736 | tf_op jit(solution)/shard_map/ppermute | solution.py:568
  125.5 39.3 %collective-permute-start.16 = (bf16[4,128,1024]{2,1,0:T(8,128)(2,1)}, bf16[4,128,1024]{2,1,0:T(8,128)(2,1)S(1)}, u32[]{:S(2)}, u32[]{:S(2)}) collective-permute-start(bf16[4,128,1024]{2,1,0:T(8,128)(2,1)} %bitcast.51), channel_id=1, source_target_pairs={{0,16},{4,20},{8,24},{12,28},{16,0},{20,4},{24,8},{28,12},{1,17},{... | collective-permute-start | bytes 3145736 | tf_op jit(solution)/shard_map/ppermute | solution.py:568
  134.0 30.8 %collective-permute-start.15 = (bf16[4,128,1024]{2,1,0:T(8,128)(2,1)}, bf16[4,128,1024]{2,1,0:T(8,128)(2,1)}, u32[]{:S(2)}, u32[]{:S(2)}) collective-permute-start(bf16[4,128,1024]{2,1,0:T(8,128)(2,1)} %bitcast.52), channel_id=1, source_target_pairs={{0,8},{4,12},{8,0},{12,4},{16,24},{20,28},{24,16},{28,20},{1,9},{5... | collective-permute-start | bytes 3145736 | tf_op jit(solution)/shard_map/ppermute | solution.py:568
  137.8 27.1 %collective-permute-start.14 = (bf16[4,128,1024]{2,1,0:T(8,128)(2,1)}, bf16[4,128,1024]{2,1,0:T(8,128)(2,1)}, u32[]{:S(2)}, u32[]{:S(2)}) collective-permute-start(bf16[4,128,1024]{2,1,0:T(8,128)(2,1)} %bitcast.53), channel_id=1, source_target_pairs={{0,4},{4,0},{8,12},{12,8},{16,20},{20,16},{24,28},{28,24},{1,5},{5... | collective-permute-start | bytes 3145736 | tf_op jit(solution)/shard_map/ppermute | solution.py:568
  164.9 12.7 %collective-permute-start.19 = (bf16[4,64,1024]{2,1,0:T(8,128)(2,1)S(1)}, bf16[4,64,1024]{2,1,0:T(8,128)(2,1)}, u32[]{:S(2)}, u32[]{:S(2)}) collective-permute-start(bf16[4,64,1024]{2,1,0:T(8,128)(2,1)S(1)} %slice.22), channel_id=1, source_target_pairs={{0,8},{4,12},{8,0},{12,4},{16,24},{20,28},{24,16},{28,20},{1,9},{5... | collective-permute-start | bytes 1572872 | tf_op jit(solution)/shard_map/ppermute | solution.py:568
  166.3 13.9 %collective-permute-start.20 = (bf16[4,64,1024]{2,1,0:T(8,128)(2,1)S(1)}, bf16[4,64,1024]{2,1,0:T(8,128)(2,1)}, u32[]{:S(2)}, u32[]{:S(2)}) collective-permute-start(bf16[4,64,1024]{2,1,0:T(8,128)(2,1)S(1)} %slice.23), channel_id=1, source_target_pairs={{0,16},{4,20},{8,24},{12,28},{16,0},{20,4},{24,8},{28,12},{1,17},{... | collective-permute-start | bytes 1572872 | tf_op jit(solution)/shard_map/ppermute | solution.py:568
  166.4 19.3 %collective-permute-start.18 = (bf16[4,144,1024]{2,1,0:T(8,128)(2,1)}, bf16[4,144,1024]{2,1,0:T(8,128)(2,1)}, u32[]{:S(2)}, u32[]{:S(2)}) collective-permute-start(bf16[4,144,1024]{2,1,0:T(8,128)(2,1)} %bitcast.44), channel_id=1, source_target_pairs={{0,4},{4,0},{8,12},{12,8},{16,20},{20,16},{24,28},{28,24},{1,5},{5... | collective-permute-start | bytes 3538952 | tf_op jit(solution)/shard_map/ppermute | solution.py:568
  167.1 13.1 %collective-permute-start.21 = (bf16[4,512,128]{2,1,0:T(8,128)(2,1)}, bf16[4,512,128]{2,1,0:T(8,128)(2,1)}, u32[]{:S(2)}, u32[]{:S(2)}) collective-permute-start(bf16[4,512,128]{2,1,0:T(8,128)(2,1)} %collective-permute-done.9.refs_10_), channel_id=1, source_target_pairs={{0,4},{4,0},{8,12},{12,8},{16,20},{20,16},{24,28},{28,24},{1,5},{5... | collective-permute-start | bytes 1572872 | tf_op jit(solution)/shard_map/ppermute | solution.py:568
  167.2 13.5 %collective-permute-start.22 = (bf16[4,512,128]{2,1,0:T(8,128)(2,1)}, bf16[4,512,128]{2,1,0:T(8,128)(2,1)}, u32[]{:S(2)}, u32[]{:S(2)}) collective-permute-start(bf16[4,512,128]{2,1,0:T(8,128)(2,1)} %collective-permute-done.10.refs_11_), channel_id=1, source_target_pairs={{0,4},{4,0},{8,12},{12,8},{16,20},{20,16},{24,28},{28,24},{1,5},{5... | collective-permute-start | bytes 1572872 | tf_op jit(solution)/shard_map/ppermute | solution.py:568
  177.6 7.1 %collective-permute-start.23 = (bf16[4,128,1024]{2,1,0:T(8,128)(2,1)}, bf16[4,128,1024]{2,1,0:T(8,128)(2,1)}, u32[]{:S(2)}, u32[]{:S(2)}) collective-permute-start(bf16[4,128,1024]{2,1,0:T(8,128)(2,1)} %collective-permute-done.15.refs_13_), channel_id=1, source_target_pairs={{0,4},{4,0},{8,12},{12,8},{16,20},{20,16},{24,28},{28,24},{1,5},{5... | collective-permute-start | bytes 3145736 | tf_op jit(solution)/shard_map/ppermute | solution.py:568
  180.2 4.5 %collective-permute-start.24 = (bf16[4,128,1024]{2,1,0:T(8,128)(2,1)S(1)}, bf16[4,128,1024]{2,1,0:T(8,128)(2,1)S(1)}, u32[]{:S(2)}, u32[]{:S(2)}) collective-permute-start(bf16[4,128,1024]{2,1,0:T(8,128)(2,1)S(1)} %collective-permute-done.16.refs_14_), channel_id=1, source_target_pairs={{0,4},{4,0},{8,12},{12,8},{16,20},{20,16},{24,28},{28,24},{1,5},{5... | collective-permute-start | bytes 3145736 | tf_op jit(solution)/shard_map/ppermute | solution.py:568
  180.7 4.0 %collective-permute-start.26 = (bf16[4,64,1024]{2,1,0:T(8,128)(2,1)}, bf16[4,64,1024]{2,1,0:T(8,128)(2,1)}, u32[]{:S(2)}, u32[]{:S(2)}) collective-permute-start(bf16[4,64,1024]{2,1,0:T(8,128)(2,1)} %collective-permute-done.20.refs_16_), channel_id=1, source_target_pairs={{0,4},{4,0},{8,12},{12,8},{16,20},{20,16},{24,28},{28,24},{1,5},{5... | collective-permute-start | bytes 1572872 | tf_op jit(solution)/shard_map/ppermute | solution.py:568
  (9 other events, 85.0 us)
Sparse Core Ops, SparseCore 0:
  39.6 27.0 all-gather.10
  68.3 27.4 all-gather.12
  97.3 29.9 all-gather.14
  128.7 27.0 all-gather.18
  166.5 28.6 all-gather.16

commit v9 on v8

--- a/solution.py
+++ b/solution.py
@@ -435,6 +435,7 @@
     ctx_cols = sum(ctx.shape[2] for ctx in contexts)
     cols = bias.shape[2] // halves
     steps = halves * groups
+    out_at = 1 if len(outs) > 1 else 0
 
     def whole(array):
         return pl.BlockSpec(
@@ -444,8 +445,11 @@
     specs, arrays = [], []
     for h, (w1s, w2s) in enumerate(sets):
         at = lambda i, *_, h=h: (jnp.clip(i - h * groups, 0, groups - 1), 0, 0)
-        for array in (*w1s, *w2s):
-            specs.append(pl.BlockSpec((1,) + array.shape[1:], at))
+        for n, array in enumerate((*w1s, *w2s)):
+            rows = array.shape[1]
+            if len(w1s) > 1 and n == len(w1s):
+                rows = w1s[0].shape[2]
+            specs.append(pl.BlockSpec((1, rows, array.shape[2]), at))
             arrays.append(array)
     head = [x, *contexts, *outs, gain1[None], bias1[None]]
     tail = [b2[None], gain[None], bias2[None], next_w, next_b[None]]
@@ -461,7 +465,15 @@
         grid_spec=pltpu.PrefetchScalarGridSpec(
             num_scalar_prefetch=1,
             grid=(steps,),
-            in_specs=[whole(array) for array in head]
+            in_specs=[whole(array) for array in head[: 1 + len(contexts)]]
+            + [
+                pl.BlockSpec(
+                    (groups, ctx_cols // len(outs), width), lambda i, *_: (0, out_at, 0),
+                    pipeline_mode=pl.Buffered(1),
+                )
+                for _ in outs
+            ]
+            + [whole(array) for array in head[1 + len(contexts) + len(outs) :]]
             + [
                 pl.BlockSpec(
                     (1, 16, bias.shape[2]),
@@ -582,13 +594,13 @@
         kv_x = [move(kv, across) for kv in kvs]
         kv_y = [move(kv, along) for kv in kvs]
         first = lax.dynamic_slice_in_dim(first_feed_weight, turn * unit, unit, 1)
-        first, kvs = lax.optimization_barrier((first, kvs))
+        first, _, _ = lax.optimization_barrier((first, ups, weight))
         first = lax.all_gather(first, "mp", axis=0)
         step = functools.partial(attend, *args)
         state = step(bases, bases, q, kvs, None, False, pages)
-        second = lax.dynamic_slice_in_dim(second_feed_weight, turn * unit, unit, 0)
-        out_half = jnp.concatenate(
+        rest = jnp.concatenate(
             [
+                lax.dynamic_slice_in_dim(second_feed_weight, turn * unit, unit, 0),
                 lax.dynamic_slice_in_dim(
                     attention_out_weight, (dp_index % 2) * (out_rows // 2), out_rows // 2, 0
                 ),
@@ -596,58 +608,63 @@
             ],
             axis=0,
         )
-        kv_x, kv_y, state, first, second, out_half = lax.optimization_barrier(
-            (kv_x, kv_y, state, first, second, out_half)
-        )
-        second = lax.all_gather(second, "mp", axis=0)
-        out_mine = lax.all_gather(out_half, "mp", axis=0)
+        rest, _ = lax.optimization_barrier((rest, kvs))
+        rest = lax.all_gather(rest, "mp", axis=0)
+        kv_x, kv_y, state, first = lax.optimization_barrier((kv_x, kv_y, state, first))
         kv_d0 = move(kv_y[0], across)
         kv_d1 = move(kv_x[1], along)
-        first_x = move(first, across)
-        first_y = move(first, along)
         near = [at(2), at(3), at(4), at(5)]
         far = [at(6), at(7)]
         swapped, own = bases[1:], bases[:1]
         late = step(
             swapped, jnp.stack(near), q, [*kv_x, *kv_y], state, False, pages, q_from=tok_rows
         )
-        kv_d0, kv_d1, late = lax.optimization_barrier((kv_d0, kv_d1, late))
+        first_other = move(first, swap)
+        kv_d0, kv_d1, late, first, first_other = lax.optimization_barrier(
+            (kv_d0, kv_d1, late, first, first_other)
+        )
+        first_x = move(first, across)
+        first_y = move(first, along)
         theirs = step(
             swapped, jnp.stack(far), q, [kv_d0, kv_d1], late, True, pages, q_from=tok_rows
         )
-        theirs, first_x, first_y, second = lax.optimization_barrier(
-            (theirs, first_x, first_y, second)
-        )
+        theirs, rest, first_x, first_y = lax.optimization_barrier((theirs, rest, first_x, first_y))
+        second = rest[:, :unit]
+        second_x = move(second, across)
+        second_y = move(second, along)
         cut = width // 2
         first_d0 = move(first_y[:, :cut], across)
         first_d1 = move(first_x[:, cut:], along)
-        second_x = move(second, across)
-        second_y = move(second, along)
-        near_others = [move(piece, swap) for piece in (first, first_x, first_y, second)]
-        theirs = lax.all_gather(move(theirs, swap), "mp", axis=0)
+        rest_other = move(rest, swap)
+        theirs, state = lax.optimization_barrier((move(theirs, swap), state))
+        theirs = lax.all_gather(theirs, "mp", axis=0)
         mine = step(
             own, jnp.stack(near + far), q, [*kv_x, *kv_y, kv_d0, kv_d1], state, True, pages
         )
-        mine, first_d0, first_d1, near_others, second_x, second_y, out_mine = (
+        mine_all = lax.all_gather(mine, "mp", axis=0)
+        theirs, _, first_x, first_y, first_d0, first_d1, second_x, second_y, rest_other = (
             lax.optimization_barrier(
-                (mine, first_d0, first_d1, near_others, second_x, second_y, out_mine)
+                (
+                    theirs, mine, first_x, first_y, first_d0, first_d1, second_x, second_y,
+                    rest_other,
+                )
             )
         )
-        contexts = [lax.all_gather(mine, "mp", axis=0), theirs]
-        bias_rows = out_mine
         half = unit // 2
         second_d0 = move(second_y[:, :half], across)
         second_d1 = move(second_x[:, half:], along)
         firsts = [first, first_x, first_y, first_d0, first_d1]
-        moved = [move(piece, swap) for piece in (first_d0, first_d1, second_x, second_y, out_mine)]
-        first_others = [*near_others[:3], *moved[:2]]
-        out_other = moved[4]
-        seconds = [second, second_x, second_y, second_d0, second_d1]
-        second_others = [
-            near_others[3], *moved[2:4], move(second_d0, swap), move(second_d1, swap)
-        ]
+        first_others = [first_other] + [move(piece, swap) for piece in firsts[1:]]
+        seconds = [second_x, second_y, second_d0, second_d1]
+        second_others = [move(piece, swap) for piece in seconds[:3]]
+        last, mine_all = lax.optimization_barrier((second_d1, mine_all))
+        second_others.append(move(last, swap))
+        contexts = [mine_all, theirs]
+        bias_rows = rest
+        seconds = [rest, *seconds]
+        second_others = [rest_other, *second_others]
         sets = [(firsts, seconds), (first_others, second_others)]
-        outs = [out_mine, out_other]
+        outs = [rest, rest_other]
     else:
         everything = lax.all_gather(kvs[0], "dp", axis=0, tiled=True)
         context = attend(

time: 238 us -> 229 us (0.962)
  waiting for transfers between devices: 52.4 us -> 39.4 us
  Pallas kernels: 119 us -> 125 us
    ppermute x27 -> x26, waiting for transfers between devices: 36.7 us -> 27.3 us  [local(): move = lambda value, pairs: lax.ppermute(value, 'dp', pairs)]
    pallas_call x4, Pallas kernels: 73.6 us -> 79.2 us  [attend(): pl.pallas_call(functools.partial(attend_kernel, requests=requests, slots=...]
    all_gather x4 -> x3, waiting for transfers between devices: 9.48 us -> 6.74 us  [the longest x1 6.71 us: local(): mine_all = lax.all_gather(mine, 'mp', axis=0)]
    ppermute x27 -> x26, starting transfers between devices: 22.2 us -> 20.7 us  [local(): move = lambda value, pairs: lax.ppermute(value, 'dp', pairs)]
    unnamed x18 -> x30, local copies, waits for them, and re-layouts: 4.31 us -> 4.87 us
  transfers between devices with their start and end apart: 33 -> 31, of which waited for: 10 -> 10; matrix products, arithmetic and copies ran while one was open for 9% -> 9% of each run, Pallas kernels for 31% -> 39%
where the time goes in v9:
time: 229 us; the launch traced here: 230 us
  Pallas kernels  125 us (55%)
  waiting for transfers between devices  39.4 us (17%)
  starting transfers between devices  26.8 us (12%)
  local copies, waits for them, and re-layouts  18.6 us (8%)
  between operations  14.8 us (6%)
  other arithmetic  5.4 us (2%)
    pallas_call x4, Pallas kernels, attend(): pl.pallas_call(functools.partial(attend_kernel, requests=requests, slots=...  79.2 us
    pallas_call x1, Pallas kernels, finish(): pl.pallas_call(functools.partial(finish_kernel, parts=len(outs), counts=t...  35.1 us
    ppermute x26, waiting for transfers between devices, local(): move = lambda value, pairs: lax.ppermute(value, 'dp', pairs)  27.3 us
    ppermute x26, starting transfers between devices, local(): move = lambda value, pairs: lax.ppermute(value, 'dp', pairs)  20.7 us
    pallas_call x1, Pallas kernels, project(): pl.pallas_call(functools.partial(project_kernel, requests=counts.shape[0]...  10.5 us
    all_gather x1, waiting for transfers between devices, local(): mine_all = lax.all_gather(mine, 'mp', axis=0)  6.71 us
    all_to_all x1, starting transfers between devices, local(): got = lax.all_to_all(sent, 'mp', split_axis=1, concat_axis=0, tiled=True)  5.95 us
    all_to_all x1, waiting for transfers between devices, local(): got = lax.all_to_all(sent, 'mp', split_axis=1, concat_axis=0, tiled=True)  5.23 us
  transfers between devices with their start and end apart: 31, of which 10 were waited for; matrix products, arithmetic and copies ran while one was open for 9% of the time, Pallas kernels for 39%

profile of v9, /device:TPU:0, one launch (start us, length us, event | category | flops | bytes accessed | tf_op | source)
XLA Modules:
  0.0 229.8 jit_solution(17401577219703788864)
XLA Ops:
  7.7 1.9 fusion.6
  10.4 1.1 dynamic-slice_bitcast_fusion.1
  12.3 5.9 %all-to-all-start = ((bf16[16,4,1792]{2,0,1:T(8,128)(2,1)}), bf16[16,4,1792]{2,0,1:T(8,128)(2,1)S(1)}, u32[]{:S(2)}, u32[]{:S(2)}) async-start(bf16[16,4,1792]{2,0,1:T(8,128)(2,1)} %pad_maximum_fusion.1), calls=%async_computation | async-start | bytes 458752 | tf_op jit(solution)/shard_map/all_to_all | solution.py:560
  18.2 1.7 copy.29
  20.1 1.7 constant_dynamic-slice_fusion.2
  21.8 5.2 %all-to-all-done = bf16[16,4,1792]{2,0,1:T(8,128)(2,1)S(1)} async-done(((bf16[16,4,1792]{2,0,1:T(8,128)(2,1)}), bf16[16,4,1792]{2,0,1:T(8,128)(2,1)S(1)}, u32[]{:S(2)}, u32[]{:S(2)}) %all-to-all-start) | async-done | bytes 229408 | tf_op jit(solution)/shard_map/all_to_all | solution.py:560
  28.2 1.2 copy.35.refs_2_
  32.7 10.5 %project.1 = (bf16[2048,128]{1,0:T(8,128)(2,1)}, bf16[8,256,128]{2,1,0:T(8,128)(2,1)}, bf16[8,256,128]{2,1,0:T(8,128)(2,1)}) custom-call(s32[4]{0:T(128)} %counts.9, s32[64]{0:T(128)} %table.9, s32[4]{0:T(128)} %get-tuple-element.81.owners, s32[2]{0:T(128)} %pad_add_fusion.2.bases.q_bases.kv_bases, bf16[1024,1024]{1,0:T(8,128)(2,1)} %x_ref.1, ...), custom_call_target="tpu_custom_call" | custom-call | flops 1610612736 | bytes 5767168 | tf_op jit(solution)/shard_map/project/pallas_call | solution.py:109
  43.3 1.6 collective-permute-start.3
  44.9 1.5 collective-permute-start.1
  47.4 23.4 %attend.4 = (f32[2048,128]{1,0:T(8,128)}, f32[2048,128]{1,0:T(8,128)}) custom-call(s32[4]{0:T(128)} %counts.9, s32[64]{0:T(128)} %table.9, s32[2]{0:T(128)} %pad_add_fusion.2.bases.q_bases.kv_bases, s32[2]{0:T(128)} %pad_add_fusion.2.bases.q_bases.kv_bases, bf16[2048,128]{1,0:T(8,128)(2,1)} %get-tuple-element.41.q_hbm, ...), custom_call_target="tpu_custom_call" | custom-call | flops 262144 | bytes 1048576 | tf_op jit(solution)/shard_map/attend/pallas_call | solution.py:315
  71.9 17.5 %attend.5 = (f32[1024,128]{1,0:T(8,128)}, f32[1024,128]{1,0:T(8,128)}) custom-call(s32[4]{0:T(128)} %counts.9, s32[64]{0:T(128)} %table.9, s32[1]{0:T(128)} %bitcast.3.q_bases, s32[4]{0:T(128)} %get-tuple-element.85.kv_bases, bf16[2048,128]{1,0:T(8,128)(2,1)} %get-tuple-element.41.q_hbm, bf16[8,256,128]{2,1,0:T(8,128)(2,1)} %copy-done.2, ...), custom_call_target="tpu_custom_call" | custom-call | flops 131072 | bytes 524288 | tf_op jit(solution)/shard_map/attend/pallas_call | solution.py:315
  89.4 3.6 %collective-permute-start.9 = (bf16[4,1024,128]{2,1,0:T(8,128)(2,1)}, bf16[4,1024,128]{2,1,0:T(8,128)(2,1)S(1)}, u32[]{:S(2)}, u32[]{:S(2)}) collective-permute-start(bf16[4,1024,128]{2,1,0:T(8,128)(2,1)} %bitcast.49), channel_id=1, source_target_pairs={{0,16},{4,20},{8,24},{12,28},{16,0},{20,4},{24,8},{28,12},{1,17},{... | collective-permute-start | bytes 3145736 | tf_op jit(solution)/shard_map/ppermute | solution.py:580
  93.0 2.8 %collective-permute-start.8 = (bf16[4,1024,128]{2,1,0:T(8,128)(2,1)}, bf16[4,1024,128]{2,1,0:T(8,128)(2,1)}, u32[]{:S(2)}, u32[]{:S(2)}) collective-permute-start(bf16[4,1024,128]{2,1,0:T(8,128)(2,1)} %bitcast.50), channel_id=1, source_target_pairs={{0,8},{4,12},{8,0},{12,4},{16,24},{20,28},{24,16},{28,20},{1,9},{5... | collective-permute-start | bytes 3145736 | tf_op jit(solution)/shard_map/ppermute | solution.py:580
  96.4 13.4 %attend.6 = bf16[1024,128]{1,0:T(8,128)(2,1)} custom-call(s32[4]{0:T(128)} %counts.9, s32[64]{0:T(128)} %table.9, s32[1]{0:T(128)} %bitcast.3.q_bases, s32[2]{0:T(128)} %pad_add_fusion.1.kv_bases, bf16[2048,128]{1,0:T(8,128)(2,1)} %get-tuple-element.41.q_hbm, bf16[8,256,128]{2,1,0:T(8,128)(2,1)} %collective-permute-done.5.refs_0_.refs_4_, ...), custom_call_target="tpu_custom_call" | custom-call | flops 131072 | bytes 524288 | tf_op jit(solution)/shard_map/attend/pallas_call | solution.py:315
  109.9 6.7 %collective-permute-done.9.refs_9_ = bf16[4,1024,128]{2,1,0:T(8,128)(2,1)S(1)} collective-permute-done((bf16[4,1024,128]{2,1,0:T(8,128)(2,1)}, bf16[4,1024,128]{2,1,0:T(8,128)(2,1)S(1)}, u32[]{:S(2)}, u32[]{:S(2)}) %collective-permute-start.9) | collective-permute-done | bytes 1048608 | tf_op jit(solution)/shard_map/ppermute | solution.py:580
  116.5 2.5 %collective-permute-done.8.refs_8_ = bf16[4,1024,128]{2,1,0:T(8,128)(2,1)} collective-permute-done((bf16[4,1024,128]{2,1,0:T(8,128)(2,1)}, bf16[4,1024,128]{2,1,0:T(8,128)(2,1)}, u32[]{:S(2)}, u32[]{:S(2)}) %collective-permute-start.8) | collective-permute-done | bytes 1048608 | tf_op jit(solution)/shard_map/ppermute | solution.py:580
  119.5 1.6 collective-permute-done.10
  121.9 1.4 slice.25
  124.1 1.3 collective-permute-start.13
  125.4 1.9 slice.24
  128.8 1.3 collective-permute-start.12
  130.8 24.8 %attend.7 = bf16[1024,128]{1,0:T(8,128)(2,1)} custom-call(s32[4]{0:T(128)} %counts.9, s32[64]{0:T(128)} %table.9, s32[1]{0:T(128)} %bitcast.6.q_bases, s32[6]{0:T(128)} %stack.85.kv_bases, bf16[2048,128]{1,0:T(8,128)(2,1)} %get-tuple-element.41.q_hbm, bf16[8,256,128]{2,1,0:T(8,128)(2,1)} %copy-done.2, bf16[8,256,128]{2,1,0:T(8,128)(2,1)} %collective-permute-done.2.refs_1_, ...), custom_call_target="tpu_custom_call" | custom-call | flops 131072 | bytes 524288 | tf_op jit(solution)/shard_map/attend/pallas_call | solution.py:315
  155.7 4.7 %collective-permute-done.11.refs_10_ = bf16[4,512,128]{2,1,0:T(8,128)(2,1)} collective-permute-done((bf16[4,512,128]{2,1,0:T(8,128)(2,1)}, bf16[4,512,128]{2,1,0:T(8,128)(2,1)}, u32[]{:S(2)}, u32[]{:S(2)}) %collective-permute-start.11) | collective-permute-done | bytes 524320 | tf_op jit(solution)/shard_map/ppermute | solution.py:580
  160.4 1.1 slice.27
  161.5 1.4 collective-permute-start.17
  162.9 1.1 slice.26
  164.0 1.7 collective-permute-start.16
  166.2 8.2 %collective-permute-done.17.refs_15_ = bf16[4,64,1024]{2,1,0:T(8,128)(2,1)S(1)} collective-permute-done((bf16[4,64,1024]{2,1,0:T(8,128)(2,1)S(1)}, bf16[4,64,1024]{2,1,0:T(8,128)(2,1)S(1)}, u32[]{:S(2)}, u32[]{:S(2)}) %collective-permute-start.17) | collective-permute-done | bytes 524320 | tf_op jit(solution)/shard_map/ppermute | solution.py:580
  174.4 2.4 %collective-permute-done.16.refs_16_ = bf16[4,64,1024]{2,1,0:T(8,128)(2,1)S(1)} collective-permute-done((bf16[4,64,1024]{2,1,0:T(8,128)(2,1)S(1)}, bf16[4,64,1024]{2,1,0:T(8,128)(2,1)S(1)}, u32[]{:S(2)}, u32[]{:S(2)}) %collective-permute-start.16) | collective-permute-done | bytes 524320 | tf_op jit(solution)/shard_map/ppermute | solution.py:580
  178.4 6.7 %all-gather.15.cloned.1.call-done = bf16[4096,128]{1,0:T(8,128)(2,1)} async-done(((bf16[1024,128]{1,0:T(8,128)(2,1)}), bf16[4096,128]{1,0:T(8,128)(2,1)}) %all-gather.15.cloned.1.call-update) | async-done | bytes 1048592 | tf_op jit(solution)/shard_map/all_gather | solution.py:644
  188.1 35.1 %finish.1 = (bf16[256,1024]{1,0:T(8,128)(2,1)}, bf16[1024,768]{1,0:T(8,128)(2,1)}) custom-call(s32[3]{0:T(128)} %pad_add_fusion.place, bf16[1024,1024]{1,0:T(8,128)(2,1)} %x_ref.1, bf16[4,1024,128]{2,1,0:T(8,128)(2,1)} %bitcast.53, bf16[4,1024,128]{2,1,0:T(8,128)(2,1)} %bitcast.52, bf16[4,272,1024]{2,1,0:T(8,128)(2,1)} %bitcast.42, ...), custom_call_target="tpu_custom_call" | custom-call | flops 17179869184 | bytes 16777216 | tf_op jit(solution)/shard_map/finish/pallas_call | solution.py:458
  (104 shorter events, 18.1 us)
Async XLA Ops:
  7.2 25.5 %collective-permute-start = (bf16[1024,1024]{1,0:T(8,128)(2,1)}, bf16[1024,1024]{1,0:T(8,128)(2,1)}, u32[]{:S(2)}, u32[]{:S(2)}) collective-permute-start(bf16[1024,1024]{1,0:T(8,128)(2,1)} %x_ref.1), channel_id=1, source_target_pairs={{0,4},{4,0},{8,12},{12,8},{16,20},{20,16},{24,28},{28,24},{1,5},{5... | collective-permute-start | bytes 6291464 | tf_op jit(solution)/shard_map/ppermute | solution.py:580
  12.3 14.7 %all-to-all-start = ((bf16[16,4,1792]{2,0,1:T(8,128)(2,1)}), bf16[16,4,1792]{2,0,1:T(8,128)(2,1)S(1)}, u32[]{:S(2)}, u32[]{:S(2)}) async-start(bf16[16,4,1792]{2,0,1:T(8,128)(2,1)} %pad_maximum_fusion.1), calls=%async_computation | async-start | bytes 458752 | tf_op jit(solution)/shard_map/all_to_all | solution.py:560
  18.2 52.6 %all-gather.9.cloned.1.call-start = ((), (), s32[]{:S(2)}) async-start(), calls=%async_computation.1 | async-start | bytes 1310720 | tf_op jit(solution)/shard_map/all_gather | solution.py:598
  28.1 90.9 %all-gather.11.cloned.1.call-start = ((), (), s32[]{:S(2)}) async-start(), calls=%async_computation.2 | async-start | bytes 2785280 | tf_op jit(solution)/shard_map/all_gather | solution.py:612
  43.3 117.2 %all-gather.13.cloned.1.call-start = ((), (), s32[]{:S(2)}) async-start(), calls=%async_computation.3 | async-start | bytes 1310720 | tf_op jit(solution)/shard_map/all_gather | solution.py:640
  43.3 27.6 %collective-permute-start.3 = (bf16[8,256,128]{2,1,0:T(8,128)(2,1)}, bf16[8,256,128]{2,1,0:T(8,128)(2,1)S(1)}, u32[]{:S(2)}, u32[]{:S(2)}) collective-permute-start(bf16[8,256,128]{2,1,0:T(8,128)(2,1)} %get-tuple-element.42.refs_0_), channel_id=1, source_target_pairs={{0,16},{4,20},{8,24},{12,28},{16,0},{20,4},{24,8},{28,12},{1,17},{... | collective-permute-start | bytes 1572872 | tf_op jit(solution)/shard_map/ppermute | solution.py:580
  44.9 26.0 %collective-permute-start.1 = (bf16[8,256,128]{2,1,0:T(8,128)(2,1)}, bf16[8,256,128]{2,1,0:T(8,128)(2,1)S(1)}, u32[]{:S(2)}, u32[]{:S(2)}) collective-permute-start(bf16[8,256,128]{2,1,0:T(8,128)(2,1)} %get-tuple-element.42.refs_0_), channel_id=1, source_target_pairs={{0,8},{4,12},{8,0},{12,4},{16,24},{20,28},{24,16},{28,20},{1,9},{5... | collective-permute-start | bytes 1572872 | tf_op jit(solution)/shard_map/ppermute | solution.py:580
  46.4 24.6 %collective-permute-start.4 = (bf16[8,256,128]{2,1,0:T(8,128)(2,1)}, bf16[8,256,128]{2,1,0:T(8,128)(2,1)}, u32[]{:S(2)}, u32[]{:S(2)}) collective-permute-start(bf16[8,256,128]{2,1,0:T(8,128)(2,1)} %get-tuple-element.43.refs_1_), channel_id=1, source_target_pairs={{0,16},{4,20},{8,24},{12,28},{16,0},{20,4},{24,8},{28,12},{1,17},{... | collective-permute-start | bytes 1572872 | tf_op jit(solution)/shard_map/ppermute | solution.py:580
  46.9 24.1 %collective-permute-start.2 = (bf16[8,256,128]{2,1,0:T(8,128)(2,1)}, bf16[8,256,128]{2,1,0:T(8,128)(2,1)}, u32[]{:S(2)}, u32[]{:S(2)}) collective-permute-start(bf16[8,256,128]{2,1,0:T(8,128)(2,1)} %get-tuple-element.43.refs_1_), channel_id=1, source_target_pairs={{0,8},{4,12},{8,0},{12,4},{16,24},{20,28},{24,16},{28,20},{1,9},{5... | collective-permute-start | bytes 1572872 | tf_op jit(solution)/shard_map/ppermute | solution.py:580
  70.9 18.5 %collective-permute-start.7 = (bf16[4,1024,128]{2,1,0:T(8,128)(2,1)}, bf16[4,1024,128]{2,1,0:T(8,128)(2,1)}, u32[]{:S(2)}, u32[]{:S(2)}) collective-permute-start(bf16[4,1024,128]{2,1,0:T(8,128)(2,1)} %bitcast.48), channel_id=1, source_target_pairs={{0,4},{4,0},{8,12},{12,8},{16,20},{20,16},{24,28},{28,24},{1,5},{5... | collective-permute-start | bytes 3145736 | tf_op jit(solution)/shard_map/ppermute | solution.py:580
  71.0 18.4 %collective-permute-start.5 = (bf16[8,256,128]{2,1,0:T(8,128)(2,1)S(1)}, bf16[8,256,128]{2,1,0:T(8,128)(2,1)}, u32[]{:S(2)}, u32[]{:S(2)}) collective-permute-start(bf16[8,256,128]{2,1,0:T(8,128)(2,1)S(1)} %collective-permute-done.3.refs_2_), channel_id=1, source_target_pairs={{0,8},{4,12},{8,0},{12,4},{16,24},{20,28},{24,16},{28,20},{1,9},{5... | collective-permute-start | bytes 1572872 | tf_op jit(solution)/shard_map/ppermute | solution.py:580
  71.9 17.5 %collective-permute-start.6 = (bf16[8,256,128]{2,1,0:T(8,128)(2,1)}, bf16[8,256,128]{2,1,0:T(8,128)(2,1)}, u32[]{:S(2)}, u32[]{:S(2)}) collective-permute-start(bf16[8,256,128]{2,1,0:T(8,128)(2,1)} %collective-permute-done.2.refs_1_), channel_id=1, source_target_pairs={{0,16},{4,20},{8,24},{12,28},{16,0},{20,4},{24,8},{28,12},{1,17},{... | collective-permute-start | bytes 1572872 | tf_op jit(solution)/shard_map/ppermute | solution.py:580
  89.4 27.1 %collective-permute-start.9 = (bf16[4,1024,128]{2,1,0:T(8,128)(2,1)}, bf16[4,1024,128]{2,1,0:T(8,128)(2,1)S(1)}, u32[]{:S(2)}, u32[]{:S(2)}) collective-permute-start(bf16[4,1024,128]{2,1,0:T(8,128)(2,1)} %bitcast.49), channel_id=1, source_target_pairs={{0,16},{4,20},{8,24},{12,28},{16,0},{20,4},{24,8},{28,12},{1,17},{... | collective-permute-start | bytes 3145736 | tf_op jit(solution)/shard_map/ppermute | solution.py:580
  93.0 26.0 %collective-permute-start.8 = (bf16[4,1024,128]{2,1,0:T(8,128)(2,1)}, bf16[4,1024,128]{2,1,0:T(8,128)(2,1)}, u32[]{:S(2)}, u32[]{:S(2)}) collective-permute-start(bf16[4,1024,128]{2,1,0:T(8,128)(2,1)} %bitcast.50), channel_id=1, source_target_pairs={{0,8},{4,12},{8,0},{12,4},{16,24},{20,28},{24,16},{28,20},{1,9},{5... | collective-permute-start | bytes 3145736 | tf_op jit(solution)/shard_map/ppermute | solution.py:580
  119.0 2.1 collective-permute-start.10
  119.0 41.4 %collective-permute-start.15 = (bf16[4,272,1024]{2,1,0:T(8,128)(2,1)}, bf16[4,272,1024]{2,1,0:T(8,128)(2,1)}, u32[]{:S(2)}, u32[]{:S(2)}) collective-permute-start(bf16[4,272,1024]{2,1,0:T(8,128)(2,1)} %bitcast.40), channel_id=1, source_target_pairs={{0,4},{4,0},{8,12},{12,8},{16,20},{20,16},{24,28},{28,24},{1,5},{5... | collective-permute-start | bytes 6684680 | tf_op jit(solution)/shard_map/ppermute | solution.py:580
  121.8 63.3 %all-gather.15.cloned.1.call-start = ((), (), s32[]{:S(2)}) async-start(), calls=%async_computation.4 | async-start | bytes 1310720 | tf_op jit(solution)/shard_map/all_gather | solution.py:644
  123.3 37.1 %collective-permute-start.14 = (bf16[4,128,1024]{2,1,0:T(8,128)(2,1)S(1)}, bf16[4,128,1024]{2,1,0:T(8,128)(2,1)}, u32[]{:S(2)}, u32[]{:S(2)}) collective-permute-start(bf16[4,128,1024]{2,1,0:T(8,128)(2,1)S(1)} %slice.25), channel_id=1, source_target_pairs={{0,16},{4,20},{8,24},{12,28},{16,0},{20,4},{24,8},{28,12},{1,17},{... | collective-permute-start | bytes 3145736 | tf_op jit(solution)/shard_map/ppermute | solution.py:580
  124.1 36.3 %collective-permute-start.13 = (bf16[4,128,1024]{2,1,0:T(8,128)(2,1)S(1)}, bf16[4,128,1024]{2,1,0:T(8,128)(2,1)}, u32[]{:S(2)}, u32[]{:S(2)}) collective-permute-start(bf16[4,128,1024]{2,1,0:T(8,128)(2,1)S(1)} %slice.25), channel_id=1, source_target_pairs={{0,8},{4,12},{8,0},{12,4},{16,24},{20,28},{24,16},{28,20},{1,9},{5... | collective-permute-start | bytes 3145736 | tf_op jit(solution)/shard_map/ppermute | solution.py:580
  128.1 32.2 %collective-permute-start.11 = (bf16[4,512,128]{2,1,0:T(8,128)(2,1)}, bf16[4,512,128]{2,1,0:T(8,128)(2,1)}, u32[]{:S(2)}, u32[]{:S(2)}) collective-permute-start(bf16[4,512,128]{2,1,0:T(8,128)(2,1)} %slice.23), channel_id=1, source_target_pairs={{0,8},{4,12},{8,0},{12,4},{16,24},{20,28},{24,16},{28,20},{1,9},{5... | collective-permute-start | bytes 1572872 | tf_op jit(solution)/shard_map/ppermute | solution.py:580
  128.8 31.5 %collective-permute-start.12 = (bf16[4,512,128]{2,1,0:T(8,128)(2,1)}, bf16[4,512,128]{2,1,0:T(8,128)(2,1)}, u32[]{:S(2)}, u32[]{:S(2)}) collective-permute-start(bf16[4,512,128]{2,1,0:T(8,128)(2,1)} %slice.24), channel_id=1, source_target_pairs={{0,16},{4,20},{8,24},{12,28},{16,0},{20,4},{24,8},{28,12},{1,17},{... | collective-permute-start | bytes 1572872 | tf_op jit(solution)/shard_map/ppermute | solution.py:580
  155.6 30.0 %copy-start.8 = (f32[768]{0:T(1024)S(1)}, f32[768]{0:T(1024)}, u32[]{:S(2)}) copy-start(f32[768]{0:T(1024)} %param.32) | copy-start | bytes 9220
  161.5 12.9 %collective-permute-start.17 = (bf16[4,64,1024]{2,1,0:T(8,128)(2,1)S(1)}, bf16[4,64,1024]{2,1,0:T(8,128)(2,1)S(1)}, u32[]{:S(2)}, u32[]{:S(2)}) collective-permute-start(bf16[4,64,1024]{2,1,0:T(8,128)(2,1)S(1)} %slice.27), channel_id=1, source_target_pairs={{0,8},{4,12},{8,0},{12,4},{16,24},{20,28},{24,16},{28,20},{1,9},{5... | collective-permute-start | bytes 1572872 | tf_op jit(solution)/shard_map/ppermute | solution.py:580
  164.0 12.8 %collective-permute-start.16 = (bf16[4,64,1024]{2,1,0:T(8,128)(2,1)S(1)}, bf16[4,64,1024]{2,1,0:T(8,128)(2,1)S(1)}, u32[]{:S(2)}, u32[]{:S(2)}) collective-permute-start(bf16[4,64,1024]{2,1,0:T(8,128)(2,1)S(1)} %slice.26), channel_id=1, source_target_pairs={{0,16},{4,20},{8,24},{12,28},{16,0},{20,4},{24,8},{28,12},{1,17},{... | collective-permute-start | bytes 1572872 | tf_op jit(solution)/shard_map/ppermute | solution.py:580
  165.7 11.1 %collective-permute-start.20 = (bf16[4,512,128]{2,1,0:T(8,128)(2,1)}, bf16[4,512,128]{2,1,0:T(8,128)(2,1)S(1)}, u32[]{:S(2)}, u32[]{:S(2)}) collective-permute-start(bf16[4,512,128]{2,1,0:T(8,128)(2,1)} %collective-permute-done.11.refs_10_), channel_id=1, source_target_pairs={{0,4},{4,0},{8,12},{12,8},{16,20},{20,16},{24,28},{28,24},{1,5},{5... | collective-permute-start | bytes 1572872 | tf_op jit(solution)/shard_map/ppermute | solution.py:580
  165.7 19.4 %collective-permute-start.18 = (bf16[4,1024,128]{2,1,0:T(8,128)(2,1)}, bf16[4,1024,128]{2,1,0:T(8,128)(2,1)S(1)}, u32[]{:S(2)}, u32[]{:S(2)}) collective-permute-start(bf16[4,1024,128]{2,1,0:T(8,128)(2,1)} %collective-permute-done.8.refs_8_), channel_id=1, source_target_pairs={{0,4},{4,0},{8,12},{12,8},{16,20},{20,16},{24,28},{28,24},{1,5},{5... | collective-permute-start | bytes 3145736 | tf_op jit(solution)/shard_map/ppermute | solution.py:580
  166.2 20.6 %collective-permute-start.22 = (bf16[4,128,1024]{2,1,0:T(8,128)(2,1)}, bf16[4,128,1024]{2,1,0:T(8,128)(2,1)}, u32[]{:S(2)}, u32[]{:S(2)}) collective-permute-start(bf16[4,128,1024]{2,1,0:T(8,128)(2,1)} %collective-permute-done.13.refs_13_), channel_id=1, source_target_pairs={{0,4},{4,0},{8,12},{12,8},{16,20},{20,16},{24,28},{28,24},{1,5},{5... | collective-permute-start | bytes 3145736 | tf_op jit(solution)/shard_map/ppermute | solution.py:580
  174.4 10.7 %collective-permute-start.21 = (bf16[4,512,128]{2,1,0:T(8,128)(2,1)}, bf16[4,512,128]{2,1,0:T(8,128)(2,1)}, u32[]{:S(2)}, u32[]{:S(2)}) collective-permute-start(bf16[4,512,128]{2,1,0:T(8,128)(2,1)} %collective-permute-done.12.refs_11_), channel_id=1, source_target_pairs={{0,4},{4,0},{8,12},{12,8},{16,20},{20,16},{24,28},{28,24},{1,5},{5... | collective-permute-start | bytes 1572872 | tf_op jit(solution)/shard_map/ppermute | solution.py:580
  176.8 10.0 %collective-permute-start.19 = (bf16[4,1024,128]{2,1,0:T(8,128)(2,1)S(1)}, bf16[4,1024,128]{2,1,0:T(8,128)(2,1)}, u32[]{:S(2)}, u32[]{:S(2)}) collective-permute-start(bf16[4,1024,128]{2,1,0:T(8,128)(2,1)S(1)} %copy-done.5), channel_id=1, source_target_pairs={{0,4},{4,0},{8,12},{12,8},{16,20},{20,16},{24,28},{28,24},{1,5},{5... | collective-permute-start | bytes 3145736 | tf_op jit(solution)/shard_map/ppermute | solution.py:580
  178.4 8.4 %collective-permute-start.23 = (bf16[4,128,1024]{2,1,0:T(8,128)(2,1)}, bf16[4,128,1024]{2,1,0:T(8,128)(2,1)}, u32[]{:S(2)}, u32[]{:S(2)}) collective-permute-start(bf16[4,128,1024]{2,1,0:T(8,128)(2,1)} %collective-permute-done.14.refs_14_), channel_id=1, source_target_pairs={{0,4},{4,0},{8,12},{12,8},{16,20},{20,16},{24,28},{28,24},{1,5},{5... | collective-permute-start | bytes 3145736 | tf_op jit(solution)/shard_map/ppermute | solution.py:580
  185.1 2.3 collective-permute-start.24
  185.1 3.0 %collective-permute-start.25 = (bf16[4,64,1024]{2,1,0:T(8,128)(2,1)}, bf16[4,64,1024]{2,1,0:T(8,128)(2,1)}, u32[]{:S(2)}, u32[]{:S(2)}) collective-permute-start(bf16[4,64,1024]{2,1,0:T(8,128)(2,1)} %copy-done.12), channel_id=1, source_target_pairs={{0,4},{4,0},{8,12},{12,8},{16,20},{20,16},{24,28},{28,24},{1,5},{5... | collective-permute-start | bytes 1572872 | tf_op jit(solution)/shard_map/ppermute | solution.py:580
  (13 other events, 60.5 us)
Sparse Core Ops, SparseCore 0:
  28.2 27.0 all-gather.8
  56.9 47.8 all-gather.10
  122.0 26.2 all-gather.12
  155.8 29.2 all-gather.14

commit v10 on v9

--- a/solution.py
+++ b/solution.py
@@ -94,7 +94,7 @@
 def project(counts, table, owners, bases, xs, weight, down, up, per_piece):
     tok, width = xs[0].shape
     cols = weight.shape[1]
-    pages = 2
+    pages = min(4, tok // PAGE)
     rows_step = pages * PAGE
     slots = table.shape[0]
     parts = len(xs)
@@ -598,33 +598,33 @@
         first = lax.all_gather(first, "mp", axis=0)
         step = functools.partial(attend, *args)
         state = step(bases, bases, q, kvs, None, False, pages)
+        second_map, out_map, bias_rows, _ = lax.optimization_barrier(
+            (second_feed_weight, attention_out_weight, bias_rows, kvs)
+        )
         rest = jnp.concatenate(
             [
-                lax.dynamic_slice_in_dim(second_feed_weight, turn * unit, unit, 0),
+                lax.dynamic_slice_in_dim(second_map, turn * unit, unit, 0),
                 lax.dynamic_slice_in_dim(
-                    attention_out_weight, (dp_index % 2) * (out_rows // 2), out_rows // 2, 0
+                    out_map, (dp_index % 2) * (out_rows // 2), out_rows // 2, 0
                 ),
                 bias_rows,
             ],
             axis=0,
         )
-        rest, _ = lax.optimization_barrier((rest, kvs))
         rest = lax.all_gather(rest, "mp", axis=0)
         kv_x, kv_y, state, first = lax.optimization_barrier((kv_x, kv_y, state, first))
         kv_d0 = move(kv_y[0], across)
         kv_d1 = move(kv_x[1], along)
+        first_x = move(first, across)
+        first_y = move(first, along)
         near = [at(2), at(3), at(4), at(5)]
         far = [at(6), at(7)]
         swapped, own = bases[1:], bases[:1]
         late = step(
             swapped, jnp.stack(near), q, [*kv_x, *kv_y], state, False, pages, q_from=tok_rows
         )
-        first_other = move(first, swap)
-        kv_d0, kv_d1, late, first, first_other = lax.optimization_barrier(
-            (kv_d0, kv_d1, late, first, first_other)
-        )
-        first_x = move(first, across)
-        first_y = move(first, along)
+        own_late = step(own, jnp.stack(near), q, [*kv_x, *kv_y], state, False, pages)
+        kv_d0, kv_d1, late, own_late = lax.optimization_barrier((kv_d0, kv_d1, late, own_late))
         theirs = step(
             swapped, jnp.stack(far), q, [kv_d0, kv_d1], late, True, pages, q_from=tok_rows
         )
@@ -635,18 +635,16 @@
         cut = width // 2
         first_d0 = move(first_y[:, :cut], across)
         first_d1 = move(first_x[:, cut:], along)
+        theirs, own_late, rest = lax.optimization_barrier((move(theirs, swap), own_late, rest))
         rest_other = move(rest, swap)
-        theirs, state = lax.optimization_barrier((move(theirs, swap), state))
         theirs = lax.all_gather(theirs, "mp", axis=0)
-        mine = step(
-            own, jnp.stack(near + far), q, [*kv_x, *kv_y, kv_d0, kv_d1], state, True, pages
-        )
+        mine = step(own, jnp.stack(far), q, [kv_d0, kv_d1], own_late, True, pages)
         mine_all = lax.all_gather(mine, "mp", axis=0)
-        theirs, _, first_x, first_y, first_d0, first_d1, second_x, second_y, rest_other = (
+        theirs, _, first, first_x, first_y, first_d0, first_d1, second_x, second_y, rest_other = (
             lax.optimization_barrier(
                 (
-                    theirs, mine, first_x, first_y, first_d0, first_d1, second_x, second_y,
-                    rest_other,
+                    theirs, mine, first, first_x, first_y, first_d0, first_d1, second_x,
+                    second_y, rest_other,
                 )
             )
         )
@@ -654,7 +652,7 @@
         second_d0 = move(second_y[:, :half], across)
         second_d1 = move(second_x[:, half:], along)
         firsts = [first, first_x, first_y, first_d0, first_d1]
-        first_others = [first_other] + [move(piece, swap) for piece in firsts[1:]]
+        first_others = [move(piece, swap) for piece in firsts]
         seconds = [second_x, second_y, second_d0, second_d1]
         second_others = [move(piece, swap) for piece in seconds[:3]]
         last, mine_all = lax.optimization_barrier((second_d1, mine_all))

time: 229 us -> 236 us (1.031)
  waiting for transfers between devices: 39.4 us -> 47.4 us
  Pallas kernels: 125 us -> 118 us
  starting transfers between devices: 26.8 us -> 30.9 us
    ppermute x26, waiting for transfers between devices: 27.3 us -> 42.1 us  [local(): move = lambda value, pairs: lax.ppermute(value, 'dp', pairs)]
    all_gather x1, waiting for transfers between devices: 6.71 us -> 0.01 us  [local(): mine_all = lax.all_gather(mine, 'mp', axis=0)]
    pallas_call x4 -> x5, Pallas kernels: 79.2 us -> 74.6 us  [attend(): pl.pallas_call(functools.partial(attend_kernel, requests=requests, slots=...]
    ppermute x26, starting transfers between devices: 20.7 us -> 24.6 us  [local(): move = lambda value, pairs: lax.ppermute(value, 'dp', pairs)]
  transfers between devices with their start and end apart: 31 -> 31, of which waited for: 10 -> 11; matrix products, arithmetic and copies ran while one was open for 9% -> 9% of each run, Pallas kernels for 39% -> 35%
where the time goes in v10:
time: 236 us; the launch traced here: 237 us
  Pallas kernels  118 us (50%)
  waiting for transfers between devices  47.4 us (20%)
  starting transfers between devices  30.9 us (13%)
  local copies, waits for them, and re-layouts  19.8 us (8%)
  between operations  14.9 us (6%)
  other arithmetic  5.45 us (2%)
    pallas_call x5, Pallas kernels, attend(): pl.pallas_call(functools.partial(attend_kernel, requests=requests, slots=...  74.6 us
    ppermute x26, waiting for transfers between devices, local(): move = lambda value, pairs: lax.ppermute(value, 'dp', pairs)  42.1 us
    pallas_call x1, Pallas kernels, finish(): pl.pallas_call(functools.partial(finish_kernel, parts=len(outs), counts=t...  35 us
    ppermute x26, starting transfers between devices, local(): move = lambda value, pairs: lax.ppermute(value, 'dp', pairs)  24.6 us
    pallas_call x1, Pallas kernels, project(): pl.pallas_call(functools.partial(project_kernel, requests=counts.shape[0]...  8.54 us
    all_to_all x1, starting transfers between devices, local(): got = lax.all_to_all(sent, 'mp', split_axis=1, concat_axis=0, tiled=True)  5.95 us
    unnamed x30, local copies, waits for them, and re-layouts  5.74 us
    all_to_all x1, waiting for transfers between devices, local(): got = lax.all_to_all(sent, 'mp', split_axis=1, concat_axis=0, tiled=True)  5.24 us
  transfers between devices with their start and end apart: 31, of which 11 were waited for; matrix products, arithmetic and copies ran while one was open for 9% of the time, Pallas kernels for 35%

profile of v10, /device:TPU:0, one launch (start us, length us, event | category | flops | bytes accessed | tf_op | source)
XLA Modules:
  0.0 236.6 jit_solution(10231250796149702800)
XLA Ops:
  7.7 2.0 fusion.6
  10.4 1.1 dynamic-slice_bitcast_fusion.1
  12.4 5.9 %all-to-all-start = ((bf16[16,4,1792]{2,0,1:T(8,128)(2,1)}), bf16[16,4,1792]{2,0,1:T(8,128)(2,1)S(1)}, u32[]{:S(2)}, u32[]{:S(2)}) async-start(bf16[16,4,1792]{2,0,1:T(8,128)(2,1)} %pad_maximum_fusion.1), calls=%async_computation | async-start | bytes 458752 | tf_op jit(solution)/shard_map/all_to_all | solution.py:560
  18.3 1.7 copy.29
  20.2 1.7 constant_dynamic-slice_fusion.2
  21.8 5.2 %all-to-all-done = bf16[16,4,1792]{2,0,1:T(8,128)(2,1)S(1)} async-done(((bf16[16,4,1792]{2,0,1:T(8,128)(2,1)}), bf16[16,4,1792]{2,0,1:T(8,128)(2,1)S(1)}, u32[]{:S(2)}, u32[]{:S(2)}) %all-to-all-start) | async-done | bytes 229408 | tf_op jit(solution)/shard_map/all_to_all | solution.py:560
  28.3 1.2 copy.35.refs_2_
  31.0 8.5 %project.1 = (bf16[2048,128]{1,0:T(8,128)(2,1)}, bf16[8,256,128]{2,1,0:T(8,128)(2,1)}, bf16[8,256,128]{2,1,0:T(8,128)(2,1)}) custom-call(s32[4]{0:T(128)} %counts.11, s32[64]{0:T(128)} %table.11, s32[4]{0:T(128)} %get-tuple-element.93.owners, s32[2]{0:T(128)} %pad_add_fusion.2.bases.q_bases.kv_bases, bf16[1024,1024]{1,0:T(8,128)(2,1)} %x_ref.1, ...), custom_call_target="tpu_custom_call" | custom-call | flops 1610612736 | bytes 5767168 | tf_op jit(solution)/shard_map/project/pallas_call | solution.py:109
  41.5 1.6 collective-permute-start.3
  43.1 1.5 collective-permute-start.1
  45.6 14.4 %attend.5 = (f32[2048,128]{1,0:T(8,128)}, f32[2048,128]{1,0:T(8,128)}) custom-call(s32[4]{0:T(128)} %counts.11, s32[64]{0:T(128)} %table.11, s32[2]{0:T(128)} %pad_add_fusion.2.bases.q_bases.kv_bases, s32[2]{0:T(128)} %pad_add_fusion.2.bases.q_bases.kv_bases, bf16[2048,128]{1,0:T(8,128)(2,1)} %get-tuple-element.47.q_hbm, ...), custom_call_target="tpu_custom_call" | custom-call | flops 262144 | bytes 1048576 | tf_op jit(solution)/shard_map/attend/pallas_call | solution.py:315
  60.1 5.0 %collective-permute-done.4.refs_3_ = bf16[8,256,128]{2,1,0:T(8,128)(2,1)} collective-permute-done((bf16[8,256,128]{2,1,0:T(8,128)(2,1)}, bf16[8,256,128]{2,1,0:T(8,128)(2,1)}, u32[]{:S(2)}, u32[]{:S(2)}) %collective-permute-start.4) | collective-permute-done | bytes 524320 | tf_op jit(solution)/shard_map/ppermute | solution.py:580
  65.1 1.2 collective-permute-done.2.refs_1_
  66.3 3.3 %collective-permute-start.8 = (bf16[4,1024,128]{2,1,0:T(8,128)(2,1)}, bf16[4,1024,128]{2,1,0:T(8,128)(2,1)}, u32[]{:S(2)}, u32[]{:S(2)}) collective-permute-start(bf16[4,1024,128]{2,1,0:T(8,128)(2,1)} %bitcast.48), channel_id=1, source_target_pairs={{0,16},{4,20},{8,24},{12,28},{16,0},{20,4},{24,8},{28,12},{1,17},{... | collective-permute-start | bytes 3145736 | tf_op jit(solution)/shard_map/ppermute | solution.py:580
  69.6 2.0 collective-permute-start.5
  72.9 18.2 %attend.7 = (f32[1024,128]{1,0:T(8,128)}, f32[1024,128]{1,0:T(8,128)}) custom-call(s32[4]{0:T(128)} %counts.11, s32[64]{0:T(128)} %table.11, s32[1]{0:T(128)} %bitcast.6.q_bases, s32[4]{0:T(128)} %get-tuple-element.97.kv_bases, bf16[2048,128]{1,0:T(8,128)(2,1)} %get-tuple-element.47.q_hbm, bf16[8,256,128]{2,1,0:T(8,128)(2,1)} %copy-done.3, ...), custom_call_target="tpu_custom_call" | custom-call | flops 131072 | bytes 524288 | tf_op jit(solution)/shard_map/attend/pallas_call | solution.py:315
  91.2 18.2 %attend.6 = (f32[1024,128]{1,0:T(8,128)}, f32[1024,128]{1,0:T(8,128)}) custom-call(s32[4]{0:T(128)} %counts.11, s32[64]{0:T(128)} %table.11, s32[1]{0:T(128)} %bitcast.3.q_bases, s32[4]{0:T(128)} %get-tuple-element.97.kv_bases, bf16[2048,128]{1,0:T(8,128)(2,1)} %get-tuple-element.47.q_hbm, bf16[8,256,128]{2,1,0:T(8,128)(2,1)} %copy-done.3, ...), custom_call_target="tpu_custom_call" | custom-call | flops 131072 | bytes 524288 | tf_op jit(solution)/shard_map/attend/pallas_call | solution.py:315
  110.4 11.9 %attend.8 = bf16[1024,128]{1,0:T(8,128)(2,1)} custom-call(s32[4]{0:T(128)} %counts.11, s32[64]{0:T(128)} %table.11, s32[1]{0:T(128)} %bitcast.3.q_bases, s32[2]{0:T(128)} %pad_add_fusion.1.kv_bases, bf16[2048,128]{1,0:T(8,128)(2,1)} %get-tuple-element.47.q_hbm, bf16[8,256,128]{2,1,0:T(8,128)(2,1)} %copy-done.1, bf16[8,256,128]{2,1,0:T(8,128)(2,1)} %copy-done.2, ...), custom_call_target="tpu_custom_call" | custom-call | flops 131072 | bytes 524288 | tf_op jit(solution)/shard_map/attend/pallas_call | solution.py:315
  122.4 1.7 collective-permute-done.9
  125.1 1.3 slice.25
  126.4 4.4 %collective-permute-start.13 = (bf16[4,128,1024]{2,1,0:T(8,128)(2,1)S(1)}, bf16[4,128,1024]{2,1,0:T(8,128)(2,1)}, u32[]{:S(2)}, u32[]{:S(2)}) collective-permute-start(bf16[4,128,1024]{2,1,0:T(8,128)(2,1)S(1)} %slice.25), channel_id=1, source_target_pairs={{0,16},{4,20},{8,24},{12,28},{16,0},{20,4},{24,8},{28,12},{1,17},{... | collective-permute-start | bytes 3145736 | tf_op jit(solution)/shard_map/ppermute | solution.py:580
  130.9 5.5 %collective-permute-start.12 = (bf16[4,128,1024]{2,1,0:T(8,128)(2,1)S(1)}, bf16[4,128,1024]{2,1,0:T(8,128)(2,1)}, u32[]{:S(2)}, u32[]{:S(2)}) collective-permute-start(bf16[4,128,1024]{2,1,0:T(8,128)(2,1)S(1)} %slice.25), channel_id=1, source_target_pairs={{0,8},{4,12},{8,0},{12,4},{16,24},{20,28},{24,16},{28,20},{1,9},{5... | collective-permute-start | bytes 3145736 | tf_op jit(solution)/shard_map/ppermute | solution.py:580
  136.3 1.9 slice.24
  138.2 1.9 slice.23
  140.2 11.9 %attend.9 = bf16[1024,128]{1,0:T(8,128)(2,1)} custom-call(s32[4]{0:T(128)} %counts.11, s32[64]{0:T(128)} %table.11, s32[1]{0:T(128)} %bitcast.6.q_bases, s32[2]{0:T(128)} %pad_add_fusion.1.kv_bases, bf16[2048,128]{1,0:T(8,128)(2,1)} %get-tuple-element.47.q_hbm, bf16[8,256,128]{2,1,0:T(8,128)(2,1)} %copy-done.1, bf16[8,256,128]{2,1,0:T(8,128)(2,1)} %copy-done.2, ...), custom_call_target="tpu_custom_call" | custom-call | flops 131072 | bytes 524288 | tf_op jit(solution)/shard_map/attend/pallas_call | solution.py:315
  152.1 18.7 %collective-permute-done.10.refs_10_ = bf16[4,512,128]{2,1,0:T(8,128)(2,1)} collective-permute-done((bf16[4,512,128]{2,1,0:T(8,128)(2,1)}, bf16[4,512,128]{2,1,0:T(8,128)(2,1)}, u32[]{:S(2)}, u32[]{:S(2)}) %collective-permute-start.10) | collective-permute-done | bytes 524320 | tf_op jit(solution)/shard_map/ppermute | solution.py:580
  170.9 1.1 slice.27
  172.0 1.8 collective-permute-start.16
  175.8 9.4 %collective-permute-done.16.refs_15_ = bf16[4,64,1024]{2,1,0:T(8,128)(2,1)S(1)} collective-permute-done((bf16[4,64,1024]{2,1,0:T(8,128)(2,1)S(1)}, bf16[4,64,1024]{2,1,0:T(8,128)(2,1)S(1)}, u32[]{:S(2)}, u32[]{:S(2)}) %collective-permute-start.16) | collective-permute-done | bytes 524320 | tf_op jit(solution)/shard_map/ppermute | solution.py:580
  185.2 2.3 collective-permute-done.15.refs_16_
  192.1 1.5 collective-permute-done.23.refs_24_
  195.1 35.0 %finish.1 = (bf16[256,1024]{1,0:T(8,128)(2,1)}, bf16[1024,768]{1,0:T(8,128)(2,1)}) custom-call(s32[3]{0:T(128)} %pad_add_fusion.place, bf16[1024,1024]{1,0:T(8,128)(2,1)} %x_ref.1, bf16[4,1024,128]{2,1,0:T(8,128)(2,1)} %bitcast.53, bf16[4,1024,128]{2,1,0:T(8,128)(2,1)} %bitcast.52, bf16[4,272,1024]{2,1,0:T(8,128)(2,1)} %bitcast.42, ...), custom_call_target="tpu_custom_call" | custom-call | flops 17179869184 | bytes 16777216 | tf_op jit(solution)/shard_map/finish/pallas_call | solution.py:458
  (105 shorter events, 18.8 us)
Async XLA Ops:
  7.2 23.9 %collective-permute-start = (bf16[1024,1024]{1,0:T(8,128)(2,1)}, bf16[1024,1024]{1,0:T(8,128)(2,1)}, u32[]{:S(2)}, u32[]{:S(2)}) collective-permute-start(bf16[1024,1024]{1,0:T(8,128)(2,1)} %x_ref.1), channel_id=1, source_target_pairs={{0,4},{4,0},{8,12},{12,8},{16,20},{20,16},{24,28},{28,24},{1,5},{5... | collective-permute-start | bytes 6291464 | tf_op jit(solution)/shard_map/ppermute | solution.py:580
  12.4 14.7 %all-to-all-start = ((bf16[16,4,1792]{2,0,1:T(8,128)(2,1)}), bf16[16,4,1792]{2,0,1:T(8,128)(2,1)S(1)}, u32[]{:S(2)}, u32[]{:S(2)}) async-start(bf16[16,4,1792]{2,0,1:T(8,128)(2,1)} %pad_maximum_fusion.1), calls=%async_computation | async-start | bytes 458752 | tf_op jit(solution)/shard_map/all_to_all | solution.py:560
  18.3 41.8 %all-gather.9.cloned.1.call-start = ((), (), s32[]{:S(2)}) async-start(), calls=%async_computation.1 | async-start | bytes 1310720 | tf_op jit(solution)/shard_map/all_gather | solution.py:598
  28.2 94.1 %all-gather.11.cloned.1.call-start = ((), (), s32[]{:S(2)}) async-start(), calls=%async_computation.2 | async-start | bytes 2785280 | tf_op jit(solution)/shard_map/all_gather | solution.py:614
  41.5 129.4 %all-gather.13.cloned.1.call-start = ((), (), s32[]{:S(2)}) async-start(), calls=%async_computation.3 | async-start | bytes 1310720 | tf_op jit(solution)/shard_map/all_gather | solution.py:640
  41.5 18.6 %collective-permute-start.3 = (bf16[8,256,128]{2,1,0:T(8,128)(2,1)}, bf16[8,256,128]{2,1,0:T(8,128)(2,1)}, u32[]{:S(2)}, u32[]{:S(2)}) collective-permute-start(bf16[8,256,128]{2,1,0:T(8,128)(2,1)} %get-tuple-element.48.refs_0_), channel_id=1, source_target_pairs={{0,16},{4,20},{8,24},{12,28},{16,0},{20,4},{24,8},{28,12},{1,17},{... | collective-permute-start | bytes 1572872 | tf_op jit(solution)/shard_map/ppermute | solution.py:580
  43.1 17.0 %collective-permute-start.1 = (bf16[8,256,128]{2,1,0:T(8,128)(2,1)}, bf16[8,256,128]{2,1,0:T(8,128)(2,1)S(1)}, u32[]{:S(2)}, u32[]{:S(2)}) collective-permute-start(bf16[8,256,128]{2,1,0:T(8,128)(2,1)} %get-tuple-element.48.refs_0_), channel_id=1, source_target_pairs={{0,8},{4,12},{8,0},{12,4},{16,24},{20,28},{24,16},{28,20},{1,9},{5... | collective-permute-start | bytes 1572872 | tf_op jit(solution)/shard_map/ppermute | solution.py:580
  44.6 20.5 %collective-permute-start.4 = (bf16[8,256,128]{2,1,0:T(8,128)(2,1)}, bf16[8,256,128]{2,1,0:T(8,128)(2,1)}, u32[]{:S(2)}, u32[]{:S(2)}) collective-permute-start(bf16[8,256,128]{2,1,0:T(8,128)(2,1)} %get-tuple-element.49.refs_1_), channel_id=1, source_target_pairs={{0,16},{4,20},{8,24},{12,28},{16,0},{20,4},{24,8},{28,12},{1,17},{... | collective-permute-start | bytes 1572872 | tf_op jit(solution)/shard_map/ppermute | solution.py:580
  45.1 21.2 %collective-permute-start.2 = (bf16[8,256,128]{2,1,0:T(8,128)(2,1)}, bf16[8,256,128]{2,1,0:T(8,128)(2,1)S(1)}, u32[]{:S(2)}, u32[]{:S(2)}) collective-permute-start(bf16[8,256,128]{2,1,0:T(8,128)(2,1)} %get-tuple-element.49.refs_1_), channel_id=1, source_target_pairs={{0,8},{4,12},{8,0},{12,4},{16,24},{20,28},{24,16},{28,20},{1,9},{5... | collective-permute-start | bytes 1572872 | tf_op jit(solution)/shard_map/ppermute | solution.py:580
  66.3 56.0 %collective-permute-start.8 = (bf16[4,1024,128]{2,1,0:T(8,128)(2,1)}, bf16[4,1024,128]{2,1,0:T(8,128)(2,1)}, u32[]{:S(2)}, u32[]{:S(2)}) collective-permute-start(bf16[4,1024,128]{2,1,0:T(8,128)(2,1)} %bitcast.48), channel_id=1, source_target_pairs={{0,16},{4,20},{8,24},{12,28},{16,0},{20,4},{24,8},{28,12},{1,17},{... | collective-permute-start | bytes 3145736 | tf_op jit(solution)/shard_map/ppermute | solution.py:580
  69.6 52.7 %collective-permute-start.7 = (bf16[4,1024,128]{2,1,0:T(8,128)(2,1)}, bf16[4,1024,128]{2,1,0:T(8,128)(2,1)}, u32[]{:S(2)}, u32[]{:S(2)}) collective-permute-start(bf16[4,1024,128]{2,1,0:T(8,128)(2,1)} %bitcast.49), channel_id=1, source_target_pairs={{0,8},{4,12},{8,0},{12,4},{16,24},{20,28},{24,16},{28,20},{1,9},{5... | collective-permute-start | bytes 3145736 | tf_op jit(solution)/shard_map/ppermute | solution.py:580
  69.6 39.8 %collective-permute-start.5 = (bf16[8,256,128]{2,1,0:T(8,128)(2,1)}, bf16[8,256,128]{2,1,0:T(8,128)(2,1)S(1)}, u32[]{:S(2)}, u32[]{:S(2)}) collective-permute-start(bf16[8,256,128]{2,1,0:T(8,128)(2,1)} %collective-permute-done.3.refs_2_), channel_id=1, source_target_pairs={{0,8},{4,12},{8,0},{12,4},{16,24},{20,28},{24,16},{28,20},{1,9},{5... | collective-permute-start | bytes 1572872 | tf_op jit(solution)/shard_map/ppermute | solution.py:580
  71.6 37.8 %collective-permute-start.6 = (bf16[8,256,128]{2,1,0:T(8,128)(2,1)}, bf16[8,256,128]{2,1,0:T(8,128)(2,1)S(1)}, u32[]{:S(2)}, u32[]{:S(2)}) collective-permute-start(bf16[8,256,128]{2,1,0:T(8,128)(2,1)} %copy-done.4), channel_id=1, source_target_pairs={{0,16},{4,20},{8,24},{12,28},{16,0},{20,4},{24,8},{28,12},{1,17},{... | collective-permute-start | bytes 1572872 | tf_op jit(solution)/shard_map/ppermute | solution.py:580
  122.3 1.8 collective-permute-start.9
  124.2 46.7 %collective-permute-start.14 = (bf16[4,272,1024]{2,1,0:T(8,128)(2,1)}, bf16[4,272,1024]{2,1,0:T(8,128)(2,1)}, u32[]{:S(2)}, u32[]{:S(2)}) collective-permute-start(bf16[4,272,1024]{2,1,0:T(8,128)(2,1)} %bitcast.40), channel_id=1, source_target_pairs={{0,4},{4,0},{8,12},{12,8},{16,20},{20,16},{24,28},{28,24},{1,5},{5... | collective-permute-start | bytes 6684680 | tf_op jit(solution)/shard_map/ppermute | solution.py:580
  124.9 64.7 %all-gather.15.cloned.1.call-start = ((), (), s32[]{:S(2)}) async-start(), calls=%async_computation.4 | async-start | bytes 1310720 | tf_op jit(solution)/shard_map/all_gather | solution.py:642
  126.4 44.4 %collective-permute-start.13 = (bf16[4,128,1024]{2,1,0:T(8,128)(2,1)S(1)}, bf16[4,128,1024]{2,1,0:T(8,128)(2,1)}, u32[]{:S(2)}, u32[]{:S(2)}) collective-permute-start(bf16[4,128,1024]{2,1,0:T(8,128)(2,1)S(1)} %slice.25), channel_id=1, source_target_pairs={{0,16},{4,20},{8,24},{12,28},{16,0},{20,4},{24,8},{28,12},{1,17},{... | collective-permute-start | bytes 3145736 | tf_op jit(solution)/shard_map/ppermute | solution.py:580
  130.9 40.0 %collective-permute-start.12 = (bf16[4,128,1024]{2,1,0:T(8,128)(2,1)S(1)}, bf16[4,128,1024]{2,1,0:T(8,128)(2,1)}, u32[]{:S(2)}, u32[]{:S(2)}) collective-permute-start(bf16[4,128,1024]{2,1,0:T(8,128)(2,1)S(1)} %slice.25), channel_id=1, source_target_pairs={{0,8},{4,12},{8,0},{12,4},{16,24},{20,28},{24,16},{28,20},{1,9},{5... | collective-permute-start | bytes 3145736 | tf_op jit(solution)/shard_map/ppermute | solution.py:580
  140.1 30.7 %collective-permute-start.10 = (bf16[4,512,128]{2,1,0:T(8,128)(2,1)}, bf16[4,512,128]{2,1,0:T(8,128)(2,1)}, u32[]{:S(2)}, u32[]{:S(2)}) collective-permute-start(bf16[4,512,128]{2,1,0:T(8,128)(2,1)} %slice.23), channel_id=1, source_target_pairs={{0,8},{4,12},{8,0},{12,4},{16,24},{20,28},{24,16},{28,20},{1,9},{5... | collective-permute-start | bytes 1572872 | tf_op jit(solution)/shard_map/ppermute | solution.py:580
  140.1 30.7 %collective-permute-start.11 = (bf16[4,512,128]{2,1,0:T(8,128)(2,1)}, bf16[4,512,128]{2,1,0:T(8,128)(2,1)}, u32[]{:S(2)}, u32[]{:S(2)}) collective-permute-start(bf16[4,512,128]{2,1,0:T(8,128)(2,1)} %slice.24), channel_id=1, source_target_pairs={{0,16},{4,20},{8,24},{12,28},{16,0},{20,4},{24,8},{28,12},{1,17},{... | collective-permute-start | bytes 1572872 | tf_op jit(solution)/shard_map/ppermute | solution.py:580
  152.1 38.0 %copy-start.7 = (f32[768]{0:T(1024)S(1)}, f32[768]{0:T(1024)}, u32[]{:S(2)}) copy-start(f32[768]{0:T(1024)} %param.32) | copy-start | bytes 9220
  172.0 13.2 %collective-permute-start.16 = (bf16[4,64,1024]{2,1,0:T(8,128)(2,1)S(1)}, bf16[4,64,1024]{2,1,0:T(8,128)(2,1)S(1)}, u32[]{:S(2)}, u32[]{:S(2)}) collective-permute-start(bf16[4,64,1024]{2,1,0:T(8,128)(2,1)S(1)} %slice.27), channel_id=1, source_target_pairs={{0,8},{4,12},{8,0},{12,4},{16,24},{20,28},{24,16},{28,20},{1,9},{5... | collective-permute-start | bytes 1572872 | tf_op jit(solution)/shard_map/ppermute | solution.py:580
  174.9 12.6 %collective-permute-start.15 = (bf16[4,64,1024]{2,1,0:T(8,128)(2,1)S(1)}, bf16[4,64,1024]{2,1,0:T(8,128)(2,1)S(1)}, u32[]{:S(2)}, u32[]{:S(2)}) collective-permute-start(bf16[4,64,1024]{2,1,0:T(8,128)(2,1)S(1)} %slice.26), channel_id=1, source_target_pairs={{0,16},{4,20},{8,24},{12,28},{16,0},{20,4},{24,8},{28,12},{1,17},{... | collective-permute-start | bytes 1572872 | tf_op jit(solution)/shard_map/ppermute | solution.py:580
  175.3 13.0 %collective-permute-start.20 = (bf16[4,512,128]{2,1,0:T(8,128)(2,1)}, bf16[4,512,128]{2,1,0:T(8,128)(2,1)S(1)}, u32[]{:S(2)}, u32[]{:S(2)}) collective-permute-start(bf16[4,512,128]{2,1,0:T(8,128)(2,1)} %collective-permute-done.10.refs_10_), channel_id=1, source_target_pairs={{0,4},{4,0},{8,12},{12,8},{16,20},{20,16},{24,28},{28,24},{1,5},{5... | collective-permute-start | bytes 1572872 | tf_op jit(solution)/shard_map/ppermute | solution.py:580
  175.3 13.8 %collective-permute-start.21 = (bf16[4,512,128]{2,1,0:T(8,128)(2,1)}, bf16[4,512,128]{2,1,0:T(8,128)(2,1)}, u32[]{:S(2)}, u32[]{:S(2)}) collective-permute-start(bf16[4,512,128]{2,1,0:T(8,128)(2,1)} %collective-permute-done.11.refs_11_), channel_id=1, source_target_pairs={{0,4},{4,0},{8,12},{12,8},{16,20},{20,16},{24,28},{28,24},{1,5},{5... | collective-permute-start | bytes 1572872 | tf_op jit(solution)/shard_map/ppermute | solution.py:580
  175.8 13.8 %collective-permute-start.17 = (bf16[4,1024,128]{2,1,0:T(8,128)(2,1)S(1)}, bf16[4,1024,128]{2,1,0:T(8,128)(2,1)S(1)}, u32[]{:S(2)}, u32[]{:S(2)}) collective-permute-start(bf16[4,1024,128]{2,1,0:T(8,128)(2,1)S(1)} %bitcast.51), channel_id=1, source_target_pairs={{0,4},{4,0},{8,12},{12,8},{16,20},{20,16},{24,28},{28,24},{1,5},{5... | collective-permute-start | bytes 3145736 | tf_op jit(solution)/shard_map/ppermute | solution.py:580
  185.2 4.5 %collective-permute-start.18 = (bf16[4,1024,128]{2,1,0:T(8,128)(2,1)}, bf16[4,1024,128]{2,1,0:T(8,128)(2,1)}, u32[]{:S(2)}, u32[]{:S(2)}) collective-permute-start(bf16[4,1024,128]{2,1,0:T(8,128)(2,1)} %collective-permute-done.7.refs_8_), channel_id=1, source_target_pairs={{0,4},{4,0},{8,12},{12,8},{16,20},{20,16},{24,28},{28,24},{1,5},{5... | collective-permute-start | bytes 3145736 | tf_op jit(solution)/shard_map/ppermute | solution.py:580
  187.5 4.6 %collective-permute-start.22 = (bf16[4,128,1024]{2,1,0:T(8,128)(2,1)}, bf16[4,128,1024]{2,1,0:T(8,128)(2,1)}, u32[]{:S(2)}, u32[]{:S(2)}) collective-permute-start(bf16[4,128,1024]{2,1,0:T(8,128)(2,1)} %collective-permute-done.12.refs_13_), channel_id=1, source_target_pairs={{0,4},{4,0},{8,12},{12,8},{16,20},{20,16},{24,28},{28,24},{1,5},{5... | collective-permute-start | bytes 3145736 | tf_op jit(solution)/shard_map/ppermute | solution.py:580
  189.1 3.0 %collective-permute-start.19 = (bf16[4,1024,128]{2,1,0:T(8,128)(2,1)}, bf16[4,1024,128]{2,1,0:T(8,128)(2,1)}, u32[]{:S(2)}, u32[]{:S(2)}) collective-permute-start(bf16[4,1024,128]{2,1,0:T(8,128)(2,1)} %collective-permute-done.8.refs_9_), channel_id=1, source_target_pairs={{0,4},{4,0},{8,12},{12,8},{16,20},{20,16},{24,28},{28,24},{1,5},{5... | collective-permute-start | bytes 3145736 | tf_op jit(solution)/shard_map/ppermute | solution.py:580
  189.1 4.5 %collective-permute-start.23 = (bf16[4,128,1024]{2,1,0:T(8,128)(2,1)}, bf16[4,128,1024]{2,1,0:T(8,128)(2,1)}, u32[]{:S(2)}, u32[]{:S(2)}) collective-permute-start(bf16[4,128,1024]{2,1,0:T(8,128)(2,1)} %collective-permute-done.13.refs_14_), channel_id=1, source_target_pairs={{0,4},{4,0},{8,12},{12,8},{16,20},{20,16},{24,28},{28,24},{1,5},{5... | collective-permute-start | bytes 3145736 | tf_op jit(solution)/shard_map/ppermute | solution.py:580
  189.6 4.7 %collective-permute-start.24 = (bf16[4,64,1024]{2,1,0:T(8,128)(2,1)}, bf16[4,64,1024]{2,1,0:T(8,128)(2,1)}, u32[]{:S(2)}, u32[]{:S(2)}) collective-permute-start(bf16[4,64,1024]{2,1,0:T(8,128)(2,1)} %copy-done.11), channel_id=1, source_target_pairs={{0,4},{4,0},{8,12},{12,8},{16,20},{20,16},{24,28},{28,24},{1,5},{5... | collective-permute-start | bytes 1572872 | tf_op jit(solution)/shard_map/ppermute | solution.py:580
  189.7 5.4 %collective-permute-start.25 = (bf16[4,64,1024]{2,1,0:T(8,128)(2,1)}, bf16[4,64,1024]{2,1,0:T(8,128)(2,1)}, u32[]{:S(2)}, u32[]{:S(2)}) collective-permute-start(bf16[4,64,1024]{2,1,0:T(8,128)(2,1)} %copy-done.12), channel_id=1, source_target_pairs={{0,4},{4,0},{8,12},{12,8},{16,20},{20,16},{24,28},{28,24},{1,5},{5... | collective-permute-start | bytes 1572872 | tf_op jit(solution)/shard_map/ppermute | solution.py:580
  (13 other events, 68.7 us)
Sparse Core Ops, SparseCore 0:
  28.3 27.0 all-gather.8
  57.0 47.8 all-gather.10
  125.0 33.8 all-gather.12
  160.3 27.4 all-gather.14

commit v11 on v9

--- a/solution.py
+++ b/solution.py
@@ -94,7 +94,7 @@
 def project(counts, table, owners, bases, xs, weight, down, up, per_piece):
     tok, width = xs[0].shape
     cols = weight.shape[1]
-    pages = 2
+    pages = min(4, tok // PAGE)
     rows_step = pages * PAGE
     slots = table.shape[0]
     parts = len(xs)
@@ -598,17 +598,19 @@
         first = lax.all_gather(first, "mp", axis=0)
         step = functools.partial(attend, *args)
         state = step(bases, bases, q, kvs, None, False, pages)
+        second_map, out_map, bias_rows, _ = lax.optimization_barrier(
+            (second_feed_weight, attention_out_weight, bias_rows, kvs)
+        )
         rest = jnp.concatenate(
             [
-                lax.dynamic_slice_in_dim(second_feed_weight, turn * unit, unit, 0),
+                lax.dynamic_slice_in_dim(second_map, turn * unit, unit, 0),
                 lax.dynamic_slice_in_dim(
-                    attention_out_weight, (dp_index % 2) * (out_rows // 2), out_rows // 2, 0
+                    out_map, (dp_index % 2) * (out_rows // 2), out_rows // 2, 0
                 ),
                 bias_rows,
             ],
             axis=0,
         )
-        rest, _ = lax.optimization_barrier((rest, kvs))
         rest = lax.all_gather(rest, "mp", axis=0)
         kv_x, kv_y, state, first = lax.optimization_barrier((kv_x, kv_y, state, first))
         kv_d0 = move(kv_y[0], across)

time: 229 us -> 227 us (level); the launches traced: 230 us -> 224 us
  Pallas kernels: 125 us -> 116 us
  waiting for transfers between devices: 39.4 us -> 43.8 us
    ppermute x26, waiting for transfers between devices: 27.3 us -> 35.3 us  [local(): move = lambda value, pairs: lax.ppermute(value, 'dp', pairs)]
    pallas_call x4, Pallas kernels: 79.2 us -> 72.8 us  [attend(): pl.pallas_call(functools.partial(attend_kernel, requests=requests, slots=...]
    all_gather x1, waiting for transfers between devices: 6.71 us -> 3.14 us  [local(): mine_all = lax.all_gather(mine, 'mp', axis=0)]
  transfers between devices with their start and end apart: 31 -> 31, of which waited for: 10 -> 12; matrix products, arithmetic and copies ran while one was open for 9% -> 10% of each run, Pallas kernels for 39% -> 36%
where the time goes in v11:
time: 227 us; the launch traced here: 224 us
  Pallas kernels  116 us (51%)
  waiting for transfers between devices  43.8 us (19%)
  starting transfers between devices  25.6 us (11%)
  local copies, waits for them, and re-layouts  18.6 us (8%)
  between operations  14.8 us (7%)
  other arithmetic  5.33 us (2%)
    pallas_call x4, Pallas kernels, attend(): pl.pallas_call(functools.partial(attend_kernel, requests=requests, slots=...  72.8 us
    ppermute x26, waiting for transfers between devices, local(): move = lambda value, pairs: lax.ppermute(value, 'dp', pairs)  35.3 us
    pallas_call x1, Pallas kernels, finish(): pl.pallas_call(functools.partial(finish_kernel, parts=len(outs), counts=t...  35 us
    ppermute x26, starting transfers between devices, local(): move = lambda value, pairs: lax.ppermute(value, 'dp', pairs)  19.3 us
    pallas_call x1, Pallas kernels, project(): pl.pallas_call(functools.partial(project_kernel, requests=counts.shape[0]...  8.55 us
    all_to_all x1, starting transfers between devices, local(): got = lax.all_to_all(sent, 'mp', split_axis=1, concat_axis=0, tiled=True)  5.95 us
    all_to_all x1, waiting for transfers between devices, local(): got = lax.all_to_all(sent, 'mp', split_axis=1, concat_axis=0, tiled=True)  5.25 us
    unnamed x30, local copies, waits for them, and re-layouts  4.89 us
  transfers between devices with their start and end apart: 31, of which 12 were waited for; matrix products, arithmetic and copies ran while one was open for 10% of the time, Pallas kernels for 36%

profile of v11, /device:TPU:0, one launch (start us, length us, event | category | flops | bytes accessed | tf_op | source)
XLA Modules:
  0.0 224.5 jit_solution(1125796571918293604)
XLA Ops:
  7.7 1.9 fusion.6
  12.2 5.9 %all-to-all-start = ((bf16[16,4,1792]{2,0,1:T(8,128)(2,1)}), bf16[16,4,1792]{2,0,1:T(8,128)(2,1)S(1)}, u32[]{:S(2)}, u32[]{:S(2)}) async-start(bf16[16,4,1792]{2,0,1:T(8,128)(2,1)} %pad_maximum_fusion.1), calls=%async_computation | async-start | bytes 458752 | tf_op jit(solution)/shard_map/all_to_all | solution.py:560
  18.2 1.7 copy.29
  20.0 1.7 constant_dynamic-slice_fusion.2
  21.7 5.2 %all-to-all-done = bf16[16,4,1792]{2,0,1:T(8,128)(2,1)S(1)} async-done(((bf16[16,4,1792]{2,0,1:T(8,128)(2,1)}), bf16[16,4,1792]{2,0,1:T(8,128)(2,1)S(1)}, u32[]{:S(2)}, u32[]{:S(2)}) %all-to-all-start) | async-done | bytes 229408 | tf_op jit(solution)/shard_map/all_to_all | solution.py:560
  28.1 1.2 copy.35.refs_2_
  30.9 8.6 %project.1 = (bf16[2048,128]{1,0:T(8,128)(2,1)}, bf16[8,256,128]{2,1,0:T(8,128)(2,1)}, bf16[8,256,128]{2,1,0:T(8,128)(2,1)}) custom-call(s32[4]{0:T(128)} %counts.9, s32[64]{0:T(128)} %table.9, s32[4]{0:T(128)} %get-tuple-element.85.owners, s32[2]{0:T(128)} %pad_add_fusion.2.bases.q_bases.kv_bases, bf16[1024,1024]{1,0:T(8,128)(2,1)} %x_ref.1, ...), custom_call_target="tpu_custom_call" | custom-call | flops 1610612736 | bytes 5767168 | tf_op jit(solution)/shard_map/project/pallas_call | solution.py:109
  41.3 1.6 collective-permute-start.3
  42.9 1.5 collective-permute-start.1
  45.4 17.1 %attend.4 = (f32[2048,128]{1,0:T(8,128)}, f32[2048,128]{1,0:T(8,128)}) custom-call(s32[4]{0:T(128)} %counts.9, s32[64]{0:T(128)} %table.9, s32[2]{0:T(128)} %pad_add_fusion.2.bases.q_bases.kv_bases, s32[2]{0:T(128)} %pad_add_fusion.2.bases.q_bases.kv_bases, bf16[2048,128]{1,0:T(8,128)(2,1)} %get-tuple-element.43.q_hbm, ...), custom_call_target="tpu_custom_call" | custom-call | flops 262144 | bytes 1048576 | tf_op jit(solution)/shard_map/attend/pallas_call | solution.py:315
  62.6 2.3 %collective-permute-done.4.refs_3_ = bf16[8,256,128]{2,1,0:T(8,128)(2,1)} collective-permute-done((bf16[8,256,128]{2,1,0:T(8,128)(2,1)}, bf16[8,256,128]{2,1,0:T(8,128)(2,1)}, u32[]{:S(2)}, u32[]{:S(2)}) %collective-permute-start.4) | collective-permute-done | bytes 524320 | tf_op jit(solution)/shard_map/ppermute | solution.py:580
  64.9 1.3 collective-permute-done.2.refs_1_
  66.2 3.3 %collective-permute-start.5 = (bf16[8,256,128]{2,1,0:T(8,128)(2,1)S(1)}, bf16[8,256,128]{2,1,0:T(8,128)(2,1)}, u32[]{:S(2)}, u32[]{:S(2)}) collective-permute-start(bf16[8,256,128]{2,1,0:T(8,128)(2,1)S(1)} %collective-permute-done.3.refs_2_), channel_id=1, source_target_pairs={{0,8},{4,12},{8,0},{12,4},{16,24},{20,28},{24,16},{28,20},{1,9},{5... | collective-permute-start | bytes 1572872 | tf_op jit(solution)/shard_map/ppermute | solution.py:580
  69.5 1.2 collective-permute-start.6
  70.7 19.0 %attend.5 = (f32[1024,128]{1,0:T(8,128)}, f32[1024,128]{1,0:T(8,128)}) custom-call(s32[4]{0:T(128)} %counts.9, s32[64]{0:T(128)} %table.9, s32[1]{0:T(128)} %bitcast.3.q_bases, s32[4]{0:T(128)} %get-tuple-element.89.kv_bases, bf16[2048,128]{1,0:T(8,128)(2,1)} %get-tuple-element.43.q_hbm, bf16[8,256,128]{2,1,0:T(8,128)(2,1)} %copy-done.2, ...), custom_call_target="tpu_custom_call" | custom-call | flops 131072 | bytes 524288 | tf_op jit(solution)/shard_map/attend/pallas_call | solution.py:315
  89.8 2.0 collective-permute-start.8
  92.4 12.0 %attend.6 = bf16[1024,128]{1,0:T(8,128)(2,1)} custom-call(s32[4]{0:T(128)} %counts.9, s32[64]{0:T(128)} %table.9, s32[1]{0:T(128)} %bitcast.3.q_bases, s32[2]{0:T(128)} %pad_add_fusion.1.kv_bases, bf16[2048,128]{1,0:T(8,128)(2,1)} %get-tuple-element.43.q_hbm, bf16[8,256,128]{2,1,0:T(8,128)(2,1)} %collective-permute-done.5.refs_0_.refs_4_, ...), custom_call_target="tpu_custom_call" | custom-call | flops 131072 | bytes 524288 | tf_op jit(solution)/shard_map/attend/pallas_call | solution.py:315
  104.4 9.4 %collective-permute-done.9.refs_9_ = bf16[4,1024,128]{2,1,0:T(8,128)(2,1)S(1)} collective-permute-done((bf16[4,1024,128]{2,1,0:T(8,128)(2,1)}, bf16[4,1024,128]{2,1,0:T(8,128)(2,1)S(1)}, u32[]{:S(2)}, u32[]{:S(2)}) %collective-permute-start.9) | collective-permute-done | bytes 1048608 | tf_op jit(solution)/shard_map/ppermute | solution.py:580
  113.8 1.5 collective-permute-done.8.refs_8_
  116.0 1.7 collective-permute-done.10
  118.7 1.4 slice.25
  120.1 2.1 collective-permute-start.14
  122.2 1.9 collective-permute-start.13
  124.1 1.9 slice.24
  127.6 24.7 %attend.7 = bf16[1024,128]{1,0:T(8,128)(2,1)} custom-call(s32[4]{0:T(128)} %counts.9, s32[64]{0:T(128)} %table.9, s32[1]{0:T(128)} %bitcast.6.q_bases, s32[6]{0:T(128)} %stack.85.kv_bases, bf16[2048,128]{1,0:T(8,128)(2,1)} %get-tuple-element.43.q_hbm, bf16[8,256,128]{2,1,0:T(8,128)(2,1)} %copy-done.2, bf16[8,256,128]{2,1,0:T(8,128)(2,1)} %collective-permute-done.2.refs_1_, ...), custom_call_target="tpu_custom_call" | custom-call | flops 131072 | bytes 524288 | tf_op jit(solution)/shard_map/attend/pallas_call | solution.py:315
  152.4 6.3 %collective-permute-done.11.refs_10_ = bf16[4,512,128]{2,1,0:T(8,128)(2,1)} collective-permute-done((bf16[4,512,128]{2,1,0:T(8,128)(2,1)}, bf16[4,512,128]{2,1,0:T(8,128)(2,1)}, u32[]{:S(2)}, u32[]{:S(2)}) %collective-permute-start.11) | collective-permute-done | bytes 524320 | tf_op jit(solution)/shard_map/ppermute | solution.py:580
  158.7 1.1 slice.27
  159.8 1.7 collective-permute-start.17
  163.6 9.4 %collective-permute-done.17.refs_15_ = bf16[4,64,1024]{2,1,0:T(8,128)(2,1)S(1)} collective-permute-done((bf16[4,64,1024]{2,1,0:T(8,128)(2,1)S(1)}, bf16[4,64,1024]{2,1,0:T(8,128)(2,1)S(1)}, u32[]{:S(2)}, u32[]{:S(2)}) %collective-permute-start.17) | collective-permute-done | bytes 524320 | tf_op jit(solution)/shard_map/ppermute | solution.py:580
  172.9 2.3 %collective-permute-done.16.refs_16_ = bf16[4,64,1024]{2,1,0:T(8,128)(2,1)S(1)} collective-permute-done((bf16[4,64,1024]{2,1,0:T(8,128)(2,1)S(1)}, bf16[4,64,1024]{2,1,0:T(8,128)(2,1)S(1)}, u32[]{:S(2)}, u32[]{:S(2)}) %collective-permute-start.16) | collective-permute-done | bytes 524320 | tf_op jit(solution)/shard_map/ppermute | solution.py:580
  176.8 3.1 %all-gather.15.cloned.1.call-done = bf16[4096,128]{1,0:T(8,128)(2,1)} async-done(((bf16[1024,128]{1,0:T(8,128)(2,1)}), bf16[4096,128]{1,0:T(8,128)(2,1)}) %all-gather.15.cloned.1.call-update) | async-done | bytes 1048592 | tf_op jit(solution)/shard_map/all_gather | solution.py:646
  183.0 35.0 %finish.1 = (bf16[256,1024]{1,0:T(8,128)(2,1)}, bf16[1024,768]{1,0:T(8,128)(2,1)}) custom-call(s32[3]{0:T(128)} %pad_add_fusion.place, bf16[1024,1024]{1,0:T(8,128)(2,1)} %x_ref.1, bf16[4,1024,128]{2,1,0:T(8,128)(2,1)} %bitcast.53, bf16[4,1024,128]{2,1,0:T(8,128)(2,1)} %bitcast.52, bf16[4,272,1024]{2,1,0:T(8,128)(2,1)} %bitcast.42, ...), custom_call_target="tpu_custom_call" | custom-call | flops 17179869184 | bytes 16777216 | tf_op jit(solution)/shard_map/finish/pallas_call | solution.py:458
  (105 shorter events, 18.9 us)
Async XLA Ops:
  7.2 23.7 %collective-permute-start = (bf16[1024,1024]{1,0:T(8,128)(2,1)}, bf16[1024,1024]{1,0:T(8,128)(2,1)}, u32[]{:S(2)}, u32[]{:S(2)}) collective-permute-start(bf16[1024,1024]{1,0:T(8,128)(2,1)} %x_ref.1), channel_id=1, source_target_pairs={{0,4},{4,0},{8,12},{12,8},{16,20},{20,16},{24,28},{28,24},{1,5},{5... | collective-permute-start | bytes 6291464 | tf_op jit(solution)/shard_map/ppermute | solution.py:580
  12.2 14.7 %all-to-all-start = ((bf16[16,4,1792]{2,0,1:T(8,128)(2,1)}), bf16[16,4,1792]{2,0,1:T(8,128)(2,1)S(1)}, u32[]{:S(2)}, u32[]{:S(2)}) async-start(bf16[16,4,1792]{2,0,1:T(8,128)(2,1)} %pad_maximum_fusion.1), calls=%async_computation | async-start | bytes 458752 | tf_op jit(solution)/shard_map/all_to_all | solution.py:560
  18.2 44.4 %all-gather.9.cloned.1.call-start = ((), (), s32[]{:S(2)}) async-start(), calls=%async_computation.1 | async-start | bytes 1310720 | tf_op jit(solution)/shard_map/all_gather | solution.py:598
  28.1 87.2 %all-gather.11.cloned.1.call-start = ((), (), s32[]{:S(2)}) async-start(), calls=%async_computation.2 | async-start | bytes 2785280 | tf_op jit(solution)/shard_map/all_gather | solution.py:614
  41.3 117.4 %all-gather.13.cloned.1.call-start = ((), (), s32[]{:S(2)}) async-start(), calls=%async_computation.3 | async-start | bytes 1310720 | tf_op jit(solution)/shard_map/all_gather | solution.py:642
  41.3 21.3 %collective-permute-start.3 = (bf16[8,256,128]{2,1,0:T(8,128)(2,1)}, bf16[8,256,128]{2,1,0:T(8,128)(2,1)S(1)}, u32[]{:S(2)}, u32[]{:S(2)}) collective-permute-start(bf16[8,256,128]{2,1,0:T(8,128)(2,1)} %get-tuple-element.44.refs_0_), channel_id=1, source_target_pairs={{0,16},{4,20},{8,24},{12,28},{16,0},{20,4},{24,8},{28,12},{1,17},{... | collective-permute-start | bytes 1572872 | tf_op jit(solution)/shard_map/ppermute | solution.py:580
  42.9 19.7 %collective-permute-start.1 = (bf16[8,256,128]{2,1,0:T(8,128)(2,1)}, bf16[8,256,128]{2,1,0:T(8,128)(2,1)S(1)}, u32[]{:S(2)}, u32[]{:S(2)}) collective-permute-start(bf16[8,256,128]{2,1,0:T(8,128)(2,1)} %get-tuple-element.44.refs_0_), channel_id=1, source_target_pairs={{0,8},{4,12},{8,0},{12,4},{16,24},{20,28},{24,16},{28,20},{1,9},{5... | collective-permute-start | bytes 1572872 | tf_op jit(solution)/shard_map/ppermute | solution.py:580
  44.4 20.5 %collective-permute-start.4 = (bf16[8,256,128]{2,1,0:T(8,128)(2,1)}, bf16[8,256,128]{2,1,0:T(8,128)(2,1)}, u32[]{:S(2)}, u32[]{:S(2)}) collective-permute-start(bf16[8,256,128]{2,1,0:T(8,128)(2,1)} %get-tuple-element.45.refs_1_), channel_id=1, source_target_pairs={{0,16},{4,20},{8,24},{12,28},{16,0},{20,4},{24,8},{28,12},{1,17},{... | collective-permute-start | bytes 1572872 | tf_op jit(solution)/shard_map/ppermute | solution.py:580
  44.9 21.3 %collective-permute-start.2 = (bf16[8,256,128]{2,1,0:T(8,128)(2,1)}, bf16[8,256,128]{2,1,0:T(8,128)(2,1)}, u32[]{:S(2)}, u32[]{:S(2)}) collective-permute-start(bf16[8,256,128]{2,1,0:T(8,128)(2,1)} %get-tuple-element.45.refs_1_), channel_id=1, source_target_pairs={{0,8},{4,12},{8,0},{12,4},{16,24},{20,28},{24,16},{28,20},{1,9},{5... | collective-permute-start | bytes 1572872 | tf_op jit(solution)/shard_map/ppermute | solution.py:580
  66.2 23.5 %collective-permute-start.7 = (bf16[4,1024,128]{2,1,0:T(8,128)(2,1)}, bf16[4,1024,128]{2,1,0:T(8,128)(2,1)}, u32[]{:S(2)}, u32[]{:S(2)}) collective-permute-start(bf16[4,1024,128]{2,1,0:T(8,128)(2,1)} %bitcast.48), channel_id=1, source_target_pairs={{0,4},{4,0},{8,12},{12,8},{16,20},{20,16},{24,28},{28,24},{1,5},{5... | collective-permute-start | bytes 3145736 | tf_op jit(solution)/shard_map/ppermute | solution.py:580
  66.2 23.5 %collective-permute-start.5 = (bf16[8,256,128]{2,1,0:T(8,128)(2,1)S(1)}, bf16[8,256,128]{2,1,0:T(8,128)(2,1)}, u32[]{:S(2)}, u32[]{:S(2)}) collective-permute-start(bf16[8,256,128]{2,1,0:T(8,128)(2,1)S(1)} %collective-permute-done.3.refs_2_), channel_id=1, source_target_pairs={{0,8},{4,12},{8,0},{12,4},{16,24},{20,28},{24,16},{28,20},{1,9},{5... | collective-permute-start | bytes 1572872 | tf_op jit(solution)/shard_map/ppermute | solution.py:580
  69.5 20.2 %collective-permute-start.6 = (bf16[8,256,128]{2,1,0:T(8,128)(2,1)}, bf16[8,256,128]{2,1,0:T(8,128)(2,1)}, u32[]{:S(2)}, u32[]{:S(2)}) collective-permute-start(bf16[8,256,128]{2,1,0:T(8,128)(2,1)} %collective-permute-done.2.refs_1_), channel_id=1, source_target_pairs={{0,16},{4,20},{8,24},{12,28},{16,0},{20,4},{24,8},{28,12},{1,17},{... | collective-permute-start | bytes 1572872 | tf_op jit(solution)/shard_map/ppermute | solution.py:580
  89.7 24.1 %collective-permute-start.9 = (bf16[4,1024,128]{2,1,0:T(8,128)(2,1)}, bf16[4,1024,128]{2,1,0:T(8,128)(2,1)S(1)}, u32[]{:S(2)}, u32[]{:S(2)}) collective-permute-start(bf16[4,1024,128]{2,1,0:T(8,128)(2,1)} %bitcast.49), channel_id=1, source_target_pairs={{0,16},{4,20},{8,24},{12,28},{16,0},{20,4},{24,8},{28,12},{1,17},{... | collective-permute-start | bytes 3145736 | tf_op jit(solution)/shard_map/ppermute | solution.py:580
  89.8 25.4 %collective-permute-start.8 = (bf16[4,1024,128]{2,1,0:T(8,128)(2,1)}, bf16[4,1024,128]{2,1,0:T(8,128)(2,1)}, u32[]{:S(2)}, u32[]{:S(2)}) collective-permute-start(bf16[4,1024,128]{2,1,0:T(8,128)(2,1)} %bitcast.50), channel_id=1, source_target_pairs={{0,8},{4,12},{8,0},{12,4},{16,24},{20,28},{24,16},{28,20},{1,9},{5... | collective-permute-start | bytes 3145736 | tf_op jit(solution)/shard_map/ppermute | solution.py:580
  115.3 2.5 %collective-permute-start.10 = (bf16[1024,128]{1,0:T(8,128)(2,1)}, bf16[1024,128]{1,0:T(8,128)(2,1)S(1)}, u32[]{:S(2)}, u32[]{:S(2)}) collective-permute-start(bf16[1024,128]{1,0:T(8,128)(2,1)} %attend.6), channel_id=1, source_target_pairs={{0,4},{4,0},{8,12},{12,8},{16,20},{20,16},{24,28},{28,24},{1,5},{5... | collective-permute-start | bytes 786440 | tf_op jit(solution)/shard_map/ppermute | solution.py:580
  116.0 42.7 %collective-permute-start.15 = (bf16[4,272,1024]{2,1,0:T(8,128)(2,1)}, bf16[4,272,1024]{2,1,0:T(8,128)(2,1)}, u32[]{:S(2)}, u32[]{:S(2)}) collective-permute-start(bf16[4,272,1024]{2,1,0:T(8,128)(2,1)} %bitcast.40), channel_id=1, source_target_pairs={{0,4},{4,0},{8,12},{12,8},{16,20},{20,16},{24,28},{28,24},{1,5},{5... | collective-permute-start | bytes 6684680 | tf_op jit(solution)/shard_map/ppermute | solution.py:580
  118.5 61.5 %all-gather.15.cloned.1.call-start = ((), (), s32[]{:S(2)}) async-start(), calls=%async_computation.4 | async-start | bytes 1310720 | tf_op jit(solution)/shard_map/all_gather | solution.py:646
  120.1 38.5 %collective-permute-start.14 = (bf16[4,128,1024]{2,1,0:T(8,128)(2,1)S(1)}, bf16[4,128,1024]{2,1,0:T(8,128)(2,1)}, u32[]{:S(2)}, u32[]{:S(2)}) collective-permute-start(bf16[4,128,1024]{2,1,0:T(8,128)(2,1)S(1)} %slice.25), channel_id=1, source_target_pairs={{0,16},{4,20},{8,24},{12,28},{16,0},{20,4},{24,8},{28,12},{1,17},{... | collective-permute-start | bytes 3145736 | tf_op jit(solution)/shard_map/ppermute | solution.py:580
  122.2 36.5 %collective-permute-start.13 = (bf16[4,128,1024]{2,1,0:T(8,128)(2,1)S(1)}, bf16[4,128,1024]{2,1,0:T(8,128)(2,1)}, u32[]{:S(2)}, u32[]{:S(2)}) collective-permute-start(bf16[4,128,1024]{2,1,0:T(8,128)(2,1)S(1)} %slice.25), channel_id=1, source_target_pairs={{0,8},{4,12},{8,0},{12,4},{16,24},{20,28},{24,16},{28,20},{1,9},{5... | collective-permute-start | bytes 3145736 | tf_op jit(solution)/shard_map/ppermute | solution.py:580
  126.8 31.8 %collective-permute-start.11 = (bf16[4,512,128]{2,1,0:T(8,128)(2,1)}, bf16[4,512,128]{2,1,0:T(8,128)(2,1)}, u32[]{:S(2)}, u32[]{:S(2)}) collective-permute-start(bf16[4,512,128]{2,1,0:T(8,128)(2,1)} %slice.23), channel_id=1, source_target_pairs={{0,8},{4,12},{8,0},{12,4},{16,24},{20,28},{24,16},{28,20},{1,9},{5... | collective-permute-start | bytes 1572872 | tf_op jit(solution)/shard_map/ppermute | solution.py:580
  126.9 31.7 %collective-permute-start.12 = (bf16[4,512,128]{2,1,0:T(8,128)(2,1)}, bf16[4,512,128]{2,1,0:T(8,128)(2,1)}, u32[]{:S(2)}, u32[]{:S(2)}) collective-permute-start(bf16[4,512,128]{2,1,0:T(8,128)(2,1)} %slice.24), channel_id=1, source_target_pairs={{0,16},{4,20},{8,24},{12,28},{16,0},{20,4},{24,8},{28,12},{1,17},{... | collective-permute-start | bytes 1572872 | tf_op jit(solution)/shard_map/ppermute | solution.py:580
  152.4 28.1 %copy-start.8 = (f32[768]{0:T(1024)S(1)}, f32[768]{0:T(1024)}, u32[]{:S(2)}) copy-start(f32[768]{0:T(1024)} %param.32) | copy-start | bytes 9220
  159.8 13.1 %collective-permute-start.17 = (bf16[4,64,1024]{2,1,0:T(8,128)(2,1)S(1)}, bf16[4,64,1024]{2,1,0:T(8,128)(2,1)S(1)}, u32[]{:S(2)}, u32[]{:S(2)}) collective-permute-start(bf16[4,64,1024]{2,1,0:T(8,128)(2,1)S(1)} %slice.27), channel_id=1, source_target_pairs={{0,8},{4,12},{8,0},{12,4},{16,24},{20,28},{24,16},{28,20},{1,9},{5... | collective-permute-start | bytes 1572872 | tf_op jit(solution)/shard_map/ppermute | solution.py:580
  162.6 12.6 %collective-permute-start.16 = (bf16[4,64,1024]{2,1,0:T(8,128)(2,1)S(1)}, bf16[4,64,1024]{2,1,0:T(8,128)(2,1)S(1)}, u32[]{:S(2)}, u32[]{:S(2)}) collective-permute-start(bf16[4,64,1024]{2,1,0:T(8,128)(2,1)S(1)} %slice.26), channel_id=1, source_target_pairs={{0,16},{4,20},{8,24},{12,28},{16,0},{20,4},{24,8},{28,12},{1,17},{... | collective-permute-start | bytes 1572872 | tf_op jit(solution)/shard_map/ppermute | solution.py:580
  163.1 12.2 %collective-permute-start.20 = (bf16[4,512,128]{2,1,0:T(8,128)(2,1)}, bf16[4,512,128]{2,1,0:T(8,128)(2,1)S(1)}, u32[]{:S(2)}, u32[]{:S(2)}) collective-permute-start(bf16[4,512,128]{2,1,0:T(8,128)(2,1)} %collective-permute-done.11.refs_10_), channel_id=1, source_target_pairs={{0,4},{4,0},{8,12},{12,8},{16,20},{20,16},{24,28},{28,24},{1,5},{5... | collective-permute-start | bytes 1572872 | tf_op jit(solution)/shard_map/ppermute | solution.py:580
  163.1 16.9 %collective-permute-start.18 = (bf16[4,1024,128]{2,1,0:T(8,128)(2,1)}, bf16[4,1024,128]{2,1,0:T(8,128)(2,1)S(1)}, u32[]{:S(2)}, u32[]{:S(2)}) collective-permute-start(bf16[4,1024,128]{2,1,0:T(8,128)(2,1)} %collective-permute-done.8.refs_8_), channel_id=1, source_target_pairs={{0,4},{4,0},{8,12},{12,8},{16,20},{20,16},{24,28},{28,24},{1,5},{5... | collective-permute-start | bytes 3145736 | tf_op jit(solution)/shard_map/ppermute | solution.py:580
  163.6 18.2 %collective-permute-start.22 = (bf16[4,128,1024]{2,1,0:T(8,128)(2,1)}, bf16[4,128,1024]{2,1,0:T(8,128)(2,1)}, u32[]{:S(2)}, u32[]{:S(2)}) collective-permute-start(bf16[4,128,1024]{2,1,0:T(8,128)(2,1)} %collective-permute-done.13.refs_13_), channel_id=1, source_target_pairs={{0,4},{4,0},{8,12},{12,8},{16,20},{20,16},{24,28},{28,24},{1,5},{5... | collective-permute-start | bytes 3145736 | tf_op jit(solution)/shard_map/ppermute | solution.py:580
  172.9 7.0 %collective-permute-start.21 = (bf16[4,512,128]{2,1,0:T(8,128)(2,1)}, bf16[4,512,128]{2,1,0:T(8,128)(2,1)}, u32[]{:S(2)}, u32[]{:S(2)}) collective-permute-start(bf16[4,512,128]{2,1,0:T(8,128)(2,1)} %collective-permute-done.12.refs_11_), channel_id=1, source_target_pairs={{0,4},{4,0},{8,12},{12,8},{16,20},{20,16},{24,28},{28,24},{1,5},{5... | collective-permute-start | bytes 1572872 | tf_op jit(solution)/shard_map/ppermute | solution.py:580
  175.2 6.5 %collective-permute-start.19 = (bf16[4,1024,128]{2,1,0:T(8,128)(2,1)S(1)}, bf16[4,1024,128]{2,1,0:T(8,128)(2,1)}, u32[]{:S(2)}, u32[]{:S(2)}) collective-permute-start(bf16[4,1024,128]{2,1,0:T(8,128)(2,1)S(1)} %copy-done.5), channel_id=1, source_target_pairs={{0,4},{4,0},{8,12},{12,8},{16,20},{20,16},{24,28},{28,24},{1,5},{5... | collective-permute-start | bytes 3145736 | tf_op jit(solution)/shard_map/ppermute | solution.py:580
  176.8 4.9 %collective-permute-start.23 = (bf16[4,128,1024]{2,1,0:T(8,128)(2,1)}, bf16[4,128,1024]{2,1,0:T(8,128)(2,1)}, u32[]{:S(2)}, u32[]{:S(2)}) collective-permute-start(bf16[4,128,1024]{2,1,0:T(8,128)(2,1)} %collective-permute-done.14.refs_14_), channel_id=1, source_target_pairs={{0,4},{4,0},{8,12},{12,8},{16,20},{20,16},{24,28},{28,24},{1,5},{5... | collective-permute-start | bytes 3145736 | tf_op jit(solution)/shard_map/ppermute | solution.py:580
  180.0 2.3 %collective-permute-start.24 = (bf16[4,64,1024]{2,1,0:T(8,128)(2,1)}, bf16[4,64,1024]{2,1,0:T(8,128)(2,1)}, u32[]{:S(2)}, u32[]{:S(2)}) collective-permute-start(bf16[4,64,1024]{2,1,0:T(8,128)(2,1)} %copy-done.11), channel_id=1, source_target_pairs={{0,4},{4,0},{8,12},{12,8},{16,20},{20,16},{24,28},{28,24},{1,5},{5... | collective-permute-start | bytes 1572872 | tf_op jit(solution)/shard_map/ppermute | solution.py:580
  180.0 3.0 %collective-permute-start.25 = (bf16[4,64,1024]{2,1,0:T(8,128)(2,1)}, bf16[4,64,1024]{2,1,0:T(8,128)(2,1)}, u32[]{:S(2)}, u32[]{:S(2)}) collective-permute-start(bf16[4,64,1024]{2,1,0:T(8,128)(2,1)} %copy-done.12), channel_id=1, source_target_pairs={{0,4},{4,0},{8,12},{12,8},{16,20},{20,16},{24,28},{28,24},{1,5},{5... | collective-permute-start | bytes 1572872 | tf_op jit(solution)/shard_map/ppermute | solution.py:580
  (13 other events, 78.8 us)
Sparse Core Ops, SparseCore 0:
  28.2 27.0 all-gather.8
  56.8 47.8 all-gather.10
  118.6 27.9 all-gather.12
  152.5 27.4 all-gather.14

commit v12 on v11

--- a/solution.py
+++ b/solution.py
@@ -634,9 +634,6 @@
         second = rest[:, :unit]
         second_x = move(second, across)
         second_y = move(second, along)
-        cut = width // 2
-        first_d0 = move(first_y[:, :cut], across)
-        first_d1 = move(first_x[:, cut:], along)
         rest_other = move(rest, swap)
         theirs, state = lax.optimization_barrier((move(theirs, swap), state))
         theirs = lax.all_gather(theirs, "mp", axis=0)
@@ -644,14 +641,12 @@
             own, jnp.stack(near + far), q, [*kv_x, *kv_y, kv_d0, kv_d1], state, True, pages
         )
         mine_all = lax.all_gather(mine, "mp", axis=0)
-        theirs, _, first_x, first_y, first_d0, first_d1, second_x, second_y, rest_other = (
-            lax.optimization_barrier(
-                (
-                    theirs, mine, first_x, first_y, first_d0, first_d1, second_x, second_y,
-                    rest_other,
-                )
-            )
-        )
+        theirs, _, first_x, first_y, second_x, second_y, rest_other = lax.optimization_barrier(
+            (theirs, mine, first_x, first_y, second_x, second_y, rest_other)
+        )
+        cut = width // 2
+        first_d0 = move(first_y[:, :cut], across)
+        first_d1 = move(first_x[:, cut:], along)
         half = unit // 2
         second_d0 = move(second_y[:, :half], across)
         second_d1 = move(second_x[:, half:], along)

time: 227 us -> 236 us (1.040)
  Pallas kernels: 116 us -> 126 us
  starting transfers between devices: 25.6 us -> 29.5 us
    pallas_call x4, Pallas kernels: 72.8 us -> 82.1 us  [attend(): pl.pallas_call(functools.partial(attend_kernel, requests=requests, slots=...]
    ppermute x26, starting transfers between devices: 19.3 us -> 23.2 us  [local(): move = lambda value, pairs: lax.ppermute(value, 'dp', pairs)]
    all_gather x1, waiting for transfers between devices: 3.14 us -> 0.01 us  [local(): mine_all = lax.all_gather(mine, 'mp', axis=0)]
    unnamed x30 -> x28, local copies, waits for them, and re-layouts: 4.89 us -> 5.37 us
  transfers between devices with their start and end apart: 31 -> 31, of which waited for: 12 -> 11; matrix products, arithmetic and copies ran while one was open for 10% -> 9% of each run, Pallas kernels for 36% -> 39%
where the time goes in v12:
time: 236 us; the launch traced here: 235 us
  Pallas kernels  126 us (53%)
  waiting for transfers between devices  42.2 us (18%)
  starting transfers between devices  29.5 us (12%)
  local copies, waits for them, and re-layouts  17.5 us (7%)
  between operations  14.8 us (6%)
  other arithmetic  5.41 us (2%)
    pallas_call x4, Pallas kernels, attend(): pl.pallas_call(functools.partial(attend_kernel, requests=requests, slots=...  82.1 us
    ppermute x26, waiting for transfers between devices, local(): move = lambda value, pairs: lax.ppermute(value, 'dp', pairs)  36.8 us
    pallas_call x1, Pallas kernels, finish(): pl.pallas_call(functools.partial(finish_kernel, parts=len(outs), counts=t...  34.9 us
    ppermute x26, starting transfers between devices, local(): move = lambda value, pairs: lax.ppermute(value, 'dp', pairs)  23.2 us
    pallas_call x1, Pallas kernels, project(): pl.pallas_call(functools.partial(project_kernel, requests=counts.shape[0]...  8.54 us
    all_to_all x1, starting transfers between devices, local(): got = lax.all_to_all(sent, 'mp', split_axis=1, concat_axis=0, tiled=True)  5.95 us
    unnamed x28, local copies, waits for them, and re-layouts  5.37 us
    all_to_all x1, waiting for transfers between devices, local(): got = lax.all_to_all(sent, 'mp', split_axis=1, concat_axis=0, tiled=True)  5.24 us
  transfers between devices with their start and end apart: 31, of which 11 were waited for; matrix products, arithmetic and copies ran while one was open for 9% of the time, Pallas kernels for 39%

profile of v12, /device:TPU:0, one launch (start us, length us, event | category | flops | bytes accessed | tf_op | source)
XLA Modules:
  0.0 235.0 jit_solution(17864290993215231492)
XLA Ops:
  7.7 1.9 fusion.6
  10.3 1.1 dynamic-slice_bitcast_fusion.1
  12.2 5.9 %all-to-all-start = ((bf16[16,4,1792]{2,0,1:T(8,128)(2,1)}), bf16[16,4,1792]{2,0,1:T(8,128)(2,1)S(1)}, u32[]{:S(2)}, u32[]{:S(2)}) async-start(bf16[16,4,1792]{2,0,1:T(8,128)(2,1)} %pad_maximum_fusion.1), calls=%async_computation | async-start | bytes 458752 | tf_op jit(solution)/shard_map/all_to_all | solution.py:560
  18.2 1.7 copy.29
  20.0 1.7 constant_dynamic-slice_fusion.2
  21.7 5.2 %all-to-all-done = bf16[16,4,1792]{2,0,1:T(8,128)(2,1)S(1)} async-done(((bf16[16,4,1792]{2,0,1:T(8,128)(2,1)}), bf16[16,4,1792]{2,0,1:T(8,128)(2,1)S(1)}, u32[]{:S(2)}, u32[]{:S(2)}) %all-to-all-start) | async-done | bytes 229408 | tf_op jit(solution)/shard_map/all_to_all | solution.py:560
  28.1 1.2 copy.35.refs_2_
  30.9 8.5 %project.1 = (bf16[2048,128]{1,0:T(8,128)(2,1)}, bf16[8,256,128]{2,1,0:T(8,128)(2,1)}, bf16[8,256,128]{2,1,0:T(8,128)(2,1)}) custom-call(s32[4]{0:T(128)} %counts.9, s32[64]{0:T(128)} %table.9, s32[4]{0:T(128)} %get-tuple-element.81.owners, s32[2]{0:T(128)} %pad_add_fusion.2.bases.q_bases.kv_bases, bf16[1024,1024]{1,0:T(8,128)(2,1)} %x_ref.1, ...), custom_call_target="tpu_custom_call" | custom-call | flops 1610612736 | bytes 5767168 | tf_op jit(solution)/shard_map/project/pallas_call | solution.py:109
  41.4 1.6 collective-permute-start.3
  42.9 1.5 collective-permute-start.1
  45.5 21.6 %attend.4 = (f32[2048,128]{1,0:T(8,128)}, f32[2048,128]{1,0:T(8,128)}) custom-call(s32[4]{0:T(128)} %counts.9, s32[64]{0:T(128)} %table.9, s32[2]{0:T(128)} %pad_add_fusion.2.bases.q_bases.kv_bases, s32[2]{0:T(128)} %pad_add_fusion.2.bases.q_bases.kv_bases, bf16[2048,128]{1,0:T(8,128)(2,1)} %get-tuple-element.41.q_hbm, ...), custom_call_target="tpu_custom_call" | custom-call | flops 262144 | bytes 1048576 | tf_op jit(solution)/shard_map/attend/pallas_call | solution.py:315
  68.7 21.3 %attend.5 = (f32[1024,128]{1,0:T(8,128)}, f32[1024,128]{1,0:T(8,128)}) custom-call(s32[4]{0:T(128)} %counts.9, s32[64]{0:T(128)} %table.9, s32[1]{0:T(128)} %bitcast.3.q_bases, s32[4]{0:T(128)} %get-tuple-element.85.kv_bases, bf16[2048,128]{1,0:T(8,128)(2,1)} %get-tuple-element.41.q_hbm, bf16[8,256,128]{2,1,0:T(8,128)(2,1)} %copy-done.2, ...), custom_call_target="tpu_custom_call" | custom-call | flops 131072 | bytes 524288 | tf_op jit(solution)/shard_map/attend/pallas_call | solution.py:315
  90.0 1.1 collective-permute-start.9
  91.8 14.2 %attend.6 = bf16[1024,128]{1,0:T(8,128)(2,1)} custom-call(s32[4]{0:T(128)} %counts.9, s32[64]{0:T(128)} %table.9, s32[1]{0:T(128)} %bitcast.3.q_bases, s32[2]{0:T(128)} %pad_add_fusion.1.kv_bases, bf16[2048,128]{1,0:T(8,128)(2,1)} %get-tuple-element.41.q_hbm, bf16[8,256,128]{2,1,0:T(8,128)(2,1)} %collective-permute-done.5.refs_0_.refs_4_, ...), custom_call_target="tpu_custom_call" | custom-call | flops 131072 | bytes 524288 | tf_op jit(solution)/shard_map/attend/pallas_call | solution.py:315
  106.0 7.2 %collective-permute-done.9.refs_9_ = bf16[4,1024,128]{2,1,0:T(8,128)(2,1)} collective-permute-done((bf16[4,1024,128]{2,1,0:T(8,128)(2,1)}, bf16[4,1024,128]{2,1,0:T(8,128)(2,1)}, u32[]{:S(2)}, u32[]{:S(2)}) %collective-permute-start.9) | collective-permute-done | bytes 1048608 | tf_op jit(solution)/shard_map/ppermute | solution.py:580
  114.3 4.1 %collective-permute-done.10 = bf16[1024,128]{1,0:T(8,128)(2,1)S(1)} collective-permute-done((bf16[1024,128]{1,0:T(8,128)(2,1)}, bf16[1024,128]{1,0:T(8,128)(2,1)S(1)}, u32[]{:S(2)}, u32[]{:S(2)}) %collective-permute-start.10) | collective-permute-done | bytes 262176 | tf_op jit(solution)/shard_map/ppermute | solution.py:580
  119.3 1.3 slice.23
  120.6 1.2 collective-permute-start.12
  121.8 1.7 collective-permute-start.11
  124.1 25.0 %attend.7 = bf16[1024,128]{1,0:T(8,128)(2,1)} custom-call(s32[4]{0:T(128)} %counts.9, s32[64]{0:T(128)} %table.9, s32[1]{0:T(128)} %bitcast.6.q_bases, s32[6]{0:T(128)} %stack.85.kv_bases, bf16[2048,128]{1,0:T(8,128)(2,1)} %get-tuple-element.41.q_hbm, bf16[8,256,128]{2,1,0:T(8,128)(2,1)} %copy-done.2, bf16[8,256,128]{2,1,0:T(8,128)(2,1)} %collective-permute-done.2.refs_1_, ...), custom_call_target="tpu_custom_call" | custom-call | flops 131072 | bytes 524288 | tf_op jit(solution)/shard_map/attend/pallas_call | solution.py:315
  149.2 1.2 slice.27
  150.5 1.1 slice.25
  151.6 2.1 collective-permute-start.15
  153.6 1.1 slice.24
  154.7 2.3 collective-permute-start.22
  157.2 6.2 %collective-permute-done.17.refs_15_ = bf16[4,64,1024]{2,1,0:T(8,128)(2,1)S(1)} collective-permute-done((bf16[4,64,1024]{2,1,0:T(8,128)(2,1)S(1)}, bf16[4,64,1024]{2,1,0:T(8,128)(2,1)S(1)}, u32[]{:S(2)}, u32[]{:S(2)}) %collective-permute-start.17) | collective-permute-done | bytes 524320 | tf_op jit(solution)/shard_map/ppermute | solution.py:580
  164.2 4.0 %collective-permute-start.19 = (bf16[4,1024,128]{2,1,0:T(8,128)(2,1)}, bf16[4,1024,128]{2,1,0:T(8,128)(2,1)}, u32[]{:S(2)}, u32[]{:S(2)}) collective-permute-start(bf16[4,1024,128]{2,1,0:T(8,128)(2,1)} %collective-permute-done.9.refs_9_), channel_id=1, source_target_pairs={{0,4},{4,0},{8,12},{12,8},{16,20},{20,16},{24,28},{28,24},{1,5},{5... | collective-permute-start | bytes 3145736 | tf_op jit(solution)/shard_map/ppermute | solution.py:580
  168.2 6.4 %collective-permute-done.15.refs_10_ = bf16[4,512,128]{2,1,0:T(8,128)(2,1)S(1)} collective-permute-done((bf16[4,512,128]{2,1,0:T(8,128)(2,1)S(1)}, bf16[4,512,128]{2,1,0:T(8,128)(2,1)S(1)}, u32[]{:S(2)}, u32[]{:S(2)}) %collective-permute-start.15) | collective-permute-done | bytes 524320 | tf_op jit(solution)/shard_map/ppermute | solution.py:580
  176.2 2.1 collective-permute-start.23
  178.3 10.0 %collective-permute-done.16.refs_11_ = bf16[4,512,128]{2,1,0:T(8,128)(2,1)} collective-permute-done((bf16[4,512,128]{2,1,0:T(8,128)(2,1)S(1)}, bf16[4,512,128]{2,1,0:T(8,128)(2,1)}, u32[]{:S(2)}, u32[]{:S(2)}) %collective-permute-start.16) | collective-permute-done | bytes 524320 | tf_op jit(solution)/shard_map/ppermute | solution.py:580
  188.4 1.0 collective-permute-start.24
  193.5 34.9 %finish.1 = (bf16[256,1024]{1,0:T(8,128)(2,1)}, bf16[1024,768]{1,0:T(8,128)(2,1)}) custom-call(s32[3]{0:T(128)} %pad_add_fusion.place, bf16[1024,1024]{1,0:T(8,128)(2,1)} %x_ref.1, bf16[4,1024,128]{2,1,0:T(8,128)(2,1)} %bitcast.53, bf16[4,1024,128]{2,1,0:T(8,128)(2,1)} %bitcast.52, bf16[4,272,1024]{2,1,0:T(8,128)(2,1)} %bitcast.42, ...), custom_call_target="tpu_custom_call" | custom-call | flops 17179869184 | bytes 16777216 | tf_op jit(solution)/shard_map/finish/pallas_call | solution.py:458
  (103 shorter events, 18.8 us)
Async XLA Ops:
  7.2 23.7 %collective-permute-start = (bf16[1024,1024]{1,0:T(8,128)(2,1)}, bf16[1024,1024]{1,0:T(8,128)(2,1)}, u32[]{:S(2)}, u32[]{:S(2)}) collective-permute-start(bf16[1024,1024]{1,0:T(8,128)(2,1)} %x_ref.1), channel_id=1, source_target_pairs={{0,4},{4,0},{8,12},{12,8},{16,20},{20,16},{24,28},{28,24},{1,5},{5... | collective-permute-start | bytes 6291464 | tf_op jit(solution)/shard_map/ppermute | solution.py:580
  12.2 14.7 %all-to-all-start = ((bf16[16,4,1792]{2,0,1:T(8,128)(2,1)}), bf16[16,4,1792]{2,0,1:T(8,128)(2,1)S(1)}, u32[]{:S(2)}, u32[]{:S(2)}) async-start(bf16[16,4,1792]{2,0,1:T(8,128)(2,1)} %pad_maximum_fusion.1), calls=%async_computation | async-start | bytes 458752 | tf_op jit(solution)/shard_map/all_to_all | solution.py:560
  18.2 49.0 %all-gather.9.cloned.1.call-start = ((), (), s32[]{:S(2)}) async-start(), calls=%async_computation.1 | async-start | bytes 1310720 | tf_op jit(solution)/shard_map/all_gather | solution.py:598
  28.1 85.7 %all-gather.11.cloned.1.call-start = ((), (), s32[]{:S(2)}) async-start(), calls=%async_computation.2 | async-start | bytes 2785280 | tf_op jit(solution)/shard_map/all_gather | solution.py:614
  41.3 107.9 %all-gather.13.cloned.1.call-start = ((), (), s32[]{:S(2)}) async-start(), calls=%async_computation.3 | async-start | bytes 1310720 | tf_op jit(solution)/shard_map/all_gather | solution.py:639
  41.4 25.8 %collective-permute-start.3 = (bf16[8,256,128]{2,1,0:T(8,128)(2,1)}, bf16[8,256,128]{2,1,0:T(8,128)(2,1)S(1)}, u32[]{:S(2)}, u32[]{:S(2)}) collective-permute-start(bf16[8,256,128]{2,1,0:T(8,128)(2,1)} %get-tuple-element.42.refs_0_), channel_id=1, source_target_pairs={{0,16},{4,20},{8,24},{12,28},{16,0},{20,4},{24,8},{28,12},{1,17},{... | collective-permute-start | bytes 1572872 | tf_op jit(solution)/shard_map/ppermute | solution.py:580
  42.9 24.2 %collective-permute-start.1 = (bf16[8,256,128]{2,1,0:T(8,128)(2,1)}, bf16[8,256,128]{2,1,0:T(8,128)(2,1)S(1)}, u32[]{:S(2)}, u32[]{:S(2)}) collective-permute-start(bf16[8,256,128]{2,1,0:T(8,128)(2,1)} %get-tuple-element.42.refs_0_), channel_id=1, source_target_pairs={{0,8},{4,12},{8,0},{12,4},{16,24},{20,28},{24,16},{28,20},{1,9},{5... | collective-permute-start | bytes 1572872 | tf_op jit(solution)/shard_map/ppermute | solution.py:580
  44.4 22.7 %collective-permute-start.4 = (bf16[8,256,128]{2,1,0:T(8,128)(2,1)}, bf16[8,256,128]{2,1,0:T(8,128)(2,1)}, u32[]{:S(2)}, u32[]{:S(2)}) collective-permute-start(bf16[8,256,128]{2,1,0:T(8,128)(2,1)} %get-tuple-element.43.refs_1_), channel_id=1, source_target_pairs={{0,16},{4,20},{8,24},{12,28},{16,0},{20,4},{24,8},{28,12},{1,17},{... | collective-permute-start | bytes 1572872 | tf_op jit(solution)/shard_map/ppermute | solution.py:580
  44.9 22.2 %collective-permute-start.2 = (bf16[8,256,128]{2,1,0:T(8,128)(2,1)}, bf16[8,256,128]{2,1,0:T(8,128)(2,1)}, u32[]{:S(2)}, u32[]{:S(2)}) collective-permute-start(bf16[8,256,128]{2,1,0:T(8,128)(2,1)} %get-tuple-element.43.refs_1_), channel_id=1, source_target_pairs={{0,8},{4,12},{8,0},{12,4},{16,24},{20,28},{24,16},{28,20},{1,9},{5... | collective-permute-start | bytes 1572872 | tf_op jit(solution)/shard_map/ppermute | solution.py:580
  67.2 22.8 %collective-permute-start.7 = (bf16[4,1024,128]{2,1,0:T(8,128)(2,1)}, bf16[4,1024,128]{2,1,0:T(8,128)(2,1)}, u32[]{:S(2)}, u32[]{:S(2)}) collective-permute-start(bf16[4,1024,128]{2,1,0:T(8,128)(2,1)} %bitcast.48), channel_id=1, source_target_pairs={{0,4},{4,0},{8,12},{12,8},{16,20},{20,16},{24,28},{28,24},{1,5},{5... | collective-permute-start | bytes 3145736 | tf_op jit(solution)/shard_map/ppermute | solution.py:580
  67.3 22.7 %collective-permute-start.5 = (bf16[8,256,128]{2,1,0:T(8,128)(2,1)S(1)}, bf16[8,256,128]{2,1,0:T(8,128)(2,1)}, u32[]{:S(2)}, u32[]{:S(2)}) collective-permute-start(bf16[8,256,128]{2,1,0:T(8,128)(2,1)S(1)} %collective-permute-done.3.refs_2_), channel_id=1, source_target_pairs={{0,8},{4,12},{8,0},{12,4},{16,24},{20,28},{24,16},{28,20},{1,9},{5... | collective-permute-start | bytes 1572872 | tf_op jit(solution)/shard_map/ppermute | solution.py:580
  67.7 22.3 %collective-permute-start.6 = (bf16[8,256,128]{2,1,0:T(8,128)(2,1)}, bf16[8,256,128]{2,1,0:T(8,128)(2,1)}, u32[]{:S(2)}, u32[]{:S(2)}) collective-permute-start(bf16[8,256,128]{2,1,0:T(8,128)(2,1)} %collective-permute-done.2.refs_1_), channel_id=1, source_target_pairs={{0,16},{4,20},{8,24},{12,28},{16,0},{20,4},{24,8},{28,12},{1,17},{... | collective-permute-start | bytes 1572872 | tf_op jit(solution)/shard_map/ppermute | solution.py:580
  90.0 23.2 %collective-permute-start.9 = (bf16[4,1024,128]{2,1,0:T(8,128)(2,1)}, bf16[4,1024,128]{2,1,0:T(8,128)(2,1)}, u32[]{:S(2)}, u32[]{:S(2)}) collective-permute-start(bf16[4,1024,128]{2,1,0:T(8,128)(2,1)} %bitcast.49), channel_id=1, source_target_pairs={{0,16},{4,20},{8,24},{12,28},{16,0},{20,4},{24,8},{28,12},{1,17},{... | collective-permute-start | bytes 3145736 | tf_op jit(solution)/shard_map/ppermute | solution.py:580
  91.1 22.6 %collective-permute-start.8 = (bf16[4,1024,128]{2,1,0:T(8,128)(2,1)}, bf16[4,1024,128]{2,1,0:T(8,128)(2,1)S(1)}, u32[]{:S(2)}, u32[]{:S(2)}) collective-permute-start(bf16[4,1024,128]{2,1,0:T(8,128)(2,1)} %bitcast.50), channel_id=1, source_target_pairs={{0,8},{4,12},{8,0},{12,4},{16,24},{20,28},{24,16},{28,20},{1,9},{5... | collective-permute-start | bytes 3145736 | tf_op jit(solution)/shard_map/ppermute | solution.py:580
  113.8 35.4 %collective-permute-start.13 = (bf16[4,272,1024]{2,1,0:T(8,128)(2,1)}, bf16[4,272,1024]{2,1,0:T(8,128)(2,1)}, u32[]{:S(2)}, u32[]{:S(2)}) collective-permute-start(bf16[4,272,1024]{2,1,0:T(8,128)(2,1)} %bitcast.40), channel_id=1, source_target_pairs={{0,4},{4,0},{8,12},{12,8},{16,20},{20,16},{24,28},{28,24},{1,5},{5... | collective-permute-start | bytes 6684680 | tf_op jit(solution)/shard_map/ppermute | solution.py:580
  113.8 4.6 %collective-permute-start.10 = (bf16[1024,128]{1,0:T(8,128)(2,1)}, bf16[1024,128]{1,0:T(8,128)(2,1)S(1)}, u32[]{:S(2)}, u32[]{:S(2)}) collective-permute-start(bf16[1024,128]{1,0:T(8,128)(2,1)} %attend.6), channel_id=1, source_target_pairs={{0,4},{4,0},{8,12},{12,8},{16,20},{20,16},{24,28},{28,24},{1,5},{5... | collective-permute-start | bytes 786440 | tf_op jit(solution)/shard_map/ppermute | solution.py:580
  119.1 59.3 %all-gather.15.cloned.1.call-start = ((), (), s32[]{:S(2)}) async-start(), calls=%async_computation.4 | async-start | bytes 1310720 | tf_op jit(solution)/shard_map/all_gather | solution.py:643
  120.6 28.5 %collective-permute-start.12 = (bf16[4,128,1024]{2,1,0:T(8,128)(2,1)S(1)}, bf16[4,128,1024]{2,1,0:T(8,128)(2,1)}, u32[]{:S(2)}, u32[]{:S(2)}) collective-permute-start(bf16[4,128,1024]{2,1,0:T(8,128)(2,1)S(1)} %slice.23), channel_id=1, source_target_pairs={{0,16},{4,20},{8,24},{12,28},{16,0},{20,4},{24,8},{28,12},{1,17},{... | collective-permute-start | bytes 3145736 | tf_op jit(solution)/shard_map/ppermute | solution.py:580
  121.8 27.4 %collective-permute-start.11 = (bf16[4,128,1024]{2,1,0:T(8,128)(2,1)S(1)}, bf16[4,128,1024]{2,1,0:T(8,128)(2,1)}, u32[]{:S(2)}, u32[]{:S(2)}) collective-permute-start(bf16[4,128,1024]{2,1,0:T(8,128)(2,1)S(1)} %slice.23), channel_id=1, source_target_pairs={{0,8},{4,12},{8,0},{12,4},{16,24},{20,28},{24,16},{28,20},{1,9},{5... | collective-permute-start | bytes 3145736 | tf_op jit(solution)/shard_map/ppermute | solution.py:580
  150.4 39.6 %copy-start.7 = (f32[768]{0:T(1024)S(1)}, f32[768]{0:T(1024)}, u32[]{:S(2)}) copy-start(f32[768]{0:T(1024)} %param.32) | copy-start | bytes 9220
  150.4 13.0 %collective-permute-start.17 = (bf16[4,64,1024]{2,1,0:T(8,128)(2,1)S(1)}, bf16[4,64,1024]{2,1,0:T(8,128)(2,1)S(1)}, u32[]{:S(2)}, u32[]{:S(2)}) collective-permute-start(bf16[4,64,1024]{2,1,0:T(8,128)(2,1)S(1)} %slice.27), channel_id=1, source_target_pairs={{0,8},{4,12},{8,0},{12,4},{16,24},{20,28},{24,16},{28,20},{1,9},{5... | collective-permute-start | bytes 1572872 | tf_op jit(solution)/shard_map/ppermute | solution.py:580
  151.6 23.1 %collective-permute-start.15 = (bf16[4,512,128]{2,1,0:T(8,128)(2,1)S(1)}, bf16[4,512,128]{2,1,0:T(8,128)(2,1)S(1)}, u32[]{:S(2)}, u32[]{:S(2)}) collective-permute-start(bf16[4,512,128]{2,1,0:T(8,128)(2,1)S(1)} %slice.25), channel_id=1, source_target_pairs={{0,8},{4,12},{8,0},{12,4},{16,24},{20,28},{24,16},{28,20},{1,9},{5... | collective-permute-start | bytes 1572872 | tf_op jit(solution)/shard_map/ppermute | solution.py:580
  154.7 34.6 %collective-permute-start.22 = (bf16[4,128,1024]{2,1,0:T(8,128)(2,1)}, bf16[4,128,1024]{2,1,0:T(8,128)(2,1)S(1)}, u32[]{:S(2)}, u32[]{:S(2)}) collective-permute-start(bf16[4,128,1024]{2,1,0:T(8,128)(2,1)} %collective-permute-done.11.refs_13_), channel_id=1, source_target_pairs={{0,4},{4,0},{8,12},{12,8},{16,20},{20,16},{24,28},{28,24},{1,5},{5... | collective-permute-start | bytes 3145736 | tf_op jit(solution)/shard_map/ppermute | solution.py:580
  157.0 17.9 %collective-permute-start.14 = (bf16[4,64,1024]{2,1,0:T(8,128)(2,1)S(1)}, bf16[4,64,1024]{2,1,0:T(8,128)(2,1)S(1)}, u32[]{:S(2)}, u32[]{:S(2)}) collective-permute-start(bf16[4,64,1024]{2,1,0:T(8,128)(2,1)S(1)} %slice.24), channel_id=1, source_target_pairs={{0,16},{4,20},{8,24},{12,28},{16,0},{20,4},{24,8},{28,12},{1,17},{... | collective-permute-start | bytes 1572872 | tf_op jit(solution)/shard_map/ppermute | solution.py:580
  157.0 32.4 %collective-permute-start.18 = (bf16[4,1024,128]{2,1,0:T(8,128)(2,1)S(1)}, bf16[4,1024,128]{2,1,0:T(8,128)(2,1)}, u32[]{:S(2)}, u32[]{:S(2)}) collective-permute-start(bf16[4,1024,128]{2,1,0:T(8,128)(2,1)S(1)} %copy-done.4), channel_id=1, source_target_pairs={{0,4},{4,0},{8,12},{12,8},{16,20},{20,16},{24,28},{28,24},{1,5},{5... | collective-permute-start | bytes 3145736 | tf_op jit(solution)/shard_map/ppermute | solution.py:580
  164.2 25.7 %collective-permute-start.19 = (bf16[4,1024,128]{2,1,0:T(8,128)(2,1)}, bf16[4,1024,128]{2,1,0:T(8,128)(2,1)}, u32[]{:S(2)}, u32[]{:S(2)}) collective-permute-start(bf16[4,1024,128]{2,1,0:T(8,128)(2,1)} %collective-permute-done.9.refs_9_), channel_id=1, source_target_pairs={{0,4},{4,0},{8,12},{12,8},{16,20},{20,16},{24,28},{28,24},{1,5},{5... | collective-permute-start | bytes 3145736 | tf_op jit(solution)/shard_map/ppermute | solution.py:580
  174.6 13.8 %collective-permute-start.16 = (bf16[4,512,128]{2,1,0:T(8,128)(2,1)S(1)}, bf16[4,512,128]{2,1,0:T(8,128)(2,1)}, u32[]{:S(2)}, u32[]{:S(2)}) collective-permute-start(bf16[4,512,128]{2,1,0:T(8,128)(2,1)S(1)} %slice.26), channel_id=1, source_target_pairs={{0,16},{4,20},{8,24},{12,28},{16,0},{20,4},{24,8},{28,12},{1,17},{... | collective-permute-start | bytes 1572872 | tf_op jit(solution)/shard_map/ppermute | solution.py:580
  176.2 14.9 %collective-permute-start.23 = (bf16[4,128,1024]{2,1,0:T(8,128)(2,1)}, bf16[4,128,1024]{2,1,0:T(8,128)(2,1)}, u32[]{:S(2)}, u32[]{:S(2)}) collective-permute-start(bf16[4,128,1024]{2,1,0:T(8,128)(2,1)} %collective-permute-done.12.refs_14_), channel_id=1, source_target_pairs={{0,4},{4,0},{8,12},{12,8},{16,20},{20,16},{24,28},{28,24},{1,5},{5... | collective-permute-start | bytes 3145736 | tf_op jit(solution)/shard_map/ppermute | solution.py:580
  188.4 2.9 %collective-permute-start.24 = (bf16[4,64,1024]{2,1,0:T(8,128)(2,1)}, bf16[4,64,1024]{2,1,0:T(8,128)(2,1)}, u32[]{:S(2)}, u32[]{:S(2)}) collective-permute-start(bf16[4,64,1024]{2,1,0:T(8,128)(2,1)} %copy-done.10), channel_id=1, source_target_pairs={{0,4},{4,0},{8,12},{12,8},{16,20},{20,16},{24,28},{28,24},{1,5},{5... | collective-permute-start | bytes 1572872 | tf_op jit(solution)/shard_map/ppermute | solution.py:580
  189.3 2.6 %collective-permute-start.20 = (bf16[4,512,128]{2,1,0:T(8,128)(2,1)}, bf16[4,512,128]{2,1,0:T(8,128)(2,1)}, u32[]{:S(2)}, u32[]{:S(2)}) collective-permute-start(bf16[4,512,128]{2,1,0:T(8,128)(2,1)} %copy-done.11), channel_id=1, source_target_pairs={{0,4},{4,0},{8,12},{12,8},{16,20},{20,16},{24,28},{28,24},{1,5},{5... | collective-permute-start | bytes 1572872 | tf_op jit(solution)/shard_map/ppermute | solution.py:580
  189.4 3.3 %collective-permute-start.21 = (bf16[4,512,128]{2,1,0:T(8,128)(2,1)}, bf16[4,512,128]{2,1,0:T(8,128)(2,1)}, u32[]{:S(2)}, u32[]{:S(2)}) collective-permute-start(bf16[4,512,128]{2,1,0:T(8,128)(2,1)} %collective-permute-done.16.refs_11_), channel_id=1, source_target_pairs={{0,4},{4,0},{8,12},{12,8},{16,20},{20,16},{24,28},{28,24},{1,5},{5... | collective-permute-start | bytes 1572872 | tf_op jit(solution)/shard_map/ppermute | solution.py:580
  189.9 3.6 %collective-permute-start.25 = (bf16[4,64,1024]{2,1,0:T(8,128)(2,1)}, bf16[4,64,1024]{2,1,0:T(8,128)(2,1)}, u32[]{:S(2)}, u32[]{:S(2)}) collective-permute-start(bf16[4,64,1024]{2,1,0:T(8,128)(2,1)} %copy-done.12), channel_id=1, source_target_pairs={{0,4},{4,0},{8,12},{12,8},{16,20},{20,16},{24,28},{28,24},{1,5},{5... | collective-permute-start | bytes 1572872 | tf_op jit(solution)/shard_map/ppermute | solution.py:580
  (12 other events, 43.6 us)
Sparse Core Ops, SparseCore 0:
  28.2 27.0 all-gather.8
  56.8 47.8 all-gather.10
  119.2 26.9 all-gather.12
  149.3 27.5 all-gather.14
